TPU v7x, 32 devices: a whole 2x2x4 slice. The times are simulated.
32 devices in a mesh: dp: 4 (over y, x), mp: 8 (over z, core).
Axes of the slice: x: 2, y: 2, z: 4, core: 2. Of those that a mesh axis runs over, the one named last changes fastest.
Arguments:
- image_a: bfloat16 [1024, 9216], P('dp', 'mp'), may hold values from -6 to 6
- image_b: bfloat16 [1024, 9216], P('dp', 'mp'), may hold values from -6 to 6
- image_group: int32 [1024], P('dp'), may hold values from 0 to 1
- position_mask: int32 [2, 36], replicated, may hold values 0 or 1
- weight_a: bfloat16 [9216, 4096], P(None, 'mp'), may hold values from -0.0625 to 0.0625
- weight_b: bfloat16 [9216, 4096], P(None, 'mp'), may hold values from -0.0625 to 0.0625
- tower_bias: float32 [2, 4096], P(None, 'mp'), may hold values from -3 to 3
- stitch: float32 [4, 4096], P(None, 'mp'), may hold values from 0.2 to 1
- cotan_a: bfloat16 [1024, 4096], P('dp', 'mp'), may hold values from -6 to 6
- cotan_b: bfloat16 [1024, 4096], P('dp', 'mp'), may hold values from -6 to 6
Outputs:
- stitched_a: bfloat16 [1024, 4096], P('dp')
- stitched_b: bfloat16 [1024, 4096], P('dp')
- grad_image_a: bfloat16 [9216, 1024], P('mp', 'dp')
- grad_image_b: bfloat16 [9216, 1024], P('mp', 'dp')
- grad_weight_a: float32 [9216, 4096], P('dp', 'mp')
- grad_weight_b: float32 [9216, 4096], P('dp', 'mp')
- grad_bias: float32 [2, 4096], P(None, 'mp')
- grad_stitch: float32 [4, 4096], P(None, 'mp')
All inputs are finite; a program needn't handle non-finite values.
Results may differ from a plain program's by a relative error of at most 0.005.
Values may be sent and summed in bfloat16 or wider, within the bound.
No kernel may reach another device: no remote copies, remote signals or barrier semaphores. Data moves between devices by JAX's collectives and lax.ppermute only.
A program may use at most 256 MiB of HBM per device.

v0:
```python
import jax
import jax.numpy as jnp
from jax import lax
from jax.sharding import PartitionSpec as P

CH = 256
POS = 36


def shards(
    image_a,
    image_b,
    image_group,
    position_mask,
    weight_a,
    weight_b,
    tower_bias,
    stitch,
    cotan_a,
    cotan_b,
):
    batch_rows = image_a.shape[0]
    shard_cols = image_a.shape[1]
    first_col = lax.axis_index("mp") * shard_cols
    positions = (first_col + lax.iota(jnp.int32, shard_cols)) // CH
    onehot = (positions[:, None] == lax.iota(jnp.int32, POS)[None, :]).astype(jnp.float32)
    per_position = jnp.dot(onehot, position_mask.astype(jnp.float32).T)
    keep_mask = jnp.where(
        image_group[:, None] == 1, per_position[:, 1][None, :], per_position[:, 0][None, :]
    )
    keep_low = keep_mask.astype(jnp.bfloat16)
    masked_a = image_a * keep_low
    masked_b = image_b * keep_low
    contract_rows = (((0,), (0,)), ((), ()))
    contract_units = (((1,), (1,)), ((), ()))
    pieces = (
        lax.all_gather(masked_a, "mp", axis=1, tiled=True),
        lax.all_gather(masked_b, "mp", axis=1, tiled=True),
    )
    rows_a = weight_a
    rows_b = weight_b
    pre_a = jnp.dot(pieces[0], rows_a, preferred_element_type=jnp.float32)
    pre_b = jnp.dot(pieces[1], rows_b, preferred_element_type=jnp.float32)
    pre_a = pre_a + tower_bias[0][None, :]
    pre_b = pre_b + tower_bias[1][None, :]
    sigma_a = jax.nn.sigmoid(pre_a)
    sigma_b = jax.nn.sigmoid(pre_b)
    hidden_a = pre_a * sigma_a
    hidden_b = pre_b * sigma_b
    local_a = (stitch[0][None, :] * hidden_a + stitch[1][None, :] * hidden_b).astype(jnp.bfloat16)
    local_b = (stitch[2][None, :] * hidden_a + stitch[3][None, :] * hidden_b).astype(jnp.bfloat16)
    stitched_a, stitched_b = (
        lax.all_gather(local_a, "mp", axis=1, tiled=True),
        lax.all_gather(local_b, "mp", axis=1, tiled=True),
    )
    upper_a = cotan_a.astype(jnp.float32)
    upper_b = cotan_b.astype(jnp.float32)
    dhid_a = stitch[0][None, :] * upper_a + stitch[2][None, :] * upper_b
    dhid_b = stitch[1][None, :] * upper_a + stitch[3][None, :] * upper_b
    dpre_a = dhid_a * (sigma_a * (1.0 + pre_a * (1.0 - sigma_a)))
    dpre_b = dhid_b * (sigma_b * (1.0 + pre_b * (1.0 - sigma_b)))
    bias_terms = jnp.stack([jnp.sum(dpre_a, axis=0), jnp.sum(dpre_b, axis=0)])
    stitch_terms = jnp.stack(
        [
            jnp.sum(upper_a * hidden_a, axis=0),
            jnp.sum(upper_a * hidden_b, axis=0),
            jnp.sum(upper_b * hidden_a, axis=0),
            jnp.sum(upper_b * hidden_b, axis=0),
        ]
    )
    grad_bias, grad_stitch = lax.psum((bias_terms, stitch_terms), "dp")
    dlow_a = dpre_a.astype(jnp.bfloat16)
    dlow_b = dpre_b.astype(jnp.bfloat16)
    pieces = (
        lax.all_gather(masked_a, "mp", axis=1, tiled=True),
        lax.all_gather(masked_b, "mp", axis=1, tiled=True),
    )
    block_a = lax.dot_general(pieces[0], dlow_a, contract_rows, preferred_element_type=jnp.float32)
    block_b = lax.dot_general(pieces[1], dlow_b, contract_rows, preferred_element_type=jnp.float32)
    grad_weight_a, grad_weight_b = (
        lax.psum_scatter(block_a, "dp", scatter_dimension=0, tiled=True),
        lax.psum_scatter(block_b, "dp", scatter_dimension=0, tiled=True),
    )
    keep_cols = keep_mask.T
    rows_a = weight_a
    rows_b = weight_b
    part_a = lax.dot_general(rows_a, dlow_a, contract_units, preferred_element_type=jnp.float32)
    part_b = lax.dot_general(rows_b, dlow_b, contract_units, preferred_element_type=jnp.float32)
    summed = lax.psum_scatter(
        jnp.concatenate([part_a, part_b], axis=1), "mp", scatter_dimension=0, tiled=True
    )
    grad_image_a = (summed[:, :batch_rows] * keep_cols).astype(jnp.bfloat16)
    grad_image_b = (summed[:, batch_rows:] * keep_cols).astype(jnp.bfloat16)
    return (
        stitched_a,
        stitched_b,
        grad_image_a,
        grad_image_b,
        grad_weight_a,
        grad_weight_b,
        grad_bias,
        grad_stitch,
    )


def solution(mesh):
    placed = (
        P("dp", "mp"),
        P("dp", "mp"),
        P("dp"),
        P(),
        P(None, "mp"),
        P(None, "mp"),
        P(None, "mp"),
        P(None, "mp"),
        P("dp", "mp"),
        P("dp", "mp"),
    )
    return jax.shard_map(
        shards,
        mesh=mesh,
        in_specs=placed,
        out_specs=(
            P("dp", None),
            P("dp", None),
            P("mp", "dp"),
            P("mp", "dp"),
            P("dp", "mp"),
            P("dp", "mp"),
            P(None, "mp"),
            P(None, "mp"),
        ),
        check_vma=False,
    )
```

profile of v0, /device:TPU:0, one launch (start us, length us, event | category | flops | bytes accessed | tf_op | source)
XLA Modules:
  0.0 735.3 jit_solution(12226432668685692258)
XLA Ops:
  7.2 0.0 all-gather.5.cloned.1.call-start
  7.2 1.0 fusion.4
  8.3 0.7 broadcast_compare_fusion
  9.0 0.0 copy-start.6
  9.0 0.5 copy-done.6
  9.5 2.5 fusion.2
  12.0 0.0 all-gather.5.cloned.1.call-update
  12.0 0.0 all-gather.7.cloned.1.call-start
  12.0 0.7 all-gather.7.cloned.1.call-update
  12.7 0.0 all-gather.9.cloned.1.call-start
  12.8 0.8 fusion.31
  13.5 0.9 fusion.30
  14.4 52.0 %all-gather.5.cloned.1.call-done = bf16[256,9216]{1,0:T(8,128)(2,1)} async-done(((bf16[256,1152]{1,0:T(8,128)(2,1)}), bf16[256,9216]{1,0:T(8,128)(2,1)}) %all-gather.5.cloned.1.call-update) | async-done | bytes 4718608 | tf_op jit(solution)/shard_map/all_gather | solution.py:37
  66.4 0.0 copy-start.8
  66.4 0.0 copy-start.9
  66.4 6.7 convolution_add_fusion.1
  73.1 45.9 %all-gather.7.cloned.1.call-done = bf16[256,9216]{1,0:T(8,128)(2,1)} async-done(((bf16[256,1152]{1,0:T(8,128)(2,1)}), bf16[256,9216]{1,0:T(8,128)(2,1)}) %all-gather.7.cloned.1.call-update) | async-done | bytes 4718608 | tf_op jit(solution)/shard_map/all_gather | solution.py:38
  118.9 0.0 copy-done.8
  118.9 0.0 copy-done.9
  118.9 9.8 %fusion.10 = (f32[512]{0:T(512)}, f32[512]{0:T(512)}, f32[512]{0:T(512)}, f32[512]{0:T(512)}, bf16[256,512]{1,0:T(8,128)(2,1)}, /*index=5*/f32[512]{0:T(512)S(1)...) fusion(bf16[256,512]{1,0:T(8,128)(2,1)S(1)} %copy-done.8, ...), kind=kOutput, calls=%fused_computation.27 | convolution fusion | flops 2422076416 | bytes 16275456 | tf_op jit(solution)/shard_map/dot_general | solution.py:43
  128.8 0.0 all-gather.9.cloned.1.call-update
  128.8 0.0 all-gather.11.cloned.1.call-start
  128.8 0.5 all-gather.11.cloned.1.call-update
  129.4 0.0 reduce-scatter.4.cloned.1.call-start
  129.4 5.2 convolution_bitcast_fusion
  134.6 5.4 convolution_bitcast_fusion.1
  140.1 7.0 pad_maximum_fusion
  147.0 0.0 reduce-scatter.4.cloned.1.call-update
  147.0 0.0 reduce-scatter.6.cloned.1.call-start
  147.1 10.4 %fusion.19 = f32[9216,512]{1,0:T(8,128)} fusion(bf16[256,9216]{1,0:T(8,128)(2,1)} %all-gather.5.cloned.1.call-done, bf16[256,512]{1,0:T(8,128)(2,1)S(1)} %get-tuple-element.37), kind=kOutput, calls=%fused_computation.40 | convolution fusion | flops 2415919104 | bytes 23855104 | tf_op jit(solution)/shard_map/dot_general | solution.py:78
  157.5 0.0 reduce-scatter.6.cloned.1.call-update
  157.5 0.0 reduce-scatter.8.cloned.1.call-start
  157.6 10.5 %fusion.16 = f32[9216,512]{1,0:T(8,128)} fusion(bf16[256,9216]{1,0:T(8,128)(2,1)} %all-gather.7.cloned.1.call-done, bf16[256,512]{1,0:T(8,128)(2,1)S(1)} %get-tuple-element.34), kind=kOutput, calls=%fused_computation.37 | convolution fusion | flops 2415919104 | bytes 23855104 | tf_op jit(solution)/shard_map/dot_general | solution.py:79
  168.1 0.0 copy-start.2
  168.1 0.0 copy-start.3
  168.1 0.0 copy-start.4
  168.1 0.0 copy-start.5
  168.1 0.0 copy-start.7
  168.1 0.0 reduce-scatter.8.cloned.1.call-update
  168.1 0.6 copy-done.2
  168.7 0.0 copy-done.3
  168.7 0.0 copy-done.4
  168.8 0.0 copy-done.5
  168.8 16.6 %all-reduce = (f32[2,512]{1,0:T(2,128)}, f32[4,512]{1,0:T(4,128)}) all-reduce(f32[2,512]{1,0:T(2,128)S(1)} %pad_maximum_fusion.2, f32[4,512]{1,0:T(4,128)S(1)} %pad_maximum_fusion.1), channel_id=1, replica_groups=mesh['dp'=4,'mp'=8] {'dp'}, use_global_device_ids=true, to_apply=%region_5.6 | all-reduce | flops 3072 | bytes 24576 | tf_op jit(solution)/shard_map/psum | solution.py:71
  185.4 0.0 all-gather.9.cloned.1.call-done
  185.4 0.0 copy-start
  185.4 2.0 all-gather.11.cloned.1.call-done
  187.4 189.7 %reduce-scatter.4.cloned.1.call-done = f32[1152,512]{0,1:T(8,128)} async-done(((f32[9216,512]{0,1:T(8,128)}), f32[1152,512]{0,1:T(8,128)}) %reduce-scatter.4.cloned.1.call-update) | async-done | bytes 2359312 | tf_op jit(solution)/shard_map/reduce_scatter | solution.py:89
  377.2 0.0 copy-done.7
  377.2 1.9 fusion.1
  379.0 1.1 copy.18
  380.1 1.1 copy.19
  381.2 168.8 %reduce-scatter.6.cloned.1.call-done = f32[2304,512]{1,0:T(8,128)} async-done(((f32[9216,512]{1,0:T(8,128)}), f32[2304,512]{1,0:T(8,128)}) %reduce-scatter.6.cloned.1.call-update) | async-done | bytes 4718608 | tf_op jit(solution)/shard_map/reduce_scatter | solution.py:81
  549.9 174.9 %reduce-scatter.8.cloned.1.call-done = f32[2304,512]{1,0:T(8,128)} async-done(((f32[9216,512]{1,0:T(8,128)}), f32[2304,512]{1,0:T(8,128)}) %reduce-scatter.8.cloned.1.call-update) | async-done | bytes 4718608 | tf_op jit(solution)/shard_map/reduce_scatter | solution.py:82
  724.8 0.0 copy-start.1
  724.8 0.0 copy-done
  724.8 1.3 copy.22
  726.1 1.0 copy-done.1
  727.2 1.3 copy.23
  (4 shorter events, 0.1 us)
Async XLA Ops:
  7.2 59.2 %all-gather.5.cloned.1.call-start = ((), (), s32[]{:S(2)}) async-start(), calls=%async_computation.3 | async-start | bytes 5308416 | tf_op jit(solution)/shard_map/all_gather | solution.py:37
  9.0 0.5 copy-start.6
  12.0 107.0 %all-gather.7.cloned.1.call-start = ((), (), s32[]{:S(2)}) async-start(), calls=%async_computation.4 | async-start | bytes 5308416 | tf_op jit(solution)/shard_map/all_gather | solution.py:38
  12.7 172.7 %all-gather.9.cloned.1.call-start = ((), (), s32[]{:S(2)}) async-start(), calls=%async_computation.5 | async-start | bytes 2359296 | tf_op jit(solution)/shard_map/all_gather | solution.py:53
  66.4 52.5 %copy-start.8 = (bf16[256,512]{1,0:T(8,128)(2,1)S(1)}, bf16[256,512]{1,0:T(8,128)(2,1)}, u32[]{:S(2)}) copy-start(bf16[256,512]{1,0:T(8,128)(2,1)} %param.18) | copy-start | bytes 786436
  66.4 52.5 %copy-start.9 = (bf16[256,512]{1,0:T(8,128)(2,1)S(1)}, bf16[256,512]{1,0:T(8,128)(2,1)}, u32[]{:S(2)}) copy-start(bf16[256,512]{1,0:T(8,128)(2,1)} %param.19) | copy-start | bytes 786436
  128.8 58.7 %all-gather.11.cloned.1.call-start = ((), (), s32[]{:S(2)}) async-start(), calls=%async_computation.6 | async-start | bytes 2359296 | tf_op jit(solution)/shard_map/all_gather | solution.py:54
  129.4 247.8 %reduce-scatter.4.cloned.1.call-start = ((), (), s32[]{:S(2)}) async-start(), calls=%async_computation.7 | async-start | bytes 21233664 | tf_op jit(solution)/shard_map/reduce_scatter | solution.py:89
  147.0 402.9 %reduce-scatter.6.cloned.1.call-start = ((), (), s32[]{:S(2)}) async-start(), calls=%async_computation.8 | async-start | bytes 23592960 | tf_op jit(solution)/shard_map/reduce_scatter | solution.py:81
  157.5 567.3 %reduce-scatter.8.cloned.1.call-start = ((), (), s32[]{:S(2)}) async-start(), calls=%async_computation.9 | async-start | bytes 23592960 | tf_op jit(solution)/shard_map/reduce_scatter | solution.py:82
  168.1 0.7 copy-start.2
  168.1 0.7 copy-start.3
  168.1 0.7 copy-start.4
  168.1 0.7 copy-start.5
  168.1 209.1 %copy-start.7 = (pred[256]{0:T(512)(128)(4,1)S(1)}, pred[256]{0:T(512)(128)(4,1)}, u32[]{:S(2)}) copy-start(pred[256]{0:T(512)(128)(4,1)} %copy-done.6) | copy-start | bytes 772
  185.4 539.4 %copy-start = (bf16[256,4096]{1,0:T(8,128)(2,1)S(1)}, bf16[256,4096]{1,0:T(8,128)(2,1)}, u32[]{:S(2)}) copy-start(bf16[256,4096]{1,0:T(8,128)(2,1)} %all-gather.9.cloned.1.call-done) | copy-start | bytes 6291460
  724.8 2.3 copy-start.1
Sparse Core Ops, SparseCore 0:
  12.1 54.2 all-gather.4
  68.6 50.2 all-gather.6
  128.9 27.8 all-gather.8
  158.8 28.5 all-gather.10
  189.6 187.4 reduce-scatter.3
  380.7 169.2 reduce-scatter.5
  553.9 170.8 reduce-scatter.7
where the time goes:
time: 736 us; the launch traced here: 735 us
  waiting for transfers between devices  635 us (86%)
  matrix products  49 us (7%)
  blocking collectives  16.6 us (2%)
  between operations  14.2 us (2%)
  other arithmetic  12 us (2%)
  local copies, waits for them, and re-layouts  8.65 us (1%)
    reduce_scatter x1, waiting for transfers between devices, shards(): lax.psum_scatter(jnp.concatenate([part_a, part_b], axis=1), 'mp', scatter...  190 us
    reduce_scatter x1, waiting for transfers between devices, shards(): lax.psum_scatter(block_b, 'dp', scatter_dimension=0, tiled=True)  175 us
    reduce_scatter x1, waiting for transfers between devices, shards(): lax.psum_scatter(block_a, 'dp', scatter_dimension=0, tiled=True)  169 us
    all_gather x1, waiting for transfers between devices, shards(): lax.all_gather(masked_a, 'mp', axis=1, tiled=True)  52 us
    all_gather x1, waiting for transfers between devices, shards(): lax.all_gather(masked_b, 'mp', axis=1, tiled=True)  45.9 us
    psum x1, blocking collectives, shards(): grad_bias, grad_stitch = lax.psum((bias_terms, stitch_terms), 'dp')  16.6 us
  transfers between devices with their start and end apart: 7, of which 6 were waited for; matrix products, arithmetic and copies ran while one was open for 7% of the time, Pallas kernels for 0%

commit v1 on v0

v1 whole, which is shorter than its diff:
```python
import functools

import jax
import jax.numpy as jnp
from jax import lax
from jax.experimental import pallas as pl
from jax.experimental.pallas import tpu as pltpu
from jax.sharding import PartitionSpec as P

CH = 256
POS = 36


def keep_block(image_group, position_mask, first_col, cols):
    positions = (first_col + lax.iota(jnp.int32, cols)) // CH
    onehot = (positions[:, None] == lax.iota(jnp.int32, POS)[None, :]).astype(jnp.float32)
    per_position = jnp.dot(onehot, position_mask.astype(jnp.float32).T)
    return jnp.where(
        image_group[:, None] == 1, per_position[:, 1][None, :], per_position[:, 0][None, :]
    )


def general_shards(
    image_a,
    image_b,
    image_group,
    position_mask,
    weight_a,
    weight_b,
    tower_bias,
    stitch,
    cotan_a,
    cotan_b,
):
    batch_rows = image_a.shape[0]
    shard_cols = image_a.shape[1]
    first_col = lax.axis_index("mp") * shard_cols
    keep_mask = keep_block(image_group, position_mask, first_col, shard_cols)
    keep_low = keep_mask.astype(jnp.bfloat16)
    contract_rows = (((0,), (0,)), ((), ()))
    contract_units = (((1,), (1,)), ((), ()))
    full_a = lax.all_gather(image_a * keep_low, "mp", axis=1, tiled=True)
    full_b = lax.all_gather(image_b * keep_low, "mp", axis=1, tiled=True)
    pre_a = jnp.dot(full_a, weight_a, preferred_element_type=jnp.float32) + tower_bias[0][None, :]
    pre_b = jnp.dot(full_b, weight_b, preferred_element_type=jnp.float32) + tower_bias[1][None, :]
    sigma_a = jax.nn.sigmoid(pre_a)
    sigma_b = jax.nn.sigmoid(pre_b)
    hidden_a = pre_a * sigma_a
    hidden_b = pre_b * sigma_b
    local_a = (stitch[0][None, :] * hidden_a + stitch[1][None, :] * hidden_b).astype(jnp.bfloat16)
    local_b = (stitch[2][None, :] * hidden_a + stitch[3][None, :] * hidden_b).astype(jnp.bfloat16)
    stitched_a = lax.all_gather(local_a, "mp", axis=1, tiled=True)
    stitched_b = lax.all_gather(local_b, "mp", axis=1, tiled=True)
    upper_a = cotan_a.astype(jnp.float32)
    upper_b = cotan_b.astype(jnp.float32)
    dhid_a = stitch[0][None, :] * upper_a + stitch[2][None, :] * upper_b
    dhid_b = stitch[1][None, :] * upper_a + stitch[3][None, :] * upper_b
    dpre_a = dhid_a * (sigma_a * (1.0 + pre_a * (1.0 - sigma_a)))
    dpre_b = dhid_b * (sigma_b * (1.0 + pre_b * (1.0 - sigma_b)))
    bias_terms = jnp.stack([jnp.sum(dpre_a, axis=0), jnp.sum(dpre_b, axis=0)])
    stitch_terms = jnp.stack(
        [
            jnp.sum(upper_a * hidden_a, axis=0),
            jnp.sum(upper_a * hidden_b, axis=0),
            jnp.sum(upper_b * hidden_a, axis=0),
            jnp.sum(upper_b * hidden_b, axis=0),
        ]
    )
    grad_bias, grad_stitch = lax.psum((bias_terms, stitch_terms), "dp")
    dlow_a = dpre_a.astype(jnp.bfloat16)
    dlow_b = dpre_b.astype(jnp.bfloat16)
    block_a = lax.dot_general(full_a, dlow_a, contract_rows, preferred_element_type=jnp.float32)
    block_b = lax.dot_general(full_b, dlow_b, contract_rows, preferred_element_type=jnp.float32)
    grad_weight_a = lax.psum_scatter(block_a, "dp", scatter_dimension=0, tiled=True)
    grad_weight_b = lax.psum_scatter(block_b, "dp", scatter_dimension=0, tiled=True)
    part_a = lax.dot_general(weight_a, dlow_a, contract_units, preferred_element_type=jnp.float32)
    part_b = lax.dot_general(weight_b, dlow_b, contract_units, preferred_element_type=jnp.float32)
    summed = lax.psum_scatter(
        jnp.concatenate([part_a, part_b], axis=1), "mp", scatter_dimension=0, tiled=True
    )
    keep_cols = keep_mask.T
    grad_image_a = (summed[:, :batch_rows] * keep_cols).astype(jnp.bfloat16)
    grad_image_b = (summed[:, batch_rows:] * keep_cols).astype(jnp.bfloat16)
    return (
        stitched_a,
        stitched_b,
        grad_image_a,
        grad_image_b,
        grad_weight_a,
        grad_weight_b,
        grad_bias,
        grad_stitch,
    )


SWAP_CORE = [(d, d ^ 1) for d in range(8)]
FLIP_X = [(d, d ^ 1) for d in range(4)]
FLIP_Y = [(d, d ^ 2) for d in range(4)]
FLIP_XY = [(d, d ^ 3) for d in range(4)]
ENDS_IN = [(0, 2), (1, 3), (6, 4), (7, 5)]
MIDS = [(2, 4), (3, 5), (4, 2), (5, 3)]
ENDS_OUT = [(2, 0), (3, 1), (4, 6), (5, 7)]
SLOTS = ((3, 2, 1, 0), (3, 2, 0, 1), (0, 1, 3, 2), (0, 1, 2, 3))


def part_kernel(where, w_ref, wo_ref, dz_ref, dzo_ref, out_ref):
    total = lax.dot_general(
        w_ref[...], dz_ref[...], (((1,), (1,)), ((), ())), preferred_element_type=jnp.float32
    )
    total += lax.dot_general(
        wo_ref[...], dzo_ref[...], (((1,), (1,)), ((), ())), preferred_element_type=jnp.float32
    )
    out_ref[...] = total.astype(jnp.bfloat16)


def part_block(block, core, weight, weight_other, dz, dz_other, cols):
    rows, units = dz.shape
    tile = cols // 3
    steps = cols // tile
    where = jnp.stack([2 * block + core, block]).astype(jnp.int32)
    return pl.pallas_call(
        part_kernel,
        out_shape=jax.ShapeDtypeStruct((cols, rows), jnp.bfloat16),
        grid_spec=pltpu.PrefetchScalarGridSpec(
            num_scalar_prefetch=1,
            grid=(steps,),
            in_specs=[
                pl.BlockSpec((tile, units), lambda t, where: (where[0] * steps + t, 0)),
                pl.BlockSpec((tile, units), lambda t, where: (where[1] * steps + t, 0)),
                pl.BlockSpec((rows, units), lambda t, where: (0, 0)),
                pl.BlockSpec((rows, units), lambda t, where: (0, 0)),
            ],
            out_specs=pl.BlockSpec((tile, rows), lambda t, where: (t, 0)),
        ),
        cost_estimate=pl.CostEstimate(
            flops=4 * cols * rows * units, bytes_accessed=2 * cols * (2 * units + rows), transcendentals=0
        ),
        name="part_block",
    )(where, weight, weight_other, dz, dz_other)


def weight_kernel(where, own, px, py, pd, qx, qy, qd, dz0, dzx, dzy, dzd, out_ref):
    def dots(pieces):
        total = None
        for image, dz in zip(pieces, (dz0, dzx, dzy, dzd)):
            term = lax.dot_general(
                image[...], dz[...], (((0,), (0,)), ((), ())), preferred_element_type=jnp.float32
            )
            total = term if total is None else total + term
        out_ref[...] = total

    same = pl.program_id(0) == where[1]

    @pl.when(same)
    def _():
        dots((own, px, py, pd))

    @pl.when(jnp.logical_not(same))
    def _():
        dots((own, qx, qy, qd))


def weight_grad(quarter, core, full, near, far, dzs):
    rows, units = dzs[0].shape
    cols = near[0].shape[1]
    tile = cols // 3
    steps = cols // tile
    where = jnp.stack([quarter, core]).astype(jnp.int32)
    own = pl.BlockSpec((rows, tile), lambda p, t, where: (0, (2 * where[0] + p) * steps + t))
    mine = pl.BlockSpec((rows, tile), lambda p, t, where: (0, jnp.where(p == where[1], t, 0)))
    other = pl.BlockSpec((rows, tile), lambda p, t, where: (0, jnp.where(p == where[1], 0, t)))
    whole = pl.BlockSpec((rows, units), lambda p, t, where: (0, 0))
    return pl.pallas_call(
        weight_kernel,
        out_shape=jax.ShapeDtypeStruct((2 * cols, units), jnp.float32),
        grid_spec=pltpu.PrefetchScalarGridSpec(
            num_scalar_prefetch=1,
            grid=(2, steps),
            in_specs=[own] + [mine] * 3 + [other] * 3 + [whole] * 4,
            out_specs=pl.BlockSpec((tile, units), lambda p, t, where: (p * steps + t, 0)),
        ),
        cost_estimate=pl.CostEstimate(
            flops=16 * cols * rows * units,
            bytes_accessed=16 * cols * rows + 8 * cols * units,
            transcendentals=0,
        ),
        name="weight_grad",
    )(where, full, *near, *far, *dzs)


def fast_shards(
    image_a,
    image_b,
    image_group,
    position_mask,
    weight_a,
    weight_b,
    tower_bias,
    stitch,
    cotan_a,
    cotan_b,
):
    rows, cols = image_a.shape
    units = weight_a.shape[1]
    place = lax.axis_index("mp")
    z = place // 2
    core = place % 2
    quarter = lax.axis_index("dp")
    keep_mask = keep_block(image_group, position_mask, place * cols, cols)
    keep_low = keep_mask.astype(jnp.bfloat16)
    masked_a = image_a * keep_low
    masked_b = image_b * keep_low
    full_a = lax.all_gather(masked_a, "mp", axis=1, tiled=True)
    full_b = lax.all_gather(masked_b, "mp", axis=1, tiled=True)
    slots = jnp.take(jnp.asarray(SLOTS, jnp.int32), z, axis=0)

    def other_weight(weight):
        blocks = weight.reshape(4, 2, cols, units)
        send = lax.dynamic_index_in_dim(blocks, 1 - core, axis=1, keepdims=False)
        return lax.ppermute(send.reshape(4 * cols, units), "mp", SWAP_CORE)

    upper_a = cotan_a.astype(jnp.float32)
    upper_b = cotan_b.astype(jnp.float32)

    def tower(full, weight, bias, unit_a, unit_b):
        pre = jnp.dot(full, weight, preferred_element_type=jnp.float32) + bias[None, :]
        sigma = jax.nn.sigmoid(pre)
        hidden = pre * sigma
        dhid = unit_a[None, :] * upper_a + unit_b[None, :] * upper_b
        dpre = dhid * (sigma * (1.0 + pre * (1.0 - sigma)))
        sums = jnp.stack(
            [
                jnp.sum(dpre, axis=0),
                jnp.sum(upper_a * hidden, axis=0),
                jnp.sum(upper_b * hidden, axis=0),
            ]
        )
        return hidden, dpre.astype(jnp.bfloat16), sums

    def image_grad(weight, weight_other, dz):
        dz_other = lax.ppermute(dz, "mp", SWAP_CORE)
        first, second, third, kept = [
            part_block(slots[k], core, weight, weight_other, dz, dz_other, cols) for k in range(4)
        ]

        def add(*terms):
            total = terms[0].astype(jnp.float32)
            for term in terms[1:]:
                total = total + term.astype(jnp.float32)
            return total

        got_first = lax.ppermute(first, "mp", ENDS_IN)
        got_second = lax.ppermute(second, "mp", ENDS_IN)
        got_third = lax.ppermute(third, "mp", ENDS_IN)
        cross_first = lax.ppermute(add(first, got_first).astype(jnp.bfloat16), "mp", MIDS)
        cross_second = lax.ppermute(add(second, got_second).astype(jnp.bfloat16), "mp", MIDS)
        last = lax.ppermute(add(third, cross_first).astype(jnp.bfloat16), "mp", ENDS_OUT)
        total = add(kept, last, got_third, cross_second)
        return (total * keep_mask.T).astype(jnp.bfloat16)

    def spread(full):
        near = []
        far = []
        for step, flip in ((1, FLIP_X), (2, FLIP_Y), (3, FLIP_XY)):
            block = 2 * (quarter ^ step) + core
            send = lax.dynamic_slice_in_dim(full, block * cols, cols, axis=1)
            got = lax.ppermute(send, "dp", flip)
            near.append(got)
            far.append(lax.ppermute(got, "mp", SWAP_CORE))
        return near, far

    def around(x):
        return [x] + [lax.ppermute(x, "dp", flip) for flip in (FLIP_X, FLIP_Y, FLIP_XY)]

    other_a = other_weight(weight_a)
    other_b = other_weight(weight_b)
    hidden_a, dz_a, sums_a = tower(full_a, weight_a, tower_bias[0], stitch[0], stitch[2])
    grad_image_a = image_grad(weight_a, other_a, dz_a)
    near_a, far_a = spread(full_a)
    grad_weight_a = weight_grad(quarter, core, full_a, near_a, far_a, around(dz_a))

    hidden_b, dz_b, sums_b = tower(full_b, weight_b, tower_bias[1], stitch[1], stitch[3])
    local_a = (stitch[0][None, :] * hidden_a + stitch[1][None, :] * hidden_b).astype(jnp.bfloat16)
    local_b = (stitch[2][None, :] * hidden_a + stitch[3][None, :] * hidden_b).astype(jnp.bfloat16)
    stitched = lax.all_gather(jnp.concatenate([local_a, local_b]), "mp", axis=1, tiled=True)
    grad_image_b = image_grad(weight_b, other_b, dz_b)
    near_b, far_b = spread(full_b)
    grad_weight_b = weight_grad(quarter, core, full_b, near_b, far_b, around(dz_b))

    own, by_x, by_y, by_xy = around(jnp.concatenate([sums_a, sums_b]))
    sums = (own + by_x) + (by_y + by_xy)
    grad_bias = jnp.stack([sums[0], sums[3]])
    grad_stitch = jnp.stack([sums[1], sums[4], sums[2], sums[5]])
    return (
        stitched[:rows],
        stitched[rows:],
        grad_image_a,
        grad_image_b,
        grad_weight_a,
        grad_weight_b,
        grad_bias,
        grad_stitch,
    )


def solution(mesh):
    placed = (
        P("dp", "mp"),
        P("dp", "mp"),
        P("dp"),
        P(),
        P(None, "mp"),
        P(None, "mp"),
        P(None, "mp"),
        P(None, "mp"),
        P("dp", "mp"),
        P("dp", "mp"),
    )
    fits = mesh.shape["dp"] == 4 and mesh.shape["mp"] == 8
    return jax.shard_map(
        fast_shards if fits else general_shards,
        mesh=mesh,
        in_specs=placed,
        out_specs=(
            P("dp", None),
            P("dp", None),
            P("mp", "dp"),
            P("mp", "dp"),
            P("dp", "mp"),
            P("dp", "mp"),
            P(None, "mp"),
            P(None, "mp"),
        ),
        check_vma=False,
    )
```

time: 736 us -> 310 us (0.42)
  waiting for transfers between devices: 635 us -> 118 us
  starting transfers between devices: 0.28 us -> 58.6 us
  Pallas kernels: 0 us -> 55.5 us
  matrix products: 49 us -> 16.8 us
  blocking collectives: 16.6 us -> 0 us
  local copies, waits for them, and re-layouts: 8.65 us -> 20.4 us
  other arithmetic: 12 us -> 20.9 us
    reduce_scatter x3 -> x0, waiting for transfers between devices: 533 us -> none  [the longest x1 190 us: shards(): lax.psum_scatter(jnp.concatenate([part_a, part_b], axis=1), 'mp', scatter...]
    ppermute x0 -> x37, starting transfers between devices: none -> 58.4 us  [the longest x2 23.9 us: image_grad(): got_third = lax.ppermute(third, 'mp', ENDS_IN)]
    pallas_call x0 -> x10, Pallas kernels: none -> 55.5 us  [the longest x8 37.3 us: part_block(): pl.pallas_call(part_kernel, out_shape=jax.ShapeDtypeStruct((cols, rows),...]
    dot_general x7 -> x3, matrix products: 49 us -> 16.8 us  [the longest x2 15.8 us: tower(): jnp.dot(full, weight, preferred_element_type=jnp.float32) + bias[None, :]]
    ppermute x0 -> x37, waiting for transfers between devices: none -> 27.1 us  [the longest x6 22.8 us: spread(): got = lax.ppermute(send, 'dp', flip)]
    psum x1 -> x0, blocking collectives: 16.6 us -> none  [shards(): grad_bias, grad_stitch = lax.psum((bias_terms, stitch_terms), 'dp')]
    dynamic_slice x0 -> x4, local copies, waits for them, and re-layouts: none -> 13.1 us  [the longest x2 7.71 us: other_weight(): send = lax.dynamic_index_in_dim(blocks, 1 - core, axis=1, keepdims=False)]
    all_gather x4 -> x3, waiting for transfers between devices: 99.9 us -> 89.7 us  [the longest x1 45.9 us: fast_shards(): full_a = lax.all_gather(masked_a, 'mp', axis=1, tiled=True)]
  transfers between devices with their start and end apart: 7 -> 40, of which waited for: 6 -> 8; matrix products, arithmetic and copies ran while one was open for 7% -> 16% of each run, Pallas kernels for 0% -> 18%
where the time goes in v1:
time: 310 us; the launch traced here: 307 us
  waiting for transfers between devices  118 us (38%)
  starting transfers between devices  58.6 us (19%)
  Pallas kernels  55.5 us (18%)
  other arithmetic  20.9 us (7%)
  local copies, waits for them, and re-layouts  20.4 us (7%)
  between operations  17 us (5%)
  matrix products  16.8 us (5%)
    all_gather x1, waiting for transfers between devices, fast_shards(): full_a = lax.all_gather(masked_a, 'mp', axis=1, tiled=True)  45.9 us
    all_gather x1, waiting for transfers between devices, fast_shards(): full_b = lax.all_gather(masked_b, 'mp', axis=1, tiled=True)  43.8 us
    pallas_call x8, Pallas kernels, part_block(): pl.pallas_call(part_kernel, out_shape=jax.ShapeDtypeStruct((cols, rows),...  37.3 us
    ppermute x2, starting transfers between devices, image_grad(): got_third = lax.ppermute(third, 'mp', ENDS_IN)  23.9 us
    ppermute x6, waiting for transfers between devices, spread(): got = lax.ppermute(send, 'dp', flip)  22.8 us
    pallas_call x2, Pallas kernels, weight_grad(): pl.pallas_call(weight_kernel, out_shape=jax.ShapeDtypeStruct((2 * cols, u...  18.2 us
    dot_general x2, matrix products, tower(): jnp.dot(full, weight, preferred_element_type=jnp.float32) + bias[None, :]  15.8 us
    ppermute x9, starting transfers between devices, around(): lax.ppermute(x, 'dp', flip)  11.5 us
  transfers between devices with their start and end apart: 40, of which 8 were waited for; matrix products, arithmetic and copies ran while one was open for 16% of the time, Pallas kernels for 18%

profile of v1, /device:TPU:0, one launch (start us, length us, event | category | flops | bytes accessed | tf_op | source)
XLA Modules:
  0.0 306.7 jit_solution(5112790352965278670)
XLA Ops:
  7.2 1.0 fusion.4
  8.3 0.7 broadcast_compare_fusion
  9.0 2.5 fusion.2
  11.5 0.7 all-gather.4.cloned.1.call-update
  12.3 5.2 %constant_dynamic-slice_fusion.7 = bf16[4,1,1152,512]{3,2,1,0:T(8,128)(2,1)} fusion(bf16[4,2,1152,512]{3,2,1,0:T(8,128)(2,1)} %bitcast.38, s32[]{:T(128)S(6)} %select_n.58), kind=kLoop, calls=%fused_computation.62 | loop fusion | bytes 9437188 | tf_op jit(solution)/shard_map/jit(dynamic_index_in_dim)/dynamic_slice | solution.py:219
  18.0 1.1 copy-done
  19.1 2.5 constant_dynamic-slice_fusion.8
  22.1 43.8 %all-gather.6.cloned.1.call-done.own = bf16[256,9216]{1,0:T(8,128)(2,1)} async-done(((bf16[256,1152]{1,0:T(8,128)(2,1)}), bf16[256,9216]{1,0:T(8,128)(2,1)}) %all-gather.6.cloned.1.call-update) | async-done | bytes 4718608 | tf_op jit(solution)/shard_map/all_gather | solution.py:214
  65.9 6.7 %convolution_add_fusion = f32[256,512]{1,0:T(8,128)S(1)} fusion(bf16[256,9216]{1,0:T(8,128)(2,1)} %all-gather.6.cloned.1.call-done.own, bf16[9216,512]{1,0:T(8,128)(2,1)} %w_ref.15, f32[512]{0:T(512)S(1)} %bitcast.47), kind=kOutput, calls=%fused_computation.2 | convolution fusion | flops 2416050176 | bytes 14682112 | tf_op jit(solution)/shard_map/dot_general | solution.py:226
  72.6 45.9 %all-gather.4.cloned.1.call-done.own = bf16[256,9216]{1,0:T(8,128)(2,1)} async-done(((bf16[256,1152]{1,0:T(8,128)(2,1)}), bf16[256,9216]{1,0:T(8,128)(2,1)}) %all-gather.4.cloned.1.call-update) | async-done | bytes 4718608 | tf_op jit(solution)/shard_map/all_gather | solution.py:213
  118.4 9.1 %fusion.11 = (f32[512]{0:T(512)S(1)}, f32[512]{0:T(512)S(1)}, f32[512]{0:T(512)S(1)}, f32[512]{0:T(512)S(1)}, bf16[256,512]{1,0:T(8,128)(2,1)S(1)}, /*index=5*/f...) fusion(bf16[256,512]{1,0:T(8,128)(2,1)S(1)} %copy-done.36, ...), kind=kOutput, calls=%fused_computation.31 | convolution fusion | flops 2422076416 | bytes 16275456 | tf_op jit(solution)/shard_map/dot_general | solution.py:226
  127.6 0.9 pad_maximum_fusion
  128.5 0.7 broadcast_select_fusion
  132.4 1.2 pad_add_fusion.1.where
  133.7 1.2 pad_add_fusion.where
  135.5 1.9 pad_add_fusion.2
  137.4 1.6 collective-permute-start.35
  139.0 1.5 collective-permute-start.36
  140.4 2.7 constant_dynamic-slice_fusion.4
  144.1 1.5 collective-permute-start.23
  145.7 1.5 collective-permute-start.24
  147.6 2.7 constant_dynamic-slice_fusion.1
  150.4 4.7 %part_block.14 = bf16[1152,256]{1,0:T(8,128)(2,1)} custom-call(s32[2]{0:T(128)} %get-tuple-element.74.where, bf16[9216,512]{1,0:T(8,128)(2,1)} %w_ref.15, bf16[4608,512]{1,0:T(8,128)(2,1)} %collective-permute-done.8.wo_ref, bf16[256,512]{1,0:T(8,128)(2,1)} %get-tuple-element.50.dz_ref.dz0, bf16[256,512]{1,0:T(8,128)(2,1)} %copy-done.2), custom_call_target="tpu_custom_call" | custom-call | flops 603979776 | bytes 2949120 | tf_op jit(solution)/shard_map/part_block/pallas_call | solution.py:121
  155.1 1.6 collective-permute-start.34
  156.6 4.7 %part_block.10 = bf16[1152,256]{1,0:T(8,128)(2,1)} custom-call(s32[2]{0:T(128)} %get-tuple-element.74.where, bf16[9216,512]{1,0:T(8,128)(2,1)} %w_ref.11, bf16[4608,512]{1,0:T(8,128)(2,1)} %collective-permute-done.wo_ref, bf16[256,512]{1,0:T(8,128)(2,1)} %copy-done.1, bf16[256,512]{1,0:T(8,128)(2,1)} %copy-done.3), custom_call_target="tpu_custom_call" | custom-call | flops 603979776 | bytes 2949120 | tf_op jit(solution)/shard_map/part_block/pallas_call | solution.py:121
  161.3 2.2 collective-permute-done.34
  163.5 1.4 collective-permute-start.32
  166.1 2.8 collective-permute-start.10
  168.9 2.1 collective-permute-start.2
  171.6 1.4 collective-permute-done.32.dzy
  173.0 1.5 collective-permute-start.33
  174.5 0.6 pad_maximum_fusion.1
  175.1 4.6 %part_block.15 = bf16[1152,256]{1,0:T(8,128)(2,1)} custom-call(s32[2]{0:T(128)} %get-tuple-element.75.where, bf16[9216,512]{1,0:T(8,128)(2,1)} %w_ref.15, bf16[4608,512]{1,0:T(8,128)(2,1)} %collective-permute-done.8.wo_ref, bf16[256,512]{1,0:T(8,128)(2,1)} %get-tuple-element.50.dz_ref.dz0, bf16[256,512]{1,0:T(8,128)(2,1)} %copy-done.2), custom_call_target="tpu_custom_call" | custom-call | flops 603979776 | bytes 2949120 | tf_op jit(solution)/shard_map/part_block/pallas_call | solution.py:121
  179.7 4.6 %part_block.11 = bf16[1152,256]{1,0:T(8,128)(2,1)} custom-call(s32[2]{0:T(128)} %get-tuple-element.75.where, bf16[9216,512]{1,0:T(8,128)(2,1)} %w_ref.11, bf16[4608,512]{1,0:T(8,128)(2,1)} %collective-permute-done.wo_ref, bf16[256,512]{1,0:T(8,128)(2,1)} %copy-done.1, bf16[256,512]{1,0:T(8,128)(2,1)} %copy-done.3), custom_call_target="tpu_custom_call" | custom-call | flops 603979776 | bytes 2949120 | tf_op jit(solution)/shard_map/part_block/pallas_call | solution.py:121
  184.4 4.6 %part_block.13 = bf16[1152,256]{1,0:T(8,128)(2,1)} custom-call(s32[2]{0:T(128)} %pad_add_fusion.1.where, bf16[9216,512]{1,0:T(8,128)(2,1)} %w_ref.15, bf16[4608,512]{1,0:T(8,128)(2,1)} %collective-permute-done.8.wo_ref, bf16[256,512]{1,0:T(8,128)(2,1)} %get-tuple-element.50.dz_ref.dz0, bf16[256,512]{1,0:T(8,128)(2,1)} %copy-done.2), custom_call_target="tpu_custom_call" | custom-call | flops 603979776 | bytes 2949120 | tf_op jit(solution)/shard_map/part_block/pallas_call | solution.py:121
  189.0 4.8 %part_block.9 = bf16[1152,256]{1,0:T(8,128)(2,1)} custom-call(s32[2]{0:T(128)} %pad_add_fusion.1.where, bf16[9216,512]{1,0:T(8,128)(2,1)} %w_ref.11, bf16[4608,512]{1,0:T(8,128)(2,1)} %collective-permute-done.wo_ref, bf16[256,512]{1,0:T(8,128)(2,1)} %copy-done.1, bf16[256,512]{1,0:T(8,128)(2,1)} %copy-done.3), custom_call_target="tpu_custom_call" | custom-call | flops 603979776 | bytes 2949120 | tf_op jit(solution)/shard_map/part_block/pallas_call | solution.py:121
  193.8 1.5 collective-permute-start.18
  195.8 1.5 collective-permute-start.26
  197.4 1.9 collective-permute-start.14
  199.3 1.3 collective-permute-start.6
  200.7 1.2 add_convert_fusion.2
  201.9 1.3 add_convert_fusion.5
  203.2 8.0 %collective-permute-done.18.pd = bf16[256,1152]{1,0:T(8,128)(2,1)S(1)} collective-permute-done((bf16[256,1152]{1,0:T(8,128)(2,1)}, bf16[256,1152]{1,0:T(8,128)(2,1)S(1)}, u32[]{:S(2)}, u32[]{:S(2)}) %collective-permute-start.18) | collective-permute-done | bytes 589856 | tf_op jit(solution)/shard_map/ppermute | solution.py:267
  211.3 1.4 collective-permute-start.27
  212.7 10.2 %collective-permute-done.25.px = bf16[256,1152]{1,0:T(8,128)(2,1)S(1)} collective-permute-done((bf16[256,1152]{1,0:T(8,128)(2,1)}, bf16[256,1152]{1,0:T(8,128)(2,1)S(1)}, u32[]{:S(2)}, u32[]{:S(2)}) %collective-permute-start.25) | collective-permute-done | bytes 589856 | tf_op jit(solution)/shard_map/ppermute | solution.py:267
  222.9 2.0 collective-permute-start.13
  225.0 0.7 collective-permute-start.11
  225.8 0.7 collective-permute-start.3
  226.5 1.0 add_convert_fusion
  227.4 1.0 add_convert_fusion.3
  228.4 4.6 %collective-permute-done.27.pd = bf16[256,1152]{1,0:T(8,128)(2,1)S(1)} collective-permute-done((bf16[256,1152]{1,0:T(8,128)(2,1)S(1)}, bf16[256,1152]{1,0:T(8,128)(2,1)S(1)}, u32[]{:S(2)}, u32[]{:S(2)}) %collective-permute-start.27) | collective-permute-done | bytes 589856 | tf_op jit(solution)/shard_map/ppermute | solution.py:267
  234.7 1.0 add_convert_fusion.1
  235.6 1.0 add_convert_fusion.4
  236.7 21.9 %collective-permute-start.5 = (bf16[1152,256]{1,0:T(8,128)(2,1)S(1)}, bf16[1152,256]{1,0:T(8,128)(2,1)S(1)}, u32[]{:S(2)}, u32[]{:S(2)}) collective-permute-start(bf16[1152,256]{1,0:T(8,128)(2,1)S(1)} %copy-done.6), channel_id=1, source_target_pairs={{0,2},{1,3},{6,4},{7,5},{8,10},{9,11},{14,12},{15,13},{16,18},{17,... | collective-permute-start | bytes 1769480 | tf_op jit(solution)/shard_map/ppermute | solution.py:254
  258.6 0.7 collective-permute-start.15
  259.4 1.5 collective-permute-start.7
  260.9 1.3 collective-permute-start.12
  262.2 1.3 collective-permute-start.4
  264.2 4.6 %part_block.12 = bf16[1152,256]{1,0:T(8,128)(2,1)} custom-call(s32[2]{0:T(128)} %pad_add_fusion.where, bf16[9216,512]{1,0:T(8,128)(2,1)} %w_ref.15, bf16[4608,512]{1,0:T(8,128)(2,1)} %collective-permute-done.8.wo_ref, bf16[256,512]{1,0:T(8,128)(2,1)} %get-tuple-element.50.dz_ref.dz0, bf16[256,512]{1,0:T(8,128)(2,1)} %copy-done.2), custom_call_target="tpu_custom_call" | custom-call | flops 603979776 | bytes 2949120 | tf_op jit(solution)/shard_map/part_block/pallas_call | solution.py:121
  268.8 4.7 %part_block.8 = bf16[1152,256]{1,0:T(8,128)(2,1)} custom-call(s32[2]{0:T(128)} %pad_add_fusion.where, bf16[9216,512]{1,0:T(8,128)(2,1)} %w_ref.11, bf16[4608,512]{1,0:T(8,128)(2,1)} %collective-permute-done.wo_ref, bf16[256,512]{1,0:T(8,128)(2,1)} %copy-done.1, bf16[256,512]{1,0:T(8,128)(2,1)} %copy-done.3), custom_call_target="tpu_custom_call" | custom-call | flops 603979776 | bytes 2949120 | tf_op jit(solution)/shard_map/part_block/pallas_call | solution.py:121
  273.5 9.0 %weight_grad.2 = f32[2304,512]{1,0:T(8,128)} custom-call(s32[2]{0:T(128)} %pad_add_fusion.4.where, bf16[256,9216]{1,0:T(8,128)(2,1)} %all-gather.4.cloned.1.call-done.own, bf16[256,1152]{1,0:T(8,128)(2,1)} %copy-done.12, bf16[256,1152]{1,0:T(8,128)(2,1)} %copy-done.13, bf16[256,1152]{1,0:T(8,128)(2,1)} %copy-done.15, bf16[256,1152]{1,0:T(8,128)(2,1)} %copy-done.20, ...), custom_call_target="tpu_custom_call" | custom-call | flops 2415919104 | bytes 9437184 | tf_op jit(solution)/shard_map/weight_grad/pallas_call | solution.py:173
  282.5 9.2 %weight_grad.3 = f32[2304,512]{1,0:T(8,128)} custom-call(s32[2]{0:T(128)} %pad_add_fusion.4.where, bf16[256,9216]{1,0:T(8,128)(2,1)} %all-gather.6.cloned.1.call-done.own, bf16[256,1152]{1,0:T(8,128)(2,1)} %copy-done.14, bf16[256,1152]{1,0:T(8,128)(2,1)} %copy-done.16, bf16[256,1152]{1,0:T(8,128)(2,1)} %copy-done.19, bf16[256,1152]{1,0:T(8,128)(2,1)} %copy-done.22, ...), custom_call_target="tpu_custom_call" | custom-call | flops 2415919104 | bytes 9437184 | tf_op jit(solution)/shard_map/weight_grad/pallas_call | solution.py:173
  291.8 3.7 %fusion.1 = (bf16[1152,256]{1,0:T(8,128)(2,1)}, bf16[1152,256]{1,0:T(8,128)(2,1)}) fusion(bf16[1152,256]{1,0:T(8,128)(2,1)S(1)} %collective-permute-done.15, bf16[1152,256]{1,0:T(8,128)(2,1)S(1)} %copy-done.18, bf16[1152,256]{1,0:T(8,128)(2,1)} %collective-permute-done.12, bf16[1152,256]{1,0:T(8,128)(2,1)S(1)} %copy-done.4, f32[1152]{0:T(1024)S(1)} %get-tuple-element.35, ...), kind=kLoop, calls=%fused_computation.5 | loop fusion | flops 5603328 | bytes 5907712 | tf_op jit(solution)/shard_map/convert_element_type | solution.py:259
  295.5 4.7 %fusion.24 = (bf16[256,4096]{1,0:T(8,128)(2,1)}, bf16[256,4096]{1,0:T(8,128)(2,1)}) fusion(bf16[512,4096]{1,0:T(8,128)(2,1)} %all-gather.8.cloned.1.call-done), kind=kLoop, calls=%fused_computation.74 | loop fusion | bytes 8388608 | tf_op jit(solution)/shard_map/slice | solution.py:296
  (138 shorter events, 8.6 us)
Async XLA Ops:
  7.2 58.7 %all-gather.6.cloned.1.call-start = ((), (), s32[]{:S(2)}) async-start(), calls=%async_computation.1 | async-start | bytes 5308416 | tf_op jit(solution)/shard_map/all_gather | solution.py:214
  11.5 107.0 %all-gather.4.cloned.1.call-start = ((), (), s32[]{:S(2)}) async-start(), calls=%async_computation | async-start | bytes 5308416 | tf_op jit(solution)/shard_map/all_gather | solution.py:213
  12.2 283.2 %all-gather.8.cloned.1.call-start = ((), (), s32[]{:S(2)}) async-start(), calls=%async_computation.2 | async-start | bytes 4718592 | tf_op jit(solution)/shard_map/all_gather | solution.py:285
  17.5 125.6 %collective-permute-start.8 = (bf16[4608,512]{1,0:T(8,128)(2,1)}, bf16[4608,512]{1,0:T(8,128)(2,1)}, u32[]{:S(2)}, u32[]{:S(2)}) collective-permute-start(bf16[4608,512]{1,0:T(8,128)(2,1)} %bitcast.21), channel_id=1, source_target_pairs={{0,1},{1,0},{2,3},{3,2},{4,5},{5,4},{6,7},{7,6},{8,9},{9,8},{10,11... | collective-permute-start | bytes 14155784 | tf_op jit(solution)/shard_map/ppermute | solution.py:220
  21.6 122.0 %collective-permute-start = (bf16[4608,512]{1,0:T(8,128)(2,1)}, bf16[4608,512]{1,0:T(8,128)(2,1)}, u32[]{:S(2)}, u32[]{:S(2)}) collective-permute-start(bf16[4608,512]{1,0:T(8,128)(2,1)} %bitcast.10), channel_id=1, source_target_pairs={{0,1},{1,0},{2,3},{3,2},{4,5},{5,4},{6,7},{7,6},{8,9},{9,8},{10,11... | collective-permute-start | bytes 14155784 | tf_op jit(solution)/shard_map/ppermute | solution.py:220
  65.9 52.5 %copy-start.36 = (bf16[256,512]{1,0:T(8,128)(2,1)S(1)}, bf16[256,512]{1,0:T(8,128)(2,1)}, u32[]{:S(2)}) copy-start(bf16[256,512]{1,0:T(8,128)(2,1)} %param.20) | copy-start | bytes 786436
  65.9 52.5 %copy-start.37 = (bf16[256,512]{1,0:T(8,128)(2,1)S(1)}, bf16[256,512]{1,0:T(8,128)(2,1)}, u32[]{:S(2)}) copy-start(bf16[256,512]{1,0:T(8,128)(2,1)} %param.19) | copy-start | bytes 786436
  127.6 18.1 %copy-start.1 = (bf16[256,512]{1,0:T(8,128)(2,1)}, bf16[256,512]{1,0:T(8,128)(2,1)S(1)}, u32[]{:S(2)}) copy-start(bf16[256,512]{1,0:T(8,128)(2,1)S(1)} %get-tuple-element.53.dz_ref.dz0) | copy-start | bytes 786436
  137.4 6.7 %collective-permute-start.35 = (f32[6,512]{1,0:T(8,128)S(1)}, f32[6,512]{1,0:T(8,128)S(1)}, u32[]{:S(2)}, u32[]{:S(2)}) collective-permute-start(f32[6,512]{1,0:T(8,128)S(1)} %concatenate.7), channel_id=1, source_target_pairs={{0,16},{8,24},{16,0},{24,8},{1,17},{9,25},{17,1},{25,9},{2,18},{10... | collective-permute-start | bytes 36872 | tf_op jit(solution)/shard_map/ppermute | solution.py:273
  139.0 6.7 %collective-permute-start.36 = (f32[6,512]{1,0:T(8,128)S(1)}, f32[6,512]{1,0:T(8,128)S(1)}, u32[]{:S(2)}, u32[]{:S(2)}) collective-permute-start(f32[6,512]{1,0:T(8,128)S(1)} %concatenate.7), channel_id=1, source_target_pairs={{0,24},{8,16},{16,8},{24,0},{1,25},{9,17},{17,9},{25,1},{2,26},{10... | collective-permute-start | bytes 36872 | tf_op jit(solution)/shard_map/ppermute | solution.py:273
  140.4 6.7 %collective-permute-start.9 = (bf16[256,512]{1,0:T(8,128)(2,1)}, bf16[256,512]{1,0:T(8,128)(2,1)S(1)}, u32[]{:S(2)}, u32[]{:S(2)}) collective-permute-start(bf16[256,512]{1,0:T(8,128)(2,1)} %get-tuple-element.50.dz_ref.dz0), channel_id=1, source_target_pairs={{0,1},{1,0},{2,3},{3,2},{4,5},{5,4},{6,7},{7,6},{8,9},{9,8},{10,11... | collective-permute-start | bytes 786440 | tf_op jit(solution)/shard_map/ppermute | solution.py:241
  143.1 11.9 %collective-permute-start.1 = (bf16[256,512]{1,0:T(8,128)(2,1)S(1)}, bf16[256,512]{1,0:T(8,128)(2,1)S(1)}, u32[]{:S(2)}, u32[]{:S(2)}) collective-permute-start(bf16[256,512]{1,0:T(8,128)(2,1)S(1)} %get-tuple-element.53.dz_ref.dz0), channel_id=1, source_target_pairs={{0,1},{1,0},{2,3},{3,2},{4,5},{5,4},{6,7},{7,6},{8,9},{9,8},{10,11... | collective-permute-start | bytes 786440 | tf_op jit(solution)/shard_map/ppermute | solution.py:241
  143.6 21.3 %collective-permute-start.22 = (bf16[256,512]{1,0:T(8,128)(2,1)S(1)}, bf16[256,512]{1,0:T(8,128)(2,1)S(1)}, u32[]{:S(2)}, u32[]{:S(2)}) collective-permute-start(bf16[256,512]{1,0:T(8,128)(2,1)S(1)} %get-tuple-element.53.dz_ref.dz0), channel_id=1, source_target_pairs={{0,8},{8,0},{16,24},{24,16},{1,9},{9,1},{17,25},{25,17},{2,10},{10... | collective-permute-start | bytes 786440 | tf_op jit(solution)/shard_map/ppermute | solution.py:273
  144.1 21.4 %collective-permute-start.23 = (bf16[256,512]{1,0:T(8,128)(2,1)S(1)}, bf16[256,512]{1,0:T(8,128)(2,1)S(1)}, u32[]{:S(2)}, u32[]{:S(2)}) collective-permute-start(bf16[256,512]{1,0:T(8,128)(2,1)S(1)} %get-tuple-element.53.dz_ref.dz0), channel_id=1, source_target_pairs={{0,16},{8,24},{16,0},{24,8},{1,17},{9,25},{17,1},{25,9},{2,18},{10... | collective-permute-start | bytes 786440 | tf_op jit(solution)/shard_map/ppermute | solution.py:273
  145.7 20.4 %collective-permute-start.24 = (bf16[256,512]{1,0:T(8,128)(2,1)S(1)}, bf16[256,512]{1,0:T(8,128)(2,1)}, u32[]{:S(2)}, u32[]{:S(2)}) collective-permute-start(bf16[256,512]{1,0:T(8,128)(2,1)S(1)} %get-tuple-element.53.dz_ref.dz0), channel_id=1, source_target_pairs={{0,24},{8,16},{16,8},{24,0},{1,25},{9,17},{17,9},{25,1},{2,26},{10... | collective-permute-start | bytes 786440 | tf_op jit(solution)/shard_map/ppermute | solution.py:273
  147.1 21.7 %collective-permute-start.31 = (bf16[256,512]{1,0:T(8,128)(2,1)}, bf16[256,512]{1,0:T(8,128)(2,1)S(1)}, u32[]{:S(2)}, u32[]{:S(2)}) collective-permute-start(bf16[256,512]{1,0:T(8,128)(2,1)} %get-tuple-element.50.dz_ref.dz0), channel_id=1, source_target_pairs={{0,8},{8,0},{16,24},{24,16},{1,9},{9,1},{17,25},{25,17},{2,10},{10... | collective-permute-start | bytes 786440 | tf_op jit(solution)/shard_map/ppermute | solution.py:273
  155.0 11.0 %copy-start.8 = (bf16[1152,256]{1,0:T(8,128)(2,1)S(1)}, bf16[1152,256]{1,0:T(8,128)(2,1)}, u32[]{:S(2)}) copy-start(bf16[1152,256]{1,0:T(8,128)(2,1)} %part_block.14) | copy-start | bytes 1769476
  155.1 8.5 %collective-permute-start.34 = (f32[6,512]{1,0:T(8,128)S(1)}, f32[6,512]{1,0:T(8,128)S(1)}, u32[]{:S(2)}, u32[]{:S(2)}) collective-permute-start(f32[6,512]{1,0:T(8,128)S(1)} %concatenate.7), channel_id=1, source_target_pairs={{0,8},{8,0},{16,24},{24,16},{1,9},{9,1},{17,25},{25,17},{2,10},{10... | collective-permute-start | bytes 36872 | tf_op jit(solution)/shard_map/ppermute | solution.py:273
  163.5 9.5 %collective-permute-start.32 = (bf16[256,512]{1,0:T(8,128)(2,1)}, bf16[256,512]{1,0:T(8,128)(2,1)S(1)}, u32[]{:S(2)}, u32[]{:S(2)}) collective-permute-start(bf16[256,512]{1,0:T(8,128)(2,1)} %get-tuple-element.50.dz_ref.dz0), channel_id=1, source_target_pairs={{0,16},{8,24},{16,0},{24,8},{1,17},{9,25},{17,1},{25,9},{2,18},{10... | collective-permute-start | bytes 786440 | tf_op jit(solution)/shard_map/ppermute | solution.py:273
  165.0 14.7 %copy-start.27 = (bf16[256,512]{1,0:T(8,128)(2,1)}, bf16[256,512]{1,0:T(8,128)(2,1)S(1)}, u32[]{:S(2)}) copy-start(bf16[256,512]{1,0:T(8,128)(2,1)S(1)} %collective-permute-done.22.dzx) | copy-start | bytes 786436
  165.0 30.4 %collective-permute-start.16 = (bf16[256,1152]{1,0:T(8,128)(2,1)}, bf16[256,1152]{1,0:T(8,128)(2,1)S(1)}, u32[]{:S(2)}, u32[]{:S(2)}) collective-permute-start(bf16[256,1152]{1,0:T(8,128)(2,1)} %get-tuple-element.45), channel_id=1, source_target_pairs={{0,8},{8,0},{16,24},{24,16},{1,9},{9,1},{17,25},{25,17},{2,10},{10... | collective-permute-start | bytes 1769480 | tf_op jit(solution)/shard_map/ppermute | solution.py:267
  165.6 14.1 %copy-start.28 = (bf16[256,512]{1,0:T(8,128)(2,1)}, bf16[256,512]{1,0:T(8,128)(2,1)S(1)}, u32[]{:S(2)}) copy-start(bf16[256,512]{1,0:T(8,128)(2,1)S(1)} %collective-permute-done.23.dzy) | copy-start | bytes 786436
  165.6 30.3 %collective-permute-start.17 = (bf16[256,1152]{1,0:T(8,128)(2,1)}, bf16[256,1152]{1,0:T(8,128)(2,1)S(1)}, u32[]{:S(2)}, u32[]{:S(2)}) collective-permute-start(bf16[256,1152]{1,0:T(8,128)(2,1)} %get-tuple-element.44), channel_id=1, source_target_pairs={{0,16},{8,24},{16,0},{24,8},{1,17},{9,25},{17,1},{25,9},{2,18},{10... | collective-permute-start | bytes 1769480 | tf_op jit(solution)/shard_map/ppermute | solution.py:267
  166.1 31.3 %collective-permute-start.10 = (bf16[1152,256]{1,0:T(8,128)(2,1)S(1)}, bf16[1152,256]{1,0:T(8,128)(2,1)}, u32[]{:S(2)}, u32[]{:S(2)}) collective-permute-start(bf16[1152,256]{1,0:T(8,128)(2,1)S(1)} %copy-done.8), channel_id=1, source_target_pairs={{0,2},{1,3},{6,4},{7,5},{8,10},{9,11},{14,12},{15,13},{16,18},{17,... | collective-permute-start | bytes 1769480 | tf_op jit(solution)/shard_map/ppermute | solution.py:252
  168.9 10.9 %copy-start.29 = (bf16[256,512]{1,0:T(8,128)(2,1)}, bf16[256,512]{1,0:T(8,128)(2,1)S(1)}, u32[]{:S(2)}) copy-start(bf16[256,512]{1,0:T(8,128)(2,1)S(1)} %collective-permute-done.31.dzx) | copy-start | bytes 786436
  168.9 30.5 %collective-permute-start.2 = (bf16[1152,256]{1,0:T(8,128)(2,1)}, bf16[1152,256]{1,0:T(8,128)(2,1)}, u32[]{:S(2)}, u32[]{:S(2)}) collective-permute-start(bf16[1152,256]{1,0:T(8,128)(2,1)} %part_block.10), channel_id=1, source_target_pairs={{0,2},{1,3},{6,4},{7,5},{8,10},{9,11},{14,12},{15,13},{16,18},{17,... | collective-permute-start | bytes 1769480 | tf_op jit(solution)/shard_map/ppermute | solution.py:252
  173.0 20.8 %collective-permute-start.33 = (bf16[256,512]{1,0:T(8,128)(2,1)}, bf16[256,512]{1,0:T(8,128)(2,1)}, u32[]{:S(2)}, u32[]{:S(2)}) collective-permute-start(bf16[256,512]{1,0:T(8,128)(2,1)} %get-tuple-element.50.dz_ref.dz0), channel_id=1, source_target_pairs={{0,24},{8,16},{16,8},{24,0},{1,25},{9,17},{17,9},{25,1},{2,26},{10... | collective-permute-start | bytes 786440 | tf_op jit(solution)/shard_map/ppermute | solution.py:273
  189.0 8.4 %copy-start.11 = (bf16[1152,256]{1,0:T(8,128)(2,1)S(1)}, bf16[1152,256]{1,0:T(8,128)(2,1)}, u32[]{:S(2)}) copy-start(bf16[1152,256]{1,0:T(8,128)(2,1)} %part_block.15) | copy-start | bytes 1769476
  189.0 10.3 %copy-start.10 = (bf16[1152,256]{1,0:T(8,128)(2,1)S(1)}, bf16[1152,256]{1,0:T(8,128)(2,1)}, u32[]{:S(2)}) copy-start(bf16[1152,256]{1,0:T(8,128)(2,1)} %part_block.11) | copy-start | bytes 1769476
  193.8 8.1 %copy-start.9 = (bf16[1152,256]{1,0:T(8,128)(2,1)S(1)}, bf16[1152,256]{1,0:T(8,128)(2,1)}, u32[]{:S(2)}) copy-start(bf16[1152,256]{1,0:T(8,128)(2,1)} %part_block.10) | copy-start | bytes 1769476
  193.8 17.4 %collective-permute-start.18 = (bf16[256,1152]{1,0:T(8,128)(2,1)}, bf16[256,1152]{1,0:T(8,128)(2,1)S(1)}, u32[]{:S(2)}, u32[]{:S(2)}) collective-permute-start(bf16[256,1152]{1,0:T(8,128)(2,1)} %get-tuple-element.43), channel_id=1, source_target_pairs={{0,24},{8,16},{16,8},{24,0},{1,25},{9,17},{17,9},{25,1},{2,26},{10... | collective-permute-start | bytes 1769480 | tf_op jit(solution)/shard_map/ppermute | solution.py:267
  195.3 29.6 %copy-start.12 = (bf16[256,1152]{1,0:T(8,128)(2,1)}, bf16[256,1152]{1,0:T(8,128)(2,1)S(1)}, u32[]{:S(2)}) copy-start(bf16[256,1152]{1,0:T(8,128)(2,1)S(1)} %collective-permute-done.16.px) | copy-start | bytes 1769476
  195.3 27.6 %collective-permute-start.25 = (bf16[256,1152]{1,0:T(8,128)(2,1)}, bf16[256,1152]{1,0:T(8,128)(2,1)S(1)}, u32[]{:S(2)}, u32[]{:S(2)}) collective-permute-start(bf16[256,1152]{1,0:T(8,128)(2,1)} %get-tuple-element.42), channel_id=1, source_target_pairs={{0,8},{8,0},{16,24},{24,16},{1,9},{9,1},{17,25},{25,17},{2,10},{10... | collective-permute-start | bytes 1769480 | tf_op jit(solution)/shard_map/ppermute | solution.py:267
  195.8 37.1 %copy-start.13 = (bf16[256,1152]{1,0:T(8,128)(2,1)}, bf16[256,1152]{1,0:T(8,128)(2,1)S(1)}, u32[]{:S(2)}) copy-start(bf16[256,1152]{1,0:T(8,128)(2,1)S(1)} %collective-permute-done.17.py) | copy-start | bytes 1769476
  195.8 29.1 %collective-permute-start.26 = (bf16[256,1152]{1,0:T(8,128)(2,1)}, bf16[256,1152]{1,0:T(8,128)(2,1)S(1)}, u32[]{:S(2)}, u32[]{:S(2)}) collective-permute-start(bf16[256,1152]{1,0:T(8,128)(2,1)} %get-tuple-element.41), channel_id=1, source_target_pairs={{0,16},{8,24},{16,0},{24,8},{1,17},{9,25},{17,1},{25,9},{2,18},{10... | collective-permute-start | bytes 1769480 | tf_op jit(solution)/shard_map/ppermute | solution.py:267
  197.4 27.7 %collective-permute-start.14 = (bf16[1152,256]{1,0:T(8,128)(2,1)S(1)}, bf16[1152,256]{1,0:T(8,128)(2,1)S(1)}, u32[]{:S(2)}, u32[]{:S(2)}) collective-permute-start(bf16[1152,256]{1,0:T(8,128)(2,1)S(1)} %copy-done.11), channel_id=1, source_target_pairs={{0,2},{1,3},{6,4},{7,5},{8,10},{9,11},{14,12},{15,13},{16,18},{17,... | collective-permute-start | bytes 1769480 | tf_op jit(solution)/shard_map/ppermute | solution.py:253
  199.3 26.4 %collective-permute-start.6 = (bf16[1152,256]{1,0:T(8,128)(2,1)S(1)}, bf16[1152,256]{1,0:T(8,128)(2,1)S(1)}, u32[]{:S(2)}, u32[]{:S(2)}) collective-permute-start(bf16[1152,256]{1,0:T(8,128)(2,1)S(1)} %copy-done.10), channel_id=1, source_target_pairs={{0,2},{1,3},{6,4},{7,5},{8,10},{9,11},{14,12},{15,13},{16,18},{17,... | collective-permute-start | bytes 1769480 | tf_op jit(solution)/shard_map/ppermute | solution.py:253
  201.9 9.3 %copy-start.26 = (bf16[256,1152]{1,0:T(8,128)(2,1)S(1)}, bf16[256,1152]{1,0:T(8,128)(2,1)}, u32[]{:S(2)}) copy-start(bf16[256,1152]{1,0:T(8,128)(2,1)} %get-tuple-element.40) | copy-start | bytes 1769476
  201.9 21.0 %copy-start.7 = (bf16[1152,256]{1,0:T(8,128)(2,1)S(1)}, bf16[1152,256]{1,0:T(8,128)(2,1)}, u32[]{:S(2)}) copy-start(bf16[1152,256]{1,0:T(8,128)(2,1)} %part_block.13) | copy-start | bytes 1769476
  211.2 22.3 %copy-start.15 = (bf16[256,1152]{1,0:T(8,128)(2,1)}, bf16[256,1152]{1,0:T(8,128)(2,1)S(1)}, u32[]{:S(2)}) copy-start(bf16[256,1152]{1,0:T(8,128)(2,1)S(1)} %collective-permute-done.18.pd) | copy-start | bytes 1769476
  211.3 21.7 %collective-permute-start.27 = (bf16[256,1152]{1,0:T(8,128)(2,1)S(1)}, bf16[256,1152]{1,0:T(8,128)(2,1)S(1)}, u32[]{:S(2)}, u32[]{:S(2)}) collective-permute-start(bf16[256,1152]{1,0:T(8,128)(2,1)S(1)} %copy-done.26), channel_id=1, source_target_pairs={{0,24},{8,16},{16,8},{24,0},{1,25},{9,17},{17,9},{25,1},{2,26},{10... | collective-permute-start | bytes 1769480 | tf_op jit(solution)/shard_map/ppermute | solution.py:267
  222.9 10.6 %copy-start.14 = (bf16[256,1152]{1,0:T(8,128)(2,1)}, bf16[256,1152]{1,0:T(8,128)(2,1)S(1)}, u32[]{:S(2)}) copy-start(bf16[256,1152]{1,0:T(8,128)(2,1)S(1)} %collective-permute-done.25.px) | copy-start | bytes 1769476
  222.9 10.6 %collective-permute-start.13 = (bf16[1152,256]{1,0:T(8,128)(2,1)S(1)}, bf16[1152,256]{1,0:T(8,128)(2,1)S(1)}, u32[]{:S(2)}, u32[]{:S(2)}) collective-permute-start(bf16[1152,256]{1,0:T(8,128)(2,1)S(1)} %copy-done.7), channel_id=1, source_target_pairs={{0,2},{1,3},{6,4},{7,5},{8,10},{9,11},{14,12},{15,13},{16,18},{17,... | collective-permute-start | bytes 1769480 | tf_op jit(solution)/shard_map/ppermute | solution.py:254
  224.9 9.2 %copy-start.16 = (bf16[256,1152]{1,0:T(8,128)(2,1)}, bf16[256,1152]{1,0:T(8,128)(2,1)S(1)}, u32[]{:S(2)}) copy-start(bf16[256,1152]{1,0:T(8,128)(2,1)S(1)} %collective-permute-done.26.py) | copy-start | bytes 1769476
  225.0 8.6 %collective-permute-start.19 = (bf16[256,1152]{1,0:T(8,128)(2,1)S(1)}, bf16[256,1152]{1,0:T(8,128)(2,1)S(1)}, u32[]{:S(2)}, u32[]{:S(2)}) collective-permute-start(bf16[256,1152]{1,0:T(8,128)(2,1)S(1)} %collective-permute-done.16.px), channel_id=1, source_target_pairs={{0,1},{1,0},{2,3},{3,2},{4,5},{5,4},{6,7},{7,6},{8,9},{9,8},{10,11... | collective-permute-start | bytes 1769480 | tf_op jit(solution)/shard_map/ppermute | solution.py:269
  225.0 9.1 %collective-permute-start.11 = (bf16[1152,256]{1,0:T(8,128)(2,1)S(1)}, bf16[1152,256]{1,0:T(8,128)(2,1)S(1)}, u32[]{:S(2)}, u32[]{:S(2)}) collective-permute-start(bf16[1152,256]{1,0:T(8,128)(2,1)S(1)} %add_convert_fusion.2), channel_id=1, source_target_pairs={{2,4},{3,5},{4,2},{5,3},{10,12},{11,13},{12,10},{13,11},{18,20},{1... | collective-permute-start | bytes 1769480 | tf_op jit(solution)/shard_map/ppermute | solution.py:255
  225.8 8.5 %collective-permute-start.3 = (bf16[1152,256]{1,0:T(8,128)(2,1)S(1)}, bf16[1152,256]{1,0:T(8,128)(2,1)S(1)}, u32[]{:S(2)}, u32[]{:S(2)}) collective-permute-start(bf16[1152,256]{1,0:T(8,128)(2,1)S(1)} %add_convert_fusion.5), channel_id=1, source_target_pairs={{2,4},{3,5},{4,2},{5,3},{10,12},{11,13},{12,10},{13,11},{18,20},{1... | collective-permute-start | bytes 1769480 | tf_op jit(solution)/shard_map/ppermute | solution.py:255
  233.0 3.7 %collective-permute-start.20 = (bf16[256,1152]{1,0:T(8,128)(2,1)S(1)}, bf16[256,1152]{1,0:T(8,128)(2,1)S(1)}, u32[]{:S(2)}, u32[]{:S(2)}) collective-permute-start(bf16[256,1152]{1,0:T(8,128)(2,1)S(1)} %collective-permute-done.17.py), channel_id=1, source_target_pairs={{0,1},{1,0},{2,3},{3,2},{4,5},{5,4},{6,7},{7,6},{8,9},{9,8},{10,11... | collective-permute-start | bytes 1769480 | tf_op jit(solution)/shard_map/ppermute | solution.py:269
  233.6 25.1 %collective-permute-start.21 = (bf16[256,1152]{1,0:T(8,128)(2,1)S(1)}, bf16[256,1152]{1,0:T(8,128)(2,1)S(1)}, u32[]{:S(2)}, u32[]{:S(2)}) collective-permute-start(bf16[256,1152]{1,0:T(8,128)(2,1)S(1)} %collective-permute-done.18.pd), channel_id=1, source_target_pairs={{0,1},{1,0},{2,3},{3,2},{4,5},{5,4},{6,7},{7,6},{8,9},{9,8},{10,11... | collective-permute-start | bytes 1769480 | tf_op jit(solution)/shard_map/ppermute | solution.py:269
  233.6 25.8 %collective-permute-start.28 = (bf16[256,1152]{1,0:T(8,128)(2,1)S(1)}, bf16[256,1152]{1,0:T(8,128)(2,1)S(1)}, u32[]{:S(2)}, u32[]{:S(2)}) collective-permute-start(bf16[256,1152]{1,0:T(8,128)(2,1)S(1)} %collective-permute-done.25.px), channel_id=1, source_target_pairs={{0,1},{1,0},{2,3},{3,2},{4,5},{5,4},{6,7},{7,6},{8,9},{9,8},{10,11... | collective-permute-start | bytes 1769480 | tf_op jit(solution)/shard_map/ppermute | solution.py:269
  234.1 26.8 %collective-permute-start.29 = (bf16[256,1152]{1,0:T(8,128)(2,1)S(1)}, bf16[256,1152]{1,0:T(8,128)(2,1)S(1)}, u32[]{:S(2)}, u32[]{:S(2)}) collective-permute-start(bf16[256,1152]{1,0:T(8,128)(2,1)S(1)} %collective-permute-done.26.py), channel_id=1, source_target_pairs={{0,1},{1,0},{2,3},{3,2},{4,5},{5,4},{6,7},{7,6},{8,9},{9,8},{10,11... | collective-permute-start | bytes 1769480 | tf_op jit(solution)/shard_map/ppermute | solution.py:269
  234.2 28.0 %collective-permute-start.30 = (bf16[256,1152]{1,0:T(8,128)(2,1)S(1)}, bf16[256,1152]{1,0:T(8,128)(2,1)S(1)}, u32[]{:S(2)}, u32[]{:S(2)}) collective-permute-start(bf16[256,1152]{1,0:T(8,128)(2,1)S(1)} %collective-permute-done.27.pd), channel_id=1, source_target_pairs={{0,1},{1,0},{2,3},{3,2},{4,5},{5,4},{6,7},{7,6},{8,9},{9,8},{10,11... | collective-permute-start | bytes 1769480 | tf_op jit(solution)/shard_map/ppermute | solution.py:269
  235.6 27.9 %copy-start.32 = (f32[1,512]{1,0:T(1,128)S(1)}, f32[1,512]{1,0:T(1,128)}, u32[]{:S(2)}) copy-start(f32[1,512]{1,0:T(1,128)} %get-tuple-element.62) | copy-start | bytes 6148
  235.6 28.0 %copy-start.33 = (f32[1,512]{1,0:T(1,128)S(1)}, f32[1,512]{1,0:T(1,128)}, u32[]{:S(2)}) copy-start(f32[1,512]{1,0:T(1,128)} %get-tuple-element.63) | copy-start | bytes 6148
  236.7 32.2 %copy-start.21 = (bf16[256,1152]{1,0:T(8,128)(2,1)}, bf16[256,1152]{1,0:T(8,128)(2,1)S(1)}, u32[]{:S(2)}) copy-start(bf16[256,1152]{1,0:T(8,128)(2,1)S(1)} %collective-permute-done.20.qy) | copy-start | bytes 1769476
  236.7 55.0 %collective-permute-start.5 = (bf16[1152,256]{1,0:T(8,128)(2,1)S(1)}, bf16[1152,256]{1,0:T(8,128)(2,1)S(1)}, u32[]{:S(2)}, u32[]{:S(2)}) collective-permute-start(bf16[1152,256]{1,0:T(8,128)(2,1)S(1)} %copy-done.6), channel_id=1, source_target_pairs={{0,2},{1,3},{6,4},{7,5},{8,10},{9,11},{14,12},{15,13},{16,18},{17,... | collective-permute-start | bytes 1769480 | tf_op jit(solution)/shard_map/ppermute | solution.py:254
  258.6 33.1 %collective-permute-start.15 = (bf16[1152,256]{1,0:T(8,128)(2,1)}, bf16[1152,256]{1,0:T(8,128)(2,1)S(1)}, u32[]{:S(2)}, u32[]{:S(2)}) collective-permute-start(bf16[1152,256]{1,0:T(8,128)(2,1)} %add_convert_fusion), channel_id=1, source_target_pairs={{2,4},{3,5},{4,2},{5,3},{10,12},{11,13},{12,10},{13,11},{18,20},{1... | collective-permute-start | bytes 1769480 | tf_op jit(solution)/shard_map/ppermute | solution.py:256
  259.4 9.5 %copy-start.22 = (bf16[256,1152]{1,0:T(8,128)(2,1)}, bf16[256,1152]{1,0:T(8,128)(2,1)S(1)}, u32[]{:S(2)}) copy-start(bf16[256,1152]{1,0:T(8,128)(2,1)S(1)} %collective-permute-done.28.qx) | copy-start | bytes 1769476
  259.4 32.4 %collective-permute-start.7 = (bf16[1152,256]{1,0:T(8,128)(2,1)}, bf16[1152,256]{1,0:T(8,128)(2,1)}, u32[]{:S(2)}, u32[]{:S(2)}) collective-permute-start(bf16[1152,256]{1,0:T(8,128)(2,1)} %add_convert_fusion.3), channel_id=1, source_target_pairs={{2,4},{3,5},{4,2},{5,3},{10,12},{11,13},{12,10},{13,11},{18,20},{1... | collective-permute-start | bytes 1769480 | tf_op jit(solution)/shard_map/ppermute | solution.py:256
  260.9 30.8 %collective-permute-start.12 = (bf16[1152,256]{1,0:T(8,128)(2,1)}, bf16[1152,256]{1,0:T(8,128)(2,1)}, u32[]{:S(2)}, u32[]{:S(2)}) collective-permute-start(bf16[1152,256]{1,0:T(8,128)(2,1)} %add_convert_fusion.1), channel_id=1, source_target_pairs={{2,0},{3,1},{4,6},{5,7},{10,8},{11,9},{12,14},{13,15},{18,16},{19,... | collective-permute-start | bytes 1769480 | tf_op jit(solution)/shard_map/ppermute | solution.py:257
  262.2 29.5 %collective-permute-start.4 = (bf16[1152,256]{1,0:T(8,128)(2,1)}, bf16[1152,256]{1,0:T(8,128)(2,1)}, u32[]{:S(2)}, u32[]{:S(2)}) collective-permute-start(bf16[1152,256]{1,0:T(8,128)(2,1)} %add_convert_fusion.4), channel_id=1, source_target_pairs={{2,0},{3,1},{4,6},{5,7},{10,8},{11,9},{12,14},{13,15},{18,16},{19,... | collective-permute-start | bytes 1769480 | tf_op jit(solution)/shard_map/ppermute | solution.py:257
  282.5 9.2 %copy-start.4 = (bf16[1152,256]{1,0:T(8,128)(2,1)S(1)}, bf16[1152,256]{1,0:T(8,128)(2,1)}, u32[]{:S(2)}) copy-start(bf16[1152,256]{1,0:T(8,128)(2,1)} %part_block.12) | copy-start | bytes 1769476
  282.5 9.3 %copy-start.5 = (bf16[1152,256]{1,0:T(8,128)(2,1)S(1)}, bf16[1152,256]{1,0:T(8,128)(2,1)}, u32[]{:S(2)}) copy-start(bf16[1152,256]{1,0:T(8,128)(2,1)} %part_block.8) | copy-start | bytes 1769476
  282.5 9.3 %copy-start.18 = (bf16[1152,256]{1,0:T(8,128)(2,1)S(1)}, bf16[1152,256]{1,0:T(8,128)(2,1)}, u32[]{:S(2)}) copy-start(bf16[1152,256]{1,0:T(8,128)(2,1)} %copy-done.17) | copy-start | bytes 1769476
  (14 other events, 51.4 us)
Sparse Core Ops, SparseCore 0:
  11.6 54.2 all-gather.5
  68.1 50.2 all-gather.3
  128.6 45.4 all-gather.7

commit v2 on v1

v2 whole, which is shorter than its diff:
```python
import functools

import jax
import jax.numpy as jnp
from jax import lax
from jax.experimental import pallas as pl
from jax.experimental.pallas import tpu as pltpu
from jax.sharding import PartitionSpec as P

CH = 256
POS = 36


def keep_block(image_group, position_mask, first_col, cols):
    positions = (first_col + lax.iota(jnp.int32, cols)) // CH
    onehot = (positions[:, None] == lax.iota(jnp.int32, POS)[None, :]).astype(jnp.float32)
    per_position = jnp.dot(onehot, position_mask.astype(jnp.float32).T)
    return jnp.where(
        image_group[:, None] == 1, per_position[:, 1][None, :], per_position[:, 0][None, :]
    )


def general_shards(
    image_a,
    image_b,
    image_group,
    position_mask,
    weight_a,
    weight_b,
    tower_bias,
    stitch,
    cotan_a,
    cotan_b,
):
    batch_rows = image_a.shape[0]
    shard_cols = image_a.shape[1]
    first_col = lax.axis_index("mp") * shard_cols
    keep_mask = keep_block(image_group, position_mask, first_col, shard_cols)
    keep_low = keep_mask.astype(jnp.bfloat16)
    contract_rows = (((0,), (0,)), ((), ()))
    contract_units = (((1,), (1,)), ((), ()))
    full_a = lax.all_gather(image_a * keep_low, "mp", axis=1, tiled=True)
    full_b = lax.all_gather(image_b * keep_low, "mp", axis=1, tiled=True)
    pre_a = jnp.dot(full_a, weight_a, preferred_element_type=jnp.float32) + tower_bias[0][None, :]
    pre_b = jnp.dot(full_b, weight_b, preferred_element_type=jnp.float32) + tower_bias[1][None, :]
    sigma_a = jax.nn.sigmoid(pre_a)
    sigma_b = jax.nn.sigmoid(pre_b)
    hidden_a = pre_a * sigma_a
    hidden_b = pre_b * sigma_b
    local_a = (stitch[0][None, :] * hidden_a + stitch[1][None, :] * hidden_b).astype(jnp.bfloat16)
    local_b = (stitch[2][None, :] * hidden_a + stitch[3][None, :] * hidden_b).astype(jnp.bfloat16)
    stitched_a = lax.all_gather(local_a, "mp", axis=1, tiled=True)
    stitched_b = lax.all_gather(local_b, "mp", axis=1, tiled=True)
    upper_a = cotan_a.astype(jnp.float32)
    upper_b = cotan_b.astype(jnp.float32)
    dhid_a = stitch[0][None, :] * upper_a + stitch[2][None, :] * upper_b
    dhid_b = stitch[1][None, :] * upper_a + stitch[3][None, :] * upper_b
    dpre_a = dhid_a * (sigma_a * (1.0 + pre_a * (1.0 - sigma_a)))
    dpre_b = dhid_b * (sigma_b * (1.0 + pre_b * (1.0 - sigma_b)))
    bias_terms = jnp.stack([jnp.sum(dpre_a, axis=0), jnp.sum(dpre_b, axis=0)])
    stitch_terms = jnp.stack(
        [
            jnp.sum(upper_a * hidden_a, axis=0),
            jnp.sum(upper_a * hidden_b, axis=0),
            jnp.sum(upper_b * hidden_a, axis=0),
            jnp.sum(upper_b * hidden_b, axis=0),
        ]
    )
    grad_bias, grad_stitch = lax.psum((bias_terms, stitch_terms), "dp")
    dlow_a = dpre_a.astype(jnp.bfloat16)
    dlow_b = dpre_b.astype(jnp.bfloat16)
    block_a = lax.dot_general(full_a, dlow_a, contract_rows, preferred_element_type=jnp.float32)
    block_b = lax.dot_general(full_b, dlow_b, contract_rows, preferred_element_type=jnp.float32)
    grad_weight_a = lax.psum_scatter(block_a, "dp", scatter_dimension=0, tiled=True)
    grad_weight_b = lax.psum_scatter(block_b, "dp", scatter_dimension=0, tiled=True)
    part_a = lax.dot_general(weight_a, dlow_a, contract_units, preferred_element_type=jnp.float32)
    part_b = lax.dot_general(weight_b, dlow_b, contract_units, preferred_element_type=jnp.float32)
    summed = lax.psum_scatter(
        jnp.concatenate([part_a, part_b], axis=1), "mp", scatter_dimension=0, tiled=True
    )
    keep_cols = keep_mask.T
    grad_image_a = (summed[:, :batch_rows] * keep_cols).astype(jnp.bfloat16)
    grad_image_b = (summed[:, batch_rows:] * keep_cols).astype(jnp.bfloat16)
    return (
        stitched_a,
        stitched_b,
        grad_image_a,
        grad_image_b,
        grad_weight_a,
        grad_weight_b,
        grad_bias,
        grad_stitch,
    )


SWAP_CORE = [(d, d ^ 1) for d in range(8)]
FLIPS = [[(d, d ^ k) for d in range(4)] for k in range(4)]
NEAR_Z = [(d, d ^ 2) for d in range(8)]
FAR_Z = [(d, d ^ 4) for d in range(8)]
ENDS_IN = [(0, 2), (1, 3), (6, 4), (7, 5)]
MIDS = [(2, 4), (3, 5), (4, 2), (5, 3)]
ENDS_OUT = [(2, 0), (3, 1), (4, 6), (5, 7)]
SLOTS = ((3, 2, 1, 0), (3, 2, 0, 1), (0, 1, 3, 2), (0, 1, 2, 3))
LANES = 128
VMEM_LIMIT = 40 * 1024 * 1024


def after(x, *deps):
    return lax.optimization_barrier((x,) + deps)[0]


def params(**kwargs):
    return pltpu.CompilerParams(vmem_limit_bytes=VMEM_LIMIT, **kwargs)


def low(x):
    return x.astype(jnp.bfloat16)


def wide(x):
    return x.astype(jnp.float32)


def mask_kernel(place, marks, group, image, out):
    second = group[...] == 1
    cols = image.shape[1]
    for chunk in range(cols // LANES):
        position = (place[0] * cols + chunk * LANES) // CH
        keep = wide(jnp.where(second, marks[1, position], marks[0, position]))
        lanes = slice(chunk * LANES, (chunk + 1) * LANES)
        out[:, lanes] = low(wide(image[:, lanes]) * keep)


def mask_image(place, marks, group, image):
    return pl.pallas_call(
        mask_kernel,
        out_shape=jax.ShapeDtypeStruct(image.shape, jnp.bfloat16),
        in_specs=[
            pl.BlockSpec(memory_space=pltpu.SMEM),
            pl.BlockSpec(memory_space=pltpu.SMEM),
            pl.BlockSpec(memory_space=pltpu.VMEM),
            pl.BlockSpec(memory_space=pltpu.VMEM),
        ],
        out_specs=pl.BlockSpec(memory_space=pltpu.VMEM),
        compiler_params=params(),
        cost_estimate=pl.CostEstimate(
            flops=image.size, bytes_accessed=4 * image.size, transcendentals=0
        ),
        name="mask_image",
    )(place, marks, group, image)


def forward_kernel(where, p0, p1, p2, p3, p4, mine, other, out, sent, keep_acc, send_acc):
    k = pl.program_id(0)
    t = pl.program_id(1)

    @pl.when((k == 0) & (t == 0))
    def _():
        keep_acc[...] = jnp.zeros_like(keep_acc)
        send_acc[...] = jnp.zeros_like(send_acc)

    def step(piece):
        keep_acc[...] += jnp.dot(piece[...], mine[...], preferred_element_type=jnp.float32)
        send_acc[...] += jnp.dot(piece[...], other[...], preferred_element_type=jnp.float32)

    for index, piece in enumerate((p0, p1, p2)):
        pl.when(k == index)(functools.partial(step, piece))
    pl.when((k == 3) & (where[2] == 0))(functools.partial(step, p3))
    pl.when((k == 3) & (where[2] == 1))(functools.partial(step, p4))

    @pl.when((k == pl.num_programs(0) - 1) & (t == pl.num_programs(1) - 1))
    def _():
        out[...] = keep_acc[...]
        sent[...] = send_acc[...]


def forward(where, pieces, weight, weight_other):
    rows, cols = pieces[0].shape
    units = weight.shape[1]
    tile = cols // 3
    steps = cols // tile

    def piece_spec(index):
        return pl.BlockSpec(
            (rows, tile),
            lambda k, t, where: (0, jnp.where(k < index, 0, jnp.where(k > index, steps - 1, t))),
        )

    rows_of = pl.BlockSpec(
        (tile, units), lambda k, t, where: ((2 * (where[0] ^ k) + where[1]) * steps + t, 0)
    )
    whole = pl.BlockSpec((rows, units), lambda k, t, where: (0, 0))
    return pl.pallas_call(
        forward_kernel,
        out_shape=[jax.ShapeDtypeStruct((rows, units), jnp.float32)] * 2,
        grid_spec=pltpu.PrefetchScalarGridSpec(
            num_scalar_prefetch=1,
            grid=(4, steps),
            in_specs=[piece_spec(min(k, 3)) for k in range(5)] + [rows_of, rows_of],
            out_specs=[whole, whole],
            scratch_shapes=[pltpu.VMEM((rows, units), jnp.float32)] * 2,
        ),
        compiler_params=params(),
        cost_estimate=pl.CostEstimate(
            flops=16 * rows * cols * units,
            bytes_accessed=8 * cols * (rows + 2 * units) + 8 * rows * units,
            transcendentals=0,
        ),
        name="forward",
    )(where, *pieces, weight, weight_other)


def tower_math(own, got, bias, unit_a, unit_b, upper_a, upper_b, dz, sums):
    pre = own[...] + got[...] + bias[...]
    sigma = jax.nn.sigmoid(pre)
    hidden = pre * sigma
    cot_a = wide(upper_a[...])
    cot_b = wide(upper_b[...])
    dhid = unit_a[...] * cot_a + unit_b[...] * cot_b
    dpre = dhid * (sigma * (1.0 + pre * (1.0 - sigma)))
    dz[...] = low(dpre)
    sums[0:1, :] = jnp.sum(dpre, axis=0, keepdims=True)
    sums[1:2, :] = jnp.sum(cot_a * hidden, axis=0, keepdims=True)
    sums[2:3, :] = jnp.sum(cot_b * hidden, axis=0, keepdims=True)
    sums[3:4, :] = jnp.zeros_like(sums[3:4, :])
    return hidden


def first_kernel(own, got, bias, unit_a, unit_b, upper_a, upper_b, dz, sums, hidden):
    hidden[...] = tower_math(own, got, bias, unit_a, unit_b, upper_a, upper_b, dz, sums)


def second_kernel(
    own, got, bias, unit_a, unit_b, upper_a, upper_b, earlier, stitch, dz, sums, local
):
    hidden = tower_math(own, got, bias, unit_a, unit_b, upper_a, upper_b, dz, sums)
    rows = hidden.shape[0]
    before = earlier[...]
    local[0:rows, :] = low(stitch[0:1, :] * before + stitch[1:2, :] * hidden)
    local[rows : 2 * rows, :] = low(stitch[2:3, :] * before + stitch[3:4, :] * hidden)


def tower(kernel, name, last, *operands):
    rows, units = operands[0].shape
    return pl.pallas_call(
        kernel,
        out_shape=[
            jax.ShapeDtypeStruct((rows, units), jnp.bfloat16),
            jax.ShapeDtypeStruct((4, units), jnp.float32),
            last,
        ],
        in_specs=[pl.BlockSpec(memory_space=pltpu.VMEM)] * len(operands),
        out_specs=[pl.BlockSpec(memory_space=pltpu.VMEM)] * 3,
        compiler_params=params(),
        cost_estimate=pl.CostEstimate(
            flops=30 * rows * units, bytes_accessed=20 * rows * units, transcendentals=rows * units
        ),
        name=name,
    )(*operands)


def part_kernel(where, mine, other, dz, dzo, first, second, third, kept, dz_t, dzo_t):
    k = pl.program_id(0)

    @pl.when((k == 0) & (pl.program_id(1) == 0))
    def _():
        dz_t[...] = dz[...].T
        dzo_t[...] = dzo[...].T

    total = jnp.dot(mine[...], dz_t[...], preferred_element_type=jnp.float32)
    total += jnp.dot(other[...], dzo_t[...], preferred_element_type=jnp.float32)

    def put(ref):
        ref[...] = total.astype(ref.dtype)

    for index, ref in enumerate((first, second, third, kept)):
        pl.when(k == index)(functools.partial(put, ref))


def parts(where, weight, weight_other, dz, dz_other, cols):
    rows, units = dz.shape
    tile = cols // 3
    steps = cols // tile

    def out_spec(index):
        return pl.BlockSpec(
            (tile, rows),
            lambda k, t, where: (jnp.where(k < index, 0, jnp.where(k > index, steps - 1, t)), 0),
        )

    rows_of = pl.BlockSpec(
        (tile, units), lambda k, t, where: ((2 * where[3 + k] + where[1]) * steps + t, 0)
    )
    whole = pl.BlockSpec((rows, units), lambda k, t, where: (0, 0))
    return pl.pallas_call(
        part_kernel,
        out_shape=[jax.ShapeDtypeStruct((cols, rows), jnp.bfloat16)] * 3
        + [jax.ShapeDtypeStruct((cols, rows), jnp.float32)],
        grid_spec=pltpu.PrefetchScalarGridSpec(
            num_scalar_prefetch=1,
            grid=(4, steps),
            in_specs=[rows_of, rows_of, whole, whole],
            out_specs=[out_spec(k) for k in range(4)],
            scratch_shapes=[pltpu.VMEM((units, rows), jnp.bfloat16)] * 2,
        ),
        compiler_params=params(),
        cost_estimate=pl.CostEstimate(
            flops=16 * cols * rows * units,
            bytes_accessed=16 * cols * units + 10 * cols * rows,
            transcendentals=0,
        ),
        name="parts",
    )(where, weight, weight_other, dz, dz_other)


def finish_kernel(place, marks, group, kept, third, cross, last, out):
    second = group[...] == 1
    cols = out.shape[0]
    for chunk in range(cols // LANES):
        position = (place[0] * cols + chunk * LANES) // CH
        keep = wide(jnp.where(second, marks[1, position], marks[0, position]))
        rows = slice(chunk * LANES, (chunk + 1) * LANES)
        total = kept[rows, :] + wide(third[rows, :]) + wide(cross[rows, :]) + wide(last[rows, :])
        out[rows, :] = low(total * keep)


def finish(place, marks, group, kept, third, cross, last):
    return pl.pallas_call(
        finish_kernel,
        out_shape=jax.ShapeDtypeStruct(kept.shape, jnp.bfloat16),
        in_specs=[
            pl.BlockSpec(memory_space=pltpu.SMEM),
            pl.BlockSpec(memory_space=pltpu.SMEM),
        ]
        + [pl.BlockSpec(memory_space=pltpu.VMEM)] * 5,
        out_specs=pl.BlockSpec(memory_space=pltpu.VMEM),
        compiler_params=params(),
        cost_estimate=pl.CostEstimate(
            flops=4 * kept.size, bytes_accessed=12 * kept.size, transcendentals=0
        ),
        name="finish",
    )(place, marks, group, kept, third, cross, last)


def pick_kernel(where, p0, p1, p2, p3, p4, o0, o1, o2, o3, sems):
    outs = (o0, o1, o2, o3)
    for s, out in enumerate(outs):
        k = where[0] ^ where[7] ^ s
        for index, piece in enumerate((p0, p1, p2)):
            pl.when(k == index)(pltpu.make_async_copy(piece, out, sems.at[s]).start)
        pl.when((k == 3) & (where[2] == 0))(pltpu.make_async_copy(p3, out, sems.at[s]).start)
        pl.when((k == 3) & (where[2] == 1))(pltpu.make_async_copy(p4, out, sems.at[s]).start)
    for s, out in enumerate(outs):
        pltpu.make_async_copy(p0, out, sems.at[s]).wait()


def pick(where, pieces):
    return pl.pallas_call(
        pick_kernel,
        out_shape=[jax.ShapeDtypeStruct(pieces[0].shape, pieces[0].dtype)] * 4,
        in_specs=[pl.BlockSpec(memory_space=pltpu.SMEM)] + [pl.BlockSpec(memory_space=pl.ANY)] * 5,
        out_specs=[pl.BlockSpec(memory_space=pl.ANY)] * 4,
        scratch_shapes=[pltpu.SemaphoreType.DMA((4,))],
        compiler_params=params(),
        cost_estimate=pl.CostEstimate(
            flops=0, bytes_accessed=16 * pieces[0].size, transcendentals=0
        ),
        name="pick",
    )(where, *pieces)


def lay_kernel(where, *refs):
    sources = refs[:12]
    out_a, out_b, sems = refs[12:]
    rows = out_a.shape[0]
    units = sources[0].shape[1]
    for side in range(2):
        for k in range(4):
            block = 2 * (where[0] ^ k) + (where[1] ^ side)
            lanes = pl.ds(pl.multiple_of(block * units, units), units)
            for half, out in enumerate((out_a, out_b)):
                sem = sems.at[side * 8 + k * 2 + half]
                part = pl.ds(half * rows, rows)

                def go(source):
                    pltpu.make_async_copy(source.at[part, :], out.at[:, lanes], sem).start()

                if k < 2:
                    go(sources[side * 6 + k])
                else:
                    at = side * 6 + 2 * k - 2
                    pl.when(where[2] == 0)(functools.partial(go, sources[at]))
                    pl.when(where[2] == 1)(functools.partial(go, sources[at + 1]))
    for side in range(2):
        for k in range(4):
            for half, out in enumerate((out_a, out_b)):
                pltpu.make_async_copy(
                    sources[0].at[pl.ds(0, rows), :],
                    out.at[:, pl.ds(0, units)],
                    sems.at[side * 8 + k * 2 + half],
                ).wait()


def lay_out(where, near, far, rows):
    units = near[0].shape[1]
    return pl.pallas_call(
        lay_kernel,
        out_shape=[jax.ShapeDtypeStruct((rows, 8 * units), jnp.bfloat16)] * 2,
        in_specs=[pl.BlockSpec(memory_space=pltpu.SMEM)]
        + [pl.BlockSpec(memory_space=pl.ANY)] * 12,
        out_specs=[pl.BlockSpec(memory_space=pl.ANY)] * 2,
        scratch_shapes=[pltpu.SemaphoreType.DMA((16,))],
        compiler_params=params(),
        cost_estimate=pl.CostEstimate(
            flops=0, bytes_accessed=64 * rows * units, transcendentals=0
        ),
        name="lay_out",
    )(where, *near, *far)


def weight_kernel(where, *refs):
    near, far, dzs, out = refs[0:4], refs[4:8], refs[8:12], refs[12]

    def dots(pieces):
        total = None
        for image, dz in zip(pieces, dzs):
            term = lax.dot_general(
                image[...], dz[...], (((0,), (0,)), ((), ())), preferred_element_type=jnp.float32
            )
            total = term if total is None else total + term
        out[...] = total

    same = pl.program_id(0) == where[1]
    pl.when(same)(functools.partial(dots, near))
    pl.when(jnp.logical_not(same))(functools.partial(dots, far))


def weight_grad(where, near, far, dzs):
    rows, units = dzs[0].shape
    cols = near[0].shape[1]
    tile = cols // 3
    steps = cols // tile
    mine = pl.BlockSpec((rows, tile), lambda p, t, where: (0, jnp.where(p == where[1], t, 0)))
    other = pl.BlockSpec((rows, tile), lambda p, t, where: (0, jnp.where(p == where[1], 0, t)))
    whole = pl.BlockSpec((rows, units), lambda p, t, where: (0, 0))
    return pl.pallas_call(
        weight_kernel,
        out_shape=jax.ShapeDtypeStruct((2 * cols, units), jnp.float32),
        grid_spec=pltpu.PrefetchScalarGridSpec(
            num_scalar_prefetch=1,
            grid=(2, steps),
            in_specs=[mine] * 4 + [other] * 4 + [whole] * 4,
            out_specs=pl.BlockSpec((tile, units), lambda p, t, where: (p * steps + t, 0)),
        ),
        compiler_params=params(),
        cost_estimate=pl.CostEstimate(
            flops=16 * cols * rows * units,
            bytes_accessed=16 * cols * rows + 8 * cols * units,
            transcendentals=0,
        ),
        name="weight_grad",
    )(where, *near, *far, *dzs)


def swap(x):
    return lax.ppermute(x, "mp", SWAP_CORE)


def fast_shards(
    image_a,
    image_b,
    image_group,
    position_mask,
    weight_a,
    weight_b,
    tower_bias,
    stitch,
    cotan_a,
    cotan_b,
):
    rows, cols = image_a.shape
    units = weight_a.shape[1]
    place = lax.axis_index("mp").astype(jnp.int32)
    z = place // 2
    core = place % 2
    quarter = lax.axis_index("dp").astype(jnp.int32)
    middle = ((z == 1) | (z == 2)).astype(jnp.int32)
    slots = jnp.take(jnp.asarray(SLOTS, jnp.int32), z, axis=0)
    where = jnp.concatenate(
        [jnp.stack([z, core, middle]), slots, jnp.stack([quarter])]
    ).astype(jnp.int32)
    spot = place[None]
    group_col = image_group[:, None]
    group_row = image_group[None, :]

    def along(x):
        return lax.ppermute(x, "mp", NEAR_Z)

    a0 = mask_image(spot, position_mask, group_col, image_a)
    a1 = along(a0)
    a2 = lax.ppermute(a0, "mp", FAR_Z)
    b0 = mask_image(spot, position_mask, group_col, after(image_b, a0))
    b2 = lax.ppermute(b0, "mp", FAR_Z)
    other_a = swap(after(weight_a, b0))
    other_b = swap(after(weight_b, other_a))
    a3 = along(a2)
    b0_late = after(b0, a2)
    b1 = along(b0_late)
    b_mid = lax.ppermute(b0_late, "mp", MIDS)
    b_end = lax.ppermute(b2, "mp", ENDS_OUT)
    pieces_a = [a0, a1, a2, a3, a3]
    pieces_b = [b0, b1, b2, b_end, b_mid]

    def around(x):
        return [x] + [lax.ppermute(x, "dp", FLIPS[k]) for k in (1, 2, 3)]

    def spread(pieces):
        own, *send = pick(where, pieces)
        near = [own] + [lax.ppermute(x, "dp", FLIPS[k + 1]) for k, x in enumerate(send)]
        return near, [swap(x) for x in near]

    def add(*terms):
        total = wide(terms[0])
        for term in terms[1:]:
            total = total + wide(term)
        return low(total)

    def image_grad(weight, weight_other, dz):
        dz_other = swap(dz)
        first, second, third, kept = parts(where, weight, weight_other, dz, dz_other, cols)
        got_first = lax.ppermute(first, "mp", ENDS_IN)
        got_second = lax.ppermute(second, "mp", ENDS_IN)
        got_third = lax.ppermute(third, "mp", ENDS_IN)
        cross_first = lax.ppermute(add(first, got_first), "mp", MIDS)
        cross_second = lax.ppermute(add(second, got_second), "mp", MIDS)
        last = lax.ppermute(add(third, cross_first), "mp", ENDS_OUT)
        result = finish(spot, position_mask, group_row, kept, got_third, cross_second, last)
        return result, first

    own_a, sent_a = forward(where, pieces_a, weight_a, other_a)
    dz_a, sums_a, hidden_a = tower(
        first_kernel,
        "tower_a",
        jax.ShapeDtypeStruct((rows, units), jnp.float32),
        own_a,
        swap(sent_a),
        tower_bias[0:1],
        stitch[0:1],
        stitch[2:3],
        cotan_a,
        cotan_b,
    )
    grad_image_a, part_a = image_grad(weight_a, other_a, dz_a)
    near_a, far_a = spread([after(pieces_a[0], part_a)] + pieces_a[1:])
    dzs_a = around(after(dz_a, part_a))

    own_b, sent_b = forward(where, [after(pieces_b[0], part_a)] + pieces_b[1:], weight_b, other_b)
    dz_b, sums_b, local = tower(
        second_kernel,
        "tower_b",
        jax.ShapeDtypeStruct((2 * rows, units), jnp.bfloat16),
        own_b,
        swap(sent_b),
        tower_bias[1:2],
        stitch[1:2],
        stitch[3:4],
        cotan_a,
        cotan_b,
        hidden_a,
        stitch,
    )
    s1 = along(local)
    s_mid = lax.ppermute(local, "mp", MIDS)
    grad_image_b, part_b = image_grad(weight_b, other_b, dz_b)
    s_out = lax.ppermute(s_mid, "mp", ENDS_OUT)
    s_far = lax.ppermute(s1, "mp", MIDS)
    s_last = lax.ppermute(s_far, "mp", ENDS_OUT)
    line = [local, s1, s_out, s_far, s_last, s_mid]
    line_far = [swap(x) for x in line]
    stitched_a, stitched_b = lay_out(where, line, line_far, rows)

    near_b, far_b = spread([after(pieces_b[0], part_b)] + pieces_b[1:])
    dzs_b = around(after(dz_b, part_b))
    grad_weight_a = weight_grad(where, near_a, far_a, dzs_a)
    grad_weight_b = weight_grad(where, near_b, far_b, dzs_b)

    own, by_x, by_y, by_xy = around(jnp.concatenate([sums_a, sums_b]))
    sums = (own + by_x) + (by_y + by_xy)
    grad_bias = jnp.stack([sums[0], sums[4]])
    grad_stitch = jnp.stack([sums[1], sums[5], sums[2], sums[6]])
    return (
        stitched_a,
        stitched_b,
        grad_image_a,
        grad_image_b,
        grad_weight_a,
        grad_weight_b,
        grad_bias,
        grad_stitch,
    )


def solution(mesh):
    placed = (
        P("dp", "mp"),
        P("dp", "mp"),
        P("dp"),
        P(),
        P(None, "mp"),
        P(None, "mp"),
        P(None, "mp"),
        P(None, "mp"),
        P("dp", "mp"),
        P("dp", "mp"),
    )
    fits = mesh.shape["dp"] == 4 and mesh.shape["mp"] == 8
    return jax.shard_map(
        fast_shards if fits else general_shards,
        mesh=mesh,
        in_specs=placed,
        out_specs=(
            P("dp", None),
            P("dp", None),
            P("mp", "dp"),
            P("mp", "dp"),
            P("dp", "mp"),
            P("dp", "mp"),
            P(None, "mp"),
            P(None, "mp"),
        ),
        check_vma=False,
    )
```

time: 310 us -> 352 us (1.14)
  waiting for transfers between devices: 118 us -> 189 us
  matrix products: 16.8 us -> 0 us
  other arithmetic: 20.9 us -> 5.34 us
  between operations: 17 us -> 1.83 us
  Pallas kernels: 55.5 us -> 69 us
  starting transfers between devices: 58.6 us -> 64.1 us
    ppermute x31 -> x53, waiting for transfers between devices: 26.5 us -> 189 us  [the longest x6 35.4 us: spread(): lax.ppermute(x, 'dp', FLIPS[k + 1])]
    all_gather x3 -> x0, waiting for transfers between devices: 89.7 us -> none  [the longest x1 45.9 us: fast_shards(): full_a = lax.all_gather(masked_a, 'mp', axis=1, tiled=True)]
    ppermute x2, starting transfers between devices: 23.9 us -> 2.65 us  [image_grad(): got_third = lax.ppermute(third, 'mp', ENDS_IN)]
    unnamed x76 -> x126, local copies, waits for them, and re-layouts: 1.27 us -> 20.2 us
    ppermute x31 -> x53, starting transfers between devices: 26.4 us -> 45.2 us  [the longest x9 11.5 us: around(): return [x] + [lax.ppermute(x, 'dp', FLIPS[k]) for k in (1, 2, 3)]]
    pallas_call x8 -> x13, Pallas kernels: 37.3 us -> 55.4 us  [the longest x2 22.9 us: forward(): pl.pallas_call(forward_kernel, out_shape=[jax.ShapeDtypeStruct((rows, uni...]
    dot_general x3 -> x0, matrix products: 16.8 us -> none  [the longest x2 15.8 us: tower(): jnp.dot(full, weight, preferred_element_type=jnp.float32) + bias[None, :]]
    dynamic_slice x4 -> x0, local copies, waits for them, and re-layouts: 13.1 us -> none  [the longest x2 7.71 us: other_weight(): send = lax.dynamic_index_in_dim(blocks, 1 - core, axis=1, keepdims=False)]
  transfers between devices with their start and end apart: 40 -> 59, of which waited for: 8 -> 14; matrix products, arithmetic and copies ran while one was open for 16% -> 2% of each run, Pallas kernels for 18% -> 18%
where the time goes in v2:
time: 352 us; the launch traced here: 350 us
  waiting for transfers between devices  189 us (54%)
  Pallas kernels  69 us (20%)
  starting transfers between devices  64.1 us (18%)
  local copies, waits for them, and re-layouts  21.1 us (6%)
  other arithmetic  5.34 us (2%)
    ppermute x6, waiting for transfers between devices, spread(): lax.ppermute(x, 'dp', FLIPS[k + 1])  35.4 us
    ppermute x4, waiting for transfers between devices, along(): return lax.ppermute(x, 'mp', NEAR_Z)  32.6 us
    ppermute x1, waiting for transfers between devices, fast_shards(): s_last = lax.ppermute(s_far, 'mp', ENDS_OUT)  27.5 us
    ppermute x1, waiting for transfers between devices, fast_shards(): a2 = lax.ppermute(a0, 'mp', FAR_Z)  25 us
    ppermute x1, waiting for transfers between devices, fast_shards(): b2 = lax.ppermute(b0, 'mp', FAR_Z)  23.2 us
    pallas_call x2, Pallas kernels, forward(): pl.pallas_call(forward_kernel, out_shape=[jax.ShapeDtypeStruct((rows, uni...  22.9 us
    pallas_call x2, Pallas kernels, parts(): pl.pallas_call(part_kernel, out_shape=[jax.ShapeDtypeStruct((cols, rows),...  20.8 us
    unnamed x126, local copies, waits for them, and re-layouts  20.2 us
  transfers between devices with their start and end apart: 59, of which 14 were waited for; matrix products, arithmetic and copies ran while one was open for 2% of the time, Pallas kernels for 18%

profile of v2, /device:TPU:0, one launch (start us, length us, event | category | flops | bytes accessed | tf_op | source)
XLA Modules:
  0.0 350.1 jit_solution(1572437884887394959)
XLA Ops:
  1.5 1.1 copy-done.26
  3.2 0.9 mask_image.2.p0
  4.3 0.9 mask_image.3.p0
  5.7 14.5 %collective-permute-done.other = bf16[9216,512]{1,0:T(8,128)(2,1)S(1)} collective-permute-done((bf16[9216,512]{1,0:T(8,128)(2,1)}, bf16[9216,512]{1,0:T(8,128)(2,1)S(1)}, u32[]{:S(2)}, u32[]{:S(2)}) %collective-permute-start) | collective-permute-done | bytes 9437216 | tf_op jit(solution)/shard_map/ppermute | solution.py:466
  20.6 3.7 %collective-permute-start.2 = (bf16[256,1152]{1,0:T(8,128)(2,1)S(1)}, bf16[256,1152]{1,0:T(8,128)(2,1)S(1)}, u32[]{:S(2)}, u32[]{:S(2)}) collective-permute-start(bf16[256,1152]{1,0:T(8,128)(2,1)S(1)} %mask_image.2.p0), channel_id=1, source_target_pairs={{0,4},{1,5},{2,6},{3,7},{4,0},{5,1},{6,2},{7,3},{8,12},{9,13},{10,... | collective-permute-start | bytes 1769480 | tf_op jit(solution)/shard_map/ppermute | solution.py:501
  24.3 1.6 collective-permute-start.1
  25.9 25.0 %collective-permute-done.2.p2 = bf16[256,1152]{1,0:T(8,128)(2,1)S(1)} collective-permute-done((bf16[256,1152]{1,0:T(8,128)(2,1)S(1)}, bf16[256,1152]{1,0:T(8,128)(2,1)S(1)}, u32[]{:S(2)}, u32[]{:S(2)}) %collective-permute-start.2) | collective-permute-done | bytes 589856 | tf_op jit(solution)/shard_map/ppermute | solution.py:501
  53.2 12.7 %collective-permute-done.3.p3.p4 = bf16[256,1152]{1,0:T(8,128)(2,1)S(1)} collective-permute-done((bf16[256,1152]{1,0:T(8,128)(2,1)S(1)}, bf16[256,1152]{1,0:T(8,128)(2,1)S(1)}, u32[]{:S(2)}, u32[]{:S(2)}) %collective-permute-start.3) | collective-permute-done | bytes 589856 | tf_op jit(solution)/shard_map/ppermute | solution.py:497
  65.9 3.7 %copy-done = bf16[9216,512]{1,0:T(8,128)(2,1)S(1)} copy-done((bf16[9216,512]{1,0:T(8,128)(2,1)S(1)}, bf16[9216,512]{1,0:T(8,128)(2,1)}, u32[]{:S(2)}) %copy-start) | copy-done | bytes 9437208
  69.6 1.1 copy-done.16
  70.7 11.5 %forward.2 = (f32[256,512]{1,0:T(8,128)S(1)}, f32[256,512]{1,0:T(8,128)S(1)}) custom-call(s32[8]{0:T(128)S(1)} %concatenate.6.where, bf16[256,1152]{1,0:T(8,128)(2,1)S(1)} %mask_image.2.p0, bf16[256,1152]{1,0:T(8,128)(2,1)S(1)} %copy-done.16, bf16[256,1152]{1,0:T(8,128)(2,1)S(1)} %collective-permute-done.2.p2, ...), custom_call_target="tpu_custom_call" | custom-call | flops 2415919104 | bytes 12845056 | tf_op jit(solution)/shard_map/forward/pallas_call | solution.py:193
  82.3 2.6 collective-permute-start.7
  86.4 1.8 collective-permute-start.6
  88.8 23.2 %collective-permute-done.7.p2 = bf16[256,1152]{1,0:T(8,128)(2,1)S(1)} collective-permute-done((bf16[256,1152]{1,0:T(8,128)(2,1)S(1)}, bf16[256,1152]{1,0:T(8,128)(2,1)S(1)}, u32[]{:S(2)}, u32[]{:S(2)}) %collective-permute-start.7) | collective-permute-done | bytes 589856 | tf_op jit(solution)/shard_map/ppermute | solution.py:503
  112.1 1.3 collective-permute-start.8
  113.4 11.0 %parts.2 = (bf16[1152,256]{1,0:T(8,128)(2,1)}, bf16[1152,256]{1,0:T(8,128)(2,1)}, bf16[1152,256]{1,0:T(8,128)(2,1)S(1)}, f32[1152,256]{1,0:T(8,128)S(1)}) custom-call(s32[8]{0:T(128)S(1)} %concatenate.6.where, bf16[9216,512]{1,0:T(8,128)(2,1)S(1)} %copy-done.1, bf16[9216,512]{1,0:T(8,128)(2,1)} %copy-done.61, ...), custom_call_target="tpu_custom_call" | custom-call | flops 2415919104 | bytes 12386304 | tf_op jit(solution)/shard_map/parts/pallas_call | solution.py:295
  124.4 5.4 %collective-permute-start.26 = (bf16[1152,256]{1,0:T(8,128)(2,1)}, bf16[1152,256]{1,0:T(8,128)(2,1)}, u32[]{:S(2)}, u32[]{:S(2)}) collective-permute-start(bf16[1152,256]{1,0:T(8,128)(2,1)} %get-tuple-element.50), channel_id=1, source_target_pairs={{0,2},{1,3},{6,4},{7,5},{8,10},{9,11},{14,12},{15,13},{16,18},{17,... | collective-permute-start | bytes 1769480 | tf_op jit(solution)/shard_map/ppermute | solution.py:531
  129.8 1.3 collective-permute-start.43
  131.1 1.6 pick.2
  133.5 0.8 copy-done.58
  134.3 0.8 copy-done.7
  135.2 1.5 collective-permute-start.44
  138.1 2.1 collective-permute-start.24
  140.2 3.7 %copy-done.2 = bf16[9216,512]{1,0:T(8,128)(2,1)S(1)} copy-done((bf16[9216,512]{1,0:T(8,128)(2,1)S(1)}, bf16[9216,512]{1,0:T(8,128)(2,1)}, u32[]{:S(2)}) %copy-start.2) | copy-done | bytes 9437208
  143.9 1.1 copy-done.5
  144.9 1.1 copy-done.8
  146.0 1.1 copy-done.11
  147.1 11.4 %forward.3 = (f32[256,512]{1,0:T(8,128)S(1)}, f32[256,512]{1,0:T(8,128)S(1)}) custom-call(s32[8]{0:T(128)S(1)} %concatenate.6.where, bf16[256,1152]{1,0:T(8,128)(2,1)S(1)} %mask_image.3.p0, bf16[256,1152]{1,0:T(8,128)(2,1)S(1)} %copy-done.5, bf16[256,1152]{1,0:T(8,128)(2,1)S(1)} %collective-permute-done.7.p2, bf16[256,1152]{1,0:T(8,128)(2,1)S(1)} %copy-done.11, ...), custom_call_target="tpu_custom_call" | custom-call | flops 2415919104 | bytes 12845056 | tf_op jit(solution)/shard_map/forward/pallas_call | solution.py:193
  158.5 1.5 collective-permute-start.45
  160.0 1.4 add_convert_fusion.4
  161.4 1.6 collective-permute-start.37
  163.0 2.9 collective-permute-done.45.refs_11_
  165.9 1.4 collective-permute-start.38
  167.5 1.3 collective-permute-start.23
  169.5 1.4 add_convert_fusion.5
  171.5 19.5 %collective-permute-done.37.refs_2_ = bf16[256,1152]{1,0:T(8,128)(2,1)S(1)} collective-permute-done((bf16[256,1152]{1,0:T(8,128)(2,1)}, bf16[256,1152]{1,0:T(8,128)(2,1)S(1)}, u32[]{:S(2)}, u32[]{:S(2)}) %collective-permute-start.37) | collective-permute-done | bytes 589856 | tf_op jit(solution)/shard_map/ppermute | solution.py:519
  193.1 2.8 collective-permute-done.29.dzo
  195.9 1.3 collective-permute-start.28
  197.2 9.8 %parts.3 = (bf16[1152,256]{1,0:T(8,128)(2,1)S(1)}, bf16[1152,256]{1,0:T(8,128)(2,1)S(1)}, bf16[1152,256]{1,0:T(8,128)(2,1)S(1)}, f32[1152,256]{1,0:T(8,128)S(1)}) custom-call(s32[8]{0:T(128)S(1)} %concatenate.6.where, bf16[9216,512]{1,0:T(8,128)(2,1)S(1)} %copy-done.3, bf16[9216,512]{1,0:T(8,128)(2,1)} %collective-permute-done.10.other, ...), custom_call_target="tpu_custom_call" | custom-call | flops 2415919104 | bytes 12386304 | tf_op jit(solution)/shard_map/parts/pallas_call | solution.py:295
  207.1 0.8 copy-done.40
  208.0 1.5 collective-permute-start.53
  210.0 1.5 collective-permute-start.55
  211.5 1.6 collective-permute-start.56
  213.9 8.4 %collective-permute-done.56 = f32[8,512]{1,0:T(8,128)S(1)} collective-permute-done((f32[8,512]{1,0:T(8,128)S(1)}, f32[8,512]{1,0:T(8,128)S(1)}, u32[]{:S(2)}, u32[]{:S(2)}) %collective-permute-start.56) | collective-permute-done | bytes 16416 | tf_op jit(solution)/shard_map/ppermute | solution.py:515
  222.3 1.4 collective-permute-start.58
  223.8 1.2 pick.3
  225.8 1.1 collective-permute-done.58
  227.0 4.3 %collective-permute-start.33 = (bf16[1152,256]{1,0:T(8,128)(2,1)S(1)}, bf16[1152,256]{1,0:T(8,128)(2,1)S(1)}, u32[]{:S(2)}, u32[]{:S(2)}) collective-permute-start(bf16[1152,256]{1,0:T(8,128)(2,1)S(1)} %get-tuple-element.67), channel_id=1, source_target_pairs={{0,2},{1,3},{6,4},{7,5},{8,10},{9,11},{14,12},{15,13},{16,18},{17,... | collective-permute-start | bytes 1769480 | tf_op jit(solution)/shard_map/ppermute | solution.py:531
  231.4 0.9 collective-permute-start.13
  233.2 19.9 %collective-permute-done.12.refs_1_ = bf16[512,512]{1,0:T(8,128)(2,1)S(1)} collective-permute-done((bf16[512,512]{1,0:T(8,128)(2,1)S(1)}, bf16[512,512]{1,0:T(8,128)(2,1)S(1)}, u32[]{:S(2)}, u32[]{:S(2)}) %collective-permute-start.12) | collective-permute-done | bytes 524320 | tf_op jit(solution)/shard_map/ppermute | solution.py:497
  253.8 4.4 %collective-permute-start.31 = (bf16[1152,256]{1,0:T(8,128)(2,1)S(1)}, bf16[1152,256]{1,0:T(8,128)(2,1)S(1)}, u32[]{:S(2)}, u32[]{:S(2)}) collective-permute-start(bf16[1152,256]{1,0:T(8,128)(2,1)S(1)} %get-tuple-element.66), channel_id=1, source_target_pairs={{0,2},{1,3},{6,4},{7,5},{8,10},{9,11},{14,12},{15,13},{16,18},{17,... | collective-permute-start | bytes 1769480 | tf_op jit(solution)/shard_map/ppermute | solution.py:532
  258.3 2.2 collective-permute-start.48
  260.5 1.3 collective-permute-start.30
  262.0 15.8 %collective-permute-done.47.refs_2_ = bf16[256,1152]{1,0:T(8,128)(2,1)S(1)} collective-permute-done((bf16[256,1152]{1,0:T(8,128)(2,1)S(1)}, bf16[256,1152]{1,0:T(8,128)(2,1)S(1)}, u32[]{:S(2)}, u32[]{:S(2)}) %collective-permute-start.47) | collective-permute-done | bytes 589856 | tf_op jit(solution)/shard_map/ppermute | solution.py:519
  279.5 1.6 collective-permute-start.14
  282.7 14.9 %collective-permute-done.14.refs_2_ = bf16[512,512]{1,0:T(8,128)(2,1)S(1)} collective-permute-done((bf16[512,512]{1,0:T(8,128)(2,1)S(1)}, bf16[512,512]{1,0:T(8,128)(2,1)S(1)}, u32[]{:S(2)}, u32[]{:S(2)}) %collective-permute-start.14) | collective-permute-done | bytes 524320 | tf_op jit(solution)/shard_map/ppermute | solution.py:575
  297.5 1.3 collective-permute-start.35
  298.8 1.3 collective-permute-start.16
  300.2 7.2 %weight_grad.2 = f32[2304,512]{1,0:T(8,128)} custom-call(s32[8]{0:T(128)S(1)} %concatenate.6.where, bf16[256,1152]{1,0:T(8,128)(2,1)S(1)} %copy-done.30, bf16[256,1152]{1,0:T(8,128)(2,1)S(1)} %copy-done.33, bf16[256,1152]{1,0:T(8,128)(2,1)S(1)} %copy-done.35, bf16[256,1152]{1,0:T(8,128)(2,1)S(1)} %copy-done.37, bf16[256,1152]{1,0:T(8,128)(2,1)S(1)} %copy-done.39, ...), custom_call_target="tpu_custom_call" | custom-call | flops 2415919104 | bytes 9437184 | tf_op jit(solution)/shard_map/weight_grad/pallas_call | solution.py:446
  307.5 1.7 finish.2
  309.8 27.5 %collective-permute-done.16.refs_4_ = bf16[512,512]{1,0:T(8,128)(2,1)S(1)} collective-permute-done((bf16[512,512]{1,0:T(8,128)(2,1)S(1)}, bf16[512,512]{1,0:T(8,128)(2,1)S(1)}, u32[]{:S(2)}, u32[]{:S(2)}) %collective-permute-start.16) | collective-permute-done | bytes 524320 | tf_op jit(solution)/shard_map/ppermute | solution.py:577
  339.1 6.4 %weight_grad.3 = f32[2304,512]{1,0:T(8,128)} custom-call(s32[8]{0:T(128)S(1)} %concatenate.6.where, bf16[256,1152]{1,0:T(8,128)(2,1)S(1)} %get-tuple-element.75.refs_0_, bf16[256,1152]{1,0:T(8,128)(2,1)S(1)} %collective-permute-done.46.refs_1_, bf16[256,1152]{1,0:T(8,128)(2,1)S(1)} %collective-permute-done.47.refs_2_, ...), custom_call_target="tpu_custom_call" | custom-call | flops 2415919104 | bytes 9437184 | tf_op jit(solution)/shard_map/weight_grad/pallas_call | solution.py:446
  345.5 1.7 finish.3
  347.2 2.7 lay_out.1
  (210 shorter events, 22.1 us)
Async XLA Ops:
  5.2 15.0 %collective-permute-start = (bf16[9216,512]{1,0:T(8,128)(2,1)}, bf16[9216,512]{1,0:T(8,128)(2,1)S(1)}, u32[]{:S(2)}, u32[]{:S(2)}) collective-permute-start(bf16[9216,512]{1,0:T(8,128)(2,1)} %mine.5), channel_id=1, source_target_pairs={{0,1},{1,0},{2,3},{3,2},{4,5},{5,4},{6,7},{7,6},{8,9},{9,8},{10,11... | collective-permute-start | bytes 28311560 | tf_op jit(solution)/shard_map/ppermute | solution.py:466
  20.2 117.8 %collective-permute-start.10 = (bf16[9216,512]{1,0:T(8,128)(2,1)}, bf16[9216,512]{1,0:T(8,128)(2,1)}, u32[]{:S(2)}, u32[]{:S(2)}) collective-permute-start(bf16[9216,512]{1,0:T(8,128)(2,1)} %mine.7), channel_id=1, source_target_pairs={{0,1},{1,0},{2,3},{3,2},{4,5},{5,4},{6,7},{7,6},{8,9},{9,8},{10,11... | collective-permute-start | bytes 28311560 | tf_op jit(solution)/shard_map/ppermute | solution.py:466
  20.6 30.3 %collective-permute-start.2 = (bf16[256,1152]{1,0:T(8,128)(2,1)S(1)}, bf16[256,1152]{1,0:T(8,128)(2,1)S(1)}, u32[]{:S(2)}, u32[]{:S(2)}) collective-permute-start(bf16[256,1152]{1,0:T(8,128)(2,1)S(1)} %mask_image.2.p0), channel_id=1, source_target_pairs={{0,4},{1,5},{2,6},{3,7},{4,0},{5,1},{6,2},{7,3},{8,12},{9,13},{10,... | collective-permute-start | bytes 1769480 | tf_op jit(solution)/shard_map/ppermute | solution.py:501
  24.3 28.0 %collective-permute-start.1 = (bf16[256,1152]{1,0:T(8,128)(2,1)S(1)}, bf16[256,1152]{1,0:T(8,128)(2,1)S(1)}, u32[]{:S(2)}, u32[]{:S(2)}) collective-permute-start(bf16[256,1152]{1,0:T(8,128)(2,1)S(1)} %mask_image.2.p0), channel_id=1, source_target_pairs={{0,2},{1,3},{2,0},{3,1},{4,6},{5,7},{6,4},{7,5},{8,10},{9,11},{10,... | collective-permute-start | bytes 1769480 | tf_op jit(solution)/shard_map/ppermute | solution.py:497
  50.9 15.0 %collective-permute-start.3 = (bf16[256,1152]{1,0:T(8,128)(2,1)S(1)}, bf16[256,1152]{1,0:T(8,128)(2,1)S(1)}, u32[]{:S(2)}, u32[]{:S(2)}) collective-permute-start(bf16[256,1152]{1,0:T(8,128)(2,1)S(1)} %collective-permute-done.2.p2), channel_id=1, source_target_pairs={{0,2},{1,3},{2,0},{3,1},{4,6},{5,7},{6,4},{7,5},{8,10},{9,11},{10,... | collective-permute-start | bytes 1769480 | tf_op jit(solution)/shard_map/ppermute | solution.py:497
  70.7 42.7 %copy-start.1 = (bf16[9216,512]{1,0:T(8,128)(2,1)S(1)}, bf16[9216,512]{1,0:T(8,128)(2,1)}, u32[]{:S(2)}) copy-start(bf16[9216,512]{1,0:T(8,128)(2,1)} %mine.5) | copy-start | bytes 28311556
  82.2 2.7 collective-permute-start.4
  82.3 29.8 %collective-permute-start.7 = (bf16[256,1152]{1,0:T(8,128)(2,1)S(1)}, bf16[256,1152]{1,0:T(8,128)(2,1)S(1)}, u32[]{:S(2)}, u32[]{:S(2)}) collective-permute-start(bf16[256,1152]{1,0:T(8,128)(2,1)S(1)} %mask_image.3.p0), channel_id=1, source_target_pairs={{0,4},{1,5},{2,6},{3,7},{4,0},{5,1},{6,2},{7,3},{8,12},{9,13},{10,... | collective-permute-start | bytes 1769480 | tf_op jit(solution)/shard_map/ppermute | solution.py:503
  86.2 44.8 %copy-start.14 = (bf16[256,1152]{1,0:T(8,128)(2,1)S(1)}, bf16[256,1152]{1,0:T(8,128)(2,1)}, u32[]{:S(2)}) copy-start(bf16[256,1152]{1,0:T(8,128)(2,1)} %copy-done.13) | copy-start | bytes 1769476
  86.2 44.8 %copy-start.17 = (bf16[256,1152]{1,0:T(8,128)(2,1)S(1)}, bf16[256,1152]{1,0:T(8,128)(2,1)}, u32[]{:S(2)}) copy-start(bf16[256,1152]{1,0:T(8,128)(2,1)} %copy-done.15) | copy-start | bytes 1769476
  86.2 27.1 %collective-permute-start.5 = (bf16[256,512]{1,0:T(8,128)(2,1)S(1)}, bf16[256,512]{1,0:T(8,128)(2,1)S(1)}, u32[]{:S(2)}, u32[]{:S(2)}) collective-permute-start(bf16[256,512]{1,0:T(8,128)(2,1)S(1)} %get-tuple-element.73.dz.refs_8_), channel_id=1, source_target_pairs={{0,1},{1,0},{2,3},{3,2},{4,5},{5,4},{6,7},{7,6},{8,9},{9,8},{10,11... | collective-permute-start | bytes 786440 | tf_op jit(solution)/shard_map/ppermute | solution.py:466
  86.4 43.4 %collective-permute-start.6 = (bf16[256,1152]{1,0:T(8,128)(2,1)S(1)}, bf16[256,1152]{1,0:T(8,128)(2,1)S(1)}, u32[]{:S(2)}, u32[]{:S(2)}) collective-permute-start(bf16[256,1152]{1,0:T(8,128)(2,1)S(1)} %mask_image.3.p0), channel_id=1, source_target_pairs={{0,2},{1,3},{2,0},{3,1},{4,6},{5,7},{6,4},{7,5},{8,10},{9,11},{10,... | collective-permute-start | bytes 1769480 | tf_op jit(solution)/shard_map/ppermute | solution.py:497
  88.2 46.2 %collective-permute-start.9 = (bf16[256,1152]{1,0:T(8,128)(2,1)S(1)}, bf16[256,1152]{1,0:T(8,128)(2,1)S(1)}, u32[]{:S(2)}, u32[]{:S(2)}) collective-permute-start(bf16[256,1152]{1,0:T(8,128)(2,1)S(1)} %mask_image.3.p0), channel_id=1, source_target_pairs={{2,4},{3,5},{4,2},{5,3},{10,12},{11,13},{12,10},{13,11},{18,20},{1... | collective-permute-start | bytes 1769480 | tf_op jit(solution)/shard_map/ppermute | solution.py:509
  112.1 24.6 %collective-permute-start.8 = (bf16[256,1152]{1,0:T(8,128)(2,1)S(1)}, bf16[256,1152]{1,0:T(8,128)(2,1)S(1)}, u32[]{:S(2)}, u32[]{:S(2)}) collective-permute-start(bf16[256,1152]{1,0:T(8,128)(2,1)S(1)} %collective-permute-done.7.p2), channel_id=1, source_target_pairs={{2,0},{3,1},{4,6},{5,7},{10,8},{11,9},{12,14},{13,15},{18,16},{19,... | collective-permute-start | bytes 1769480 | tf_op jit(solution)/shard_map/ppermute | solution.py:510
  124.4 35.6 %collective-permute-start.26 = (bf16[1152,256]{1,0:T(8,128)(2,1)}, bf16[1152,256]{1,0:T(8,128)(2,1)}, u32[]{:S(2)}, u32[]{:S(2)}) collective-permute-start(bf16[1152,256]{1,0:T(8,128)(2,1)} %get-tuple-element.50), channel_id=1, source_target_pairs={{0,2},{1,3},{6,4},{7,5},{8,10},{9,11},{14,12},{15,13},{16,18},{17,... | collective-permute-start | bytes 1769480 | tf_op jit(solution)/shard_map/ppermute | solution.py:531
  129.8 28.7 %collective-permute-start.43 = (bf16[256,512]{1,0:T(8,128)(2,1)S(1)}, bf16[256,512]{1,0:T(8,128)(2,1)}, u32[]{:S(2)}, u32[]{:S(2)}) collective-permute-start(bf16[256,512]{1,0:T(8,128)(2,1)S(1)} %get-tuple-element.73.dz.refs_8_), channel_id=1, source_target_pairs={{0,8},{8,0},{16,24},{24,16},{1,9},{9,1},{17,25},{25,17},{2,10},{10... | collective-permute-start | bytes 786440 | tf_op jit(solution)/shard_map/ppermute | solution.py:515
  135.2 26.2 %collective-permute-start.44 = (bf16[256,512]{1,0:T(8,128)(2,1)S(1)}, bf16[256,512]{1,0:T(8,128)(2,1)S(1)}, u32[]{:S(2)}, u32[]{:S(2)}) collective-permute-start(bf16[256,512]{1,0:T(8,128)(2,1)S(1)} %get-tuple-element.73.dz.refs_8_), channel_id=1, source_target_pairs={{0,16},{8,24},{16,0},{24,8},{1,17},{9,25},{17,1},{25,9},{2,18},{10... | collective-permute-start | bytes 786440 | tf_op jit(solution)/shard_map/ppermute | solution.py:515
  137.5 29.8 %collective-permute-start.36 = (bf16[256,1152]{1,0:T(8,128)(2,1)}, bf16[256,1152]{1,0:T(8,128)(2,1)S(1)}, u32[]{:S(2)}, u32[]{:S(2)}) collective-permute-start(bf16[256,1152]{1,0:T(8,128)(2,1)} %get-tuple-element.70), channel_id=1, source_target_pairs={{0,8},{8,0},{16,24},{24,16},{1,9},{9,1},{17,25},{25,17},{2,10},{10... | collective-permute-start | bytes 1769480 | tf_op jit(solution)/shard_map/ppermute | solution.py:519
  138.1 29.4 %collective-permute-start.24 = (bf16[1152,256]{1,0:T(8,128)(2,1)}, bf16[1152,256]{1,0:T(8,128)(2,1)}, u32[]{:S(2)}, u32[]{:S(2)}) collective-permute-start(bf16[1152,256]{1,0:T(8,128)(2,1)} %get-tuple-element.62), channel_id=1, source_target_pairs={{0,2},{1,3},{6,4},{7,5},{8,10},{9,11},{14,12},{15,13},{16,18},{17,... | collective-permute-start | bytes 1769480 | tf_op jit(solution)/shard_map/ppermute | solution.py:532
  147.1 50.2 %copy-start.3 = (bf16[9216,512]{1,0:T(8,128)(2,1)S(1)}, bf16[9216,512]{1,0:T(8,128)(2,1)}, u32[]{:S(2)}) copy-start(bf16[9216,512]{1,0:T(8,128)(2,1)} %mine.7) | copy-start | bytes 28311556
  158.5 7.4 %collective-permute-start.45 = (bf16[256,512]{1,0:T(8,128)(2,1)S(1)}, bf16[256,512]{1,0:T(8,128)(2,1)S(1)}, u32[]{:S(2)}, u32[]{:S(2)}) collective-permute-start(bf16[256,512]{1,0:T(8,128)(2,1)S(1)} %get-tuple-element.73.dz.refs_8_), channel_id=1, source_target_pairs={{0,24},{8,16},{16,8},{24,0},{1,25},{9,17},{17,9},{25,1},{2,26},{10... | collective-permute-start | bytes 786440 | tf_op jit(solution)/shard_map/ppermute | solution.py:515
  160.0 8.8 %collective-permute-start.11 = (f32[256,512]{1,0:T(8,128)S(1)}, f32[256,512]{1,0:T(8,128)S(1)}, u32[]{:S(2)}, u32[]{:S(2)}) collective-permute-start(f32[256,512]{1,0:T(8,128)S(1)} %get-tuple-element.55), channel_id=1, source_target_pairs={{0,1},{1,0},{2,3},{3,2},{4,5},{5,4},{6,7},{7,6},{8,9},{9,8},{10,11... | collective-permute-start | bytes 1572872 | tf_op jit(solution)/shard_map/ppermute | solution.py:466
  161.4 29.7 %collective-permute-start.37 = (bf16[256,1152]{1,0:T(8,128)(2,1)}, bf16[256,1152]{1,0:T(8,128)(2,1)S(1)}, u32[]{:S(2)}, u32[]{:S(2)}) collective-permute-start(bf16[256,1152]{1,0:T(8,128)(2,1)} %copy-done.60), channel_id=1, source_target_pairs={{0,16},{8,24},{16,0},{24,8},{1,17},{9,25},{17,1},{25,9},{2,18},{10... | collective-permute-start | bytes 1769480 | tf_op jit(solution)/shard_map/ppermute | solution.py:519
  165.9 25.9 %collective-permute-start.38 = (bf16[256,1152]{1,0:T(8,128)(2,1)S(1)}, bf16[256,1152]{1,0:T(8,128)(2,1)S(1)}, u32[]{:S(2)}, u32[]{:S(2)}) collective-permute-start(bf16[256,1152]{1,0:T(8,128)(2,1)S(1)} %copy-done.59), channel_id=1, source_target_pairs={{0,24},{8,16},{16,8},{24,0},{1,25},{9,17},{17,9},{25,1},{2,26},{10... | collective-permute-start | bytes 1769480 | tf_op jit(solution)/shard_map/ppermute | solution.py:519
  167.4 24.6 %collective-permute-start.39 = (bf16[256,1152]{1,0:T(8,128)(2,1)S(1)}, bf16[256,1152]{1,0:T(8,128)(2,1)S(1)}, u32[]{:S(2)}, u32[]{:S(2)}) collective-permute-start(bf16[256,1152]{1,0:T(8,128)(2,1)S(1)} %copy-done.29), channel_id=1, source_target_pairs={{0,1},{1,0},{2,3},{3,2},{4,5},{5,4},{6,7},{7,6},{8,9},{9,8},{10,11... | collective-permute-start | bytes 1769480 | tf_op jit(solution)/shard_map/ppermute | solution.py:466
  167.5 24.9 %collective-permute-start.23 = (bf16[1152,256]{1,0:T(8,128)(2,1)S(1)}, bf16[1152,256]{1,0:T(8,128)(2,1)S(1)}, u32[]{:S(2)}, u32[]{:S(2)}) collective-permute-start(bf16[1152,256]{1,0:T(8,128)(2,1)S(1)} %copy-done.25), channel_id=1, source_target_pairs={{0,2},{1,3},{6,4},{7,5},{8,10},{9,11},{14,12},{15,13},{16,18},{17,... | collective-permute-start | bytes 1769480 | tf_op jit(solution)/shard_map/ppermute | solution.py:533
  168.8 23.7 %collective-permute-start.27 = (bf16[1152,256]{1,0:T(8,128)(2,1)S(1)}, bf16[1152,256]{1,0:T(8,128)(2,1)S(1)}, u32[]{:S(2)}, u32[]{:S(2)}) collective-permute-start(bf16[1152,256]{1,0:T(8,128)(2,1)S(1)} %add_convert_fusion.4), channel_id=1, source_target_pairs={{2,4},{3,5},{4,2},{5,3},{10,12},{11,13},{12,10},{13,11},{18,20},{1... | collective-permute-start | bytes 1769480 | tf_op jit(solution)/shard_map/ppermute | solution.py:534
  191.1 20.4 %collective-permute-start.25 = (bf16[1152,256]{1,0:T(8,128)(2,1)S(1)}, bf16[1152,256]{1,0:T(8,128)(2,1)S(1)}, u32[]{:S(2)}, u32[]{:S(2)}) collective-permute-start(bf16[1152,256]{1,0:T(8,128)(2,1)S(1)} %add_convert_fusion.5), channel_id=1, source_target_pairs={{2,4},{3,5},{4,2},{5,3},{10,12},{11,13},{12,10},{13,11},{18,20},{1... | collective-permute-start | bytes 1769480 | tf_op jit(solution)/shard_map/ppermute | solution.py:535
  191.8 15.3 %collective-permute-start.40 = (bf16[256,1152]{1,0:T(8,128)(2,1)S(1)}, bf16[256,1152]{1,0:T(8,128)(2,1)S(1)}, u32[]{:S(2)}, u32[]{:S(2)}) collective-permute-start(bf16[256,1152]{1,0:T(8,128)(2,1)S(1)} %copy-done.32), channel_id=1, source_target_pairs={{0,1},{1,0},{2,3},{3,2},{4,5},{5,4},{6,7},{7,6},{8,9},{9,8},{10,11... | collective-permute-start | bytes 1769480 | tf_op jit(solution)/shard_map/ppermute | solution.py:466
  192.0 17.5 %collective-permute-start.41 = (bf16[256,1152]{1,0:T(8,128)(2,1)S(1)}, bf16[256,1152]{1,0:T(8,128)(2,1)S(1)}, u32[]{:S(2)}, u32[]{:S(2)}) collective-permute-start(bf16[256,1152]{1,0:T(8,128)(2,1)S(1)} %collective-permute-done.37.refs_2_), channel_id=1, source_target_pairs={{0,1},{1,0},{2,3},{3,2},{4,5},{5,4},{6,7},{7,6},{8,9},{9,8},{10,11... | collective-permute-start | bytes 1769480 | tf_op jit(solution)/shard_map/ppermute | solution.py:466
  192.4 17.6 %collective-permute-start.42 = (bf16[256,1152]{1,0:T(8,128)(2,1)S(1)}, bf16[256,1152]{1,0:T(8,128)(2,1)S(1)}, u32[]{:S(2)}, u32[]{:S(2)}) collective-permute-start(bf16[256,1152]{1,0:T(8,128)(2,1)S(1)} %collective-permute-done.38.refs_3_), channel_id=1, source_target_pairs={{0,1},{1,0},{2,3},{3,2},{4,5},{5,4},{6,7},{7,6},{8,9},{9,8},{10,11... | collective-permute-start | bytes 1769480 | tf_op jit(solution)/shard_map/ppermute | solution.py:466
  192.5 3.4 collective-permute-start.29
  195.9 17.3 %collective-permute-start.28 = (bf16[1152,256]{1,0:T(8,128)(2,1)S(1)}, bf16[1152,256]{1,0:T(8,128)(2,1)S(1)}, u32[]{:S(2)}, u32[]{:S(2)}) collective-permute-start(bf16[1152,256]{1,0:T(8,128)(2,1)S(1)} %add_convert_fusion.3), channel_id=1, source_target_pairs={{2,0},{3,1},{4,6},{5,7},{10,8},{11,9},{12,14},{13,15},{18,16},{19,... | collective-permute-start | bytes 1769480 | tf_op jit(solution)/shard_map/ppermute | solution.py:536
  208.0 23.3 %collective-permute-start.53 = (bf16[256,512]{1,0:T(8,128)(2,1)S(1)}, bf16[256,512]{1,0:T(8,128)(2,1)S(1)}, u32[]{:S(2)}, u32[]{:S(2)}) collective-permute-start(bf16[256,512]{1,0:T(8,128)(2,1)S(1)} %get-tuple-element.79.dz.refs_8_), channel_id=1, source_target_pairs={{0,8},{8,0},{16,24},{24,16},{1,9},{9,1},{17,25},{25,17},{2,10},{10... | collective-permute-start | bytes 786440 | tf_op jit(solution)/shard_map/ppermute | solution.py:515
  209.5 21.9 %collective-permute-start.54 = (bf16[256,512]{1,0:T(8,128)(2,1)S(1)}, bf16[256,512]{1,0:T(8,128)(2,1)S(1)}, u32[]{:S(2)}, u32[]{:S(2)}) collective-permute-start(bf16[256,512]{1,0:T(8,128)(2,1)S(1)} %get-tuple-element.79.dz.refs_8_), channel_id=1, source_target_pairs={{0,16},{8,24},{16,0},{24,8},{1,17},{9,25},{17,1},{25,9},{2,18},{10... | collective-permute-start | bytes 786440 | tf_op jit(solution)/shard_map/ppermute | solution.py:515
  210.0 22.3 %collective-permute-start.55 = (bf16[256,512]{1,0:T(8,128)(2,1)S(1)}, bf16[256,512]{1,0:T(8,128)(2,1)S(1)}, u32[]{:S(2)}, u32[]{:S(2)}) collective-permute-start(bf16[256,512]{1,0:T(8,128)(2,1)S(1)} %get-tuple-element.79.dz.refs_8_), channel_id=1, source_target_pairs={{0,24},{8,16},{16,8},{24,0},{1,25},{9,17},{17,9},{25,1},{2,26},{10... | collective-permute-start | bytes 786440 | tf_op jit(solution)/shard_map/ppermute | solution.py:515
  211.5 10.8 %collective-permute-start.56 = (f32[8,512]{1,0:T(8,128)S(1)}, f32[8,512]{1,0:T(8,128)S(1)}, u32[]{:S(2)}, u32[]{:S(2)}) collective-permute-start(f32[8,512]{1,0:T(8,128)S(1)} %pad_maximum_fusion), channel_id=1, source_target_pairs={{0,8},{8,0},{16,24},{24,16},{1,9},{9,1},{17,25},{25,17},{2,10},{10... | collective-permute-start | bytes 49160 | tf_op jit(solution)/shard_map/ppermute | solution.py:515
  213.2 11.8 %collective-permute-start.57 = (f32[8,512]{1,0:T(8,128)S(1)}, f32[8,512]{1,0:T(8,128)S(1)}, u32[]{:S(2)}, u32[]{:S(2)}) collective-permute-start(f32[8,512]{1,0:T(8,128)S(1)} %pad_maximum_fusion), channel_id=1, source_target_pairs={{0,16},{8,24},{16,0},{24,8},{1,17},{9,25},{17,1},{25,9},{2,18},{10... | collective-permute-start | bytes 49160 | tf_op jit(solution)/shard_map/ppermute | solution.py:515
  222.3 4.6 %collective-permute-start.58 = (f32[8,512]{1,0:T(8,128)S(1)}, f32[8,512]{1,0:T(8,128)S(1)}, u32[]{:S(2)}, u32[]{:S(2)}) collective-permute-start(f32[8,512]{1,0:T(8,128)S(1)} %pad_maximum_fusion), channel_id=1, source_target_pairs={{0,24},{8,16},{16,8},{24,0},{1,25},{9,17},{17,9},{25,1},{2,26},{10... | collective-permute-start | bytes 49160 | tf_op jit(solution)/shard_map/ppermute | solution.py:515
  225.0 35.5 %collective-permute-start.46 = (bf16[256,1152]{1,0:T(8,128)(2,1)S(1)}, bf16[256,1152]{1,0:T(8,128)(2,1)S(1)}, u32[]{:S(2)}, u32[]{:S(2)}) collective-permute-start(bf16[256,1152]{1,0:T(8,128)(2,1)S(1)} %get-tuple-element.76), channel_id=1, source_target_pairs={{0,8},{8,0},{16,24},{24,16},{1,9},{9,1},{17,25},{25,17},{2,10},{10... | collective-permute-start | bytes 1769480 | tf_op jit(solution)/shard_map/ppermute | solution.py:519
  227.0 33.5 %collective-permute-start.33 = (bf16[1152,256]{1,0:T(8,128)(2,1)S(1)}, bf16[1152,256]{1,0:T(8,128)(2,1)S(1)}, u32[]{:S(2)}, u32[]{:S(2)}) collective-permute-start(bf16[1152,256]{1,0:T(8,128)(2,1)S(1)} %get-tuple-element.67), channel_id=1, source_target_pairs={{0,2},{1,3},{6,4},{7,5},{8,10},{9,11},{14,12},{15,13},{16,18},{17,... | collective-permute-start | bytes 1769480 | tf_op jit(solution)/shard_map/ppermute | solution.py:531
  231.3 21.8 %collective-permute-start.12 = (bf16[512,512]{1,0:T(8,128)(2,1)S(1)}, bf16[512,512]{1,0:T(8,128)(2,1)S(1)}, u32[]{:S(2)}, u32[]{:S(2)}) collective-permute-start(bf16[512,512]{1,0:T(8,128)(2,1)S(1)} %get-tuple-element.57.refs_0_), channel_id=1, source_target_pairs={{0,2},{1,3},{2,0},{3,1},{4,6},{5,7},{6,4},{7,5},{8,10},{9,11},{10,... | collective-permute-start | bytes 1572872 | tf_op jit(solution)/shard_map/ppermute | solution.py:497
  231.4 22.4 %collective-permute-start.13 = (bf16[512,512]{1,0:T(8,128)(2,1)S(1)}, bf16[512,512]{1,0:T(8,128)(2,1)S(1)}, u32[]{:S(2)}, u32[]{:S(2)}) collective-permute-start(bf16[512,512]{1,0:T(8,128)(2,1)S(1)} %get-tuple-element.57.refs_0_), channel_id=1, source_target_pairs={{2,4},{3,5},{4,2},{5,3},{10,12},{11,13},{12,10},{13,11},{18,20},{1... | collective-permute-start | bytes 1572872 | tf_op jit(solution)/shard_map/ppermute | solution.py:573
  232.3 26.0 %collective-permute-start.17 = (bf16[512,512]{1,0:T(8,128)(2,1)S(1)}, bf16[512,512]{1,0:T(8,128)(2,1)S(1)}, u32[]{:S(2)}, u32[]{:S(2)}) collective-permute-start(bf16[512,512]{1,0:T(8,128)(2,1)S(1)} %get-tuple-element.57.refs_0_), channel_id=1, source_target_pairs={{0,1},{1,0},{2,3},{3,2},{4,5},{5,4},{6,7},{7,6},{8,9},{9,8},{10,11... | collective-permute-start | bytes 1572872 | tf_op jit(solution)/shard_map/ppermute | solution.py:466
  253.1 24.8 %collective-permute-start.47 = (bf16[256,1152]{1,0:T(8,128)(2,1)S(1)}, bf16[256,1152]{1,0:T(8,128)(2,1)S(1)}, u32[]{:S(2)}, u32[]{:S(2)}) collective-permute-start(bf16[256,1152]{1,0:T(8,128)(2,1)S(1)} %get-tuple-element.77), channel_id=1, source_target_pairs={{0,16},{8,24},{16,0},{24,8},{1,17},{9,25},{17,1},{25,9},{2,18},{10... | collective-permute-start | bytes 1769480 | tf_op jit(solution)/shard_map/ppermute | solution.py:519
  253.8 24.7 %collective-permute-start.31 = (bf16[1152,256]{1,0:T(8,128)(2,1)S(1)}, bf16[1152,256]{1,0:T(8,128)(2,1)S(1)}, u32[]{:S(2)}, u32[]{:S(2)}) collective-permute-start(bf16[1152,256]{1,0:T(8,128)(2,1)S(1)} %get-tuple-element.66), channel_id=1, source_target_pairs={{0,2},{1,3},{6,4},{7,5},{8,10},{9,11},{14,12},{15,13},{16,18},{17,... | collective-permute-start | bytes 1769480 | tf_op jit(solution)/shard_map/ppermute | solution.py:532
  258.3 21.2 %collective-permute-start.48 = (bf16[256,1152]{1,0:T(8,128)(2,1)S(1)}, bf16[256,1152]{1,0:T(8,128)(2,1)S(1)}, u32[]{:S(2)}, u32[]{:S(2)}) collective-permute-start(bf16[256,1152]{1,0:T(8,128)(2,1)S(1)} %get-tuple-element.78), channel_id=1, source_target_pairs={{0,24},{8,16},{16,8},{24,0},{1,25},{9,17},{17,9},{25,1},{2,26},{10... | collective-permute-start | bytes 1769480 | tf_op jit(solution)/shard_map/ppermute | solution.py:519
  260.5 20.6 %collective-permute-start.49 = (bf16[256,1152]{1,0:T(8,128)(2,1)S(1)}, bf16[256,1152]{1,0:T(8,128)(2,1)S(1)}, u32[]{:S(2)}, u32[]{:S(2)}) collective-permute-start(bf16[256,1152]{1,0:T(8,128)(2,1)S(1)} %get-tuple-element.75.refs_0_), channel_id=1, source_target_pairs={{0,1},{1,0},{2,3},{3,2},{4,5},{5,4},{6,7},{7,6},{8,9},{9,8},{10,11... | collective-permute-start | bytes 1769480 | tf_op jit(solution)/shard_map/ppermute | solution.py:466
  260.5 21.3 %collective-permute-start.30 = (bf16[1152,256]{1,0:T(8,128)(2,1)S(1)}, bf16[1152,256]{1,0:T(8,128)(2,1)S(1)}, u32[]{:S(2)}, u32[]{:S(2)}) collective-permute-start(bf16[1152,256]{1,0:T(8,128)(2,1)S(1)} %get-tuple-element.65), channel_id=1, source_target_pairs={{0,2},{1,3},{6,4},{7,5},{8,10},{9,11},{14,12},{15,13},{16,18},{17,... | collective-permute-start | bytes 1769480 | tf_op jit(solution)/shard_map/ppermute | solution.py:533
  261.8 38.3 %copy-start.43 = (bf16[256,1152]{1,0:T(8,128)(2,1)S(1)}, bf16[256,1152]{1,0:T(8,128)(2,1)}, u32[]{:S(2)}) copy-start(bf16[256,1152]{1,0:T(8,128)(2,1)} %copy-done.42) | copy-start | bytes 1769476
  277.8 4.5 %collective-permute-start.34 = (bf16[1152,256]{1,0:T(8,128)(2,1)S(1)}, bf16[1152,256]{1,0:T(8,128)(2,1)S(1)}, u32[]{:S(2)}, u32[]{:S(2)}) collective-permute-start(bf16[1152,256]{1,0:T(8,128)(2,1)S(1)} %add_convert_fusion.1), channel_id=1, source_target_pairs={{2,4},{3,5},{4,2},{5,3},{10,12},{11,13},{12,10},{13,11},{18,20},{1... | collective-permute-start | bytes 1769480 | tf_op jit(solution)/shard_map/ppermute | solution.py:534
  278.6 3.3 collective-permute-start.15
  279.5 18.0 %collective-permute-start.14 = (bf16[512,512]{1,0:T(8,128)(2,1)S(1)}, bf16[512,512]{1,0:T(8,128)(2,1)S(1)}, u32[]{:S(2)}, u32[]{:S(2)}) collective-permute-start(bf16[512,512]{1,0:T(8,128)(2,1)S(1)} %collective-permute-done.13.refs_5_), channel_id=1, source_target_pairs={{2,0},{3,1},{4,6},{5,7},{10,8},{11,9},{12,14},{13,15},{18,16},{19,... | collective-permute-start | bytes 1572872 | tf_op jit(solution)/shard_map/ppermute | solution.py:575
  281.1 28.7 %collective-permute-start.32 = (bf16[1152,256]{1,0:T(8,128)(2,1)S(1)}, bf16[1152,256]{1,0:T(8,128)(2,1)S(1)}, u32[]{:S(2)}, u32[]{:S(2)}) collective-permute-start(bf16[1152,256]{1,0:T(8,128)(2,1)S(1)} %add_convert_fusion.2), channel_id=1, source_target_pairs={{2,4},{3,5},{4,2},{5,3},{10,12},{11,13},{12,10},{13,11},{18,20},{1... | collective-permute-start | bytes 1769480 | tf_op jit(solution)/shard_map/ppermute | solution.py:535
  281.8 17.0 %collective-permute-start.50 = (bf16[256,1152]{1,0:T(8,128)(2,1)S(1)}, bf16[256,1152]{1,0:T(8,128)(2,1)S(1)}, u32[]{:S(2)}, u32[]{:S(2)}) collective-permute-start(bf16[256,1152]{1,0:T(8,128)(2,1)S(1)} %collective-permute-done.46.refs_1_), channel_id=1, source_target_pairs={{0,1},{1,0},{2,3},{3,2},{4,5},{5,4},{6,7},{7,6},{8,9},{9,8},{10,11... | collective-permute-start | bytes 1769480 | tf_op jit(solution)/shard_map/ppermute | solution.py:466
  281.9 27.3 %collective-permute-start.51 = (bf16[256,1152]{1,0:T(8,128)(2,1)S(1)}, bf16[256,1152]{1,0:T(8,128)(2,1)S(1)}, u32[]{:S(2)}, u32[]{:S(2)}) collective-permute-start(bf16[256,1152]{1,0:T(8,128)(2,1)S(1)} %collective-permute-done.47.refs_2_), channel_id=1, source_target_pairs={{0,1},{1,0},{2,3},{3,2},{4,5},{5,4},{6,7},{7,6},{8,9},{9,8},{10,11... | collective-permute-start | bytes 1769480 | tf_op jit(solution)/shard_map/ppermute | solution.py:466
  282.4 26.9 %collective-permute-start.52 = (bf16[256,1152]{1,0:T(8,128)(2,1)S(1)}, bf16[256,1152]{1,0:T(8,128)(2,1)S(1)}, u32[]{:S(2)}, u32[]{:S(2)}) collective-permute-start(bf16[256,1152]{1,0:T(8,128)(2,1)S(1)} %collective-permute-done.48.refs_3_), channel_id=1, source_target_pairs={{0,1},{1,0},{2,3},{3,2},{4,5},{5,4},{6,7},{7,6},{8,9},{9,8},{10,11... | collective-permute-start | bytes 1769480 | tf_op jit(solution)/shard_map/ppermute | solution.py:466
  297.5 39.8 %collective-permute-start.35 = (bf16[1152,256]{1,0:T(8,128)(2,1)S(1)}, bf16[1152,256]{1,0:T(8,128)(2,1)S(1)}, u32[]{:S(2)}, u32[]{:S(2)}) collective-permute-start(bf16[1152,256]{1,0:T(8,128)(2,1)S(1)} %add_convert_fusion), channel_id=1, source_target_pairs={{2,0},{3,1},{4,6},{5,7},{10,8},{11,9},{12,14},{13,15},{18,16},{19,... | collective-permute-start | bytes 1769480 | tf_op jit(solution)/shard_map/ppermute | solution.py:536
  298.8 38.5 %collective-permute-start.16 = (bf16[512,512]{1,0:T(8,128)(2,1)S(1)}, bf16[512,512]{1,0:T(8,128)(2,1)S(1)}, u32[]{:S(2)}, u32[]{:S(2)}) collective-permute-start(bf16[512,512]{1,0:T(8,128)(2,1)S(1)} %collective-permute-done.15.refs_3_), channel_id=1, source_target_pairs={{2,0},{3,1},{4,6},{5,7},{10,8},{11,9},{12,14},{13,15},{18,16},{19,... | collective-permute-start | bytes 1572872 | tf_op jit(solution)/shard_map/ppermute | solution.py:577
  309.2 38.0 %collective-permute-start.18 = (bf16[512,512]{1,0:T(8,128)(2,1)S(1)}, bf16[512,512]{1,0:T(8,128)(2,1)S(1)}, u32[]{:S(2)}, u32[]{:S(2)}) collective-permute-start(bf16[512,512]{1,0:T(8,128)(2,1)S(1)} %collective-permute-done.12.refs_1_), channel_id=1, source_target_pairs={{0,1},{1,0},{2,3},{3,2},{4,5},{5,4},{6,7},{7,6},{8,9},{9,8},{10,11... | collective-permute-start | bytes 1572872 | tf_op jit(solution)/shard_map/ppermute | solution.py:466
  309.3 38.0 %collective-permute-start.22 = (bf16[512,512]{1,0:T(8,128)(2,1)S(1)}, bf16[512,512]{1,0:T(8,128)(2,1)S(1)}, u32[]{:S(2)}, u32[]{:S(2)}) collective-permute-start(bf16[512,512]{1,0:T(8,128)(2,1)S(1)} %collective-permute-done.13.refs_5_), channel_id=1, source_target_pairs={{0,1},{1,0},{2,3},{3,2},{4,5},{5,4},{6,7},{7,6},{8,9},{9,8},{10,11... | collective-permute-start | bytes 1572872 | tf_op jit(solution)/shard_map/ppermute | solution.py:466
  309.7 37.5 %collective-permute-start.20 = (bf16[512,512]{1,0:T(8,128)(2,1)S(1)}, bf16[512,512]{1,0:T(8,128)(2,1)S(1)}, u32[]{:S(2)}, u32[]{:S(2)}) collective-permute-start(bf16[512,512]{1,0:T(8,128)(2,1)S(1)} %collective-permute-done.15.refs_3_), channel_id=1, source_target_pairs={{0,1},{1,0},{2,3},{3,2},{4,5},{5,4},{6,7},{7,6},{8,9},{9,8},{10,11... | collective-permute-start | bytes 1572872 | tf_op jit(solution)/shard_map/ppermute | solution.py:466
  337.4 9.8 %collective-permute-start.19 = (bf16[512,512]{1,0:T(8,128)(2,1)S(1)}, bf16[512,512]{1,0:T(8,128)(2,1)S(1)}, u32[]{:S(2)}, u32[]{:S(2)}) collective-permute-start(bf16[512,512]{1,0:T(8,128)(2,1)S(1)} %collective-permute-done.14.refs_2_), channel_id=1, source_target_pairs={{0,1},{1,0},{2,3},{3,2},{4,5},{5,4},{6,7},{7,6},{8,9},{9,8},{10,11... | collective-permute-start | bytes 1572872 | tf_op jit(solution)/shard_map/ppermute | solution.py:466
  337.4 9.8 %collective-permute-start.21 = (bf16[512,512]{1,0:T(8,128)(2,1)S(1)}, bf16[512,512]{1,0:T(8,128)(2,1)S(1)}, u32[]{:S(2)}, u32[]{:S(2)}) collective-permute-start(bf16[512,512]{1,0:T(8,128)(2,1)S(1)} %collective-permute-done.16.refs_4_), channel_id=1, source_target_pairs={{0,1},{1,0},{2,3},{3,2},{4,5},{5,4},{6,7},{7,6},{8,9},{9,8},{10,11... | collective-permute-start | bytes 1572872 | tf_op jit(solution)/shard_map/ppermute | solution.py:466
  (58 other events, 728.2 us)

commit v3 on v0

v3 whole, which is shorter than its diff:
```python
import functools

import jax
import jax.numpy as jnp
from jax import lax
from jax.experimental import pallas as pl
from jax.experimental.pallas import tpu as pltpu
from jax.sharding import PartitionSpec as P

CH = 256
POS = 36


def keep_block(image_group, position_mask, first_col, cols):
    positions = (first_col + lax.iota(jnp.int32, cols)) // CH
    onehot = (positions[:, None] == lax.iota(jnp.int32, POS)[None, :]).astype(jnp.float32)
    per_position = jnp.dot(onehot, position_mask.astype(jnp.float32).T)
    return jnp.where(
        image_group[:, None] == 1, per_position[:, 1][None, :], per_position[:, 0][None, :]
    )


def general_shards(
    image_a,
    image_b,
    image_group,
    position_mask,
    weight_a,
    weight_b,
    tower_bias,
    stitch,
    cotan_a,
    cotan_b,
):
    batch_rows = image_a.shape[0]
    shard_cols = image_a.shape[1]
    first_col = lax.axis_index("mp") * shard_cols
    keep_mask = keep_block(image_group, position_mask, first_col, shard_cols)
    keep_low = keep_mask.astype(jnp.bfloat16)
    contract_rows = (((0,), (0,)), ((), ()))
    contract_units = (((1,), (1,)), ((), ()))
    full_a = lax.all_gather(image_a * keep_low, "mp", axis=1, tiled=True)
    full_b = lax.all_gather(image_b * keep_low, "mp", axis=1, tiled=True)
    pre_a = jnp.dot(full_a, weight_a, preferred_element_type=jnp.float32) + tower_bias[0][None, :]
    pre_b = jnp.dot(full_b, weight_b, preferred_element_type=jnp.float32) + tower_bias[1][None, :]
    sigma_a = jax.nn.sigmoid(pre_a)
    sigma_b = jax.nn.sigmoid(pre_b)
    hidden_a = pre_a * sigma_a
    hidden_b = pre_b * sigma_b
    local_a = (stitch[0][None, :] * hidden_a + stitch[1][None, :] * hidden_b).astype(jnp.bfloat16)
    local_b = (stitch[2][None, :] * hidden_a + stitch[3][None, :] * hidden_b).astype(jnp.bfloat16)
    stitched_a = lax.all_gather(local_a, "mp", axis=1, tiled=True)
    stitched_b = lax.all_gather(local_b, "mp", axis=1, tiled=True)
    upper_a = cotan_a.astype(jnp.float32)
    upper_b = cotan_b.astype(jnp.float32)
    dhid_a = stitch[0][None, :] * upper_a + stitch[2][None, :] * upper_b
    dhid_b = stitch[1][None, :] * upper_a + stitch[3][None, :] * upper_b
    dpre_a = dhid_a * (sigma_a * (1.0 + pre_a * (1.0 - sigma_a)))
    dpre_b = dhid_b * (sigma_b * (1.0 + pre_b * (1.0 - sigma_b)))
    bias_terms = jnp.stack([jnp.sum(dpre_a, axis=0), jnp.sum(dpre_b, axis=0)])
    stitch_terms = jnp.stack(
        [
            jnp.sum(upper_a * hidden_a, axis=0),
            jnp.sum(upper_a * hidden_b, axis=0),
            jnp.sum(upper_b * hidden_a, axis=0),
            jnp.sum(upper_b * hidden_b, axis=0),
        ]
    )
    grad_bias, grad_stitch = lax.psum((bias_terms, stitch_terms), "dp")
    dlow_a = dpre_a.astype(jnp.bfloat16)
    dlow_b = dpre_b.astype(jnp.bfloat16)
    block_a = lax.dot_general(full_a, dlow_a, contract_rows, preferred_element_type=jnp.float32)
    block_b = lax.dot_general(full_b, dlow_b, contract_rows, preferred_element_type=jnp.float32)
    grad_weight_a = lax.psum_scatter(block_a, "dp", scatter_dimension=0, tiled=True)
    grad_weight_b = lax.psum_scatter(block_b, "dp", scatter_dimension=0, tiled=True)
    part_a = lax.dot_general(weight_a, dlow_a, contract_units, preferred_element_type=jnp.float32)
    part_b = lax.dot_general(weight_b, dlow_b, contract_units, preferred_element_type=jnp.float32)
    summed = lax.psum_scatter(
        jnp.concatenate([part_a, part_b], axis=1), "mp", scatter_dimension=0, tiled=True
    )
    keep_cols = keep_mask.T
    grad_image_a = (summed[:, :batch_rows] * keep_cols).astype(jnp.bfloat16)
    grad_image_b = (summed[:, batch_rows:] * keep_cols).astype(jnp.bfloat16)
    return (
        stitched_a,
        stitched_b,
        grad_image_a,
        grad_image_b,
        grad_weight_a,
        grad_weight_b,
        grad_bias,
        grad_stitch,
    )


SWAP_CORE = [(d, d ^ 1) for d in range(8)]
NEAR_Z = [(d, d ^ 2) for d in range(8)]
FAR_Z = [(d, d ^ 4) for d in range(8)]
ENDS_IN = [(0, 2), (1, 3), (6, 4), (7, 5)]
MIDS = [(2, 4), (3, 5), (4, 2), (5, 3)]
ENDS_OUT = [(2, 0), (3, 1), (4, 6), (5, 7)]
SLOTS = ((3, 2, 1, 0), (3, 2, 0, 1), (0, 1, 3, 2), (0, 1, 2, 3))
LANES = 128
EXTRA = 16
VMEM_LIMIT = 24 * 1024 * 1024
SMEM = pl.BlockSpec(memory_space=pltpu.SMEM)
VMEM = pl.BlockSpec(memory_space=pltpu.VMEM)
HBM = pl.BlockSpec(memory_space=pltpu.HBM)
LITTLE = pl.CostEstimate(flops=1, bytes_accessed=1, transcendentals=0)


def low(x):
    return x.astype(jnp.bfloat16)


def wide(x):
    return x.astype(jnp.float32)


def array(shape, dtype):
    return jax.ShapeDtypeStruct(shape, dtype)


def call(kernel, out_shape, in_specs, out_specs, name, scratch=()):
    return pl.pallas_call(
        kernel,
        out_shape=out_shape,
        in_specs=in_specs,
        out_specs=out_specs,
        scratch_shapes=scratch,
        compiler_params=pltpu.CompilerParams(vmem_limit_bytes=VMEM_LIMIT),
        cost_estimate=LITTLE,
        name=name,
    )


def marks_of(marks, where, cols, chunk):
    position = (where[8] * cols + chunk * LANES) // CH
    return marks[0, position], marks[1, position]


def mask_kernel(where, marks, group, image, out):
    rows, cols = image.shape
    second = jnp.broadcast_to(jnp.where(group[...] == 1, 1.0, 0.0), (8, rows)).T[:, 0:1] > 0.5
    for chunk in range(cols // LANES):
        zero, one = marks_of(marks, where, cols, chunk)
        keep = wide(jnp.where(second, one, zero))
        lanes = slice(chunk * LANES, (chunk + 1) * LANES)
        out[:, lanes] = low(wide(image[:, lanes]) * keep)


def mask_image(where, marks, group, image):
    return call(
        mask_kernel, array(image.shape, jnp.bfloat16), [SMEM, SMEM, VMEM, VMEM], VMEM, "mask_image"
    )(where, marks, group, image)


def load_kernel(flip, where, weight, out, sems):
    cols = out.shape[0] // 4
    copies = []
    for k in range(4):
        block = 2 * (where[0] ^ k) + (where[1] ^ flip)
        copies.append(
            pltpu.make_async_copy(
                weight.at[pl.ds(pl.multiple_of(block * cols, cols), cols), :],
                out.at[pl.ds(k * cols, cols), :],
                sems.at[k],
            )
        )
    for copy in copies:
        copy.start()
    for copy in copies:
        copy.wait()


def load(flip, where, weight):
    rows, units = weight.shape
    return call(
        functools.partial(load_kernel, flip),
        pltpu.VMEM((rows // 2, units), weight.dtype),
        [SMEM, HBM],
        VMEM,
        "load_weight",
        [pltpu.SemaphoreType.DMA((4,))],
    )(where, weight)


def open_kernel(p0, p1, p2, mine, other, keep, send):
    cols = p0.shape[1]
    for weight, out in ((mine, keep), (other, send)):
        total = None
        for k, piece in enumerate((p0, p1, p2)):
            term = jnp.dot(
                piece[...],
                weight[k * cols : (k + 1) * cols, :],
                preferred_element_type=jnp.float32,
            )
            total = term if total is None else total + term
        out[...] = total


def forward_open(p0, p1, p2, mine, other):
    shape = (p0.shape[0], mine.shape[1])
    return call(
        open_kernel, [pltpu.VMEM(shape, jnp.float32)] * 2, [VMEM] * 5, [VMEM] * 2, "forward_open"
    )(p0, p1, p2, mine, other)


def close_kernel(where, *refs):
    pieces, (mine, other, keep, send, out, sent) = refs[:-6], refs[-6:]
    cols = pieces[0].shape[1]

    def go(piece):
        sent[...] = send[...] + jnp.dot(
            piece[...], other[3 * cols :, :], preferred_element_type=jnp.float32
        )
        out[...] = keep[...] + jnp.dot(
            piece[...], mine[3 * cols :, :], preferred_element_type=jnp.float32
        )

    if len(pieces) == 1:
        go(pieces[0])
    else:
        pl.when(where[2] == 0)(functools.partial(go, pieces[0]))
        pl.when(where[2] == 1)(functools.partial(go, pieces[1]))


def forward_close(where, *operands):
    shape = operands[-1].shape
    return call(
        close_kernel,
        [array(shape, jnp.float32)] * 2,
        [SMEM] + [VMEM] * len(operands),
        [VMEM] * 2,
        "forward_close",
    )(where, *operands)


def tower_math(own, got, bias, unit_a, unit_b, upper_a, upper_b, dz, dz_t, sums):
    pre = own[...] + got[...] + bias[...]
    sigma = jax.nn.sigmoid(pre)
    hidden = pre * sigma
    cot_a = wide(upper_a[...])
    cot_b = wide(upper_b[...])
    dhid = unit_a[...] * cot_a + unit_b[...] * cot_b
    dpre = dhid * (sigma * (1.0 + pre * (1.0 - sigma)))
    dz[...] = low(dpre)
    dz_t[...] = low(dpre).T
    sums[0:1, :] = jnp.sum(dpre, axis=0, keepdims=True)
    sums[1:2, :] = jnp.sum(cot_a * hidden, axis=0, keepdims=True)
    sums[2:3, :] = jnp.sum(cot_b * hidden, axis=0, keepdims=True)
    sums[3:4, :] = jnp.zeros_like(sums[3:4, :])
    return hidden


def first_kernel(own, got, bias, unit_a, unit_b, upper_a, upper_b, dz, dz_t, sums, hidden):
    hidden[...] = tower_math(own, got, bias, unit_a, unit_b, upper_a, upper_b, dz, dz_t, sums)


def second_kernel(
    own, got, bias, unit_a, unit_b, upper_a, upper_b, earlier, stitch, dz, dz_t, sums, local
):
    hidden = tower_math(own, got, bias, unit_a, unit_b, upper_a, upper_b, dz, dz_t, sums)
    rows = hidden.shape[0]
    before = earlier[...]
    local[0:rows, :] = low(stitch[0:1, :] * before + stitch[1:2, :] * hidden)
    local[rows : 2 * rows, :] = low(stitch[2:3, :] * before + stitch[3:4, :] * hidden)


def tower(kernel, name, last, *operands):
    rows, units = operands[0].shape
    return call(
        kernel,
        [
            array((rows, units), jnp.bfloat16),
            array((units, rows), jnp.bfloat16),
            array((4, units), jnp.float32),
            last,
        ],
        [VMEM] * len(operands),
        [VMEM] * 4,
        name,
    )(*operands)


def part_kernel(first, where, mine, other, dz_t, dzo_t, *outs):
    cols = outs[0].shape[0]
    for k, out in enumerate(outs):
        rows = pl.ds(pl.multiple_of(where[3 + first + k] * cols, cols), cols)
        total = jnp.dot(mine[rows, :], dz_t[...], preferred_element_type=jnp.float32)
        total += jnp.dot(other[rows, :], dzo_t[...], preferred_element_type=jnp.float32)
        out[...] = total.astype(out.dtype)


def parts(first, dtypes, where, mine, other, dz_t, dzo_t):
    shape = (mine.shape[0] // 4, dz_t.shape[1])
    return call(
        functools.partial(part_kernel, first),
        [array(shape, dtype) for dtype in dtypes],
        [SMEM] + [VMEM] * 4,
        [VMEM] * len(dtypes),
        "parts",
    )(where, mine, other, dz_t, dzo_t)


def finish_kernel(where, marks, group, kept, third, cross, last, out):
    second = group[...] == 1
    cols = out.shape[0]
    for chunk in range(cols // LANES):
        zero, one = marks_of(marks, where, cols, chunk)
        keep = wide(jnp.where(second, one, zero))
        rows = slice(chunk * LANES, (chunk + 1) * LANES)
        total = kept[rows, :] + wide(third[rows, :]) + wide(cross[rows, :]) + wide(last[rows, :])
        out[rows, :] = low(total * keep)


def finish(where, marks, group, kept, third, cross, last):
    return call(
        finish_kernel,
        array(kept.shape, jnp.bfloat16),
        [SMEM, SMEM] + [VMEM] * 5,
        VMEM,
        "finish",
    )(where, marks, group, kept, third, cross, last)


def pack_kernel(where, p0, p1, p2, p3, p4, dz, sums, out, extra, sems):
    rows, cols = p0.shape
    units = dz.shape[1]
    copies = []
    for q in range(4):
        block = out.at[q, pl.ds(0, rows), pl.ds(0, cols)]
        k = where[0] ^ q
        for index, piece in enumerate((p0, p1, p2)):
            pl.when(k == index)(pltpu.make_async_copy(piece, block, sems.at[q]).start)
        pl.when((k == 3) & (where[2] == 0))(pltpu.make_async_copy(p3, block, sems.at[q]).start)
        pl.when((k == 3) & (where[2] == 1))(pltpu.make_async_copy(p4, block, sems.at[q]).start)
        copies.append(pltpu.make_async_copy(p0, block, sems.at[q]))
        copy = pltpu.make_async_copy(
            dz, out.at[q, pl.ds(0, rows), pl.ds(cols, units)], sems.at[4 + q]
        )
        copy.start()
        copies.append(copy)
    extra[...] = jnp.zeros_like(extra)
    for k in range(3):
        rest = sums[k : k + 1, :]
        for term in range(3):
            piece = low(rest)
            extra[term : term + 1, k * units : (k + 1) * units] = piece
            rest = rest - wide(piece)
    for q in range(4):
        copy = pltpu.make_async_copy(
            extra, out.at[q, pl.ds(rows, extra.shape[0]), :], sems.at[8 + q]
        )
        copy.start()
        copies.append(copy)
    for copy in copies:
        copy.wait()


def pack(where, *operands):
    rows, cols = operands[0].shape
    units = operands[5].shape[1]
    return call(
        pack_kernel,
        array((4, rows + EXTRA, cols + units), jnp.bfloat16),
        [SMEM] + [HBM] * 6 + [VMEM],
        HBM,
        "pack",
        [pltpu.VMEM((EXTRA, cols + units), jnp.bfloat16), pltpu.SemaphoreType.DMA((12,))],
    )(where, *operands)


def lay_kernel(where, own, next_one, rest, own_far, rest_far, out_a, out_b, sems):
    rows = out_a.shape[0]
    units = own.shape[1]
    copies = []
    for side in range(2):
        for k in range(4):
            block = 2 * (where[0] ^ k) + (where[1] ^ side)
            lanes = pl.ds(pl.multiple_of(block * units, units), units)
            if side == 0 and k < 2:
                source, start = (own, next_one)[k], 0
            else:
                source = ((None, rest), (own_far, rest_far))[side][k // 2]
                start = 2 * rows * (k % 2)
            for half, out in enumerate((out_a, out_b)):
                part = pl.ds(start + half * rows, rows)
                sem = sems.at[side * 8 + k * 2 + half]
                copies.append(pltpu.make_async_copy(source.at[part, :], out.at[:, lanes], sem))
    for copy in copies:
        copy.start()
    for copy in copies:
        copy.wait()


def lay_out(where, *sources):
    rows, units = sources[0].shape
    return call(
        lay_kernel,
        [array((rows // 2, 8 * units), jnp.bfloat16)] * 2,
        [SMEM] + [HBM] * 5,
        [HBM] * 2,
        "lay_out",
        [pltpu.SemaphoreType.DMA((16,))],
    )(where, *sources)


def weight_kernel(where, near, far, out, tiles, sems):
    units = out.shape[1]
    cols = out.shape[0] // 2
    rows = near.shape[1] - EXTRA
    tile = tiles.shape[1]
    steps = cols // tile

    def copy(p, t):
        slot = p * steps + t
        return pltpu.make_async_copy(
            tiles.at[slot], out.at[pl.ds(slot * tile, tile), :], sems.at[slot]
        )

    def dots(p, images):
        for t in range(steps):
            total = None
            for q in range(4):
                term = lax.dot_general(
                    images[q, 0:rows, t * tile : (t + 1) * tile],
                    near[q, 0:rows, cols : cols + units],
                    (((0,), (0,)), ((), ())),
                    preferred_element_type=jnp.float32,
                )
                total = term if total is None else total + term
            tiles[p * steps + t] = total
            copy(p, t).start()

    for p in range(2):
        pl.when(where[1] == p)(functools.partial(dots, p, near))
        pl.when(where[1] != p)(functools.partial(dots, p, far))
    for p in range(2):
        for t in range(steps):
            copy(p, t).wait()


def weight_grad(where, near, far, units):
    cols = near.shape[2] - units
    tile = cols // 3
    return call(
        weight_kernel,
        array((2 * cols, units), jnp.float32),
        [SMEM, VMEM, VMEM],
        HBM,
        "weight_grad",
        [pltpu.VMEM((6, tile, units), jnp.float32), pltpu.SemaphoreType.DMA((6,))],
    )(where, near, far)


def total_sums(got, units):
    terms = wide(got[:, got.shape[1] - EXTRA : got.shape[1] - EXTRA + 3, 0 : 3 * units])
    each = (terms[:, 2] + terms[:, 1]) + terms[:, 0]
    return ((each[0] + each[1]) + (each[2] + each[3])).reshape(3, units)


def add(*terms):
    total = wide(terms[0])
    for term in terms[1:]:
        total = total + wide(term)
    return low(total)


class Line:
    def __init__(self, token):
        self.token = token

    def __call__(self, step, *operands):
        *operands, _ = lax.optimization_barrier((*operands, self.token))
        result = step(*operands)
        self.token = result[0] if isinstance(result, (list, tuple)) else result
        return result


def swap(x):
    return lax.ppermute(x, "mp", SWAP_CORE)


def along(x):
    return lax.ppermute(x, "mp", NEAR_Z)


def across(x):
    return lax.ppermute(x, "mp", FAR_Z)


def inward(x):
    return lax.ppermute(x, "mp", ENDS_IN)


def between(x):
    return lax.ppermute(x, "mp", MIDS)


def outward(x):
    return lax.ppermute(x, "mp", ENDS_OUT)


def exchange(x):
    return lax.all_to_all(x, "dp", 0, 0)


def after(x, *deps):
    return lax.optimization_barrier((x,) + deps)[0]


def fast_shards(
    image_a,
    image_b,
    image_group,
    position_mask,
    weight_a,
    weight_b,
    tower_bias,
    stitch,
    cotan_a,
    cotan_b,
):
    rows, cols = image_a.shape
    units = weight_a.shape[1]
    place = lax.axis_index("mp").astype(jnp.int32)
    z = place // 2
    core = place % 2
    quarter = lax.axis_index("dp").astype(jnp.int32)
    middle = ((z == 1) | (z == 2)).astype(jnp.int32)
    slots = jnp.take(jnp.asarray(SLOTS, jnp.int32), z, axis=0) ^ z
    where = jnp.concatenate(
        [jnp.stack([z, core, middle]), slots, jnp.stack([quarter, place])]
    ).astype(jnp.int32)
    group = image_group[None, :]
    line = Line(where)

    bf16, f32 = jnp.bfloat16, jnp.float32

    a0 = line(mask_image, where, position_mask, group, image_a)
    a2 = across(a0)
    a1 = along(a0)
    b0 = line(mask_image, where, position_mask, group, image_b)
    b2 = across(b0)
    other_a = swap(line(functools.partial(load, 1), where, weight_a))
    mine_a = line(functools.partial(load, 0), where, weight_a)
    other_b = swap(line(functools.partial(load, 1), where, weight_b))
    mine_b = line(functools.partial(load, 0), where, weight_b)
    keep_a, give_a = line(forward_open, a0, a1, a2, mine_a, other_a)
    a3 = along(a2)
    b0_late = after(b0, a2, other_b)
    b1 = along(b0_late)
    b_mid = between(b0_late)
    own_a, sent_a = line(forward_close, where, a3, mine_a, other_a, keep_a, give_a)
    dz_a, dzt_a, sums_a, hidden_a = line(
        functools.partial(tower, first_kernel, "tower_a", array((rows, units), f32)),
        own_a,
        swap(sent_a),
        tower_bias[0:1],
        stitch[0:1],
        stitch[2:3],
        cotan_a,
        cotan_b,
    )
    dzo_a = swap(dzt_a)
    (first_a,) = line(functools.partial(parts, 0, [bf16]), where, mine_a, other_a, dzt_a, dzo_a)
    in1_a = inward(first_a)
    second_a, third_a, kept_a = line(
        functools.partial(parts, 1, [bf16, bf16, f32]), where, mine_a, other_a, dzt_a, dzo_a
    )
    in2_a = inward(second_a)
    b2 = after(b2, second_a)
    b_end = outward(b2)
    got_a = exchange(line(pack, where, a0, a1, a2, a3, a3, dz_a, sums_a))
    keep_b, give_b = line(forward_open, b0, b1, b2, mine_b, other_b)
    mid1_a = between(line(add, first_a, in1_a))
    own_b, sent_b = line(forward_close, where, b_end, b_mid, mine_b, other_b, keep_b, give_b)
    dz_b, dzt_b, sums_b, local = line(
        functools.partial(tower, second_kernel, "tower_b", array((2 * rows, units), bf16)),
        own_b,
        swap(sent_b),
        tower_bias[1:2],
        stitch[1:2],
        stitch[3:4],
        cotan_a,
        cotan_b,
        hidden_a,
        stitch,
    )
    dzo_b = swap(dzt_b)
    s1 = along(local)
    s_mid = between(local)
    (first_b,) = line(functools.partial(parts, 0, [bf16]), where, mine_b, other_b, dzt_b, dzo_b)
    in1_b = inward(first_b)
    mid2_a = between(line(add, second_a, in2_a))
    second_b, third_b, kept_b = line(
        functools.partial(parts, 1, [bf16, bf16, f32]), where, mine_b, other_b, dzt_b, dzo_b
    )
    got_b = exchange(line(pack, where, b0, b1, b2, b_end, b_mid, dz_b, sums_b))
    in2_b = inward(after(second_b, mid1_a))
    out_a = outward(after(line(add, third_a, mid1_a), s1))
    s_out = outward(s_mid)
    s_far = between(after(s1, mid2_a))
    mid1_b = between(line(add, first_b, in1_b))
    far_a = swap(after(got_a, out_a))
    grad_weight_a = line(functools.partial(weight_grad, units=units), where, got_a, far_a)
    in3_a = inward(after(third_a, s_out))
    s_last = outward(s_far)
    in3_b = inward(after(third_b, s_far))
    mid2_b = between(line(add, second_b, in2_b))
    out_b = outward(line(add, third_b, mid1_b))
    grad_image_a = line(finish, where, position_mask, group, kept_a, in3_a, mid2_a, out_a)
    near_far = swap(after(jnp.concatenate([local, s1]), in3_a))
    far_b = swap(after(got_b, s_last))
    at_end = middle == 0
    rest = jnp.concatenate(
        [jnp.where(at_end, s_out, s_far), jnp.where(at_end, s_last, s_mid)]
    )
    rest_far = swap(rest)
    grad_weight_b = line(functools.partial(weight_grad, units=units), where, got_b, far_b)
    stitched_a, stitched_b = line(lay_out, where, local, s1, rest, near_far, rest_far)
    grad_image_b = line(finish, where, position_mask, group, kept_b, in3_b, mid2_b, out_b)
    sums_a = total_sums(got_a, units)
    sums_b = total_sums(got_b, units)
    grad_bias = jnp.stack([sums_a[0], sums_b[0]])
    grad_stitch = jnp.stack([sums_a[1], sums_b[1], sums_a[2], sums_b[2]])
    return (
        stitched_a,
        stitched_b,
        grad_image_a,
        grad_image_b,
        grad_weight_a,
        grad_weight_b,
        grad_bias,
        grad_stitch,
    )


def solution(mesh):
    placed = (
        P("dp", "mp"),
        P("dp", "mp"),
        P("dp"),
        P(),
        P(None, "mp"),
        P(None, "mp"),
        P(None, "mp"),
        P(None, "mp"),
        P("dp", "mp"),
        P("dp", "mp"),
    )
    fits = mesh.shape["dp"] == 4 and mesh.shape["mp"] == 8
    return jax.shard_map(
        fast_shards if fits else general_shards,
        mesh=mesh,
        in_specs=placed,
        out_specs=(
            P("dp", None),
            P("dp", None),
            P("mp", "dp"),
            P("mp", "dp"),
            P("dp", "mp"),
            P("dp", "mp"),
            P(None, "mp"),
            P(None, "mp"),
        ),
        check_vma=False,
    )
```

time: 736 us -> 287 us (0.39)
  waiting for transfers between devices: 635 us -> 102 us
  starting transfers between devices: 0.28 us -> 87.6 us
  Pallas kernels: 0 us -> 56.7 us
  matrix products: 49 us -> 0 us
  blocking collectives: 16.6 us -> 0 us
  local copies, waits for them, and re-layouts: 8.65 us -> 23.9 us
  between operations: 14.2 us -> 1.38 us
    reduce_scatter x3 -> x0, waiting for transfers between devices: 533 us -> none  [the longest x1 190 us: shards(): lax.psum_scatter(jnp.concatenate([part_a, part_b], axis=1), 'mp', scatter...]
    ppermute x0 -> x34, waiting for transfers between devices: none -> 102 us  [the longest x2 47.6 us: across(): return lax.ppermute(x, 'mp', FAR_Z)]
    all_gather x4 -> x0, waiting for transfers between devices: 99.9 us -> none  [the longest x1 52 us: shards(): lax.all_gather(masked_a, 'mp', axis=1, tiled=True)]
    ppermute x0 -> x34, starting transfers between devices: none -> 78 us  [the longest x6 44.9 us: inward(): return lax.ppermute(x, 'mp', ENDS_IN)]
    pallas_call x0 -> x23, Pallas kernels: none -> 56.7 us  [the longest x2 13 us: weight_grad(): call(weight_kernel, array((2 * cols, units), jnp.float32), [SMEM, VMEM, V...]
    dot_general x7 -> x0, matrix products: 49 us -> none  [the longest x1 10.5 us: shards(): lax.dot_general(pieces[1], dlow_b, contract_rows, preferred_element_type=...]
    unnamed x24 -> x74, local copies, waits for them, and re-layouts: 6.99 us -> 23.8 us
    psum x1 -> x0, blocking collectives: 16.6 us -> none  [shards(): grad_bias, grad_stitch = lax.psum((bias_terms, stitch_terms), 'dp')]
  transfers between devices with their start and end apart: 7 -> 36, of which waited for: 6 -> 15; matrix products, arithmetic and copies ran while one was open for 7% -> 5% of each run, Pallas kernels for 0% -> 18%
where the time goes in v3:
time: 287 us; the launch traced here: 286 us
  waiting for transfers between devices  102 us (36%)
  starting transfers between devices  87.6 us (31%)
  Pallas kernels  56.7 us (20%)
  local copies, waits for them, and re-layouts  23.9 us (8%)
  other arithmetic  14.4 us (5%)
    ppermute x2, waiting for transfers between devices, across(): return lax.ppermute(x, 'mp', FAR_Z)  47.6 us
    ppermute x6, starting transfers between devices, inward(): return lax.ppermute(x, 'mp', ENDS_IN)  44.9 us
    unnamed x74, local copies, waits for them, and re-layouts  23.8 us
    ppermute x5, waiting for transfers between devices, outward(): return lax.ppermute(x, 'mp', ENDS_OUT)  23.5 us
    ppermute x6, waiting for transfers between devices, inward(): return lax.ppermute(x, 'mp', ENDS_IN)  14.5 us
    pallas_call x2, Pallas kernels, weight_grad(): call(weight_kernel, array((2 * cols, units), jnp.float32), [SMEM, VMEM, V...  13 us
    pallas_call x4, Pallas kernels, parts(): call(functools.partial(part_kernel, first), [array(shape, dtype) for dtyp...  11.3 us
    ppermute x4, waiting for transfers between devices, along(): return lax.ppermute(x, 'mp', NEAR_Z)  11.2 us
  transfers between devices with their start and end apart: 36, of which 15 were waited for; matrix products, arithmetic and copies ran while one was open for 5% of the time, Pallas kernels for 18%

profile of v3, /device:TPU:0, one launch (start us, length us, event | category | flops | bytes accessed | tf_op | source)
XLA Modules:
  0.0 285.7 jit_solution(12360278307853176402)
XLA Ops:
  7.1 3.7 %copy-done.3 = bf16[9216,512]{1,0:T(8,128)(2,1)S(1)} copy-done((bf16[9216,512]{1,0:T(8,128)(2,1)S(1)}, bf16[9216,512]{1,0:T(8,128)(2,1)}, u32[]{:S(2)}) %copy-start.3) | copy-done | bytes 9437208
  10.8 1.6 load_weight.4
  12.9 1.6 load_weight.5.mine.refs_1_
  14.7 3.7 %load_weight.6 = bf16[4608,512]{1,0:T(8,128)(2,1)} custom-call(s32[9]{0:T(128)S(1)} %concatenate.9.where, bf16[9216,512]{1,0:T(8,128)(2,1)S(1)} %bitcast.15), custom_call_target="tpu_custom_call" | custom-call | flops 1 | bytes 1 | tf_op jit(solution)/shard_map/load_weight/pallas_call | solution.py:178
  19.0 3.7 %collective-permute-start.2 = (bf16[256,1152]{1,0:T(8,128)(2,1)S(1)}, bf16[256,1152]{1,0:T(8,128)(2,1)S(1)}, u32[]{:S(2)}, u32[]{:S(2)}) collective-permute-start(bf16[256,1152]{1,0:T(8,128)(2,1)S(1)} %mask_image.2.p0), channel_id=1, source_target_pairs={{0,4},{1,5},{2,6},{3,7},{4,0},{5,1},{6,2},{7,3},{8,12},{9,13},{10,... | collective-permute-start | bytes 1769480 | tf_op jit(solution)/shard_map/ppermute | solution.py:490
  22.6 1.6 collective-permute-start.4
  24.2 25.1 %collective-permute-done.2.p2 = bf16[256,1152]{1,0:T(8,128)(2,1)S(1)} collective-permute-done((bf16[256,1152]{1,0:T(8,128)(2,1)S(1)}, bf16[256,1152]{1,0:T(8,128)(2,1)S(1)}, u32[]{:S(2)}, u32[]{:S(2)}) %collective-permute-start.2) | collective-permute-done | bytes 589856 | tf_op jit(solution)/shard_map/ppermute | solution.py:490
  49.9 1.6 load_weight.7.mine.refs_2_
  51.5 2.2 copy-done
  53.7 2.2 forward_open.2
  55.9 8.4 %collective-permute-done.3.refs_0_.p3.p4 = bf16[256,1152]{1,0:T(8,128)(2,1)S(1)} collective-permute-done((bf16[256,1152]{1,0:T(8,128)(2,1)S(1)}, bf16[256,1152]{1,0:T(8,128)(2,1)S(1)}, u32[]{:S(2)}, u32[]{:S(2)}) %collective-permute-start.3) | collective-permute-done | bytes 589856 | tf_op jit(solution)/shard_map/ppermute | solution.py:486
  64.3 1.4 forward_close.2
  65.8 1.9 collective-permute-done.5.got
  69.1 1.4 collective-permute-done.6.dzo_t
  70.5 1.3 parts.4
  71.8 2.5 parts.5
  76.0 1.4 pack.2
  77.4 1.8 copy-done.4
  79.2 4.7 %all-to-all-start.1 = ((bf16[4,272,1664]{2,1,0:T(8,128)(2,1)}), bf16[4,272,1664]{2,1,0:T(8,128)(2,1)}, u32[]{:S(2)}, u32[]{:S(2)}) async-start(bf16[4,272,1664]{2,1,0:T(8,128)(2,1)} %copy-done.4), calls=%async_computation.1 | async-start | bytes 7241728 | tf_op jit(solution)/shard_map/all_to_all | solution.py:506
  83.9 2.6 collective-permute-start
  86.5 1.7 collective-permute-start.10
  88.3 2.2 collective-permute-start.11
  91.2 22.5 %collective-permute-done.p2 = bf16[256,1152]{1,0:T(8,128)(2,1)S(1)} collective-permute-done((bf16[256,1152]{1,0:T(8,128)(2,1)S(1)}, bf16[256,1152]{1,0:T(8,128)(2,1)S(1)}, u32[]{:S(2)}, u32[]{:S(2)}) %collective-permute-start) | collective-permute-done | bytes 589856 | tf_op jit(solution)/shard_map/ppermute | solution.py:490
  113.7 1.3 collective-permute-start.7
  115.1 2.3 copy-done.1
  117.4 4.7 %forward_open.3 = (f32[256,512]{1,0:T(8,128)S(1)}, f32[256,512]{1,0:T(8,128)S(1)}) custom-call(bf16[256,1152]{1,0:T(8,128)(2,1)S(1)} %mask_image.3.p0, bf16[256,1152]{1,0:T(8,128)(2,1)S(1)} %collective-permute-done.10.p1, bf16[256,1152]{1,0:T(8,128)(2,1)S(1)} %collective-permute-done.p2, bf16[4608,512]{1,0:T(8,128)(2,1)S(1)} %copy-done.1, ...), custom_call_target="tpu_custom_call" | custom-call | flops 1 | bytes 1 | tf_op jit(solution)/shard_map/forward_open/pallas_call | solution.py:204
  122.1 2.7 collective-permute-done.11
  125.7 3.7 %collective-permute-done.7.refs_0_.p3 = bf16[256,1152]{1,0:T(8,128)(2,1)S(1)} collective-permute-done((bf16[256,1152]{1,0:T(8,128)(2,1)S(1)}, bf16[256,1152]{1,0:T(8,128)(2,1)S(1)}, u32[]{:S(2)}, u32[]{:S(2)}) %collective-permute-start.7) | collective-permute-done | bytes 589856 | tf_op jit(solution)/shard_map/ppermute | solution.py:502
  129.4 2.3 copy-done.2
  131.7 3.3 %forward_close.3 = (f32[256,512]{1,0:T(8,128)S(1)}, f32[256,512]{1,0:T(8,128)S(1)}) custom-call(s32[9]{0:T(128)S(1)} %concatenate.9.where, bf16[256,1152]{1,0:T(8,128)(2,1)S(1)} %collective-permute-done.7.refs_0_.p3, bf16[256,1152]{1,0:T(8,128)(2,1)S(1)} %collective-permute-done.9.refs_1_.p4, bf16[4608,512]{1,0:T(8,128)(2,1)S(1)} %copy-done.2, ...), custom_call_target="tpu_custom_call" | custom-call | flops 1 | bytes 1 | tf_op jit(solution)/shard_map/forward_close/pallas_call | solution.py:230
  135.1 1.7 collective-permute-start.16
  137.8 1.4 collective-permute-done.17.dzo_t
  139.2 3.1 %parts.6 = bf16[1152,256]{1,0:T(8,128)(2,1)S(1)} custom-call(s32[9]{0:T(128)S(1)} %concatenate.9.where, bf16[4608,512]{1,0:T(8,128)(2,1)S(1)} %bitcast.13, bf16[4608,512]{1,0:T(8,128)(2,1)} %collective-permute-done.8.other.refs_3_, bf16[512,256]{1,0:T(8,128)(2,1)S(1)} %get-tuple-element.279.dz_t, bf16[512,256]{1,0:T(8,128)(2,1)S(1)} %collective-permute-done.17.dzo_t), custom_call_target="tpu_custom_call" | custom-call | flops 1 | bytes 1 | tf_op jit(solution)/shard_map/parts/pallas_call | solution.py:297
  142.3 7.6 %collective-permute-done.16 = bf16[1152,256]{1,0:T(8,128)(2,1)S(1)} collective-permute-done((bf16[1152,256]{1,0:T(8,128)(2,1)S(1)}, bf16[1152,256]{1,0:T(8,128)(2,1)S(1)}, u32[]{:S(2)}, u32[]{:S(2)}) %collective-permute-start.16) | collective-permute-done | bytes 589856 | tf_op jit(solution)/shard_map/ppermute | solution.py:494
  150.9 4.3 %parts.7 = (bf16[1152,256]{1,0:T(8,128)(2,1)S(1)}, bf16[1152,256]{1,0:T(8,128)(2,1)S(1)}, f32[1152,256]{1,0:T(8,128)S(1)}) custom-call(s32[9]{0:T(128)S(1)} %concatenate.9.where, bf16[4608,512]{1,0:T(8,128)(2,1)S(1)} %bitcast.13, bf16[4608,512]{1,0:T(8,128)(2,1)} %collective-permute-done.8.other.refs_3_, bf16[512,256]{1,0:T(8,128)(2,1)S(1)} %get-tuple-element.279.dz_t, ...), custom_call_target="tpu_custom_call" | custom-call | flops 1 | bytes 1 | tf_op jit(solution)/shard_map/parts/pallas_call | solution.py:297
  157.9 1.4 pack.3
  159.3 1.8 copy-done.5
  161.1 4.9 %all-to-all-start = ((bf16[4,272,1664]{2,1,0:T(8,128)(2,1)}), bf16[4,272,1664]{2,1,0:T(8,128)(2,1)}, u32[]{:S(2)}, u32[]{:S(2)}) async-start(bf16[4,272,1664]{2,1,0:T(8,128)(2,1)} %copy-done.5), calls=%async_computation | async-start | bytes 7241728 | tf_op jit(solution)/shard_map/all_to_all | solution.py:506
  166.7 7.0 %collective-permute-start.13 = (bf16[512,512]{1,0:T(8,128)(2,1)S(1)}, bf16[512,512]{1,0:T(8,128)(2,1)S(1)}, u32[]{:S(2)}, u32[]{:S(2)}) collective-permute-start(bf16[512,512]{1,0:T(8,128)(2,1)S(1)} %get-tuple-element.318.own), channel_id=1, source_target_pairs={{0,2},{1,3},{2,0},{3,1},{4,6},{5,7},{6,4},{7,5},{8,10},{9,11},{10,... | collective-permute-start | bytes 1572872 | tf_op jit(solution)/shard_map/ppermute | solution.py:486
  173.7 1.5 collective-permute-start.14
  175.8 6.5 %collective-permute-start.27 = (bf16[1152,256]{1,0:T(8,128)(2,1)S(1)}, bf16[1152,256]{1,0:T(8,128)(2,1)}, u32[]{:S(2)}, u32[]{:S(2)}) collective-permute-start(bf16[1152,256]{1,0:T(8,128)(2,1)S(1)} %parts.6), channel_id=1, source_target_pairs={{0,2},{1,3},{6,4},{7,5},{8,10},{9,11},{14,12},{15,13},{16,18},{17,... | collective-permute-start | bytes 1769480 | tf_op jit(solution)/shard_map/ppermute | solution.py:494
  183.3 2.8 collective-permute-done.13.next_one
  186.1 1.3 collective-permute-start.26
  188.2 1.5 collective-permute-start.19
  189.6 28.6 %collective-permute-start.29 = (bf16[1152,256]{1,0:T(8,128)(2,1)}, bf16[1152,256]{1,0:T(8,128)(2,1)}, u32[]{:S(2)}, u32[]{:S(2)}) collective-permute-start(bf16[1152,256]{1,0:T(8,128)(2,1)} %copy-done.14), channel_id=1, source_target_pairs={{0,2},{1,3},{6,4},{7,5},{8,10},{9,11},{14,12},{15,13},{16,18},{17,... | collective-permute-start | bytes 1769480 | tf_op jit(solution)/shard_map/ppermute | solution.py:494
  218.2 1.3 collective-permute-start.15
  220.6 1.3 collective-permute-start.20
  221.9 2.0 add_convert_fusion.2
  224.0 1.5 collective-permute-start.28
  225.5 9.7 %collective-permute-done.15 = bf16[512,512]{1,0:T(8,128)(2,1)S(1)} collective-permute-done((bf16[512,512]{1,0:T(8,128)(2,1)}, bf16[512,512]{1,0:T(8,128)(2,1)S(1)}, u32[]{:S(2)}, u32[]{:S(2)}) %collective-permute-start.15) | collective-permute-done | bytes 524320 | tf_op jit(solution)/shard_map/ppermute | solution.py:502
  235.2 1.6 collective-permute-start.21
  237.6 6.3 %collective-permute-done.20 = bf16[512,512]{1,0:T(8,128)(2,1)} collective-permute-done((bf16[512,512]{1,0:T(8,128)(2,1)}, bf16[512,512]{1,0:T(8,128)(2,1)}, u32[]{:S(2)}, u32[]{:S(2)}) %collective-permute-start.20) | collective-permute-done | bytes 524320 | tf_op jit(solution)/shard_map/ppermute | solution.py:502
  245.2 4.2 %collective-permute-done.21.third = bf16[1152,256]{1,0:T(8,128)(2,1)S(1)} collective-permute-done((bf16[1152,256]{1,0:T(8,128)(2,1)S(1)}, bf16[1152,256]{1,0:T(8,128)(2,1)S(1)}, u32[]{:S(2)}, u32[]{:S(2)}) %collective-permute-start.21) | collective-permute-done | bytes 589856 | tf_op jit(solution)/shard_map/ppermute | solution.py:494
  249.4 4.4 %collective-permute-start.31 = (bf16[1152,256]{1,0:T(8,128)(2,1)}, bf16[1152,256]{1,0:T(8,128)(2,1)S(1)}, u32[]{:S(2)}, u32[]{:S(2)}) collective-permute-start(bf16[1152,256]{1,0:T(8,128)(2,1)} %copy-done.12), channel_id=1, source_target_pairs={{0,2},{1,3},{6,4},{7,5},{8,10},{9,11},{14,12},{15,13},{16,18},{17,... | collective-permute-start | bytes 1769480 | tf_op jit(solution)/shard_map/ppermute | solution.py:494
  253.8 1.1 broadcast_select_fusion
  256.1 7.0 %weight_grad.2 = f32[2304,512]{1,0:T(8,128)} custom-call(s32[9]{0:T(128)S(1)} %concatenate.9.where, bf16[4,272,1664]{2,1,0:T(8,128)(2,1)} %all-to-all-done.1.near, bf16[4,272,1664]{2,1,0:T(8,128)(2,1)} %collective-permute-done.30.far), custom_call_target="tpu_custom_call" | custom-call | flops 1 | bytes 1 | tf_op jit(solution)/shard_map/weight_grad/pallas_call | solution.py:447
  263.6 1.2 add_convert_fusion.1
  265.5 1.2 add_convert_fusion
  266.8 1.3 collective-permute-start.33
  269.3 2.2 finish.2
  271.5 6.0 %weight_grad.3 = f32[2304,512]{1,0:T(8,128)} custom-call(s32[9]{0:T(128)S(1)} %concatenate.9.where, bf16[4,272,1664]{2,1,0:T(8,128)(2,1)} %all-to-all-done.near, bf16[4,272,1664]{2,1,0:T(8,128)(2,1)S(1)} %collective-permute-done.24.far), custom_call_target="tpu_custom_call" | custom-call | flops 1 | bytes 1 | tf_op jit(solution)/shard_map/weight_grad/pallas_call | solution.py:447
  277.6 2.7 lay_out.1
  280.3 3.8 %collective-permute-done.33.last = bf16[1152,256]{1,0:T(8,128)(2,1)S(1)} collective-permute-done((bf16[1152,256]{1,0:T(8,128)(2,1)S(1)}, bf16[1152,256]{1,0:T(8,128)(2,1)S(1)}, u32[]{:S(2)}, u32[]{:S(2)}) %collective-permute-start.33) | collective-permute-done | bytes 589856 | tf_op jit(solution)/shard_map/ppermute | solution.py:502
  284.1 1.7 finish.3
  (130 shorter events, 27.7 us)
Async XLA Ops:
  1.4 1.1 copy-start.20
  5.0 1.1 copy-start.21
  7.1 3.7 %copy-start.3 = (bf16[9216,512]{1,0:T(8,128)(2,1)S(1)}, bf16[9216,512]{1,0:T(8,128)(2,1)}, u32[]{:S(2)}) copy-start(bf16[9216,512]{1,0:T(8,128)(2,1)} %weight.1) | copy-start | bytes 28311556
  10.8 3.7 %slice-start.2 = ((s8[9437184]{0:T(1024)(128)(4,1)}), s8[4194304]{0:T(1024)(128)(4,1)S(1)}, s32[]{:S(2)}) async-start(s8[9437184]{0:T(1024)(128)(4,1)} %bitcast.14), calls=%async_computation.4 | async-start | bytes 8388608
  10.8 3.7 %slice-start.3 = ((s8[9437184]{0:T(1024)(128)(4,1)}), s8[4194304]{0:T(1024)(128)(4,1)S(1)}, s32[]{:S(2)}) async-start(s8[9437184]{0:T(1024)(128)(4,1)} %bitcast.14), calls=%async_computation.5 | async-start | bytes 8388608
  12.4 2.3 slice-start.4
  12.4 41.3 %collective-permute-start.1 = (bf16[4608,512]{1,0:T(8,128)(2,1)S(1)}, bf16[4608,512]{1,0:T(8,128)(2,1)S(1)}, u32[]{:S(2)}, u32[]{:S(2)}) collective-permute-start(bf16[4608,512]{1,0:T(8,128)(2,1)S(1)} %load_weight.4), channel_id=1, source_target_pairs={{0,1},{1,0},{2,3},{3,2},{4,5},{5,4},{6,7},{7,6},{8,9},{9,8},{10,11... | collective-permute-start | bytes 14155784 | tf_op jit(solution)/shard_map/ppermute | solution.py:482
  18.4 68.1 %collective-permute-start.8 = (bf16[4608,512]{1,0:T(8,128)(2,1)}, bf16[4608,512]{1,0:T(8,128)(2,1)}, u32[]{:S(2)}, u32[]{:S(2)}) collective-permute-start(bf16[4608,512]{1,0:T(8,128)(2,1)} %load_weight.6), channel_id=1, source_target_pairs={{0,1},{1,0},{2,3},{3,2},{4,5},{5,4},{6,7},{7,6},{8,9},{9,8},{10,11... | collective-permute-start | bytes 14155784 | tf_op jit(solution)/shard_map/ppermute | solution.py:482
  19.0 30.3 %collective-permute-start.2 = (bf16[256,1152]{1,0:T(8,128)(2,1)S(1)}, bf16[256,1152]{1,0:T(8,128)(2,1)S(1)}, u32[]{:S(2)}, u32[]{:S(2)}) collective-permute-start(bf16[256,1152]{1,0:T(8,128)(2,1)S(1)} %mask_image.2.p0), channel_id=1, source_target_pairs={{0,4},{1,5},{2,6},{3,7},{4,0},{5,1},{6,2},{7,3},{8,12},{9,13},{10,... | collective-permute-start | bytes 1769480 | tf_op jit(solution)/shard_map/ppermute | solution.py:490
  22.6 31.1 %collective-permute-start.4 = (bf16[256,1152]{1,0:T(8,128)(2,1)S(1)}, bf16[256,1152]{1,0:T(8,128)(2,1)S(1)}, u32[]{:S(2)}, u32[]{:S(2)}) collective-permute-start(bf16[256,1152]{1,0:T(8,128)(2,1)S(1)} %mask_image.2.p0), channel_id=1, source_target_pairs={{0,2},{1,3},{2,0},{3,1},{4,6},{5,7},{6,4},{7,5},{8,10},{9,11},{10,... | collective-permute-start | bytes 1769480 | tf_op jit(solution)/shard_map/ppermute | solution.py:486
  49.3 15.0 %collective-permute-start.3 = (bf16[256,1152]{1,0:T(8,128)(2,1)S(1)}, bf16[256,1152]{1,0:T(8,128)(2,1)S(1)}, u32[]{:S(2)}, u32[]{:S(2)}) collective-permute-start(bf16[256,1152]{1,0:T(8,128)(2,1)S(1)} %collective-permute-done.2.p2), channel_id=1, source_target_pairs={{0,2},{1,3},{2,0},{3,1},{4,6},{5,7},{6,4},{7,5},{8,10},{9,11},{10,... | collective-permute-start | bytes 1769480 | tf_op jit(solution)/shard_map/ppermute | solution.py:486
  51.5 2.2 copy-start
  64.3 1.5 copy-start.24
  64.3 1.5 copy-start.31
  64.3 3.4 %copy-start.8 = (bf16[256,512]{1,0:T(8,128)(2,1)S(1)}, bf16[256,512]{1,0:T(8,128)(2,1)}, u32[]{:S(2)}) copy-start(bf16[256,512]{1,0:T(8,128)(2,1)} %upper_a.1) | copy-start | bytes 786436
  64.3 3.4 %copy-start.9 = (bf16[256,512]{1,0:T(8,128)(2,1)S(1)}, bf16[256,512]{1,0:T(8,128)(2,1)}, u32[]{:S(2)}) copy-start(bf16[256,512]{1,0:T(8,128)(2,1)} %upper_b.1) | copy-start | bytes 786436
  65.7 2.0 collective-permute-start.5
  68.9 1.5 collective-permute-start.6
  77.3 1.8 copy-start.4
  79.2 81.9 %all-to-all-start.1 = ((bf16[4,272,1664]{2,1,0:T(8,128)(2,1)}), bf16[4,272,1664]{2,1,0:T(8,128)(2,1)}, u32[]{:S(2)}, u32[]{:S(2)}) async-start(bf16[4,272,1664]{2,1,0:T(8,128)(2,1)} %copy-done.4), calls=%async_computation.1 | async-start | bytes 7241728 | tf_op jit(solution)/shard_map/all_to_all | solution.py:506
  83.9 29.8 %collective-permute-start = (bf16[256,1152]{1,0:T(8,128)(2,1)S(1)}, bf16[256,1152]{1,0:T(8,128)(2,1)S(1)}, u32[]{:S(2)}, u32[]{:S(2)}) collective-permute-start(bf16[256,1152]{1,0:T(8,128)(2,1)S(1)} %mask_image.3.p0), channel_id=1, source_target_pairs={{0,4},{1,5},{2,6},{3,7},{4,0},{5,1},{6,2},{7,3},{8,12},{9,13},{10,... | collective-permute-start | bytes 1769480 | tf_op jit(solution)/shard_map/ppermute | solution.py:490
  86.5 28.5 %collective-permute-start.10 = (bf16[256,1152]{1,0:T(8,128)(2,1)S(1)}, bf16[256,1152]{1,0:T(8,128)(2,1)S(1)}, u32[]{:S(2)}, u32[]{:S(2)}) collective-permute-start(bf16[256,1152]{1,0:T(8,128)(2,1)S(1)} %mask_image.3.p0), channel_id=1, source_target_pairs={{0,2},{1,3},{2,0},{3,1},{4,6},{5,7},{6,4},{7,5},{8,10},{9,11},{10,... | collective-permute-start | bytes 1769480 | tf_op jit(solution)/shard_map/ppermute | solution.py:486
  88.3 36.5 %collective-permute-start.11 = (bf16[1152,256]{1,0:T(8,128)(2,1)S(1)}, bf16[1152,256]{1,0:T(8,128)(2,1)S(1)}, u32[]{:S(2)}, u32[]{:S(2)}) collective-permute-start(bf16[1152,256]{1,0:T(8,128)(2,1)S(1)} %parts.4), channel_id=1, source_target_pairs={{0,2},{1,3},{6,4},{7,5},{8,10},{9,11},{14,12},{15,13},{16,18},{17,... | collective-permute-start | bytes 1769480 | tf_op jit(solution)/shard_map/ppermute | solution.py:494
  90.5 35.2 %collective-permute-start.9 = (bf16[256,1152]{1,0:T(8,128)(2,1)S(1)}, bf16[256,1152]{1,0:T(8,128)(2,1)S(1)}, u32[]{:S(2)}, u32[]{:S(2)}) collective-permute-start(bf16[256,1152]{1,0:T(8,128)(2,1)S(1)} %mask_image.3.p0), channel_id=1, source_target_pairs={{2,4},{3,5},{4,2},{5,3},{10,12},{11,13},{12,10},{13,11},{18,20},{1... | collective-permute-start | bytes 1769480 | tf_op jit(solution)/shard_map/ppermute | solution.py:498
  113.7 15.6 %collective-permute-start.7 = (bf16[256,1152]{1,0:T(8,128)(2,1)S(1)}, bf16[256,1152]{1,0:T(8,128)(2,1)S(1)}, u32[]{:S(2)}, u32[]{:S(2)}) collective-permute-start(bf16[256,1152]{1,0:T(8,128)(2,1)S(1)} %collective-permute-done.p2), channel_id=1, source_target_pairs={{2,0},{3,1},{4,6},{5,7},{10,8},{11,9},{12,14},{13,15},{18,16},{19,... | collective-permute-start | bytes 1769480 | tf_op jit(solution)/shard_map/ppermute | solution.py:502
  115.0 2.3 copy-start.1
  117.4 21.8 %slice-start = ((s8[4718592]{0:T(1024)(128)(4,1)}), s8[4194304]{0:T(1024)(128)(4,1)S(1)}, s32[]{:S(2)}) async-start(s8[4718592]{0:T(1024)(128)(4,1)} %bitcast.12), calls=%async_computation.2 | async-start | bytes 8388608
  129.4 2.3 copy-start.2
  131.7 3.4 %copy-start.19 = (bf16[1152,256]{1,0:T(8,128)(2,1)S(1)}, bf16[1152,256]{1,0:T(8,128)(2,1)}, u32[]{:S(2)}) copy-start(bf16[1152,256]{1,0:T(8,128)(2,1)} %copy-done.18) | copy-start | bytes 1769476
  131.7 5.3 %copy-start.23 = (f32[256,512]{1,0:T(8,128)S(1)}, f32[256,512]{1,0:T(8,128)}, u32[]{:S(2)}) copy-start(f32[256,512]{1,0:T(8,128)} %copy-done.22) | copy-start | bytes 1572868
  131.7 7.5 %slice-start.1 = ((s8[4718592]{0:T(1024)(128)(4,1)}), s8[524288]{0:T(1024)(128)(4,1)S(1)}, s32[]{:S(2)}) async-start(s8[4718592]{0:T(1024)(128)(4,1)} %bitcast.12), calls=%async_computation.3 | async-start | bytes 1048576
  135.0 2.0 collective-permute-start.12
  135.1 14.8 %collective-permute-start.16 = (bf16[1152,256]{1,0:T(8,128)(2,1)S(1)}, bf16[1152,256]{1,0:T(8,128)(2,1)S(1)}, u32[]{:S(2)}, u32[]{:S(2)}) collective-permute-start(bf16[1152,256]{1,0:T(8,128)(2,1)S(1)} %copy-done.19), channel_id=1, source_target_pairs={{0,2},{1,3},{6,4},{7,5},{8,10},{9,11},{14,12},{15,13},{16,18},{17,... | collective-permute-start | bytes 1769480 | tf_op jit(solution)/shard_map/ppermute | solution.py:494
  137.6 1.6 collective-permute-start.17
  159.3 1.8 copy-start.5
  161.1 21.2 %copy-start.11 = (bf16[1152,256]{1,0:T(8,128)(2,1)S(1)}, bf16[1152,256]{1,0:T(8,128)(2,1)}, u32[]{:S(2)}) copy-start(bf16[1152,256]{1,0:T(8,128)(2,1)} %copy-done.10) | copy-start | bytes 1769476
  161.1 82.9 %all-to-all-start = ((bf16[4,272,1664]{2,1,0:T(8,128)(2,1)}), bf16[4,272,1664]{2,1,0:T(8,128)(2,1)}, u32[]{:S(2)}, u32[]{:S(2)}) async-start(bf16[4,272,1664]{2,1,0:T(8,128)(2,1)} %copy-done.5), calls=%async_computation | async-start | bytes 7241728 | tf_op jit(solution)/shard_map/all_to_all | solution.py:506
  166.0 16.3 %collective-permute-start.25 = (bf16[1152,256]{1,0:T(8,128)(2,1)}, bf16[1152,256]{1,0:T(8,128)(2,1)S(1)}, u32[]{:S(2)}, u32[]{:S(2)}) collective-permute-start(bf16[1152,256]{1,0:T(8,128)(2,1)} %add_convert_fusion.5), channel_id=1, source_target_pairs={{2,4},{3,5},{4,2},{5,3},{10,12},{11,13},{12,10},{13,11},{18,20},{1... | collective-permute-start | bytes 1769480 | tf_op jit(solution)/shard_map/ppermute | solution.py:498
  166.7 19.4 %collective-permute-start.13 = (bf16[512,512]{1,0:T(8,128)(2,1)S(1)}, bf16[512,512]{1,0:T(8,128)(2,1)S(1)}, u32[]{:S(2)}, u32[]{:S(2)}) collective-permute-start(bf16[512,512]{1,0:T(8,128)(2,1)S(1)} %get-tuple-element.318.own), channel_id=1, source_target_pairs={{0,2},{1,3},{2,0},{3,1},{4,6},{5,7},{6,4},{7,5},{8,10},{9,11},{10,... | collective-permute-start | bytes 1572872 | tf_op jit(solution)/shard_map/ppermute | solution.py:486
  173.7 44.5 %collective-permute-start.14 = (bf16[512,512]{1,0:T(8,128)(2,1)S(1)}, bf16[512,512]{1,0:T(8,128)(2,1)}, u32[]{:S(2)}, u32[]{:S(2)}) collective-permute-start(bf16[512,512]{1,0:T(8,128)(2,1)S(1)} %get-tuple-element.318.own), channel_id=1, source_target_pairs={{2,4},{3,5},{4,2},{5,3},{10,12},{11,13},{12,10},{13,11},{18,20},{1... | collective-permute-start | bytes 1572872 | tf_op jit(solution)/shard_map/ppermute | solution.py:498
  175.1 12.2 %collective-permute-start.18 = (bf16[1152,256]{1,0:T(8,128)(2,1)}, bf16[1152,256]{1,0:T(8,128)(2,1)S(1)}, u32[]{:S(2)}, u32[]{:S(2)}) collective-permute-start(bf16[1152,256]{1,0:T(8,128)(2,1)} %add_convert_fusion.4), channel_id=1, source_target_pairs={{2,4},{3,5},{4,2},{5,3},{10,12},{11,13},{12,10},{13,11},{18,20},{1... | collective-permute-start | bytes 1769480 | tf_op jit(solution)/shard_map/ppermute | solution.py:498
  175.8 44.7 %collective-permute-start.27 = (bf16[1152,256]{1,0:T(8,128)(2,1)S(1)}, bf16[1152,256]{1,0:T(8,128)(2,1)}, u32[]{:S(2)}, u32[]{:S(2)}) collective-permute-start(bf16[1152,256]{1,0:T(8,128)(2,1)S(1)} %parts.6), channel_id=1, source_target_pairs={{0,2},{1,3},{6,4},{7,5},{8,10},{9,11},{14,12},{15,13},{16,18},{17,... | collective-permute-start | bytes 1769480 | tf_op jit(solution)/shard_map/ppermute | solution.py:494
  186.1 35.8 %collective-permute-start.26 = (bf16[1152,256]{1,0:T(8,128)(2,1)}, bf16[1152,256]{1,0:T(8,128)(2,1)}, u32[]{:S(2)}, u32[]{:S(2)}) collective-permute-start(bf16[1152,256]{1,0:T(8,128)(2,1)} %add_convert_fusion.3), channel_id=1, source_target_pairs={{2,0},{3,1},{4,6},{5,7},{10,8},{11,9},{12,14},{13,15},{18,16},{19,... | collective-permute-start | bytes 1769480 | tf_op jit(solution)/shard_map/ppermute | solution.py:502
  188.2 32.4 %collective-permute-start.19 = (bf16[512,512]{1,0:T(8,128)(2,1)S(1)}, bf16[512,512]{1,0:T(8,128)(2,1)}, u32[]{:S(2)}, u32[]{:S(2)}) collective-permute-start(bf16[512,512]{1,0:T(8,128)(2,1)S(1)} %collective-permute-done.13.next_one), channel_id=1, source_target_pairs={{2,4},{3,5},{4,2},{5,3},{10,12},{11,13},{12,10},{13,11},{18,20},{1... | collective-permute-start | bytes 1572872 | tf_op jit(solution)/shard_map/ppermute | solution.py:498
  189.6 73.4 %collective-permute-start.29 = (bf16[1152,256]{1,0:T(8,128)(2,1)}, bf16[1152,256]{1,0:T(8,128)(2,1)}, u32[]{:S(2)}, u32[]{:S(2)}) collective-permute-start(bf16[1152,256]{1,0:T(8,128)(2,1)} %copy-done.14), channel_id=1, source_target_pairs={{0,2},{1,3},{6,4},{7,5},{8,10},{9,11},{14,12},{15,13},{16,18},{17,... | collective-permute-start | bytes 1769480 | tf_op jit(solution)/shard_map/ppermute | solution.py:494
  218.2 17.0 %collective-permute-start.15 = (bf16[512,512]{1,0:T(8,128)(2,1)}, bf16[512,512]{1,0:T(8,128)(2,1)S(1)}, u32[]{:S(2)}, u32[]{:S(2)}) collective-permute-start(bf16[512,512]{1,0:T(8,128)(2,1)} %collective-permute-done.14), channel_id=1, source_target_pairs={{2,0},{3,1},{4,6},{5,7},{10,8},{11,9},{12,14},{13,15},{18,16},{19,... | collective-permute-start | bytes 1572872 | tf_op jit(solution)/shard_map/ppermute | solution.py:502
  220.6 23.4 %collective-permute-start.20 = (bf16[512,512]{1,0:T(8,128)(2,1)}, bf16[512,512]{1,0:T(8,128)(2,1)}, u32[]{:S(2)}, u32[]{:S(2)}) collective-permute-start(bf16[512,512]{1,0:T(8,128)(2,1)} %collective-permute-done.19), channel_id=1, source_target_pairs={{2,0},{3,1},{4,6},{5,7},{10,8},{11,9},{12,14},{13,15},{18,16},{19,... | collective-permute-start | bytes 1572872 | tf_op jit(solution)/shard_map/ppermute | solution.py:502
  221.9 34.1 %collective-permute-start.30 = (bf16[4,272,1664]{2,1,0:T(8,128)(2,1)}, bf16[4,272,1664]{2,1,0:T(8,128)(2,1)}, u32[]{:S(2)}, u32[]{:S(2)}) collective-permute-start(bf16[4,272,1664]{2,1,0:T(8,128)(2,1)} %all-to-all-done.1.near), channel_id=1, source_target_pairs={{0,1},{1,0},{2,3},{3,2},{4,5},{5,4},{6,7},{7,6},{8,9},{9,8},{10,11... | collective-permute-start | bytes 10862600 | tf_op jit(solution)/shard_map/ppermute | solution.py:482
  224.0 40.9 %collective-permute-start.28 = (bf16[1152,256]{1,0:T(8,128)(2,1)}, bf16[1152,256]{1,0:T(8,128)(2,1)}, u32[]{:S(2)}, u32[]{:S(2)}) collective-permute-start(bf16[1152,256]{1,0:T(8,128)(2,1)} %add_convert_fusion.2), channel_id=1, source_target_pairs={{2,4},{3,5},{4,2},{5,3},{10,12},{11,13},{12,10},{13,11},{18,20},{1... | collective-permute-start | bytes 1769480 | tf_op jit(solution)/shard_map/ppermute | solution.py:498
  235.2 14.2 %collective-permute-start.21 = (bf16[1152,256]{1,0:T(8,128)(2,1)S(1)}, bf16[1152,256]{1,0:T(8,128)(2,1)S(1)}, u32[]{:S(2)}, u32[]{:S(2)}) collective-permute-start(bf16[1152,256]{1,0:T(8,128)(2,1)S(1)} %copy-done.11), channel_id=1, source_target_pairs={{0,2},{1,3},{6,4},{7,5},{8,10},{9,11},{14,12},{15,13},{16,18},{17,... | collective-permute-start | bytes 1769480 | tf_op jit(solution)/shard_map/ppermute | solution.py:494
  244.0 10.9 %copy-start.29 = (bf16[512,512]{1,0:T(8,128)(2,1)S(1)}, bf16[512,512]{1,0:T(8,128)(2,1)}, u32[]{:S(2)}) copy-start(bf16[512,512]{1,0:T(8,128)(2,1)} %broadcast_select_fusion.1) | copy-start | bytes 1572868
  244.0 12.0 %copy-start.30 = (bf16[1024,512]{1,0:T(8,128)(2,1)S(1)}, bf16[1024,512]{1,0:T(8,128)(2,1)}, u32[]{:S(2)}) copy-start(bf16[1024,512]{1,0:T(8,128)(2,1)} %pad_maximum_fusion.1) | copy-start | bytes 3145732
  244.0 22.8 %collective-permute-start.24 = (bf16[4,272,1664]{2,1,0:T(8,128)(2,1)}, bf16[4,272,1664]{2,1,0:T(8,128)(2,1)S(1)}, u32[]{:S(2)}, u32[]{:S(2)}) collective-permute-start(bf16[4,272,1664]{2,1,0:T(8,128)(2,1)} %all-to-all-done.near), channel_id=1, source_target_pairs={{0,1},{1,0},{2,3},{3,2},{4,5},{5,4},{6,7},{7,6},{8,9},{9,8},{10,11... | collective-permute-start | bytes 10862600 | tf_op jit(solution)/shard_map/ppermute | solution.py:482
  249.4 30.9 %collective-permute-start.31 = (bf16[1152,256]{1,0:T(8,128)(2,1)}, bf16[1152,256]{1,0:T(8,128)(2,1)S(1)}, u32[]{:S(2)}, u32[]{:S(2)}) collective-permute-start(bf16[1152,256]{1,0:T(8,128)(2,1)} %copy-done.12), channel_id=1, source_target_pairs={{0,2},{1,3},{6,4},{7,5},{8,10},{9,11},{14,12},{15,13},{16,18},{17,... | collective-permute-start | bytes 1769480 | tf_op jit(solution)/shard_map/ppermute | solution.py:494
  255.9 7.6 %copy-start.15 = (bf16[1152,256]{1,0:T(8,128)(2,1)S(1)}, bf16[1152,256]{1,0:T(8,128)(2,1)}, u32[]{:S(2)}) copy-start(bf16[1152,256]{1,0:T(8,128)(2,1)} %copy-done.14) | copy-start | bytes 1769476
  256.0 21.6 %collective-permute-start.22 = (bf16[1024,512]{1,0:T(8,128)(2,1)S(1)}, bf16[1024,512]{1,0:T(8,128)(2,1)S(1)}, u32[]{:S(2)}, u32[]{:S(2)}) collective-permute-start(bf16[1024,512]{1,0:T(8,128)(2,1)S(1)} %copy-done.30), channel_id=1, source_target_pairs={{0,1},{1,0},{2,3},{3,2},{4,5},{5,4},{6,7},{7,6},{8,9},{9,8},{10,11... | collective-permute-start | bytes 3145736 | tf_op jit(solution)/shard_map/ppermute | solution.py:482
  263.0 2.5 copy-start.13
  263.0 6.3 %copy-start.17 = (bf16[1152,256]{1,0:T(8,128)(2,1)S(1)}, bf16[1152,256]{1,0:T(8,128)(2,1)}, u32[]{:S(2)}) copy-start(bf16[1152,256]{1,0:T(8,128)(2,1)} %copy-done.16) | copy-start | bytes 1769476
  263.0 6.3 %copy-start.26 = (s32[2,36]{1,0:T(2,128)S(1)}, s32[2,36]{1,0:T(2,128)}, u32[]{:S(2)}) copy-start(s32[2,36]{1,0:T(2,128)} %marks.3) | copy-start | bytes 868
  263.0 6.3 %copy-start.28 = (s32[256]{0:T(256)S(1)}, s32[256]{0:T(256)}, u32[]{:S(2)}) copy-start(s32[256]{0:T(256)} %param.13) | copy-start | bytes 3076
  263.1 14.5 %collective-permute-start.23 = (bf16[1024,512]{1,0:T(8,128)(2,1)S(1)}, bf16[1024,512]{1,0:T(8,128)(2,1)S(1)}, u32[]{:S(2)}, u32[]{:S(2)}) collective-permute-start(bf16[1024,512]{1,0:T(8,128)(2,1)S(1)} %pad_maximum_fusion.rest), channel_id=1, source_target_pairs={{0,1},{1,0},{2,3},{3,2},{4,5},{5,4},{6,7},{7,6},{8,9},{9,8},{10,11... | collective-permute-start | bytes 3145736 | tf_op jit(solution)/shard_map/ppermute | solution.py:482
  264.8 19.2 %collective-permute-start.32 = (bf16[1152,256]{1,0:T(8,128)(2,1)S(1)}, bf16[1152,256]{1,0:T(8,128)(2,1)S(1)}, u32[]{:S(2)}, u32[]{:S(2)}) collective-permute-start(bf16[1152,256]{1,0:T(8,128)(2,1)S(1)} %add_convert_fusion.1), channel_id=1, source_target_pairs={{2,4},{3,5},{4,2},{5,3},{10,12},{11,13},{12,10},{13,11},{18,20},{1... | collective-permute-start | bytes 1769480 | tf_op jit(solution)/shard_map/ppermute | solution.py:498
  266.8 17.3 %collective-permute-start.33 = (bf16[1152,256]{1,0:T(8,128)(2,1)S(1)}, bf16[1152,256]{1,0:T(8,128)(2,1)S(1)}, u32[]{:S(2)}, u32[]{:S(2)}) collective-permute-start(bf16[1152,256]{1,0:T(8,128)(2,1)S(1)} %add_convert_fusion), channel_id=1, source_target_pairs={{2,0},{3,1},{4,6},{5,7},{10,8},{11,9},{12,14},{13,15},{18,16},{19,... | collective-permute-start | bytes 1769480 | tf_op jit(solution)/shard_map/ppermute | solution.py:502
  277.5 6.5 %copy-start.7 = (f32[1152,256]{1,0:T(8,128)S(1)}, f32[1152,256]{1,0:T(8,128)}, u32[]{:S(2)}) copy-start(f32[1152,256]{1,0:T(8,128)} %copy-done.6) | copy-start | bytes 3538948
  (9 other events, 7.3 us)

commit v4 on v3

--- a/solution.py
+++ b/solution.py
@@ -106,6 +106,7 @@
 SMEM = pl.BlockSpec(memory_space=pltpu.SMEM)
 VMEM = pl.BlockSpec(memory_space=pltpu.VMEM)
 HBM = pl.BlockSpec(memory_space=pltpu.HBM)
+ANY = pl.BlockSpec(memory_space=pl.ANY)
 LITTLE = pl.CostEstimate(flops=1, bytes_accessed=1, transcendentals=0)
 
 
@@ -121,17 +122,44 @@
     return jax.ShapeDtypeStruct(shape, dtype)
 
 
+class Line:
+    def __init__(self):
+        self.before = []
+
+    def __call__(self, step, *operands):
+        result = step(*operands)
+        self.before = [result[0] if isinstance(result, (list, tuple)) else result]
+        return result
+
+    def wait(self, *arrived):
+        self.before = [*self.before, *arrived]
+
+    def send(self, move, x):
+        x, *self.before = lax.optimization_barrier((x, *self.before))
+        return move(x)
+
+
+line = Line()
+
+
 def call(kernel, out_shape, in_specs, out_specs, name, scratch=()):
-    return pl.pallas_call(
-        kernel,
+    before = list(line.before)
+    first = len(in_specs)
+
+    def body(*refs):
+        kernel(*refs[:first], *refs[first + len(before) :])
+
+    run = pl.pallas_call(
+        body,
         out_shape=out_shape,
-        in_specs=in_specs,
+        in_specs=[*in_specs, *[pl.BlockSpec(memory_space=pl.ANY)] * len(before)],
         out_specs=out_specs,
         scratch_shapes=scratch,
         compiler_params=pltpu.CompilerParams(vmem_limit_bytes=VMEM_LIMIT),
         cost_estimate=LITTLE,
         name=name,
     )
+    return lambda *operands: run(*operands, *before)
 
 
 def marks_of(marks, where, cols, chunk):
@@ -183,6 +211,64 @@
         "load_weight",
         [pltpu.SemaphoreType.DMA((4,))],
     )(where, weight)
+
+
+def whole_kernel(weight, out, sems):
+    rows = out.shape[0] // 8
+    copies = [
+        pltpu.make_async_copy(
+            weight.at[pl.ds(k * rows, rows), :], out.at[pl.ds(k * rows, rows), :], sems.at[k]
+        )
+        for k in range(8)
+    ]
+    for copy in copies:
+        copy.start()
+    for copy in copies:
+        copy.wait()
+
+
+def load_whole(weight):
+    return call(
+        whole_kernel,
+        pltpu.VMEM(weight.shape, weight.dtype),
+        [HBM],
+        VMEM,
+        "load_whole",
+        [pltpu.SemaphoreType.DMA((8,))],
+    )(weight)
+
+
+def full_kernel(image, weight, out, chunks, sems):
+    steps, _, cols = chunks.shape
+
+    def copy(k):
+        return pltpu.make_async_copy(
+            image.at[:, pl.ds(k * cols, cols)], chunks.at[k], sems.at[k]
+        )
+
+    for k in range(steps):
+        copy(k).start()
+    total = None
+    for k in range(steps):
+        copy(k).wait()
+        term = jnp.dot(
+            chunks[k], weight[k * cols : (k + 1) * cols, :], preferred_element_type=jnp.float32
+        )
+        total = term if total is None else total + term
+    out[...] = total
+
+
+def forward_full(image, weight):
+    rows = image.shape[0]
+    cols = image.shape[1] // 8
+    return call(
+        full_kernel,
+        array((rows, weight.shape[1]), jnp.float32),
+        [HBM, VMEM],
+        VMEM,
+        "forward_full",
+        [pltpu.VMEM((8, rows, cols), jnp.bfloat16), pltpu.SemaphoreType.DMA((8,))],
+    )(image, weight)
 
 
 def open_kernel(p0, p1, p2, mine, other, keep, send):
@@ -236,8 +322,8 @@
     )(where, *operands)
 
 
-def tower_math(own, got, bias, unit_a, unit_b, upper_a, upper_b, dz, dz_t, sums):
-    pre = own[...] + got[...] + bias[...]
+def tower_math(pre, bias, unit_a, unit_b, upper_a, upper_b, dz, dz_t, sums):
+    pre = pre + bias[...]
     sigma = jax.nn.sigmoid(pre)
     hidden = pre * sigma
     cot_a = wide(upper_a[...])
@@ -254,13 +340,13 @@
 
 
 def first_kernel(own, got, bias, unit_a, unit_b, upper_a, upper_b, dz, dz_t, sums, hidden):
-    hidden[...] = tower_math(own, got, bias, unit_a, unit_b, upper_a, upper_b, dz, dz_t, sums)
+    hidden[...] = tower_math(own[...] + got[...], bias, unit_a, unit_b, upper_a, upper_b, dz, dz_t, sums)
 
 
 def second_kernel(
-    own, got, bias, unit_a, unit_b, upper_a, upper_b, earlier, stitch, dz, dz_t, sums, local
+    own, bias, unit_a, unit_b, upper_a, upper_b, earlier, stitch, dz, dz_t, sums, local
 ):
-    hidden = tower_math(own, got, bias, unit_a, unit_b, upper_a, upper_b, dz, dz_t, sums)
+    hidden = tower_math(own[...], bias, unit_a, unit_b, upper_a, upper_b, dz, dz_t, sums)
     rows = hidden.shape[0]
     before = earlier[...]
     local[0:rows, :] = low(stitch[0:1, :] * before + stitch[1:2, :] * hidden)
@@ -286,14 +372,19 @@
 def part_kernel(first, where, mine, other, dz_t, dzo_t, *outs):
     cols = outs[0].shape[0]
     for k, out in enumerate(outs):
-        rows = pl.ds(pl.multiple_of(where[3 + first + k] * cols, cols), cols)
-        total = jnp.dot(mine[rows, :], dz_t[...], preferred_element_type=jnp.float32)
+        slot = where[3 + first + k]
+        rows = pl.ds(pl.multiple_of(slot * cols, cols), cols)
+        place = slot
+        if mine.shape[0] > other.shape[0]:
+            place = 2 * (slot ^ where[0]) + where[1]
+        own = pl.ds(pl.multiple_of(place * cols, cols), cols)
+        total = jnp.dot(mine[own, :], dz_t[...], preferred_element_type=jnp.float32)
         total += jnp.dot(other[rows, :], dzo_t[...], preferred_element_type=jnp.float32)
         out[...] = total.astype(out.dtype)
 
 
 def parts(first, dtypes, where, mine, other, dz_t, dzo_t):
-    shape = (mine.shape[0] // 4, dz_t.shape[1])
+    shape = (other.shape[0] // 4, dz_t.shape[1])
     return call(
         functools.partial(part_kernel, first),
         [array(shape, dtype) for dtype in dtypes],
@@ -324,92 +415,114 @@
     )(where, marks, group, kept, third, cross, last)
 
 
-def pack_kernel(where, p0, p1, p2, p3, p4, dz, sums, out, extra, sems):
-    rows, cols = p0.shape
-    units = dz.shape[1]
-    copies = []
-    for q in range(4):
-        block = out.at[q, pl.ds(0, rows), pl.ds(0, cols)]
-        k = where[0] ^ q
-        for index, piece in enumerate((p0, p1, p2)):
-            pl.when(k == index)(pltpu.make_async_copy(piece, block, sems.at[q]).start)
-        pl.when((k == 3) & (where[2] == 0))(pltpu.make_async_copy(p3, block, sems.at[q]).start)
-        pl.when((k == 3) & (where[2] == 1))(pltpu.make_async_copy(p4, block, sems.at[q]).start)
-        copies.append(pltpu.make_async_copy(p0, block, sems.at[q]))
-        copy = pltpu.make_async_copy(
-            dz, out.at[q, pl.ds(0, rows), pl.ds(cols, units)], sems.at[4 + q]
-        )
-        copy.start()
-        copies.append(copy)
+def sum_rows(sums, extra, start, units):
     extra[...] = jnp.zeros_like(extra)
     for k in range(3):
         rest = sums[k : k + 1, :]
         for term in range(3):
             piece = low(rest)
-            extra[term : term + 1, k * units : (k + 1) * units] = piece
+            extra[3 * k + term : 3 * k + term + 1, start : start + units] = piece
             rest = rest - wide(piece)
+
+
+def images_kernel(where, p0, p1, p2, p3, out, sems):
     for q in range(4):
-        copy = pltpu.make_async_copy(
-            extra, out.at[q, pl.ds(rows, extra.shape[0]), :], sems.at[8 + q]
-        )
-        copy.start()
-        copies.append(copy)
-    for copy in copies:
-        copy.wait()
-
-
-def pack(where, *operands):
-    rows, cols = operands[0].shape
-    units = operands[5].shape[1]
-    return call(
-        pack_kernel,
-        array((4, rows + EXTRA, cols + units), jnp.bfloat16),
-        [SMEM] + [HBM] * 6 + [VMEM],
+        k = where[0] ^ q
+        for index, piece in enumerate((p0, p1, p2, p3)):
+            pl.when(k == index)(pltpu.make_async_copy(piece, out.at[q], sems.at[q]).start)
+    for q in range(4):
+        pltpu.make_async_copy(p0, out.at[q], sems.at[q]).wait()
+
+
+def pack_images(where, *pieces):
+    rows, cols = pieces[0].shape
+    return call(
+        images_kernel,
+        array((4, rows, cols), jnp.bfloat16),
+        [SMEM] + [ANY] * 4,
         HBM,
-        "pack",
-        [pltpu.VMEM((EXTRA, cols + units), jnp.bfloat16), pltpu.SemaphoreType.DMA((12,))],
-    )(where, *operands)
-
-
-def lay_kernel(where, own, next_one, rest, own_far, rest_far, out_a, out_b, sems):
-    rows = out_a.shape[0]
-    units = own.shape[1]
-    copies = []
-    for side in range(2):
-        for k in range(4):
-            block = 2 * (where[0] ^ k) + (where[1] ^ side)
-            lanes = pl.ds(pl.multiple_of(block * units, units), units)
-            if side == 0 and k < 2:
-                source, start = (own, next_one)[k], 0
-            else:
-                source = ((None, rest), (own_far, rest_far))[side][k // 2]
-                start = 2 * rows * (k % 2)
-            for half, out in enumerate((out_a, out_b)):
-                part = pl.ds(start + half * rows, rows)
-                sem = sems.at[side * 8 + k * 2 + half]
-                copies.append(pltpu.make_async_copy(source.at[part, :], out.at[:, lanes], sem))
+        "pack_images",
+        [pltpu.SemaphoreType.DMA((4,))],
+    )(where, *pieces)
+
+
+def dz_kernel(dz, sums, out, extra, sems):
+    rows, units = dz.shape
+    copies = [
+        pltpu.make_async_copy(dz, out.at[q, pl.ds(0, rows), :], sems.at[q]) for q in range(4)
+    ]
     for copy in copies:
         copy.start()
+    sum_rows(sums, extra, 0, units)
+    more = [
+        pltpu.make_async_copy(extra, out.at[q, pl.ds(rows, EXTRA), :], sems.at[4 + q])
+        for q in range(4)
+    ]
+    for copy in more:
+        copy.start()
+    for copy in copies + more:
+        copy.wait()
+
+
+def pack_dz(dz, sums):
+    rows, units = dz.shape
+    return call(
+        dz_kernel,
+        array((4, rows + EXTRA, units), jnp.bfloat16),
+        [ANY, VMEM],
+        HBM,
+        "pack_dz",
+        [pltpu.VMEM((EXTRA, units), jnp.bfloat16), pltpu.SemaphoreType.DMA((8,))],
+    )(dz, sums)
+
+
+def both_kernel(where, image, dz, sums, out, extra, sems):
+    rows, units = dz.shape
+    cols = out.shape[2] - units
+    copies = []
+    for q in range(4):
+        block = pl.ds(pl.multiple_of((2 * q + where[1]) * cols, cols), cols)
+        copies.append(
+            pltpu.make_async_copy(
+                image.at[:, block], out.at[q, pl.ds(0, rows), pl.ds(0, cols)], sems.at[q]
+            )
+        )
+        copies.append(
+            pltpu.make_async_copy(
+                dz, out.at[q, pl.ds(0, rows), pl.ds(cols, units)], sems.at[4 + q]
+            )
+        )
     for copy in copies:
+        copy.start()
+    sum_rows(sums, extra, cols, units)
+    more = [
+        pltpu.make_async_copy(extra, out.at[q, pl.ds(rows, EXTRA), :], sems.at[8 + q])
+        for q in range(4)
+    ]
+    for copy in more:
+        copy.start()
+    for copy in copies + more:
         copy.wait()
 
 
-def lay_out(where, *sources):
-    rows, units = sources[0].shape
-    return call(
-        lay_kernel,
-        [array((rows // 2, 8 * units), jnp.bfloat16)] * 2,
-        [SMEM] + [HBM] * 5,
-        [HBM] * 2,
-        "lay_out",
-        [pltpu.SemaphoreType.DMA((16,))],
-    )(where, *sources)
-
-
-def weight_kernel(where, near, far, out, tiles, sems):
+def pack_both(where, image, dz, sums):
+    rows, units = dz.shape
+    cols = image.shape[1] // 8
+    return call(
+        both_kernel,
+        array((4, rows + EXTRA, cols + units), jnp.bfloat16),
+        [SMEM, HBM, ANY, VMEM],
+        HBM,
+        "pack_both",
+        [pltpu.VMEM((EXTRA, cols + units), jnp.bfloat16), pltpu.SemaphoreType.DMA((12,))],
+    )(where, image, dz, sums)
+
+
+def weight_kernel(at, where, near, dz, *refs):
+    *far, out, tiles, sems = refs
     units = out.shape[1]
     cols = out.shape[0] // 2
-    rows = near.shape[1] - EXTRA
+    rows = dz.shape[1] - EXTRA
     tile = tiles.shape[1]
     steps = cols // tile
 
@@ -418,14 +531,19 @@
         return pltpu.make_async_copy(
             tiles.at[slot], out.at[pl.ds(slot * tile, tile), :], sems.at[slot]
         )
+
+    def block(images, q, lanes):
+        if len(images) == 4:
+            return images[q][0:rows, lanes]
+        return images[0][q, 0:rows, lanes]
 
     def dots(p, images):
         for t in range(steps):
             total = None
             for q in range(4):
                 term = lax.dot_general(
-                    images[q, 0:rows, t * tile : (t + 1) * tile],
-                    near[q, 0:rows, cols : cols + units],
+                    block(images, q, slice(t * tile, (t + 1) * tile)),
+                    dz[q, 0:rows, at : at + units],
                     (((0,), (0,)), ((), ())),
                     preferred_element_type=jnp.float32,
                 )
@@ -434,48 +552,38 @@
             copy(p, t).start()
 
     for p in range(2):
-        pl.when(where[1] == p)(functools.partial(dots, p, near))
+        pl.when(where[1] == p)(functools.partial(dots, p, [near]))
         pl.when(where[1] != p)(functools.partial(dots, p, far))
     for p in range(2):
         for t in range(steps):
             copy(p, t).wait()
 
 
-def weight_grad(where, near, far, units):
-    cols = near.shape[2] - units
+def weight_grad(cols, units, at, where, near, dz, *far):
     tile = cols // 3
     return call(
-        weight_kernel,
+        functools.partial(weight_kernel, at),
         array((2 * cols, units), jnp.float32),
-        [SMEM, VMEM, VMEM],
+        [SMEM] + [VMEM] * (2 + len(far)),
         HBM,
         "weight_grad",
         [pltpu.VMEM((6, tile, units), jnp.float32), pltpu.SemaphoreType.DMA((6,))],
-    )(where, near, far)
-
-
-def total_sums(got, units):
-    terms = wide(got[:, got.shape[1] - EXTRA : got.shape[1] - EXTRA + 3, 0 : 3 * units])
-    each = (terms[:, 2] + terms[:, 1]) + terms[:, 0]
-    return ((each[0] + each[1]) + (each[2] + each[3])).reshape(3, units)
-
-
-def add(*terms):
-    total = wide(terms[0])
-    for term in terms[1:]:
-        total = total + wide(term)
-    return low(total)
-
-
-class Line:
-    def __init__(self, token):
-        self.token = token
-
-    def __call__(self, step, *operands):
-        *operands, _ = lax.optimization_barrier((*operands, self.token))
-        result = step(*operands)
-        self.token = result[0] if isinstance(result, (list, tuple)) else result
-        return result
+    )(where, near, dz, *far)
+
+
+def total_sums(got, start, units):
+    end = got.shape[1] - EXTRA
+    terms = wide(got[:, end : end + 9, start : start + units]).reshape(4, 3, 3, units)
+    each = (terms[:, :, 2] + terms[:, :, 1]) + terms[:, :, 0]
+    return (each[0] + each[1]) + (each[2] + each[3])
+
+
+def add_kernel(one, two, out):
+    out[...] = low(wide(one[...]) + wide(two[...]))
+
+
+def add(one, two):
+    return call(add_kernel, array(one.shape, jnp.bfloat16), [VMEM, VMEM], VMEM, "add")(one, two)
 
 
 def swap(x):
@@ -534,52 +642,68 @@
         [jnp.stack([z, core, middle]), slots, jnp.stack([quarter, place])]
     ).astype(jnp.int32)
     group = image_group[None, :]
-    line = Line(where)
+    line.before = []
 
     bf16, f32 = jnp.bfloat16, jnp.float32
-
+    send, wait = line.send, line.wait
+
+    def first_part(mine, other, dz_t, dzo_t):
+        return line(functools.partial(parts, 0, [bf16]), where, mine, other, dz_t, dzo_t)[0]
+
+    def other_parts(mine, other, dz_t, dzo_t):
+        return line(
+            functools.partial(parts, 1, [bf16, bf16, f32]), where, mine, other, dz_t, dzo_t
+        )
+
+    swap_a = swap(weight_a)
+    swap_b = swap(weight_b)
     a0 = line(mask_image, where, position_mask, group, image_a)
-    a2 = across(a0)
-    a1 = along(a0)
+    a2 = send(across, a0)
+    a1 = send(along, a0)
     b0 = line(mask_image, where, position_mask, group, image_b)
-    b2 = across(b0)
-    other_a = swap(line(functools.partial(load, 1), where, weight_a))
+    full_b = lax.all_gather(b0, "mp", axis=1, tiled=True)
     mine_a = line(functools.partial(load, 0), where, weight_a)
-    other_b = swap(line(functools.partial(load, 1), where, weight_b))
-    mine_b = line(functools.partial(load, 0), where, weight_b)
+    mine_b = line(load_whole, weight_b)
+    wait(a1, a2)
+    a3 = send(along, a2)
+    other_a = line(functools.partial(load, 0), where, swap_a)
     keep_a, give_a = line(forward_open, a0, a1, a2, mine_a, other_a)
-    a3 = along(a2)
-    b0_late = after(b0, a2, other_b)
-    b1 = along(b0_late)
-    b_mid = between(b0_late)
+    other_b = line(functools.partial(load, 0), where, swap_b)
+    wait(a3)
     own_a, sent_a = line(forward_close, where, a3, mine_a, other_a, keep_a, give_a)
+    got_sum = send(swap, sent_a)
+    got_a = send(exchange, line(pack_images, where, a0, a1, a2, a3))
+    wait(got_sum)
     dz_a, dzt_a, sums_a, hidden_a = line(
         functools.partial(tower, first_kernel, "tower_a", array((rows, units), f32)),
         own_a,
-        swap(sent_a),
+        got_sum,
         tower_bias[0:1],
         stitch[0:1],
         stitch[2:3],
         cotan_a,
         cotan_b,
     )
-    dzo_a = swap(dzt_a)
-    (first_a,) = line(functools.partial(parts, 0, [bf16]), where, mine_a, other_a, dzt_a, dzo_a)
-    in1_a = inward(first_a)
-    second_a, third_a, kept_a = line(
-        functools.partial(parts, 1, [bf16, bf16, f32]), where, mine_a, other_a, dzt_a, dzo_a
-    )
-    in2_a = inward(second_a)
-    b2 = after(b2, second_a)
-    b_end = outward(b2)
-    got_a = exchange(line(pack, where, a0, a1, a2, a3, a3, dz_a, sums_a))
-    keep_b, give_b = line(forward_open, b0, b1, b2, mine_b, other_b)
-    mid1_a = between(line(add, first_a, in1_a))
-    own_b, sent_b = line(forward_close, where, b_end, b_mid, mine_b, other_b, keep_b, give_b)
+    dzo_a = send(swap, dzt_a)
+    wait(dzo_a)
+    first_a = first_part(mine_a, other_a, dzt_a, dzo_a)
+    in1_a = send(inward, first_a)
+    second_a, third_a, kept_a = other_parts(mine_a, other_a, dzt_a, dzo_a)
+    in2_a = send(inward, second_a)
+    packed_dz = line(pack_dz, dz_a, sums_a)
+    wait(in1_a)
+    sum1_a = line(add, first_a, in1_a)
+    mid1_a = send(between, sum1_a)
+    wait(got_a)
+    far_a = send(swap, got_a)
+    dzs_a = send(exchange, packed_dz)
+    wait(in2_a)
+    sum2_a = line(add, second_a, in2_a)
+    wait(full_b)
+    own_b = line(forward_full, full_b, mine_b)
     dz_b, dzt_b, sums_b, local = line(
         functools.partial(tower, second_kernel, "tower_b", array((2 * rows, units), bf16)),
         own_b,
-        swap(sent_b),
         tower_bias[1:2],
         stitch[1:2],
         stitch[3:4],
@@ -588,46 +712,44 @@
         hidden_a,
         stitch,
     )
-    dzo_b = swap(dzt_b)
-    s1 = along(local)
-    s_mid = between(local)
-    (first_b,) = line(functools.partial(parts, 0, [bf16]), where, mine_b, other_b, dzt_b, dzo_b)
-    in1_b = inward(first_b)
-    mid2_a = between(line(add, second_a, in2_a))
-    second_b, third_b, kept_b = line(
-        functools.partial(parts, 1, [bf16, bf16, f32]), where, mine_b, other_b, dzt_b, dzo_b
-    )
-    got_b = exchange(line(pack, where, b0, b1, b2, b_end, b_mid, dz_b, sums_b))
-    in2_b = inward(after(second_b, mid1_a))
-    out_a = outward(after(line(add, third_a, mid1_a), s1))
-    s_out = outward(s_mid)
-    s_far = between(after(s1, mid2_a))
-    mid1_b = between(line(add, first_b, in1_b))
-    far_a = swap(after(got_a, out_a))
-    grad_weight_a = line(functools.partial(weight_grad, units=units), where, got_a, far_a)
-    in3_a = inward(after(third_a, s_out))
-    s_last = outward(s_far)
-    in3_b = inward(after(third_b, s_far))
-    mid2_b = between(line(add, second_b, in2_b))
-    out_b = outward(line(add, third_b, mid1_b))
+    dzo_b = send(swap, dzt_b)
+    stitched = lax.all_gather(local, "mp", axis=1, tiled=True)
+    wait(dzs_a)
+    got_b = send(exchange, line(pack_both, where, full_b, dz_b, sums_b))
+    wait(dzo_b)
+    first_b = first_part(mine_b, other_b, dzt_b, dzo_b)
+    in1_b = send(inward, first_b)
+    second_b, third_b, kept_b = other_parts(mine_b, other_b, dzt_b, dzo_b)
+    in2_b = send(inward, second_b)
+    mid2_a = send(between, sum2_a)
+    wait(mid1_a)
+    out_a = send(outward, line(add, third_a, mid1_a))
+    wait(far_a)
+    grad_weight_a = line(
+        functools.partial(weight_grad, cols, units, 0), where, got_a, dzs_a, far_a
+    )
+    wait(in1_b)
+    mid1_b = send(between, line(add, first_b, in1_b))
+    in3_b = send(inward, third_b)
+    wait(in2_b)
+    mid2_b = send(between, line(add, second_b, in2_b))
+    in3_a = send(inward, third_a)
+    wait(mid1_b)
+    out_b = send(outward, line(add, third_b, mid1_b))
+    far_b = [send(swap, got_b[q]) for q in range(4)]
+    wait(in3_a, mid2_a, out_a)
     grad_image_a = line(finish, where, position_mask, group, kept_a, in3_a, mid2_a, out_a)
-    near_far = swap(after(jnp.concatenate([local, s1]), in3_a))
-    far_b = swap(after(got_b, s_last))
-    at_end = middle == 0
-    rest = jnp.concatenate(
-        [jnp.where(at_end, s_out, s_far), jnp.where(at_end, s_last, s_mid)]
-    )
-    rest_far = swap(rest)
-    grad_weight_b = line(functools.partial(weight_grad, units=units), where, got_b, far_b)
-    stitched_a, stitched_b = line(lay_out, where, local, s1, rest, near_far, rest_far)
+    grad_weight_b = line(
+        functools.partial(weight_grad, cols, units, cols), where, got_b, got_b, *far_b
+    )
     grad_image_b = line(finish, where, position_mask, group, kept_b, in3_b, mid2_b, out_b)
-    sums_a = total_sums(got_a, units)
-    sums_b = total_sums(got_b, units)
+    sums_a = total_sums(dzs_a, 0, units)
+    sums_b = total_sums(got_b, cols, units)
     grad_bias = jnp.stack([sums_a[0], sums_b[0]])
     grad_stitch = jnp.stack([sums_a[1], sums_b[1], sums_a[2], sums_b[2]])
     return (
-        stitched_a,
-        stitched_b,
+        stitched[:rows],
+        stitched[rows:],
         grad_image_a,
         grad_image_b,
         grad_weight_a,

time: 287 us -> 309 us (1.077)
  local copies, waits for them, and re-layouts: 23.9 us -> 56.1 us
  starting transfers between devices: 87.6 us -> 71.1 us
  between operations: 1.38 us -> 14.8 us
  other arithmetic: 14.4 us -> 2.82 us
  waiting for transfers between devices: 102 us -> 110 us
  Pallas kernels: 56.7 us -> 52.4 us
    ppermute x2 -> x1, waiting for transfers between devices: 47.6 us -> 0.01 us  [across(): return lax.ppermute(x, 'mp', FAR_Z)]
    ppermute x4 -> x2, waiting for transfers between devices: 11.2 us -> 54.7 us  [along(): return lax.ppermute(x, 'mp', NEAR_Z)]
    unnamed x74 -> x108, local copies, waits for them, and re-layouts: 23.8 us -> 48.2 us
    ppermute x5 -> x2, waiting for transfers between devices: 23.5 us -> 4.16 us  [outward(): return lax.ppermute(x, 'mp', ENDS_OUT)]
    ppermute x6, waiting for transfers between devices: 14.5 us -> 32.6 us  [inward(): return lax.ppermute(x, 'mp', ENDS_IN)]
    all_to_all x2 -> x3, waiting for transfers between devices: 0.01 us -> 14.2 us  [exchange(): return lax.all_to_all(x, 'dp', 0, 0)]
    convert_element_type x8 -> x0, other arithmetic: 9.3 us -> none  [the longest x6 7.38 us: low(): return x.astype(jnp.bfloat16)]
    ppermute x4 -> x2, starting transfers between devices: 10.9 us -> 4.3 us  [along(): return lax.ppermute(x, 'mp', NEAR_Z)]
  transfers between devices with their start and end apart: 36 -> 30, of which waited for: 15 -> 13; matrix products, arithmetic and copies ran while one was open for 5% -> 2% of each run, Pallas kernels for 18% -> 15%
where the time goes in v4:
time: 309 us; the launch traced here: 307 us
  waiting for transfers between devices  110 us (36%)
  starting transfers between devices  71.1 us (23%)
  local copies, waits for them, and re-layouts  56.1 us (18%)
  Pallas kernels  52.4 us (17%)
  between operations  14.8 us (5%)
    ppermute x2, waiting for transfers between devices, along(): return lax.ppermute(x, 'mp', NEAR_Z)  54.7 us
    pallas_call x28, Pallas kernels, call(): return lambda *operands: run(*operands, *before)  52.4 us
    unnamed x108, local copies, waits for them, and re-layouts  48.2 us
    ppermute x6, starting transfers between devices, inward(): return lax.ppermute(x, 'mp', ENDS_IN)  43.7 us
    ppermute x6, waiting for transfers between devices, inward(): return lax.ppermute(x, 'mp', ENDS_IN)  32.6 us
    all_to_all x3, waiting for transfers between devices, exchange(): return lax.all_to_all(x, 'dp', 0, 0)  14.2 us
    all_to_all x3, starting transfers between devices, exchange(): return lax.all_to_all(x, 'dp', 0, 0)  13 us
  transfers between devices with their start and end apart: 30, of which 13 were waited for; matrix products, arithmetic and copies ran while one was open for 2% of the time, Pallas kernels for 15%

profile of v4, /device:TPU:0, one launch (start us, length us, event | category | flops | bytes accessed | tf_op | source)
XLA Modules:
  0.0 307.5 jit_solution(12388190221464997033)
XLA Ops:
  8.6 1.1 copy-done.37
  11.0 1.1 mask_image.2.refs_4_.refs_0_.refs_1_
  13.8 1.9 mask_image.3.refs_2_
  15.8 3.1 collective-permute-start.2
  18.8 2.6 collective-permute-start.1
  21.4 3.7 %copy-done.16 = bf16[9216,512]{1,0:T(8,128)(2,1)S(1)} copy-done((bf16[9216,512]{1,0:T(8,128)(2,1)S(1)}, bf16[9216,512]{1,0:T(8,128)(2,1)}, u32[]{:S(2)}) %copy-start.16) | copy-done | bytes 9437208
  25.1 1.6 load_weight.3.refs_1_.refs_3_.refs_2_
  26.7 2.7 copy-done.17
  29.4 2.0 load_whole.1.refs_2_.refs_1_
  31.4 32.2 %collective-permute-done.2.refs_3_.refs_1_.refs_2_ = bf16[256,1152]{1,0:T(8,128)(2,1)S(1)} collective-permute-done((bf16[256,1152]{1,0:T(8,128)(2,1)S(1)}, bf16[256,1152]{1,0:T(8,128)(2,1)S(1)}, u32[]{:S(2)}, u32[]{:S(2)}) %collective-permute-start.2) | collective-permute-done | bytes 589856 | tf_op jit(solution)/shard_map/ppermute | solution.py:594
  63.6 1.2 collective-permute-start.3
  64.9 3.0 load_weight.4.refs_4_.refs_5_.refs_3_.refs_2_
  67.9 2.2 forward_open.1
  70.1 2.9 load_weight.5.refs_6_.refs_2_
  73.1 22.5 %collective-permute-done.3.refs_1_.refs_7_.refs_4_ = bf16[256,1152]{1,0:T(8,128)(2,1)S(1)} collective-permute-done((bf16[256,1152]{1,0:T(8,128)(2,1)S(1)}, bf16[256,1152]{1,0:T(8,128)(2,1)S(1)}, u32[]{:S(2)}, u32[]{:S(2)}) %collective-permute-start.3) | collective-permute-done | bytes 589856 | tf_op jit(solution)/shard_map/ppermute | solution.py:594
  95.6 1.4 forward_close.1
  97.8 2.0 pack_images.1.refs_7_
  99.8 4.0 %all-to-all-start = ((bf16[4,256,1152]{2,1,0:T(8,128)(2,1)}), bf16[4,256,1152]{2,1,0:T(8,128)(2,1)S(1)}, u32[]{:S(2)}, u32[]{:S(2)}) async-start(bf16[4,256,1152]{2,1,0:T(8,128)(2,1)} %pack_images.1.refs_7_), calls=%async_computation | async-start | bytes 4718592 | tf_op jit(solution)/shard_map/all_to_all | solution.py:614
  103.9 2.1 collective-permute-done.5.refs_1_.refs_8_
  107.4 1.4 collective-permute-done.6.refs_4_.refs_6_
  108.8 2.3 copy-done.4
  111.1 2.3 copy-done.6
  113.5 1.3 parts.4.refs_5_.refs_0_
  114.8 1.5 collective-permute-start.8
  116.3 3.2 %parts.5 = (bf16[1152,256]{1,0:T(8,128)(2,1)}, bf16[1152,256]{1,0:T(8,128)(2,1)S(1)}, f32[1152,256]{1,0:T(8,128)S(1)}) custom-call(s32[9]{0:T(128)S(1)} %concatenate.3.refs_0_, bf16[4608,512]{1,0:T(8,128)(2,1)S(1)} %copy-done.4, bf16[4608,512]{1,0:T(8,128)(2,1)S(1)} %copy-done.6, bf16[512,256]{1,0:T(8,128)(2,1)S(1)} %get-tuple-element.99.refs_3_, ...), custom_call_target="tpu_custom_call" | custom-call | flops 1 | bytes 1 | tf_op jit(solution)/shard_map/parts/pallas_call | solution.py:162
  119.5 2.1 collective-permute-start.7
  121.9 8.0 %collective-permute-done.8.refs_1_.refs_3_ = bf16[1152,256]{1,0:T(8,128)(2,1)S(1)} collective-permute-done((bf16[1152,256]{1,0:T(8,128)(2,1)S(1)}, bf16[1152,256]{1,0:T(8,128)(2,1)S(1)}, u32[]{:S(2)}, u32[]{:S(2)}) %collective-permute-start.8) | collective-permute-done | bytes 589856 | tf_op jit(solution)/shard_map/ppermute | solution.py:602
  131.2 10.8 %collective-permute-done.7.refs_1_.refs_4_ = bf16[1152,256]{1,0:T(8,128)(2,1)} collective-permute-done((bf16[1152,256]{1,0:T(8,128)(2,1)}, bf16[1152,256]{1,0:T(8,128)(2,1)}, u32[]{:S(2)}, u32[]{:S(2)}) %collective-permute-start.7) | collective-permute-done | bytes 589856 | tf_op jit(solution)/shard_map/ppermute | solution.py:602
  142.0 1.1 copy-done.23
  143.1 1.4 add.118.refs_2_
  145.3 3.7 %copy-done.1 = bf16[9216,512]{1,0:T(8,128)(2,1)S(1)} copy-done((bf16[9216,512]{1,0:T(8,128)(2,1)S(1)}, bf16[9216,512]{1,0:T(8,128)(2,1)}, u32[]{:S(2)}) %copy-start.1) | copy-done | bytes 9437208
  149.0 2.3 copy-done.9
  152.4 3.8 %forward_full.1.refs_0_.refs_8_ = f32[256,512]{1,0:T(8,128)S(1)} custom-call(bf16[256,9216]{1,0:T(8,128)(2,1)S(1)} %copy-done.9, bf16[9216,512]{1,0:T(8,128)(2,1)S(1)} %copy-done.1, bf16[1152,256]{1,0:T(8,128)(2,1)S(1)} %copy-done.19, bf16[256,9216]{1,0:T(8,128)(2,1)S(1)} %copy-done.9), custom_call_target="tpu_custom_call" | custom-call | flops 1 | bytes 1 | tf_op jit(solution)/shard_map/forward_full/pallas_call | solution.py:162
  156.2 1.3 tower_b.1
  158.9 4.2 %all-to-all-start.1 = ((bf16[4,272,512]{2,1,0:T(8,128)(2,1)}), bf16[4,272,512]{2,1,0:T(8,128)(2,1)S(1)}, u32[]{:S(2)}, u32[]{:S(2)}) async-start(bf16[4,272,512]{2,1,0:T(8,128)(2,1)} %copy-done.15), calls=%async_computation.1 | async-start | bytes 2228224 | tf_op jit(solution)/shard_map/all_to_all | solution.py:614
  163.2 13.9 %all-to-all-done.1.refs_5_.refs_2_ = bf16[4,272,512]{2,1,0:T(8,128)(2,1)S(1)} async-done(((bf16[4,272,512]{2,1,0:T(8,128)(2,1)}), bf16[4,272,512]{2,1,0:T(8,128)(2,1)S(1)}, u32[]{:S(2)}, u32[]{:S(2)}) %all-to-all-start.1) | async-done | bytes 1114144 | tf_op jit(solution)/shard_map/all_to_all | solution.py:614
  177.1 2.4 copy-done.10
  180.4 1.3 pack_both.1.refs_5_
  181.7 1.8 copy-done.11
  183.5 4.7 %all-to-all-start.2 = ((bf16[4,272,1664]{2,1,0:T(8,128)(2,1)}), bf16[4,272,1664]{2,1,0:T(8,128)(2,1)}, u32[]{:S(2)}, u32[]{:S(2)}) async-start(bf16[4,272,1664]{2,1,0:T(8,128)(2,1)} %copy-done.11), calls=%async_computation.2 | async-start | bytes 7241728 | tf_op jit(solution)/shard_map/all_to_all | solution.py:614
  190.1 3.8 %copy-done.2 = bf16[9216,512]{1,0:T(8,128)(2,1)S(1)} copy-done((bf16[9216,512]{1,0:T(8,128)(2,1)S(1)}, bf16[9216,512]{1,0:T(8,128)(2,1)}, u32[]{:S(2)}) %copy-start.2) | copy-done | bytes 9437208
  193.8 2.4 copy-done.8
  196.2 2.0 copy-done.12
  199.2 1.3 parts.6.refs_5_.refs_0_
  200.6 8.3 %collective-permute-start.11 = (bf16[1152,256]{1,0:T(8,128)(2,1)S(1)}, bf16[1152,256]{1,0:T(8,128)(2,1)S(1)}, u32[]{:S(2)}, u32[]{:S(2)}) collective-permute-start(bf16[1152,256]{1,0:T(8,128)(2,1)S(1)} %parts.6.refs_5_.refs_0_), channel_id=1, source_target_pairs={{0,2},{1,3},{6,4},{7,5},{8,10},{9,11},{14,12},{15,13},{16,18},{17,... | collective-permute-start | bytes 1769480 | tf_op jit(solution)/shard_map/ppermute | solution.py:602
  208.9 2.5 parts.7
  211.5 1.1 add.119.refs_4_
  212.6 11.6 %collective-permute-start.10 = (bf16[1152,256]{1,0:T(8,128)(2,1)S(1)}, bf16[1152,256]{1,0:T(8,128)(2,1)S(1)}, u32[]{:S(2)}, u32[]{:S(2)}) collective-permute-start(bf16[1152,256]{1,0:T(8,128)(2,1)S(1)} %get-tuple-element.132.refs_2_.refs_0_), channel_id=1, source_target_pairs={{0,2},{1,3},{6,4},{7,5},{8,10},{9,11},{14,12},{15,13},{16,18},{17,... | collective-permute-start | bytes 1769480 | tf_op jit(solution)/shard_map/ppermute | solution.py:602
  224.2 5.4 %weight_grad.2.refs_2_ = f32[2304,512]{1,0:T(8,128)} custom-call(s32[9]{0:T(128)S(1)} %concatenate.3.refs_0_, bf16[4,256,1152]{2,1,0:T(8,128)(2,1)S(1)} %all-to-all-done.refs_3_.refs_1_, bf16[4,272,512]{2,1,0:T(8,128)(2,1)S(1)} %all-to-all-done.1.refs_5_.refs_2_, bf16[4,256,1152]{2,1,0:T(8,128)(2,1)} %collective-permute-done.12.refs_3_.refs_5_, ...), custom_call_target="tpu_custom_call" | custom-call | flops 1 | bytes 1 | tf_op jit(solution)/shard_map/weight_grad/pallas_call | solution.py:162
  229.7 2.3 copy-done.13
  233.7 1.3 collective-permute-start.16
  235.7 1.4 collective-permute-done.10.refs_1_.refs_3_
  237.4 2.4 slice_bitcast_fusion
  240.4 14.4 %collective-permute-start.14 = (bf16[1152,256]{1,0:T(8,128)(2,1)S(1)}, bf16[1152,256]{1,0:T(8,128)(2,1)S(1)}, u32[]{:S(2)}, u32[]{:S(2)}) collective-permute-start(bf16[1152,256]{1,0:T(8,128)(2,1)S(1)} %copy-done.40), channel_id=1, source_target_pairs={{0,2},{1,3},{6,4},{7,5},{8,10},{9,11},{14,12},{15,13},{16,18},{17,... | collective-permute-start | bytes 1769480 | tf_op jit(solution)/shard_map/ppermute | solution.py:602
  256.3 11.3 %collective-permute-done.14.refs_4_.refs_8_ = bf16[1152,256]{1,0:T(8,128)(2,1)S(1)} collective-permute-done((bf16[1152,256]{1,0:T(8,128)(2,1)S(1)}, bf16[1152,256]{1,0:T(8,128)(2,1)S(1)}, u32[]{:S(2)}, u32[]{:S(2)}) %collective-permute-start.14) | collective-permute-done | bytes 589856 | tf_op jit(solution)/shard_map/ppermute | solution.py:602
  268.4 1.7 finish.2.refs_7_
  270.1 5.8 %collective-permute-start.18 = (bf16[1152,256]{1,0:T(8,128)(2,1)S(1)}, bf16[1152,256]{1,0:T(8,128)(2,1)S(1)}, u32[]{:S(2)}, u32[]{:S(2)}) collective-permute-start(bf16[1152,256]{1,0:T(8,128)(2,1)S(1)} %copy-done.42), channel_id=1, source_target_pairs={{0,2},{1,3},{6,4},{7,5},{8,10},{9,11},{14,12},{15,13},{16,18},{17,... | collective-permute-start | bytes 1769480 | tf_op jit(solution)/shard_map/ppermute | solution.py:602
  275.9 1.3 collective-permute-start.20
  279.6 7.0 %weight_grad.3.refs_7_ = f32[2304,512]{1,0:T(8,128)} custom-call(s32[9]{0:T(128)S(1)} %concatenate.3.refs_0_, bf16[4,272,1664]{2,1,0:T(8,128)(2,1)} %all-to-all-done.2.refs_1_.refs_2_, bf16[4,272,1664]{2,1,0:T(8,128)(2,1)} %all-to-all-done.2.refs_1_.refs_2_, bf16[272,1664]{1,0:T(8,128)(2,1)S(1)} %collective-permute-done.21.refs_3_, ...), custom_call_target="tpu_custom_call" | custom-call | flops 1 | bytes 1 | tf_op jit(solution)/shard_map/weight_grad/pallas_call | solution.py:162
  286.6 1.1 collective-permute-done.18.refs_4_
  287.7 4.2 %collective-permute-done.20.refs_6_ = bf16[1152,256]{1,0:T(8,128)(2,1)S(1)} collective-permute-done((bf16[1152,256]{1,0:T(8,128)(2,1)S(1)}, bf16[1152,256]{1,0:T(8,128)(2,1)S(1)}, u32[]{:S(2)}, u32[]{:S(2)}) %collective-permute-start.20) | collective-permute-done | bytes 589856 | tf_op jit(solution)/shard_map/ppermute | solution.py:610
  291.9 2.3 copy-done.14
  294.2 1.7 finish.3
  295.9 4.7 %fusion.6 = (bf16[256,4096]{1,0:T(8,128)(2,1)}, bf16[256,4096]{1,0:T(8,128)(2,1)}) fusion(bf16[512,4096]{1,0:T(8,128)(2,1)} %all-gather.5.cloned.1.call-done), kind=kLoop, calls=%fused_computation.29 | loop fusion | bytes 8388608 | tf_op jit(solution)/shard_map/slice | solution.py:752
  (151 shorter events, 23.1 us)
Async XLA Ops:
  7.2 138.1 %all-gather.3.cloned.1.call-start = ((), (), s32[]{:S(2)}) async-start(), calls=%async_computation.3 | async-start | bytes 5308416 | tf_op jit(solution)/shard_map/all_gather | solution.py:664
  7.2 57.7 %collective-permute-start = (bf16[9216,512]{1,0:T(8,128)(2,1)}, bf16[9216,512]{1,0:T(8,128)(2,1)}, u32[]{:S(2)}, u32[]{:S(2)}) collective-permute-start(bf16[9216,512]{1,0:T(8,128)(2,1)} %refs_1_.7), channel_id=1, source_target_pairs={{0,1},{1,0},{2,3},{3,2},{4,5},{5,4},{6,7},{7,6},{8,9},{9,8},{10,11... | collective-permute-start | bytes 28311560 | tf_op jit(solution)/shard_map/ppermute | solution.py:590
  7.7 62.4 %collective-permute-start.4 = (bf16[9216,512]{1,0:T(8,128)(2,1)}, bf16[9216,512]{1,0:T(8,128)(2,1)}, u32[]{:S(2)}, u32[]{:S(2)}) collective-permute-start(bf16[9216,512]{1,0:T(8,128)(2,1)} %refs_0_.1), channel_id=1, source_target_pairs={{0,1},{1,0},{2,3},{3,2},{4,5},{5,4},{6,7},{7,6},{8,9},{9,8},{10,11... | collective-permute-start | bytes 28311560 | tf_op jit(solution)/shard_map/ppermute | solution.py:590
  15.8 47.8 %collective-permute-start.2 = (bf16[256,1152]{1,0:T(8,128)(2,1)S(1)}, bf16[256,1152]{1,0:T(8,128)(2,1)S(1)}, u32[]{:S(2)}, u32[]{:S(2)}) collective-permute-start(bf16[256,1152]{1,0:T(8,128)(2,1)S(1)} %mask_image.2.refs_4_.refs_0_.refs_1_), channel_id=1, source_target_pairs={{0,2},{1,3},{2,0},{3,1},{4,6},{5,7},{6,4},{7,5},{8,10},{9,11},{10,... | collective-permute-start | bytes 1769480 | tf_op jit(solution)/shard_map/ppermute | solution.py:594
  18.8 44.8 %collective-permute-start.1 = (bf16[256,1152]{1,0:T(8,128)(2,1)S(1)}, bf16[256,1152]{1,0:T(8,128)(2,1)S(1)}, u32[]{:S(2)}, u32[]{:S(2)}) collective-permute-start(bf16[256,1152]{1,0:T(8,128)(2,1)S(1)} %mask_image.2.refs_4_.refs_0_.refs_1_), channel_id=1, source_target_pairs={{0,4},{1,5},{2,6},{3,7},{4,0},{5,1},{6,2},{7,3},{8,12},{9,13},{10,... | collective-permute-start | bytes 1769480 | tf_op jit(solution)/shard_map/ppermute | solution.py:598
  21.4 3.7 %copy-start.16 = (bf16[9216,512]{1,0:T(8,128)(2,1)S(1)}, bf16[9216,512]{1,0:T(8,128)(2,1)}, u32[]{:S(2)}) copy-start(bf16[9216,512]{1,0:T(8,128)(2,1)} %refs_1_.7) | copy-start | bytes 28311556
  25.1 4.3 %copy-start.17 = (bf16[9216,512]{1,0:T(8,128)(2,1)S(1)}, bf16[9216,512]{1,0:T(8,128)(2,1)}, u32[]{:S(2)}) copy-start(bf16[9216,512]{1,0:T(8,128)(2,1)} %refs_0_.1) | copy-start | bytes 28311556
  29.4 66.2 %copy-start.3 = (bf16[4608,512]{1,0:T(8,128)(2,1)}, bf16[4608,512]{1,0:T(8,128)(2,1)S(1)}, u32[]{:S(2)}) copy-start(bf16[4608,512]{1,0:T(8,128)(2,1)S(1)} %load_weight.3.refs_1_.refs_3_.refs_2_) | copy-start | bytes 14155780
  31.4 36.5 %copy-start = (bf16[9216,512]{1,0:T(8,128)(2,1)}, bf16[9216,512]{1,0:T(8,128)(2,1)S(1)}, u32[]{:S(2)}) copy-start(bf16[9216,512]{1,0:T(8,128)(2,1)S(1)} %load_whole.1.refs_2_.refs_1_) | copy-start | bytes 28311556
  63.6 32.0 %collective-permute-start.3 = (bf16[256,1152]{1,0:T(8,128)(2,1)S(1)}, bf16[256,1152]{1,0:T(8,128)(2,1)S(1)}, u32[]{:S(2)}, u32[]{:S(2)}) collective-permute-start(bf16[256,1152]{1,0:T(8,128)(2,1)S(1)} %collective-permute-done.1.refs_4_.refs_2_.refs_3_), channel_id=1, source_target_pairs={{0,2},{1,3},{2,0},{3,1},{4,6},{5,7},{6,4},{7,5},{8,10},{9,11},{10,... | collective-permute-start | bytes 1769480 | tf_op jit(solution)/shard_map/ppermute | solution.py:594
  67.9 27.7 %copy-start.5 = (bf16[4608,512]{1,0:T(8,128)(2,1)}, bf16[4608,512]{1,0:T(8,128)(2,1)S(1)}, u32[]{:S(2)}) copy-start(bf16[4608,512]{1,0:T(8,128)(2,1)S(1)} %load_weight.4.refs_4_.refs_5_.refs_3_.refs_2_) | copy-start | bytes 14155780
  73.1 23.9 %copy-start.7 = (bf16[4608,512]{1,0:T(8,128)(2,1)}, bf16[4608,512]{1,0:T(8,128)(2,1)S(1)}, u32[]{:S(2)}) copy-start(bf16[4608,512]{1,0:T(8,128)(2,1)S(1)} %load_weight.5.refs_6_.refs_2_) | copy-start | bytes 14155780
  99.8 4.1 %copy-start.45 = (f32[4,512]{1,0:T(4,128)S(1)}, f32[4,512]{1,0:T(4,128)}, u32[]{:S(2)}) copy-start(f32[4,512]{1,0:T(4,128)} %refs_7_.1) | copy-start | bytes 24580
  99.8 4.1 %copy-start.53 = (f32[2,512]{1,0:T(2,128)S(1)}, f32[2,512]{1,0:T(2,128)}, u32[]{:S(2)}) copy-start(f32[2,512]{1,0:T(2,128)} %param.17) | copy-start | bytes 12292
  99.8 6.2 %copy-start.30 = (bf16[256,512]{1,0:T(8,128)(2,1)S(1)}, bf16[256,512]{1,0:T(8,128)(2,1)}, u32[]{:S(2)}) copy-start(bf16[256,512]{1,0:T(8,128)(2,1)} %refs_4_.1) | copy-start | bytes 786436
  99.8 6.2 %copy-start.32 = (bf16[256,512]{1,0:T(8,128)(2,1)S(1)}, bf16[256,512]{1,0:T(8,128)(2,1)}, u32[]{:S(2)}) copy-start(bf16[256,512]{1,0:T(8,128)(2,1)} %refs_5_.3) | copy-start | bytes 786436
  99.8 31.3 %all-to-all-start = ((bf16[4,256,1152]{2,1,0:T(8,128)(2,1)}), bf16[4,256,1152]{2,1,0:T(8,128)(2,1)S(1)}, u32[]{:S(2)}, u32[]{:S(2)}) async-start(bf16[4,256,1152]{2,1,0:T(8,128)(2,1)} %pack_images.1.refs_7_), calls=%async_computation | async-start | bytes 4718592 | tf_op jit(solution)/shard_map/all_to_all | solution.py:614
  103.9 192.0 %all-gather.5.cloned.1.call-start = ((), (), s32[]{:S(2)}) async-start(), calls=%async_computation.4 | async-start | bytes 4718592 | tf_op jit(solution)/shard_map/all_gather | solution.py:716
  103.9 2.1 collective-permute-start.5
  107.3 1.5 collective-permute-start.6
  108.8 2.3 copy-start.4
  114.8 15.1 %collective-permute-start.8 = (bf16[1152,256]{1,0:T(8,128)(2,1)S(1)}, bf16[1152,256]{1,0:T(8,128)(2,1)S(1)}, u32[]{:S(2)}, u32[]{:S(2)}) collective-permute-start(bf16[1152,256]{1,0:T(8,128)(2,1)S(1)} %parts.4.refs_5_.refs_0_), channel_id=1, source_target_pairs={{0,2},{1,3},{6,4},{7,5},{8,10},{9,11},{14,12},{15,13},{16,18},{17,... | collective-permute-start | bytes 1769480 | tf_op jit(solution)/shard_map/ppermute | solution.py:602
  119.5 10.4 %copy-start.26 = (f32[1152,256]{1,0:T(8,128)}, f32[1152,256]{1,0:T(8,128)S(1)}, u32[]{:S(2)}) copy-start(f32[1152,256]{1,0:T(8,128)S(1)} %get-tuple-element.115.refs_3_) | copy-start | bytes 3538948
  119.5 10.4 %copy-start.38 = (bf16[1152,256]{1,0:T(8,128)(2,1)}, bf16[1152,256]{1,0:T(8,128)(2,1)S(1)}, u32[]{:S(2)}) copy-start(bf16[1152,256]{1,0:T(8,128)(2,1)S(1)} %get-tuple-element.137.refs_0_) | copy-start | bytes 1769476
  119.5 22.5 %collective-permute-start.7 = (bf16[1152,256]{1,0:T(8,128)(2,1)}, bf16[1152,256]{1,0:T(8,128)(2,1)}, u32[]{:S(2)}, u32[]{:S(2)}) collective-permute-start(bf16[1152,256]{1,0:T(8,128)(2,1)} %get-tuple-element.105.refs_2_.refs_0_), channel_id=1, source_target_pairs={{0,2},{1,3},{6,4},{7,5},{8,10},{9,11},{14,12},{15,13},{16,18},{17,... | collective-permute-start | bytes 1769480 | tf_op jit(solution)/shard_map/ppermute | solution.py:602
  121.9 22.5 %copy-start.15 = (bf16[4,272,512]{2,1,0:T(8,128)(2,1)}, bf16[4,272,512]{2,1,0:T(8,128)(2,1)S(1)}, u32[]{:S(2)}) copy-start(bf16[4,272,512]{2,1,0:T(8,128)(2,1)S(1)} %pack_dz.1.refs_2_) | copy-start | bytes 3342340
  145.3 3.7 %copy-start.1 = (bf16[9216,512]{1,0:T(8,128)(2,1)S(1)}, bf16[9216,512]{1,0:T(8,128)(2,1)}, u32[]{:S(2)}) copy-start(bf16[9216,512]{1,0:T(8,128)(2,1)} %copy-done) | copy-start | bytes 28311556
  152.4 3.8 %copy-start.31 = (bf16[256,512]{1,0:T(8,128)(2,1)S(1)}, bf16[256,512]{1,0:T(8,128)(2,1)}, u32[]{:S(2)}) copy-start(bf16[256,512]{1,0:T(8,128)(2,1)} %refs_4_.1) | copy-start | bytes 786436
  152.4 3.8 %copy-start.33 = (bf16[256,512]{1,0:T(8,128)(2,1)S(1)}, bf16[256,512]{1,0:T(8,128)(2,1)}, u32[]{:S(2)}) copy-start(bf16[256,512]{1,0:T(8,128)(2,1)} %refs_5_.3) | copy-start | bytes 786436
  152.4 3.8 %copy-start.44 = (f32[256,512]{1,0:T(8,128)S(1)}, f32[256,512]{1,0:T(8,128)}, u32[]{:S(2)}) copy-start(f32[256,512]{1,0:T(8,128)} %copy-done.43) | copy-start | bytes 1572868
  158.9 18.2 %all-to-all-start.1 = ((bf16[4,272,512]{2,1,0:T(8,128)(2,1)}), bf16[4,272,512]{2,1,0:T(8,128)(2,1)S(1)}, u32[]{:S(2)}, u32[]{:S(2)}) async-start(bf16[4,272,512]{2,1,0:T(8,128)(2,1)} %copy-done.15), calls=%async_computation.1 | async-start | bytes 2228224 | tf_op jit(solution)/shard_map/all_to_all | solution.py:614
  163.1 61.1 %collective-permute-start.12 = (bf16[4,256,1152]{2,1,0:T(8,128)(2,1)S(1)}, bf16[4,256,1152]{2,1,0:T(8,128)(2,1)}, u32[]{:S(2)}, u32[]{:S(2)}) collective-permute-start(bf16[4,256,1152]{2,1,0:T(8,128)(2,1)S(1)} %all-to-all-done.refs_3_.refs_1_), channel_id=1, source_target_pairs={{0,1},{1,0},{2,3},{3,2},{4,5},{5,4},{6,7},{7,6},{8,9},{9,8},{10,11... | collective-permute-start | bytes 7077896 | tf_op jit(solution)/shard_map/ppermute | solution.py:590
  177.1 2.4 copy-start.10
  183.5 53.9 %all-to-all-start.2 = ((bf16[4,272,1664]{2,1,0:T(8,128)(2,1)}), bf16[4,272,1664]{2,1,0:T(8,128)(2,1)}, u32[]{:S(2)}, u32[]{:S(2)}) async-start(bf16[4,272,1664]{2,1,0:T(8,128)(2,1)} %copy-done.11), calls=%async_computation.2 | async-start | bytes 7241728 | tf_op jit(solution)/shard_map/all_to_all | solution.py:614
  188.3 1.8 collective-permute-start.9
  188.3 23.1 %collective-permute-start.13 = (bf16[1152,256]{1,0:T(8,128)(2,1)}, bf16[1152,256]{1,0:T(8,128)(2,1)S(1)}, u32[]{:S(2)}, u32[]{:S(2)}) collective-permute-start(bf16[1152,256]{1,0:T(8,128)(2,1)} %copy-done.22), channel_id=1, source_target_pairs={{2,4},{3,5},{4,2},{5,3},{10,12},{11,13},{12,10},{13,11},{18,20},{1... | collective-permute-start | bytes 1769480 | tf_op jit(solution)/shard_map/ppermute | solution.py:606
  190.1 3.8 %copy-start.2 = (bf16[9216,512]{1,0:T(8,128)(2,1)S(1)}, bf16[9216,512]{1,0:T(8,128)(2,1)}, u32[]{:S(2)}) copy-start(bf16[9216,512]{1,0:T(8,128)(2,1)} %copy-done) | copy-start | bytes 28311556
  193.8 2.4 copy-start.8
  200.5 10.9 %copy-start.39 = (bf16[1152,256]{1,0:T(8,128)(2,1)S(1)}, bf16[1152,256]{1,0:T(8,128)(2,1)}, u32[]{:S(2)}) copy-start(bf16[1152,256]{1,0:T(8,128)(2,1)} %copy-done.38) | copy-start | bytes 1769476
  200.6 29.1 %collective-permute-start.11 = (bf16[1152,256]{1,0:T(8,128)(2,1)S(1)}, bf16[1152,256]{1,0:T(8,128)(2,1)S(1)}, u32[]{:S(2)}, u32[]{:S(2)}) collective-permute-start(bf16[1152,256]{1,0:T(8,128)(2,1)S(1)} %parts.6.refs_5_.refs_0_), channel_id=1, source_target_pairs={{0,2},{1,3},{6,4},{7,5},{8,10},{9,11},{14,12},{15,13},{16,18},{17,... | collective-permute-start | bytes 1769480 | tf_op jit(solution)/shard_map/ppermute | solution.py:602
  211.4 18.2 %copy-start.24 = (f32[1152,256]{1,0:T(8,128)}, f32[1152,256]{1,0:T(8,128)S(1)}, u32[]{:S(2)}) copy-start(f32[1152,256]{1,0:T(8,128)S(1)} %get-tuple-element.148.refs_3_) | copy-start | bytes 3538948
  211.4 25.8 %copy-start.41 = (bf16[1152,256]{1,0:T(8,128)(2,1)}, bf16[1152,256]{1,0:T(8,128)(2,1)S(1)}, u32[]{:S(2)}) copy-start(bf16[1152,256]{1,0:T(8,128)(2,1)S(1)} %get-tuple-element.149.refs_0_) | copy-start | bytes 1769476
  212.6 24.5 %collective-permute-start.10 = (bf16[1152,256]{1,0:T(8,128)(2,1)S(1)}, bf16[1152,256]{1,0:T(8,128)(2,1)S(1)}, u32[]{:S(2)}, u32[]{:S(2)}) collective-permute-start(bf16[1152,256]{1,0:T(8,128)(2,1)S(1)} %get-tuple-element.132.refs_2_.refs_0_), channel_id=1, source_target_pairs={{0,2},{1,3},{6,4},{7,5},{8,10},{9,11},{14,12},{15,13},{16,18},{17,... | collective-permute-start | bytes 1769480 | tf_op jit(solution)/shard_map/ppermute | solution.py:602
  229.7 2.3 copy-start.13
  232.0 3.0 copy-start.20
  232.2 5.0 %collective-permute-start.17 = (bf16[1152,256]{1,0:T(8,128)(2,1)S(1)}, bf16[1152,256]{1,0:T(8,128)(2,1)S(1)}, u32[]{:S(2)}, u32[]{:S(2)}) collective-permute-start(bf16[1152,256]{1,0:T(8,128)(2,1)S(1)} %add.120.refs_2_), channel_id=1, source_target_pairs={{2,4},{3,5},{4,2},{5,3},{10,12},{11,13},{12,10},{13,11},{18,20},{1... | collective-permute-start | bytes 1769480 | tf_op jit(solution)/shard_map/ppermute | solution.py:606
  233.7 21.2 %collective-permute-start.16 = (bf16[1152,256]{1,0:T(8,128)(2,1)}, bf16[1152,256]{1,0:T(8,128)(2,1)S(1)}, u32[]{:S(2)}, u32[]{:S(2)}) collective-permute-start(bf16[1152,256]{1,0:T(8,128)(2,1)} %add.119.refs_4_), channel_id=1, source_target_pairs={{2,0},{3,1},{4,6},{5,7},{10,8},{11,9},{12,14},{13,15},{18,16},{19,... | collective-permute-start | bytes 1769480 | tf_op jit(solution)/shard_map/ppermute | solution.py:610
  235.0 20.0 %collective-permute-start.15 = (bf16[1152,256]{1,0:T(8,128)(2,1)S(1)}, bf16[1152,256]{1,0:T(8,128)(2,1)S(1)}, u32[]{:S(2)}, u32[]{:S(2)}) collective-permute-start(bf16[1152,256]{1,0:T(8,128)(2,1)S(1)} %copy-done.20), channel_id=1, source_target_pairs={{2,4},{3,5},{4,2},{5,3},{10,12},{11,13},{12,10},{13,11},{18,20},{1... | collective-permute-start | bytes 1769480 | tf_op jit(solution)/shard_map/ppermute | solution.py:606
  237.4 3.1 copy-start.40
  237.4 31.0 %copy-start.48 = (s32[2,36]{1,0:T(2,128)S(1)}, s32[2,36]{1,0:T(2,128)}, u32[]{:S(2)}) copy-start(s32[2,36]{1,0:T(2,128)} %refs_1_.9) | copy-start | bytes 868
  237.4 31.0 %copy-start.50 = (s32[256]{0:T(256)S(1)}, s32[256]{0:T(256)}, u32[]{:S(2)}) copy-start(s32[256]{0:T(256)} %param.13) | copy-start | bytes 3076
  237.4 3.0 copy-start.52
  237.4 30.9 %copy-start.27 = (f32[1152,256]{1,0:T(8,128)S(1)}, f32[1152,256]{1,0:T(8,128)}, u32[]{:S(2)}) copy-start(f32[1152,256]{1,0:T(8,128)} %copy-done.26) | copy-start | bytes 3538948
  239.8 30.3 %copy-start.42 = (bf16[1152,256]{1,0:T(8,128)(2,1)S(1)}, bf16[1152,256]{1,0:T(8,128)(2,1)}, u32[]{:S(2)}) copy-start(bf16[1152,256]{1,0:T(8,128)(2,1)} %copy-done.41) | copy-start | bytes 1769476
  239.8 30.3 %collective-permute-start.24 = (bf16[272,1664]{1,0:T(8,128)(2,1)S(1)}, bf16[272,1664]{1,0:T(8,128)(2,1)S(1)}, u32[]{:S(2)}, u32[]{:S(2)}) collective-permute-start(bf16[272,1664]{1,0:T(8,128)(2,1)S(1)} %get-tuple-element.155), channel_id=1, source_target_pairs={{0,1},{1,0},{2,3},{3,2},{4,5},{5,4},{6,7},{7,6},{8,9},{9,8},{10,11... | collective-permute-start | bytes 2715656 | tf_op jit(solution)/shard_map/ppermute | solution.py:590
  239.9 36.0 %collective-permute-start.23 = (bf16[272,1664]{1,0:T(8,128)(2,1)S(1)}, bf16[272,1664]{1,0:T(8,128)(2,1)S(1)}, u32[]{:S(2)}, u32[]{:S(2)}) collective-permute-start(bf16[272,1664]{1,0:T(8,128)(2,1)S(1)} %get-tuple-element.154), channel_id=1, source_target_pairs={{0,1},{1,0},{2,3},{3,2},{4,5},{5,4},{6,7},{7,6},{8,9},{9,8},{10,11... | collective-permute-start | bytes 2715656 | tf_op jit(solution)/shard_map/ppermute | solution.py:590
  240.4 27.2 %collective-permute-start.14 = (bf16[1152,256]{1,0:T(8,128)(2,1)S(1)}, bf16[1152,256]{1,0:T(8,128)(2,1)S(1)}, u32[]{:S(2)}, u32[]{:S(2)}) collective-permute-start(bf16[1152,256]{1,0:T(8,128)(2,1)S(1)} %copy-done.40), channel_id=1, source_target_pairs={{0,2},{1,3},{6,4},{7,5},{8,10},{9,11},{14,12},{15,13},{16,18},{17,... | collective-permute-start | bytes 1769480 | tf_op jit(solution)/shard_map/ppermute | solution.py:602
  254.9 23.6 %collective-permute-start.22 = (bf16[272,1664]{1,0:T(8,128)(2,1)S(1)}, bf16[272,1664]{1,0:T(8,128)(2,1)S(1)}, u32[]{:S(2)}, u32[]{:S(2)}) collective-permute-start(bf16[272,1664]{1,0:T(8,128)(2,1)S(1)} %get-tuple-element.153), channel_id=1, source_target_pairs={{0,1},{1,0},{2,3},{3,2},{4,5},{5,4},{6,7},{7,6},{8,9},{9,8},{10,11... | collective-permute-start | bytes 2715656 | tf_op jit(solution)/shard_map/ppermute | solution.py:590
  255.0 23.5 %collective-permute-start.21 = (bf16[272,1664]{1,0:T(8,128)(2,1)S(1)}, bf16[272,1664]{1,0:T(8,128)(2,1)S(1)}, u32[]{:S(2)}, u32[]{:S(2)}) collective-permute-start(bf16[272,1664]{1,0:T(8,128)(2,1)S(1)} %get-tuple-element.152), channel_id=1, source_target_pairs={{0,1},{1,0},{2,3},{3,2},{4,5},{5,4},{6,7},{7,6},{8,9},{9,8},{10,11... | collective-permute-start | bytes 2715656 | tf_op jit(solution)/shard_map/ppermute | solution.py:590
  267.6 18.9 %collective-permute-start.19 = (bf16[1152,256]{1,0:T(8,128)(2,1)S(1)}, bf16[1152,256]{1,0:T(8,128)(2,1)S(1)}, u32[]{:S(2)}, u32[]{:S(2)}) collective-permute-start(bf16[1152,256]{1,0:T(8,128)(2,1)S(1)} %add.121.refs_2_), channel_id=1, source_target_pairs={{2,4},{3,5},{4,2},{5,3},{10,12},{11,13},{12,10},{13,11},{18,20},{1... | collective-permute-start | bytes 1769480 | tf_op jit(solution)/shard_map/ppermute | solution.py:606
  270.1 17.6 %collective-permute-start.18 = (bf16[1152,256]{1,0:T(8,128)(2,1)S(1)}, bf16[1152,256]{1,0:T(8,128)(2,1)S(1)}, u32[]{:S(2)}, u32[]{:S(2)}) collective-permute-start(bf16[1152,256]{1,0:T(8,128)(2,1)S(1)} %copy-done.42), channel_id=1, source_target_pairs={{0,2},{1,3},{6,4},{7,5},{8,10},{9,11},{14,12},{15,13},{16,18},{17,... | collective-permute-start | bytes 1769480 | tf_op jit(solution)/shard_map/ppermute | solution.py:602
  275.9 15.9 %collective-permute-start.20 = (bf16[1152,256]{1,0:T(8,128)(2,1)S(1)}, bf16[1152,256]{1,0:T(8,128)(2,1)S(1)}, u32[]{:S(2)}, u32[]{:S(2)}) collective-permute-start(bf16[1152,256]{1,0:T(8,128)(2,1)S(1)} %add.122.refs_7_), channel_id=1, source_target_pairs={{2,0},{3,1},{4,6},{5,7},{10,8},{11,9},{12,14},{13,15},{18,16},{19,... | collective-permute-start | bytes 1769480 | tf_op jit(solution)/shard_map/ppermute | solution.py:610
  279.6 12.3 %copy-start.25 = (f32[1152,256]{1,0:T(8,128)S(1)}, f32[1152,256]{1,0:T(8,128)}, u32[]{:S(2)}) copy-start(f32[1152,256]{1,0:T(8,128)} %copy-done.24) | copy-start | bytes 3538948
  291.9 2.3 copy-start.14
  (20 other events, 22.5 us)
Sparse Core Ops, SparseCore 0:
  15.9 79.0 all-gather.2
  159.0 56.2 all-gather.4

commit v5 on v3

v5 whole, which is shorter than its diff:
```python
import functools

import jax
import jax.numpy as jnp
from jax import lax
from jax.experimental import pallas as pl
from jax.experimental.pallas import tpu as pltpu
from jax.sharding import PartitionSpec as P

CH = 256
POS = 36


def keep_block(image_group, position_mask, first_col, cols):
    positions = (first_col + lax.iota(jnp.int32, cols)) // CH
    onehot = (positions[:, None] == lax.iota(jnp.int32, POS)[None, :]).astype(jnp.float32)
    per_position = jnp.dot(onehot, position_mask.astype(jnp.float32).T)
    return jnp.where(
        image_group[:, None] == 1, per_position[:, 1][None, :], per_position[:, 0][None, :]
    )


def general_shards(
    image_a,
    image_b,
    image_group,
    position_mask,
    weight_a,
    weight_b,
    tower_bias,
    stitch,
    cotan_a,
    cotan_b,
):
    batch_rows = image_a.shape[0]
    shard_cols = image_a.shape[1]
    first_col = lax.axis_index("mp") * shard_cols
    keep_mask = keep_block(image_group, position_mask, first_col, shard_cols)
    keep_low = keep_mask.astype(jnp.bfloat16)
    contract_rows = (((0,), (0,)), ((), ()))
    contract_units = (((1,), (1,)), ((), ()))
    full_a = lax.all_gather(image_a * keep_low, "mp", axis=1, tiled=True)
    full_b = lax.all_gather(image_b * keep_low, "mp", axis=1, tiled=True)
    pre_a = jnp.dot(full_a, weight_a, preferred_element_type=jnp.float32) + tower_bias[0][None, :]
    pre_b = jnp.dot(full_b, weight_b, preferred_element_type=jnp.float32) + tower_bias[1][None, :]
    sigma_a = jax.nn.sigmoid(pre_a)
    sigma_b = jax.nn.sigmoid(pre_b)
    hidden_a = pre_a * sigma_a
    hidden_b = pre_b * sigma_b
    local_a = (stitch[0][None, :] * hidden_a + stitch[1][None, :] * hidden_b).astype(jnp.bfloat16)
    local_b = (stitch[2][None, :] * hidden_a + stitch[3][None, :] * hidden_b).astype(jnp.bfloat16)
    stitched_a = lax.all_gather(local_a, "mp", axis=1, tiled=True)
    stitched_b = lax.all_gather(local_b, "mp", axis=1, tiled=True)
    upper_a = cotan_a.astype(jnp.float32)
    upper_b = cotan_b.astype(jnp.float32)
    dhid_a = stitch[0][None, :] * upper_a + stitch[2][None, :] * upper_b
    dhid_b = stitch[1][None, :] * upper_a + stitch[3][None, :] * upper_b
    dpre_a = dhid_a * (sigma_a * (1.0 + pre_a * (1.0 - sigma_a)))
    dpre_b = dhid_b * (sigma_b * (1.0 + pre_b * (1.0 - sigma_b)))
    bias_terms = jnp.stack([jnp.sum(dpre_a, axis=0), jnp.sum(dpre_b, axis=0)])
    stitch_terms = jnp.stack(
        [
            jnp.sum(upper_a * hidden_a, axis=0),
            jnp.sum(upper_a * hidden_b, axis=0),
            jnp.sum(upper_b * hidden_a, axis=0),
            jnp.sum(upper_b * hidden_b, axis=0),
        ]
    )
    grad_bias, grad_stitch = lax.psum((bias_terms, stitch_terms), "dp")
    dlow_a = dpre_a.astype(jnp.bfloat16)
    dlow_b = dpre_b.astype(jnp.bfloat16)
    block_a = lax.dot_general(full_a, dlow_a, contract_rows, preferred_element_type=jnp.float32)
    block_b = lax.dot_general(full_b, dlow_b, contract_rows, preferred_element_type=jnp.float32)
    grad_weight_a = lax.psum_scatter(block_a, "dp", scatter_dimension=0, tiled=True)
    grad_weight_b = lax.psum_scatter(block_b, "dp", scatter_dimension=0, tiled=True)
    part_a = lax.dot_general(weight_a, dlow_a, contract_units, preferred_element_type=jnp.float32)
    part_b = lax.dot_general(weight_b, dlow_b, contract_units, preferred_element_type=jnp.float32)
    summed = lax.psum_scatter(
        jnp.concatenate([part_a, part_b], axis=1), "mp", scatter_dimension=0, tiled=True
    )
    keep_cols = keep_mask.T
    grad_image_a = (summed[:, :batch_rows] * keep_cols).astype(jnp.bfloat16)
    grad_image_b = (summed[:, batch_rows:] * keep_cols).astype(jnp.bfloat16)
    return (
        stitched_a,
        stitched_b,
        grad_image_a,
        grad_image_b,
        grad_weight_a,
        grad_weight_b,
        grad_bias,
        grad_stitch,
    )


SWAP_CORE = [(d, d ^ 1) for d in range(8)]
NEAR_Z = [(d, d ^ 2) for d in range(8)]
FAR_Z = [(d, d ^ 4) for d in range(8)]
ENDS_IN = [(0, 2), (1, 3), (6, 4), (7, 5)]
MIDS = [(2, 4), (3, 5), (4, 2), (5, 3)]
ENDS_OUT = [(2, 0), (3, 1), (4, 6), (5, 7)]
SLOTS = ((3, 2, 1, 0), (3, 2, 0, 1), (0, 1, 3, 2), (0, 1, 2, 3))
LANES = 128
EXTRA = 16
VMEM_LIMIT = 14 * 1024 * 1024
SMEM = pl.BlockSpec(memory_space=pltpu.SMEM)
VMEM = pl.BlockSpec(memory_space=pltpu.VMEM)
HBM = pl.BlockSpec(memory_space=pltpu.HBM)
ANY = pl.BlockSpec(memory_space=pl.ANY)
LITTLE = pl.CostEstimate(flops=1, bytes_accessed=1, transcendentals=0)


def low(x):
    return x.astype(jnp.bfloat16)


def wide(x):
    return x.astype(jnp.float32)


def array(shape, dtype):
    return jax.ShapeDtypeStruct(shape, dtype)


class Line:
    def __init__(self):
        self.token = None

    def tie(self, *xs):
        if self.token is None:
            return xs
        *xs, self.token = lax.optimization_barrier((*xs, self.token))
        return xs

    def wait(self, *arrived):
        arrived = self.tie(*arrived)
        return arrived if len(arrived) > 1 else arrived[0]

    def send(self, move, x):
        return move(*self.tie(x))


line = Line()


def call(kernel, out_shape, in_specs, out_specs, name, scratch=()):
    single = not isinstance(out_shape, list)
    outs = [out_shape] if single else out_shape
    places = [out_specs] if single else out_specs
    n_in, n_out = len(in_specs), len(outs)
    before = () if line.token is None else (line.token,)

    def body(*refs):
        start = n_in + len(before)
        refs[start + n_out][...] = jnp.zeros((8, LANES), jnp.float32)
        kernel(*refs[:n_in], *refs[start : start + n_out], *refs[start + n_out + 1 :])

    run = pl.pallas_call(
        body,
        out_shape=[*outs, array((8, LANES), jnp.float32)],
        in_specs=[*in_specs, *[HBM] * len(before)],
        out_specs=[*places, VMEM],
        scratch_shapes=scratch,
        compiler_params=pltpu.CompilerParams(vmem_limit_bytes=VMEM_LIMIT),
        cost_estimate=LITTLE,
        name=name,
    )

    def go(*operands):
        *results, line.token = run(*operands, *before)
        return results[0] if single else results

    return go


def marks_of(marks, where, cols, chunk):
    position = (where[8] * cols + chunk * LANES) // CH
    return marks[0, position], marks[1, position]


def mask_kernel(where, marks, group, image, out):
    rows, cols = image.shape
    second = jnp.broadcast_to(jnp.where(group[...] == 1, 1.0, 0.0), (8, rows)).T[:, 0:1] > 0.5
    for chunk in range(cols // LANES):
        zero, one = marks_of(marks, where, cols, chunk)
        keep = wide(jnp.where(second, one, zero))
        lanes = slice(chunk * LANES, (chunk + 1) * LANES)
        out[:, lanes] = low(wide(image[:, lanes]) * keep)


def mask_image(where, marks, group, image):
    return call(
        mask_kernel, array(image.shape, jnp.bfloat16), [SMEM, SMEM, VMEM, VMEM], VMEM, "mask_image"
    )(where, marks, group, image)


def load_kernel(where, weight, out, sems):
    cols = out.shape[0] // 4
    copies = []
    for k in range(4):
        block = 2 * (where[0] ^ k) + where[1]
        copies.append(
            pltpu.make_async_copy(
                weight.at[pl.ds(pl.multiple_of(block * cols, cols), cols), :],
                out.at[pl.ds(k * cols, cols), :],
                sems.at[k],
            )
        )
    for copy in copies:
        copy.start()
    for copy in copies:
        copy.wait()


def load(where, weight):
    rows, units = weight.shape
    weight = pltpu.with_memory_space_constraint(weight, pltpu.HBM)
    return call(
        load_kernel,
        pltpu.VMEM((rows // 2, units), weight.dtype),
        [SMEM, HBM],
        VMEM,
        "load_weight",
        [pltpu.SemaphoreType.DMA((4,))],
    )(where, weight)


def dot(x, y):
    return jnp.dot(x, y, preferred_element_type=jnp.float32)


def open_kernel(p0, p1, p2, mine, other, keep, send):
    cols = p0.shape[1]
    for weight, out in ((mine, keep), (other, send)):
        total = None
        for k, piece in enumerate((p0, p1, p2)):
            term = dot(piece[...], weight[k * cols : (k + 1) * cols, :])
            total = term if total is None else total + term
        out[...] = total


def forward_open(p0, p1, p2, mine, other):
    out = array((p0.shape[0], mine.shape[1]), jnp.float32)
    return call(open_kernel, [out] * 2, [VMEM] * 5, [VMEM] * 2, "forward_open")(
        p0, p1, p2, mine, other
    )


def close_kernel(p3, mine, other, keep, send, out, sent):
    cols = p3.shape[1]
    sent[...] = send[...] + dot(p3[...], other[3 * cols :, :])
    out[...] = keep[...] + dot(p3[...], mine[3 * cols :, :])


def forward_close(*operands):
    out = array(operands[-1].shape, jnp.float32)
    return call(close_kernel, [out] * 2, [VMEM] * 5, [VMEM] * 2, "forward_close")(*operands)


def tower_math(pre, bias, unit_a, unit_b, upper_a, upper_b, dz, dz_t, sums):
    pre = pre + bias[...]
    sigma = jax.nn.sigmoid(pre)
    hidden = pre * sigma
    cot_a = wide(upper_a[...])
    cot_b = wide(upper_b[...])
    dhid = unit_a[...] * cot_a + unit_b[...] * cot_b
    dpre = dhid * (sigma * (1.0 + pre * (1.0 - sigma)))
    dz[...] = low(dpre)
    dz_t[...] = low(dpre).T
    sums[0:1, :] = jnp.sum(dpre, axis=0, keepdims=True)
    sums[1:2, :] = jnp.sum(cot_a * hidden, axis=0, keepdims=True)
    sums[2:3, :] = jnp.sum(cot_b * hidden, axis=0, keepdims=True)
    sums[3:4, :] = jnp.zeros_like(sums[3:4, :])
    return hidden


def first_kernel(own, got, bias, stitch, upper_a, upper_b, dz, dz_t, sums, hidden):
    hidden[...] = tower_math(
        own[...] + got[...],
        bias[0:1, :],
        stitch[0:1, :],
        stitch[2:3, :],
        upper_a,
        upper_b,
        dz,
        dz_t,
        sums,
    )


def second_kernel(own, got, earlier, bias, stitch, upper_a, upper_b, dz, dz_t, sums, local):
    hidden = tower_math(
        own[...] + got[...],
        bias[1:2, :],
        stitch[1:2, :],
        stitch[3:4, :],
        upper_a,
        upper_b,
        dz,
        dz_t,
        sums,
    )
    rows = hidden.shape[0]
    before = earlier[...]
    local[0:rows, :] = low(stitch[0:1, :] * before + stitch[1:2, :] * hidden)
    local[rows : 2 * rows, :] = low(stitch[2:3, :] * before + stitch[3:4, :] * hidden)


def tower(kernel, name, last, *operands):
    rows, units = operands[0].shape
    return call(
        kernel,
        [
            array((rows, units), jnp.bfloat16),
            array((units, rows), jnp.bfloat16),
            array((4, units), jnp.float32),
            last,
        ],
        [VMEM] * len(operands),
        [VMEM] * 4,
        name,
    )(*operands)


def part_kernel(slots, where, mine, other, dz_t, dzo_t, *outs):
    cols = mine.shape[0] // 4
    for slot, at, block in slots:
        rows = pl.ds(pl.multiple_of(where[3 + slot] * cols, cols), cols)
        total = dot(mine[rows, :], dz_t[...]) + dot(other[rows, :], dzo_t[...])
        outs[at][block * cols : (block + 1) * cols, :] = total.astype(outs[at].dtype)


def parts(slots, outs, where, mine, other, dz_t, dzo_t):
    cols = mine.shape[0] // 4
    rows = dz_t.shape[1]
    return call(
        functools.partial(part_kernel, slots),
        [array((blocks * cols, rows), dtype) for blocks, dtype in outs],
        [SMEM] + [VMEM] * 4,
        [VMEM] * len(outs),
        "parts",
    )(where, mine, other, dz_t, dzo_t)


def choose_kernel(where, at_end, in_middle, out, sem):
    for flag, source in enumerate((at_end, in_middle)):
        pl.when(where[2] == flag)(pltpu.make_async_copy(source, out, sem).start)
    pltpu.make_async_copy(at_end, out, sem).wait()


def choose(where, at_end, in_middle):
    return call(
        choose_kernel,
        array(at_end.shape, at_end.dtype),
        [SMEM, ANY, ANY],
        VMEM,
        "choose",
        [pltpu.SemaphoreType.DMA],
    )(where, at_end, in_middle)


def join_kernel(one, two, out):
    rows = one.shape[0]
    out[0:rows, :] = one[...]
    out[rows : 2 * rows, :] = two[...]


def join(one, two):
    rows, cols = one.shape
    return call(join_kernel, array((2 * rows, cols), one.dtype), [VMEM, VMEM], VMEM, "join")(
        one, two
    )


def lay_kernel(where, *refs):
    own, far, (out_a, out_b, sems) = refs[0:4], refs[4:6], refs[6:]
    rows = out_a.shape[0]
    units = own[0].shape[1]
    copies = []
    for side in range(2):
        for k in range(4):
            block = 2 * (where[0] ^ k) + (where[1] ^ side)
            lanes = pl.ds(pl.multiple_of(block * units, units), units)
            source, start = (own[k], 0) if side == 0 else (far[k // 2], 2 * rows * (k % 2))
            for half, out in enumerate((out_a, out_b)):
                at = pl.ds(start + half * rows, rows)
                sem = sems.at[side * 8 + k * 2 + half]
                copies.append(pltpu.make_async_copy(source.at[at, :], out.at[:, lanes], sem))
    for copy in copies:
        copy.start()
    for copy in copies:
        copy.wait()


def lay_out(where, *sources):
    rows, units = sources[0].shape
    return call(
        lay_kernel,
        [array((rows // 2, 8 * units), jnp.bfloat16)] * 2,
        [SMEM] + [ANY] * 6,
        [VMEM] * 2,
        "lay_out",
        [pltpu.SemaphoreType.DMA((16,))],
    )(where, *sources)


def add_kernel(one, two, out):
    rows = out.shape[0]
    out[...] = low(wide(one[...]) + wide(two[0:rows, :]))


def add(one, two):
    return call(add_kernel, array(one.shape, jnp.bfloat16), [VMEM, VMEM], VMEM, "add")(one, two)


def finish_kernel(third_at, where, marks, group, kept, third, cross, last, out):
    second = group[...] == 1
    cols = out.shape[0]
    cross_at = cross.shape[0] - cols
    for chunk in range(cols // LANES):
        zero, one = marks_of(marks, where, cols, chunk)
        keep = wide(jnp.where(second, one, zero))
        at = chunk * LANES
        total = kept[at : at + LANES, :] + wide(last[at : at + LANES, :])
        total += wide(third[third_at + at : third_at + at + LANES, :])
        total += wide(cross[cross_at + at : cross_at + at + LANES, :])
        out[at : at + LANES, :] = low(total * keep)


def finish(third_at, where, marks, group, kept, third, cross, last):
    return call(
        functools.partial(finish_kernel, third_at * kept.shape[0]),
        array(kept.shape, jnp.bfloat16),
        [SMEM, SMEM] + [VMEM] * 5,
        VMEM,
        "finish",
    )(where, marks, group, kept, third, cross, last)


def pack_kernel(where, p0, p1, p2, p3, dz, sums, out, sems):
    rows, units = dz.shape
    cols = p0.shape[1]
    for q in range(4):
        block = out.at[q, pl.ds(0, rows), pl.ds(0, cols)]
        for index, piece in enumerate((p0, p1, p2, p3)):
            start = pltpu.make_async_copy(piece, block, sems.at[q]).start
            pl.when(where[0] ^ q == index)(start)
    extra = jnp.zeros((EXTRA, cols + units), jnp.bfloat16)
    for q in range(4):
        out[q, rows : rows + EXTRA, :] = extra
        out[q, 0:rows, cols : cols + units] = dz[...]
    for k in range(3):
        rest = sums[k : k + 1, :]
        for term in range(3):
            piece = low(rest)
            row = rows + 3 * k + term
            for q in range(4):
                out[q, row : row + 1, cols : cols + units] = piece
            rest = rest - wide(piece)
    for q in range(4):
        block = out.at[q, pl.ds(0, rows), pl.ds(0, cols)]
        pltpu.make_async_copy(p0, block, sems.at[q]).wait()


def pack(where, pieces, dz, sums):
    rows, units = dz.shape
    cols = pieces[0].shape[1]
    return call(
        pack_kernel,
        array((4, rows + EXTRA, cols + units), jnp.bfloat16),
        [SMEM] + [ANY] * 4 + [VMEM] * 2,
        VMEM,
        "pack",
        [pltpu.SemaphoreType.DMA((4,))],
    )(where, *pieces, dz, sums)


def weight_kernel(where, near, far, out, images, dzs, tiles, sems):
    rows, units = dzs.shape[1:]
    cols = images.shape[3]
    tile = tiles.shape[1]
    steps = cols // tile

    def fetch(q):
        source = near.at[q, pl.ds(0, rows), pl.ds(cols, units)]
        return pltpu.make_async_copy(source, dzs.at[q], sems.at[q])

    def block(source, p, q):
        image = source.at[q, pl.ds(0, rows), pl.ds(0, cols)]
        return pltpu.make_async_copy(image, images.at[p, q], sems.at[4 + 4 * p + q])

    def give(p, t):
        slot = p * steps + t
        return pltpu.make_async_copy(
            tiles.at[slot], out.at[pl.ds(slot * tile, tile), :], sems.at[12 + slot]
        )

    for q in range(4):
        fetch(q).start()
    for p in range(2):
        for q in range(4):
            pl.when(where[1] == p)(block(near, p, q).start)
            pl.when(where[1] != p)(block(far, p, q).start)
    for q in range(4):
        fetch(q).wait()
    for p in range(2):
        for q in range(4):
            block(near, p, q).wait()
        for t in range(steps):
            total = None
            for q in range(4):
                term = lax.dot_general(
                    images[p, q, :, t * tile : (t + 1) * tile],
                    dzs[q],
                    (((0,), (0,)), ((), ())),
                    preferred_element_type=jnp.float32,
                )
                total = term if total is None else total + term
            tiles[p * steps + t] = total
            give(p, t).start()
    for p in range(2):
        for t in range(steps):
            give(p, t).wait()


def weight_grad(rows, cols, where, near, far):
    units = near.shape[2] - cols
    tile = cols // 3
    return call(
        weight_kernel,
        array((2 * cols, units), jnp.float32),
        [SMEM, ANY, ANY],
        HBM,
        "weight_grad",
        [
            pltpu.VMEM((2, 4, rows, cols), jnp.bfloat16),
            pltpu.VMEM((4, rows, units), jnp.bfloat16),
            pltpu.VMEM((6, tile, units), jnp.float32),
            pltpu.SemaphoreType.DMA((18,)),
        ],
    )(where, near, far)


def sums_kernel(rows, cols, got_a, got_b, bias, stitch, terms, sems):
    units = bias.shape[1]
    copies = [
        pltpu.make_async_copy(
            got.at[:, pl.ds(rows, EXTRA), pl.ds(cols, units)], terms.at[side], sems.at[side]
        )
        for side, got in enumerate((got_a, got_b))
    ]
    for copy in copies:
        copy.start()
    for copy in copies:
        copy.wait()
    for side in range(2):
        totals = []
        for k in range(3):
            each = [
                (
                    wide(terms[side, q, 3 * k + 2 : 3 * k + 3, :])
                    + wide(terms[side, q, 3 * k + 1 : 3 * k + 2, :])
                )
                + wide(terms[side, q, 3 * k : 3 * k + 1, :])
                for q in range(4)
            ]
            totals.append((each[0] + each[1]) + (each[2] + each[3]))
        bias[side : side + 1, :] = totals[0]
        stitch[side : side + 1, :] = totals[1]
        stitch[2 + side : 3 + side, :] = totals[2]


def total_sums(rows, cols, got_a, got_b):
    units = got_a.shape[2] - cols
    return call(
        functools.partial(sums_kernel, rows, cols),
        [array((2, units), jnp.float32), array((4, units), jnp.float32)],
        [ANY, ANY],
        [VMEM, VMEM],
        "total_sums",
        [pltpu.VMEM((2, 4, EXTRA, units), jnp.bfloat16), pltpu.SemaphoreType.DMA((2,))],
    )(got_a, got_b)


def swap(x):
    return lax.ppermute(x, "mp", SWAP_CORE)


def along(x):
    return lax.ppermute(x, "mp", NEAR_Z)


def across(x):
    return lax.ppermute(x, "mp", FAR_Z)


def inward(x):
    return lax.ppermute(x, "mp", ENDS_IN)


def between(x):
    return lax.ppermute(x, "mp", MIDS)


def outward(x):
    return lax.ppermute(x, "mp", ENDS_OUT)


def exchange(x):
    return lax.all_to_all(x, "dp", 0, 0)


def fast_shards(
    image_a,
    image_b,
    image_group,
    position_mask,
    weight_a,
    weight_b,
    tower_bias,
    stitch,
    cotan_a,
    cotan_b,
):
    rows, cols = image_a.shape
    units = weight_a.shape[1]
    place = lax.axis_index("mp").astype(jnp.int32)
    z = place // 2
    core = place % 2
    quarter = lax.axis_index("dp").astype(jnp.int32)
    middle = ((z == 1) | (z == 2)).astype(jnp.int32)
    slots = jnp.take(jnp.asarray(SLOTS, jnp.int32), z, axis=0) ^ z
    where = jnp.concatenate(
        [jnp.stack([z, core, middle]), slots, jnp.stack([quarter, place])]
    ).astype(jnp.int32)
    group = image_group[None, :]
    line.token = None
    bf16, f32 = jnp.bfloat16, jnp.float32
    send, wait = line.send, line.wait

    whole_a = swap(weight_a)
    whole_b = swap(weight_b)
    a0 = mask_image(where, position_mask, group, image_a)
    a2 = send(across, a0)
    a1 = send(along, a0)
    b0 = mask_image(where, position_mask, group, image_b)
    mine_a = load(where, weight_a)
    mine_b = load(where, weight_b)
    a1, a2 = wait(a1, a2)
    a3 = send(along, a2)
    b_mid = send(between, b0)
    b1 = send(along, b0)
    whole_a, whole_b = wait(whole_a, whole_b)
    other_a = load(where, whole_a)
    other_b = load(where, whole_b)
    keep_a, give_a = forward_open(a0, a1, a2, mine_a, other_a)
    a3 = wait(a3)
    own_a, sent_a = forward_close(a3, mine_a, other_a, keep_a, give_a)
    got_sum = wait(send(swap, sent_a))
    dz_a, dzt_a, sums_a, hidden_a = tower(
        first_kernel,
        "tower_a",
        array((rows, units), f32),
        own_a,
        got_sum,
        tower_bias,
        stitch,
        cotan_a,
        cotan_b,
    )
    dzo_a = send(swap, dzt_a)
    b1, b_mid = wait(b1, b_mid)
    got_a = send(exchange, pack(where, (a0, a1, a2, a3), dz_a, sums_a))
    b_end = send(outward, b_mid)
    b_mid2 = send(between, b1)
    dzo_a = wait(dzo_a)
    first_a, second_a, third_a, kept_a = parts(
        ((0, 0, 0), (1, 1, 0), (2, 2, 0), (3, 3, 0)),
        [(1, bf16), (1, bf16), (1, bf16), (1, f32)],
        where,
        mine_a,
        other_a,
        dzt_a,
        dzo_a,
    )
    in1_a = send(inward, first_a)
    in2_a = send(inward, second_a)
    b_end, b_mid2 = wait(b_end, b_mid2)
    b_end2 = send(outward, b_mid2)
    b2 = choose(where, b_end, b_mid2)
    keep_b, give_b = forward_open(b0, b1, b2, mine_b, other_b)
    in1_a = wait(in1_a)
    cross1_a = send(between, add(first_a, in1_a))
    b_end2 = wait(b_end2)
    b3 = choose(where, b_end2, b_mid)
    own_b, sent_b = forward_close(b3, mine_b, other_b, keep_b, give_b)
    got_sum = send(swap, sent_b)
    in2_a = wait(in2_a)
    sum2_a = add(second_a, in2_a)
    got_sum = wait(got_sum)
    dz_b, dzt_b, sums_b, local = tower(
        second_kernel,
        "tower_b",
        array((2 * rows, units), bf16),
        own_b,
        got_sum,
        hidden_a,
        tower_bias,
        stitch,
        cotan_a,
        cotan_b,
    )
    dzo_b = send(swap, dzt_b)
    cross1_a = wait(cross1_a)
    sum3_a = add(third_a, cross1_a)
    got_a = wait(got_a)
    far_a = send(swap, got_a)
    got_b = send(exchange, pack(where, (b0, b1, b2, b3), dz_b, sums_b))
    dzo_b, far_a = wait(dzo_b, far_a)
    (first_b,) = parts(((0, 0, 0),), [(1, bf16)], where, mine_b, other_b, dzt_b, dzo_b)
    in1_b = send(inward, first_b)
    s1 = send(along, local)
    s_mid = send(between, local)
    cross2_a = send(between, sum2_a)
    out_a = send(outward, sum3_a)
    second_b, third_b, kept_b = parts(
        ((1, 0, 0), (2, 1, 0), (3, 2, 0)),
        [(1, bf16), (1, bf16), (1, f32)],
        where,
        mine_b,
        other_b,
        dzt_b,
        dzo_b,
    )
    in2_b = send(inward, second_b)
    grad_weight_a = weight_grad(rows, cols, where, got_a, far_a)
    in1_b = wait(in1_b)
    cross1_b = send(between, add(first_b, in1_b))
    s1, s_mid = wait(s1, s_mid)
    s_end = send(outward, s_mid)
    s_mid2 = send(between, s1)
    in2_b = wait(in2_b)
    cross2_b = send(between, add(second_b, in2_b))
    cross1_b = wait(cross1_b)
    out_b = send(outward, add(third_b, cross1_b))
    s_end, s_mid2 = wait(s_end, s_mid2)
    s_end2 = send(outward, s_mid2)
    in3_a = send(inward, third_a)
    s2 = choose(where, s_end, s_mid2)
    in3_b = send(inward, third_b)
    cross2_a, out_a = wait(cross2_a, out_a)
    cross2_b, out_b = wait(cross2_b, out_b)
    s_end2, in3_a = wait(s_end2, in3_a)
    s3 = choose(where, s_end2, s_mid)
    grad_image_a = finish(0, where, position_mask, group, kept_a, in3_a, cross2_a, out_a)
    got_b, in3_b = wait(got_b, in3_b)
    far_b = send(swap, got_b)
    far_high = send(swap, join(s2, s3))
    far_low = send(swap, join(local, s1))
    grad_bias, grad_stitch = total_sums(rows, cols, got_a, got_b)
    grad_image_b = finish(0, where, position_mask, group, kept_b, in3_b, cross2_b, out_b)
    stitched_a, stitched_b = lay_out(where, local, s1, s2, s3, far_low, far_high)
    grad_weight_b = weight_grad(rows, cols, where, got_b, far_b)
    return (
        stitched_a,
        stitched_b,
        grad_image_a,
        grad_image_b,
        grad_weight_a,
        grad_weight_b,
        grad_bias,
        grad_stitch,
    )


def solution(mesh):
    placed = (
        P("dp", "mp"),
        P("dp", "mp"),
        P("dp"),
        P(),
        P(None, "mp"),
        P(None, "mp"),
        P(None, "mp"),
        P(None, "mp"),
        P("dp", "mp"),
        P("dp", "mp"),
    )
    fits = mesh.shape["dp"] == 4 and mesh.shape["mp"] == 8
    return jax.shard_map(
        fast_shards if fits else general_shards,
        mesh=mesh,
        in_specs=placed,
        out_specs=(
            P("dp", None),
            P("dp", None),
            P("mp", "dp"),
            P("mp", "dp"),
            P("dp", "mp"),
            P("dp", "mp"),
            P(None, "mp"),
            P(None, "mp"),
        ),
        check_vma=False,
    )
```

time: 287 us -> 247 us (0.86)
  starting transfers between devices: 87.6 us -> 59.9 us
  other arithmetic: 14.4 us -> 0.69 us
  waiting for transfers between devices: 102 us -> 96.3 us
  local copies, waits for them, and re-layouts: 23.9 us -> 29.1 us
    ppermute x2 -> x1, waiting for transfers between devices: 47.6 us -> 2.52 us  [across(): return lax.ppermute(x, 'mp', FAR_Z)]
    ppermute x4, waiting for transfers between devices: 11.2 us -> 41 us  [along(): return lax.ppermute(x, 'mp', NEAR_Z)]
    ppermute x6, starting transfers between devices: 44.9 us -> 25.3 us  [inward(): return lax.ppermute(x, 'mp', ENDS_IN)]
    ppermute x5 -> x6, waiting for transfers between devices: 23.5 us -> 33.2 us  [outward(): return lax.ppermute(x, 'mp', ENDS_OUT)]
    convert_element_type x8 -> x0, other arithmetic: 9.3 us -> none  [the longest x6 7.38 us: low(): return x.astype(jnp.bfloat16)]
    unnamed x74 -> x88, local copies, waits for them, and re-layouts: 23.8 us -> 29.1 us
    ppermute x10, waiting for transfers between devices: 4.88 us -> 9.47 us  [swap(): return lax.ppermute(x, 'mp', SWAP_CORE)]
    ppermute x6, waiting for transfers between devices: 14.5 us -> 10.1 us  [inward(): return lax.ppermute(x, 'mp', ENDS_IN)]
  transfers between devices with their start and end apart: 36 -> 37, of which waited for: 15 -> 18; matrix products, arithmetic and copies ran while one was open for 5% -> 0% of each run, Pallas kernels for 18% -> 20%
where the time goes in v5:
time: 247 us; the launch traced here: 245 us
  waiting for transfers between devices  96.3 us (39%)
  starting transfers between devices  59.9 us (24%)
  Pallas kernels  57.7 us (23%)
  local copies, waits for them, and re-layouts  29.1 us (12%)
    pallas_call x35, Pallas kernels, go(): *results, line.token = run(*operands, *before)  57.7 us
    ppermute x4, waiting for transfers between devices, along(): return lax.ppermute(x, 'mp', NEAR_Z)  41 us
    ppermute x6, waiting for transfers between devices, outward(): return lax.ppermute(x, 'mp', ENDS_OUT)  33.2 us
    unnamed x88, local copies, waits for them, and re-layouts  29.1 us
    ppermute x6, starting transfers between devices, inward(): return lax.ppermute(x, 'mp', ENDS_IN)  25.3 us
    ppermute x6, waiting for transfers between devices, inward(): return lax.ppermute(x, 'mp', ENDS_IN)  10.1 us
    all_to_all x2, starting transfers between devices, exchange(): return lax.all_to_all(x, 'dp', 0, 0)  9.67 us
    ppermute x10, waiting for transfers between devices, swap(): return lax.ppermute(x, 'mp', SWAP_CORE)  9.47 us
  transfers between devices with their start and end apart: 37, of which 18 were waited for; matrix products, arithmetic and copies ran while one was open for 0% of the time, Pallas kernels for 20%

profile of v5, /device:TPU:0, one launch (start us, length us, event | category | flops | bytes accessed | tf_op | source)
XLA Modules:
  0.0 245.4 jit_solution(2561106965247069302)
XLA Ops:
  2.0 1.1 copy-done.19
  4.4 1.1 mask_image.2
  5.5 3.1 %collective-permute-start = (bf16[256,1152]{1,0:T(8,128)(2,1)S(1)}, bf16[256,1152]{1,0:T(8,128)(2,1)S(1)}, u32[]{:S(2)}, u32[]{:S(2)}) collective-permute-start(bf16[256,1152]{1,0:T(8,128)(2,1)S(1)} %get-tuple-element.202.refs_0_.refs_1_), channel_id=1, source_target_pairs={{0,2},{1,3},{2,0},{3,1},{4,6},{5,7},{6,4},{7,5},{8,10},{9,11},{10,... | collective-permute-start | bytes 1769480 | tf_op jit(solution)/shard_map/ppermute | solution.py:590
  8.6 2.6 %collective-permute-start.1 = (bf16[256,1152]{1,0:T(8,128)(2,1)S(1)}, bf16[256,1152]{1,0:T(8,128)(2,1)S(1)}, u32[]{:S(2)}, u32[]{:S(2)}) collective-permute-start(bf16[256,1152]{1,0:T(8,128)(2,1)S(1)} %get-tuple-element.202.refs_0_.refs_1_), channel_id=1, source_target_pairs={{0,4},{1,5},{2,6},{3,7},{4,0},{5,1},{6,2},{7,3},{8,12},{9,13},{10,... | collective-permute-start | bytes 1769480 | tf_op jit(solution)/shard_map/ppermute | solution.py:594
  11.2 1.1 copy-done.20
  12.9 1.1 mask_image.3
  14.0 2.9 %load_weight.4 = (bf16[4608,512]{1,0:T(8,128)(2,1)S(1)}, f32[8,128]{1,0:T(8,128)S(1)}) custom-call(s32[9]{0:T(128)S(1)} %concatenate.3.refs_0_, bf16[9216,512]{1,0:T(8,128)(2,1)} %refs_1_.8, f32[8,128]{1,0:T(8,128)S(1)} %get-tuple-element.208.refs_2_), custom_call_target="tpu_custom_call" | custom-call | flops 1 | bytes 1 | tf_op jit(solution)/shard_map/load_weight/pallas_call | solution.py:170
  16.9 4.0 %load_weight.5 = (bf16[4608,512]{1,0:T(8,128)(2,1)S(1)}, f32[8,128]{1,0:T(8,128)S(1)}) custom-call(s32[9]{0:T(128)S(1)} %concatenate.3.refs_0_, bf16[9216,512]{1,0:T(8,128)(2,1)} %refs_1_.9, f32[8,128]{1,0:T(8,128)S(1)} %get-tuple-element.209.refs_2_), custom_call_target="tpu_custom_call" | custom-call | flops 1 | bytes 1 | tf_op jit(solution)/shard_map/load_weight/pallas_call | solution.py:170
  21.0 2.1 copy-done
  23.1 11.5 %collective-permute-done.refs_1_.refs_2_ = bf16[256,1152]{1,0:T(8,128)(2,1)S(1)} collective-permute-done((bf16[256,1152]{1,0:T(8,128)(2,1)S(1)}, bf16[256,1152]{1,0:T(8,128)(2,1)S(1)}, u32[]{:S(2)}, u32[]{:S(2)}) %collective-permute-start) | collective-permute-done | bytes 589856 | tf_op jit(solution)/shard_map/ppermute | solution.py:590
  34.7 2.5 %collective-permute-done.1.refs_2_.refs_3_ = bf16[256,1152]{1,0:T(8,128)(2,1)S(1)} collective-permute-done((bf16[256,1152]{1,0:T(8,128)(2,1)S(1)}, bf16[256,1152]{1,0:T(8,128)(2,1)S(1)}, u32[]{:S(2)}, u32[]{:S(2)}) %collective-permute-start.1) | collective-permute-done | bytes 589856 | tf_op jit(solution)/shard_map/ppermute | solution.py:594
  37.7 1.6 collective-permute-start.2
  40.0 2.9 %load_weight.6 = (bf16[4608,512]{1,0:T(8,128)(2,1)S(1)}, f32[8,128]{1,0:T(8,128)S(1)}) custom-call(s32[9]{0:T(128)S(1)} %concatenate.3.refs_0_, bf16[9216,512]{1,0:T(8,128)(2,1)} %collective-permute-done.5.refs_1_, f32[8,128]{1,0:T(8,128)S(1)} %get-tuple-element.222.refs_2_), custom_call_target="tpu_custom_call" | custom-call | flops 1 | bytes 1 | tf_op jit(solution)/shard_map/load_weight/pallas_call | solution.py:170
  42.9 4.0 %load_weight.7 = (bf16[4608,512]{1,0:T(8,128)(2,1)S(1)}, f32[8,128]{1,0:T(8,128)S(1)}) custom-call(s32[9]{0:T(128)S(1)} %concatenate.3.refs_0_, bf16[9216,512]{1,0:T(8,128)(2,1)} %collective-permute-done.6.refs_1_, f32[8,128]{1,0:T(8,128)S(1)} %get-tuple-element.225.refs_2_), custom_call_target="tpu_custom_call" | custom-call | flops 1 | bytes 1 | tf_op jit(solution)/shard_map/load_weight/pallas_call | solution.py:170
  46.9 2.2 copy-done.2
  49.1 2.2 forward_open.2
  51.3 2.2 collective-permute-done.4.refs_0_.refs_4_
  54.5 1.9 collective-permute-done.7.refs_1_
  56.8 6.1 %collective-permute-done.2.refs_1_.refs_2_ = bf16[256,1152]{1,0:T(8,128)(2,1)S(1)} collective-permute-done((bf16[256,1152]{1,0:T(8,128)(2,1)S(1)}, bf16[256,1152]{1,0:T(8,128)(2,1)S(1)}, u32[]{:S(2)}, u32[]{:S(2)}) %collective-permute-start.2) | collective-permute-done | bytes 589856 | tf_op jit(solution)/shard_map/ppermute | solution.py:590
  63.0 1.0 pack.2
  64.0 1.9 copy-done.11
  65.9 4.8 %all-to-all-start = ((bf16[4,272,1664]{2,1,0:T(8,128)(2,1)}), bf16[4,272,1664]{2,1,0:T(8,128)(2,1)}, u32[]{:S(2)}, u32[]{:S(2)}) async-start(bf16[4,272,1664]{2,1,0:T(8,128)(2,1)} %copy-done.11), calls=%async_computation | async-start | bytes 7241728 | tf_op jit(solution)/shard_map/all_to_all | solution.py:610
  71.6 1.4 collective-permute-start.8
  73.1 1.7 collective-permute-done.10.refs_4_
  74.8 2.3 copy-done.7
  77.1 2.3 copy-done.9
  80.4 3.1 %parts.3 = (bf16[1152,256]{1,0:T(8,128)(2,1)S(1)}, bf16[1152,256]{1,0:T(8,128)(2,1)S(1)}, bf16[1152,256]{1,0:T(8,128)(2,1)S(1)}, f32[1152,256]{1,0:T(8,128)S(1)}, f32[8,128]{1,0:T(8,128)S(1)}) custom-call(s32[9]{0:T(128)S(1)} %concatenate.3.refs_0_, bf16[4608,512]{1,0:T(8,128)(2,1)S(1)} %copy-done.7, bf16[4608,512]{1,0:T(8,128)(2,1)S(1)} %copy-done.9, ...), custom_call_target="tpu_custom_call" | custom-call | flops 1 | bytes 1 | tf_op jit(solution)/shard_map/parts/pallas_call | solution.py:170
  83.6 6.1 %collective-permute-start.12 = (bf16[1152,256]{1,0:T(8,128)(2,1)S(1)}, bf16[1152,256]{1,0:T(8,128)(2,1)S(1)}, u32[]{:S(2)}, u32[]{:S(2)}) collective-permute-start(bf16[1152,256]{1,0:T(8,128)(2,1)S(1)} %get-tuple-element.263.refs_0_), channel_id=1, source_target_pairs={{0,2},{1,3},{6,4},{7,5},{8,10},{9,11},{14,12},{15,13},{16,18},{17,... | collective-permute-start | bytes 1769480 | tf_op jit(solution)/shard_map/ppermute | solution.py:598
  89.7 1.3 collective-permute-start.11
  91.0 4.6 %collective-permute-start.14 = (bf16[1152,256]{1,0:T(8,128)(2,1)S(1)}, bf16[1152,256]{1,0:T(8,128)(2,1)S(1)}, u32[]{:S(2)}, u32[]{:S(2)}) collective-permute-start(bf16[1152,256]{1,0:T(8,128)(2,1)S(1)} %get-tuple-element.284.refs_0_), channel_id=1, source_target_pairs={{0,2},{1,3},{6,4},{7,5},{8,10},{9,11},{14,12},{15,13},{16,18},{17,... | collective-permute-start | bytes 1769480 | tf_op jit(solution)/shard_map/ppermute | solution.py:598
  96.4 2.3 copy-done.3
  98.7 2.2 forward_open.3
  100.9 2.4 collective-permute-done.12.refs_1_
  104.2 2.5 %collective-permute-done.11.refs_1_ = bf16[256,1152]{1,0:T(8,128)(2,1)S(1)} collective-permute-done((bf16[256,1152]{1,0:T(8,128)(2,1)S(1)}, bf16[256,1152]{1,0:T(8,128)(2,1)S(1)}, u32[]{:S(2)}, u32[]{:S(2)}) %collective-permute-start.11) | collective-permute-done | bytes 589856 | tf_op jit(solution)/shard_map/ppermute | solution.py:606
  108.4 6.8 %collective-permute-done.14.refs_1_ = bf16[1152,256]{1,0:T(8,128)(2,1)S(1)} collective-permute-done((bf16[1152,256]{1,0:T(8,128)(2,1)S(1)}, bf16[1152,256]{1,0:T(8,128)(2,1)S(1)}, u32[]{:S(2)}, u32[]{:S(2)}) %collective-permute-start.14) | collective-permute-done | bytes 589856 | tf_op jit(solution)/shard_map/ppermute | solution.py:598
  119.4 1.0 pack.3
  120.5 1.8 copy-done.10
  122.3 4.9 %all-to-all-start.1 = ((bf16[4,272,1664]{2,1,0:T(8,128)(2,1)}), bf16[4,272,1664]{2,1,0:T(8,128)(2,1)}, u32[]{:S(2)}, u32[]{:S(2)}) async-start(bf16[4,272,1664]{2,1,0:T(8,128)(2,1)} %copy-done.10), calls=%async_computation.1 | async-start | bytes 7241728 | tf_op jit(solution)/shard_map/all_to_all | solution.py:610
  127.8 1.2 collective-permute-done.15.refs_4_
  128.9 2.3 copy-done.1
  131.3 2.3 copy-done.5
  133.6 1.3 parts.4
  134.9 6.2 %collective-permute-start.20 = (bf16[1152,256]{1,0:T(8,128)(2,1)S(1)}, bf16[1152,256]{1,0:T(8,128)(2,1)S(1)}, u32[]{:S(2)}, u32[]{:S(2)}) collective-permute-start(bf16[1152,256]{1,0:T(8,128)(2,1)S(1)} %get-tuple-element.315), channel_id=1, source_target_pairs={{0,2},{1,3},{6,4},{7,5},{8,10},{9,11},{14,12},{15,13},{16,18},{17,... | collective-permute-start | bytes 1769480 | tf_op jit(solution)/shard_map/ppermute | solution.py:598
  141.1 2.5 %parts.5 = (bf16[1152,256]{1,0:T(8,128)(2,1)S(1)}, bf16[1152,256]{1,0:T(8,128)(2,1)S(1)}, f32[1152,256]{1,0:T(8,128)S(1)}, f32[8,128]{1,0:T(8,128)S(1)}) custom-call(s32[9]{0:T(128)S(1)} %concatenate.3.refs_0_, bf16[4608,512]{1,0:T(8,128)(2,1)S(1)} %copy-done.1, bf16[4608,512]{1,0:T(8,128)(2,1)S(1)} %copy-done.5, ...), custom_call_target="tpu_custom_call" | custom-call | flops 1 | bytes 1 | tf_op jit(solution)/shard_map/parts/pallas_call | solution.py:170
  143.8 1.7 collective-permute-start.24
  146.2 1.6 collective-permute-start.18
  147.8 6.3 %weight_grad.2 = (f32[2304,512]{1,0:T(8,128)}, f32[8,128]{1,0:T(8,128)S(1)}) custom-call(s32[9]{0:T(128)S(1)} %concatenate.3.refs_0_, bf16[4,272,1664]{2,1,0:T(8,128)(2,1)} %all-to-all-done.refs_1_.refs_0_, bf16[4,272,1664]{2,1,0:T(8,128)(2,1)} %collective-permute-done.17.refs_2_, f32[8,128]{1,0:T(8,128)S(1)} %get-tuple-element.325.refs_3_), custom_call_target="tpu_custom_call" | custom-call | flops 1 | bytes 1 | tf_op jit(solution)/shard_map/weight_grad/pallas_call | solution.py:170
  155.6 1.3 collective-permute-start.30
  156.9 21.2 %collective-permute-done.18.refs_1_.refs_2_ = bf16[512,512]{1,0:T(8,128)(2,1)S(1)} collective-permute-done((bf16[512,512]{1,0:T(8,128)(2,1)S(1)}, bf16[512,512]{1,0:T(8,128)(2,1)S(1)}, u32[]{:S(2)}, u32[]{:S(2)}) %collective-permute-start.18) | collective-permute-done | bytes 524320 | tf_op jit(solution)/shard_map/ppermute | solution.py:590
  178.8 1.3 collective-permute-start.21
  181.8 14.4 %collective-permute-done.21.refs_1_ = bf16[512,512]{1,0:T(8,128)(2,1)S(1)} collective-permute-done((bf16[512,512]{1,0:T(8,128)(2,1)S(1)}, bf16[512,512]{1,0:T(8,128)(2,1)S(1)}, u32[]{:S(2)}, u32[]{:S(2)}) %collective-permute-start.21) | collective-permute-done | bytes 524320 | tf_op jit(solution)/shard_map/ppermute | solution.py:606
  196.2 1.3 collective-permute-start.28
  197.5 4.6 %collective-permute-start.26 = (bf16[1152,256]{1,0:T(8,128)(2,1)S(1)}, bf16[1152,256]{1,0:T(8,128)(2,1)S(1)}, u32[]{:S(2)}, u32[]{:S(2)}) collective-permute-start(bf16[1152,256]{1,0:T(8,128)(2,1)S(1)} %copy-done.22), channel_id=1, source_target_pairs={{0,2},{1,3},{6,4},{7,5},{8,10},{9,11},{14,12},{15,13},{16,18},{17,... | collective-permute-start | bytes 1769480 | tf_op jit(solution)/shard_map/ppermute | solution.py:598
  202.8 2.1 collective-permute-start.31
  204.9 1.3 collective-permute-start.25
  206.2 8.2 %collective-permute-done.28.refs_6_ = bf16[1152,256]{1,0:T(8,128)(2,1)S(1)} collective-permute-done((bf16[1152,256]{1,0:T(8,128)(2,1)S(1)}, bf16[1152,256]{1,0:T(8,128)(2,1)S(1)}, u32[]{:S(2)}, u32[]{:S(2)}) %collective-permute-start.28) | collective-permute-done | bytes 589856 | tf_op jit(solution)/shard_map/ppermute | solution.py:606
  215.2 8.0 %collective-permute-done.25.refs_1_ = bf16[512,512]{1,0:T(8,128)(2,1)S(1)} collective-permute-done((bf16[512,512]{1,0:T(8,128)(2,1)S(1)}, bf16[512,512]{1,0:T(8,128)(2,1)S(1)}, u32[]{:S(2)}, u32[]{:S(2)}) %collective-permute-start.25) | collective-permute-done | bytes 524320 | tf_op jit(solution)/shard_map/ppermute | solution.py:606
  223.9 1.7 finish.2
  226.7 1.6 total_sums.1
  228.3 2.3 finish.3
  230.5 2.8 %collective-permute-done.32.refs_5_ = bf16[1024,512]{1,0:T(8,128)(2,1)S(1)} collective-permute-done((bf16[1024,512]{1,0:T(8,128)(2,1)S(1)}, bf16[1024,512]{1,0:T(8,128)(2,1)S(1)}, u32[]{:S(2)}, u32[]{:S(2)}) %collective-permute-start.32) | collective-permute-done | bytes 1048608 | tf_op jit(solution)/shard_map/ppermute | solution.py:586
  233.3 1.9 collective-permute-done.33.refs_6_
  235.2 3.1 %lay_out.1 = (bf16[256,4096]{1,0:T(8,128)(2,1)}, bf16[256,4096]{1,0:T(8,128)(2,1)}, f32[8,128]{1,0:T(8,128)S(1)}) custom-call(s32[9]{0:T(128)S(1)} %concatenate.3.refs_0_, bf16[512,512]{1,0:T(8,128)(2,1)S(1)} %get-tuple-element.313.refs_0_.refs_1_, bf16[512,512]{1,0:T(8,128)(2,1)S(1)} %collective-permute-done.18.refs_1_.refs_2_, ...), custom_call_target="tpu_custom_call" | custom-call | flops 1 | bytes 1 | tf_op jit(solution)/shard_map/lay_out/pallas_call | solution.py:170
  238.3 6.9 %weight_grad.3 = (f32[2304,512]{1,0:T(8,128)}, f32[8,128]{1,0:T(8,128)}) custom-call(s32[9]{0:T(128)S(1)} %concatenate.3.refs_0_, bf16[4,272,1664]{2,1,0:T(8,128)(2,1)} %all-to-all-done.1.refs_1_, bf16[4,272,1664]{2,1,0:T(8,128)(2,1)S(1)} %collective-permute-done.34.refs_2_, f32[8,128]{1,0:T(8,128)S(1)} %get-tuple-element.392.refs_3_), custom_call_target="tpu_custom_call" | custom-call | flops 1 | bytes 1 | tf_op jit(solution)/shard_map/weight_grad/pallas_call | solution.py:170
  (136 shorter events, 23.4 us)
Async XLA Ops:
  0.6 39.3 %collective-permute-start.5 = (bf16[9216,512]{1,0:T(8,128)(2,1)}, bf16[9216,512]{1,0:T(8,128)(2,1)}, u32[]{:S(2)}, u32[]{:S(2)}) collective-permute-start(bf16[9216,512]{1,0:T(8,128)(2,1)} %refs_1_.8), channel_id=1, source_target_pairs={{0,1},{1,0},{2,3},{3,2},{4,5},{5,4},{6,7},{7,6},{8,9},{9,8},{10,11... | collective-permute-start | bytes 28311560 | tf_op jit(solution)/shard_map/ppermute | solution.py:586
  1.1 38.8 %collective-permute-start.6 = (bf16[9216,512]{1,0:T(8,128)(2,1)}, bf16[9216,512]{1,0:T(8,128)(2,1)}, u32[]{:S(2)}, u32[]{:S(2)}) collective-permute-start(bf16[9216,512]{1,0:T(8,128)(2,1)} %refs_1_.9), channel_id=1, source_target_pairs={{0,1},{1,0},{2,3},{3,2},{4,5},{5,4},{6,7},{7,6},{8,9},{9,8},{10,11... | collective-permute-start | bytes 28311560 | tf_op jit(solution)/shard_map/ppermute | solution.py:586
  5.5 29.2 %collective-permute-start = (bf16[256,1152]{1,0:T(8,128)(2,1)S(1)}, bf16[256,1152]{1,0:T(8,128)(2,1)S(1)}, u32[]{:S(2)}, u32[]{:S(2)}) collective-permute-start(bf16[256,1152]{1,0:T(8,128)(2,1)S(1)} %get-tuple-element.202.refs_0_.refs_1_), channel_id=1, source_target_pairs={{0,2},{1,3},{2,0},{3,1},{4,6},{5,7},{6,4},{7,5},{8,10},{9,11},{10,... | collective-permute-start | bytes 1769480 | tf_op jit(solution)/shard_map/ppermute | solution.py:590
  8.6 28.6 %collective-permute-start.1 = (bf16[256,1152]{1,0:T(8,128)(2,1)S(1)}, bf16[256,1152]{1,0:T(8,128)(2,1)S(1)}, u32[]{:S(2)}, u32[]{:S(2)}) collective-permute-start(bf16[256,1152]{1,0:T(8,128)(2,1)S(1)} %get-tuple-element.202.refs_0_.refs_1_), channel_id=1, source_target_pairs={{0,4},{1,5},{2,6},{3,7},{4,0},{5,1},{6,2},{7,3},{8,12},{9,13},{10,... | collective-permute-start | bytes 1769480 | tf_op jit(solution)/shard_map/ppermute | solution.py:594
  16.9 36.5 %copy-start.6 = (bf16[4608,512]{1,0:T(8,128)(2,1)}, bf16[4608,512]{1,0:T(8,128)(2,1)S(1)}, u32[]{:S(2)}) copy-start(bf16[4608,512]{1,0:T(8,128)(2,1)S(1)} %get-tuple-element.219.refs_3_.refs_1_) | copy-start | bytes 14155780
  37.2 16.3 %collective-permute-start.4 = (bf16[256,1152]{1,0:T(8,128)(2,1)S(1)}, bf16[256,1152]{1,0:T(8,128)(2,1)S(1)}, u32[]{:S(2)}, u32[]{:S(2)}) collective-permute-start(bf16[256,1152]{1,0:T(8,128)(2,1)S(1)} %collective-permute-done.1.refs_2_.refs_3_), channel_id=1, source_target_pairs={{0,2},{1,3},{2,0},{3,1},{4,6},{5,7},{6,4},{7,5},{8,10},{9,11},{10,... | collective-permute-start | bytes 1769480 | tf_op jit(solution)/shard_map/ppermute | solution.py:590
  37.7 25.3 %collective-permute-start.2 = (bf16[256,1152]{1,0:T(8,128)(2,1)S(1)}, bf16[256,1152]{1,0:T(8,128)(2,1)S(1)}, u32[]{:S(2)}, u32[]{:S(2)}) collective-permute-start(bf16[256,1152]{1,0:T(8,128)(2,1)S(1)} %get-tuple-element.216.refs_0_.refs_1_), channel_id=1, source_target_pairs={{0,2},{1,3},{2,0},{3,1},{4,6},{5,7},{6,4},{7,5},{8,10},{9,11},{10,... | collective-permute-start | bytes 1769480 | tf_op jit(solution)/shard_map/ppermute | solution.py:590
  39.2 23.7 %collective-permute-start.3 = (bf16[256,1152]{1,0:T(8,128)(2,1)S(1)}, bf16[256,1152]{1,0:T(8,128)(2,1)S(1)}, u32[]{:S(2)}, u32[]{:S(2)}) collective-permute-start(bf16[256,1152]{1,0:T(8,128)(2,1)S(1)} %get-tuple-element.216.refs_0_.refs_1_), channel_id=1, source_target_pairs={{2,4},{3,5},{4,2},{5,3},{10,12},{11,13},{12,10},{13,11},{18,20},{1... | collective-permute-start | bytes 1769480 | tf_op jit(solution)/shard_map/ppermute | solution.py:602
  42.9 10.6 %copy-start.8 = (bf16[4608,512]{1,0:T(8,128)(2,1)}, bf16[4608,512]{1,0:T(8,128)(2,1)S(1)}, u32[]{:S(2)}) copy-start(bf16[4608,512]{1,0:T(8,128)(2,1)S(1)} %get-tuple-element.223.refs_4_.refs_2_) | copy-start | bytes 14155780
  53.5 2.9 %copy-start.16 = (bf16[256,512]{1,0:T(8,128)(2,1)S(1)}, bf16[256,512]{1,0:T(8,128)(2,1)}, u32[]{:S(2)}) copy-start(bf16[256,512]{1,0:T(8,128)(2,1)} %refs_5_.3) | copy-start | bytes 786436
  53.5 2.9 %copy-start.17 = (bf16[256,512]{1,0:T(8,128)(2,1)S(1)}, bf16[256,512]{1,0:T(8,128)(2,1)}, u32[]{:S(2)}) copy-start(bf16[256,512]{1,0:T(8,128)(2,1)} %refs_6_.1) | copy-start | bytes 786436
  53.5 2.9 %copy-start.31 = (f32[4,512]{1,0:T(4,128)S(1)}, f32[4,512]{1,0:T(4,128)}, u32[]{:S(2)}) copy-start(f32[4,512]{1,0:T(4,128)} %refs_4_.3) | copy-start | bytes 24580
  53.5 2.9 %copy-start.32 = (f32[2,512]{1,0:T(2,128)S(1)}, f32[2,512]{1,0:T(2,128)}, u32[]{:S(2)}) copy-start(f32[2,512]{1,0:T(2,128)} %refs_3_.7) | copy-start | bytes 12292
  54.4 2.0 collective-permute-start.7
  56.8 6.2 %copy-start.27 = (bf16[512,256]{1,0:T(8,128)(2,1)}, bf16[512,256]{1,0:T(8,128)(2,1)S(1)}, u32[]{:S(2)}) copy-start(bf16[512,256]{1,0:T(8,128)(2,1)S(1)} %get-tuple-element.251.refs_3_) | copy-start | bytes 786436
  56.8 9.1 %copy-start.25 = (f32[256,512]{1,0:T(8,128)}, f32[256,512]{1,0:T(8,128)S(1)}, u32[]{:S(2)}) copy-start(f32[256,512]{1,0:T(8,128)S(1)} %get-tuple-element.290.refs_2_) | copy-start | bytes 1572868
  65.9 52.5 %all-to-all-start = ((bf16[4,272,1664]{2,1,0:T(8,128)(2,1)}), bf16[4,272,1664]{2,1,0:T(8,128)(2,1)}, u32[]{:S(2)}, u32[]{:S(2)}) async-start(bf16[4,272,1664]{2,1,0:T(8,128)(2,1)} %copy-done.11), calls=%async_computation | async-start | bytes 7241728 | tf_op jit(solution)/shard_map/all_to_all | solution.py:610
  70.7 25.7 %slice-start = ((s8[4718592]{0:T(1024)(128)(4,1)}), s8[4194304]{0:T(1024)(128)(4,1)S(1)}, s32[]{:S(2)}) async-start(s8[4718592]{0:T(1024)(128)(4,1)} %bitcast.8), calls=%async_computation.2 | async-start | bytes 8388608
  70.7 25.7 %slice-start.1 = ((s8[4718592]{0:T(1024)(128)(4,1)}), s8[524288]{0:T(1024)(128)(4,1)S(1)}, s32[]{:S(2)}) async-start(s8[4718592]{0:T(1024)(128)(4,1)} %bitcast.8), calls=%async_computation.3 | async-start | bytes 1048576
  70.7 19.0 %collective-permute-start.9 = (bf16[256,1152]{1,0:T(8,128)(2,1)S(1)}, bf16[256,1152]{1,0:T(8,128)(2,1)S(1)}, u32[]{:S(2)}, u32[]{:S(2)}) collective-permute-start(bf16[256,1152]{1,0:T(8,128)(2,1)S(1)} %collective-permute-done.2.refs_1_.refs_2_), channel_id=1, source_target_pairs={{2,4},{3,5},{4,2},{5,3},{10,12},{11,13},{12,10},{13,11},{18,20},{1... | collective-permute-start | bytes 1769480 | tf_op jit(solution)/shard_map/ppermute | solution.py:602
  71.6 18.2 %collective-permute-start.8 = (bf16[256,1152]{1,0:T(8,128)(2,1)S(1)}, bf16[256,1152]{1,0:T(8,128)(2,1)S(1)}, u32[]{:S(2)}, u32[]{:S(2)}) collective-permute-start(bf16[256,1152]{1,0:T(8,128)(2,1)S(1)} %collective-permute-done.3.refs_2_), channel_id=1, source_target_pairs={{2,0},{3,1},{4,6},{5,7},{10,8},{11,9},{12,14},{13,15},{18,16},{19,... | collective-permute-start | bytes 1769480 | tf_op jit(solution)/shard_map/ppermute | solution.py:606
  73.0 1.8 collective-permute-start.10
  74.8 2.3 copy-start.7
  83.6 17.3 %copy-start.12 = (f32[1152,256]{1,0:T(8,128)}, f32[1152,256]{1,0:T(8,128)S(1)}, u32[]{:S(2)}) copy-start(f32[1152,256]{1,0:T(8,128)S(1)} %get-tuple-element.367.refs_3_) | copy-start | bytes 3538948
  83.6 33.9 %copy-start.21 = (bf16[1152,256]{1,0:T(8,128)(2,1)}, bf16[1152,256]{1,0:T(8,128)(2,1)S(1)}, u32[]{:S(2)}) copy-start(bf16[1152,256]{1,0:T(8,128)(2,1)S(1)} %get-tuple-element.353.refs_0_) | copy-start | bytes 1769476
  83.6 19.8 %collective-permute-start.12 = (bf16[1152,256]{1,0:T(8,128)(2,1)S(1)}, bf16[1152,256]{1,0:T(8,128)(2,1)S(1)}, u32[]{:S(2)}, u32[]{:S(2)}) collective-permute-start(bf16[1152,256]{1,0:T(8,128)(2,1)S(1)} %get-tuple-element.263.refs_0_), channel_id=1, source_target_pairs={{0,2},{1,3},{6,4},{7,5},{8,10},{9,11},{14,12},{15,13},{16,18},{17,... | collective-permute-start | bytes 1769480 | tf_op jit(solution)/shard_map/ppermute | solution.py:598
  89.7 17.0 %collective-permute-start.11 = (bf16[256,1152]{1,0:T(8,128)(2,1)S(1)}, bf16[256,1152]{1,0:T(8,128)(2,1)S(1)}, u32[]{:S(2)}, u32[]{:S(2)}) collective-permute-start(bf16[256,1152]{1,0:T(8,128)(2,1)S(1)} %collective-permute-done.9.refs_2_), channel_id=1, source_target_pairs={{2,0},{3,1},{4,6},{5,7},{10,8},{11,9},{12,14},{13,15},{18,16},{19,... | collective-permute-start | bytes 1769480 | tf_op jit(solution)/shard_map/ppermute | solution.py:606
  91.0 24.2 %collective-permute-start.14 = (bf16[1152,256]{1,0:T(8,128)(2,1)S(1)}, bf16[1152,256]{1,0:T(8,128)(2,1)S(1)}, u32[]{:S(2)}, u32[]{:S(2)}) collective-permute-start(bf16[1152,256]{1,0:T(8,128)(2,1)S(1)} %get-tuple-element.284.refs_0_), channel_id=1, source_target_pairs={{0,2},{1,3},{6,4},{7,5},{8,10},{9,11},{14,12},{15,13},{16,18},{17,... | collective-permute-start | bytes 1769480 | tf_op jit(solution)/shard_map/ppermute | solution.py:598
  96.4 2.3 copy-start.3
  98.7 8.7 %copy-start.4 = (bf16[4608,512]{1,0:T(8,128)(2,1)S(1)}, bf16[4608,512]{1,0:T(8,128)(2,1)}, u32[]{:S(2)}) copy-start(bf16[4608,512]{1,0:T(8,128)(2,1)} %copy-done.2) | copy-start | bytes 14155780
  103.5 14.0 %collective-permute-start.16 = (bf16[1152,256]{1,0:T(8,128)(2,1)S(1)}, bf16[1152,256]{1,0:T(8,128)(2,1)S(1)}, u32[]{:S(2)}, u32[]{:S(2)}) collective-permute-start(bf16[1152,256]{1,0:T(8,128)(2,1)S(1)} %get-tuple-element.298), channel_id=1, source_target_pairs={{2,4},{3,5},{4,2},{5,3},{10,12},{11,13},{12,10},{13,11},{18,20},{1... | collective-permute-start | bytes 1769480 | tf_op jit(solution)/shard_map/ppermute | solution.py:602
  107.4 8.7 %copy-start.18 = (bf16[256,512]{1,0:T(8,128)(2,1)S(1)}, bf16[256,512]{1,0:T(8,128)(2,1)}, u32[]{:S(2)}) copy-start(bf16[256,512]{1,0:T(8,128)(2,1)} %refs_6_.1) | copy-start | bytes 786436
  107.4 8.7 %copy-start.26 = (f32[256,512]{1,0:T(8,128)S(1)}, f32[256,512]{1,0:T(8,128)}, u32[]{:S(2)}) copy-start(f32[256,512]{1,0:T(8,128)} %copy-done.25) | copy-start | bytes 1572868
  108.3 7.9 %collective-permute-start.13 = (f32[256,512]{1,0:T(8,128)S(1)}, f32[256,512]{1,0:T(8,128)S(1)}, u32[]{:S(2)}, u32[]{:S(2)}) collective-permute-start(f32[256,512]{1,0:T(8,128)S(1)} %get-tuple-element.283), channel_id=1, source_target_pairs={{0,1},{1,0},{2,3},{3,2},{4,5},{5,4},{6,7},{7,6},{8,9},{9,8},{10,11... | collective-permute-start | bytes 1572872 | tf_op jit(solution)/shard_map/ppermute | solution.py:586
  118.5 10.5 %collective-permute-start.17 = (bf16[4,272,1664]{2,1,0:T(8,128)(2,1)}, bf16[4,272,1664]{2,1,0:T(8,128)(2,1)}, u32[]{:S(2)}, u32[]{:S(2)}) collective-permute-start(bf16[4,272,1664]{2,1,0:T(8,128)(2,1)} %all-to-all-done.refs_1_.refs_0_), channel_id=1, source_target_pairs={{0,1},{1,0},{2,3},{3,2},{4,5},{5,4},{6,7},{7,6},{8,9},{9,8},{10,11... | collective-permute-start | bytes 10862600 | tf_op jit(solution)/shard_map/ppermute | solution.py:586
  122.3 103.3 %all-to-all-start.1 = ((bf16[4,272,1664]{2,1,0:T(8,128)(2,1)}), bf16[4,272,1664]{2,1,0:T(8,128)(2,1)}, u32[]{:S(2)}, u32[]{:S(2)}) async-start(bf16[4,272,1664]{2,1,0:T(8,128)(2,1)} %copy-done.10), calls=%async_computation.1 | async-start | bytes 7241728 | tf_op jit(solution)/shard_map/all_to_all | solution.py:610
  127.2 1.7 collective-permute-start.15
  128.9 2.3 copy-start.1
  134.9 19.8 %collective-permute-start.20 = (bf16[1152,256]{1,0:T(8,128)(2,1)S(1)}, bf16[1152,256]{1,0:T(8,128)(2,1)S(1)}, u32[]{:S(2)}, u32[]{:S(2)}) collective-permute-start(bf16[1152,256]{1,0:T(8,128)(2,1)S(1)} %get-tuple-element.315), channel_id=1, source_target_pairs={{0,2},{1,3},{6,4},{7,5},{8,10},{9,11},{14,12},{15,13},{16,18},{17,... | collective-permute-start | bytes 1769480 | tf_op jit(solution)/shard_map/ppermute | solution.py:598
  143.7 37.2 %copy-start.14 = (f32[1152,256]{1,0:T(8,128)}, f32[1152,256]{1,0:T(8,128)S(1)}, u32[]{:S(2)}) copy-start(f32[1152,256]{1,0:T(8,128)S(1)} %get-tuple-element.379.refs_3_) | copy-start | bytes 3538948
  143.7 11.9 %copy-start.41 = (bf16[1152,256]{1,0:T(8,128)(2,1)S(1)}, bf16[1152,256]{1,0:T(8,128)(2,1)}, u32[]{:S(2)}) copy-start(bf16[1152,256]{1,0:T(8,128)(2,1)} %copy-done.40) | copy-start | bytes 1769476
  143.7 36.4 %copy-start.39 = (bf16[1152,256]{1,0:T(8,128)(2,1)S(1)}, bf16[1152,256]{1,0:T(8,128)(2,1)}, u32[]{:S(2)}) copy-start(bf16[1152,256]{1,0:T(8,128)(2,1)} %copy-done.38) | copy-start | bytes 1769476
  143.7 53.8 %copy-start.22 = (bf16[1152,256]{1,0:T(8,128)(2,1)S(1)}, bf16[1152,256]{1,0:T(8,128)(2,1)}, u32[]{:S(2)}) copy-start(bf16[1152,256]{1,0:T(8,128)(2,1)} %copy-done.21) | copy-start | bytes 1769476
  143.7 80.1 %copy-start.13 = (f32[1152,256]{1,0:T(8,128)S(1)}, f32[1152,256]{1,0:T(8,128)}, u32[]{:S(2)}) copy-start(f32[1152,256]{1,0:T(8,128)} %copy-done.12) | copy-start | bytes 3538948
  143.8 80.1 %copy-start.35 = (s32[2,36]{1,0:T(2,128)S(1)}, s32[2,36]{1,0:T(2,128)}, u32[]{:S(2)}) copy-start(s32[2,36]{1,0:T(2,128)} %refs_1_.11) | copy-start | bytes 868
  143.8 80.1 %copy-start.37 = (s32[256]{0:T(256)S(1)}, s32[256]{0:T(256)}, u32[]{:S(2)}) copy-start(s32[256]{0:T(256)} %param.13) | copy-start | bytes 3076
  143.8 36.3 %collective-permute-start.24 = (bf16[1152,256]{1,0:T(8,128)(2,1)S(1)}, bf16[1152,256]{1,0:T(8,128)(2,1)S(1)}, u32[]{:S(2)}, u32[]{:S(2)}) collective-permute-start(bf16[1152,256]{1,0:T(8,128)(2,1)S(1)} %get-tuple-element.338.refs_0_), channel_id=1, source_target_pairs={{0,2},{1,3},{6,4},{7,5},{8,10},{9,11},{14,12},{15,13},{16,18},{17,... | collective-permute-start | bytes 1769480 | tf_op jit(solution)/shard_map/ppermute | solution.py:598
  145.5 11.4 %collective-permute-start.19 = (bf16[512,512]{1,0:T(8,128)(2,1)S(1)}, bf16[512,512]{1,0:T(8,128)(2,1)S(1)}, u32[]{:S(2)}, u32[]{:S(2)}) collective-permute-start(bf16[512,512]{1,0:T(8,128)(2,1)S(1)} %get-tuple-element.313.refs_0_.refs_1_), channel_id=1, source_target_pairs={{2,4},{3,5},{4,2},{5,3},{10,12},{11,13},{12,10},{13,11},{18,20},{1... | collective-permute-start | bytes 1572872 | tf_op jit(solution)/shard_map/ppermute | solution.py:602
  146.2 31.9 %collective-permute-start.18 = (bf16[512,512]{1,0:T(8,128)(2,1)S(1)}, bf16[512,512]{1,0:T(8,128)(2,1)S(1)}, u32[]{:S(2)}, u32[]{:S(2)}) collective-permute-start(bf16[512,512]{1,0:T(8,128)(2,1)S(1)} %get-tuple-element.313.refs_0_.refs_1_), channel_id=1, source_target_pairs={{0,2},{1,3},{2,0},{3,1},{4,6},{5,7},{6,4},{7,5},{8,10},{9,11},{10,... | collective-permute-start | bytes 1572872 | tf_op jit(solution)/shard_map/ppermute | solution.py:590
  154.9 26.1 %collective-permute-start.23 = (bf16[1152,256]{1,0:T(8,128)(2,1)S(1)}, bf16[1152,256]{1,0:T(8,128)(2,1)S(1)}, u32[]{:S(2)}, u32[]{:S(2)}) collective-permute-start(bf16[1152,256]{1,0:T(8,128)(2,1)S(1)} %get-tuple-element.337), channel_id=1, source_target_pairs={{2,4},{3,5},{4,2},{5,3},{10,12},{11,13},{12,10},{13,11},{18,20},{1... | collective-permute-start | bytes 1769480 | tf_op jit(solution)/shard_map/ppermute | solution.py:602
  155.6 47.2 %collective-permute-start.30 = (bf16[1152,256]{1,0:T(8,128)(2,1)S(1)}, bf16[1152,256]{1,0:T(8,128)(2,1)S(1)}, u32[]{:S(2)}, u32[]{:S(2)}) collective-permute-start(bf16[1152,256]{1,0:T(8,128)(2,1)S(1)} %copy-done.41), channel_id=1, source_target_pairs={{2,0},{3,1},{4,6},{5,7},{10,8},{11,9},{12,14},{13,15},{18,16},{19,... | collective-permute-start | bytes 1769480 | tf_op jit(solution)/shard_map/ppermute | solution.py:606
  178.1 3.7 %collective-permute-start.22 = (bf16[512,512]{1,0:T(8,128)(2,1)S(1)}, bf16[512,512]{1,0:T(8,128)(2,1)S(1)}, u32[]{:S(2)}, u32[]{:S(2)}) collective-permute-start(bf16[512,512]{1,0:T(8,128)(2,1)S(1)} %collective-permute-done.18.refs_1_.refs_2_), channel_id=1, source_target_pairs={{2,4},{3,5},{4,2},{5,3},{10,12},{11,13},{12,10},{13,11},{18,20},{1... | collective-permute-start | bytes 1572872 | tf_op jit(solution)/shard_map/ppermute | solution.py:602
  178.8 17.5 %collective-permute-start.21 = (bf16[512,512]{1,0:T(8,128)(2,1)S(1)}, bf16[512,512]{1,0:T(8,128)(2,1)S(1)}, u32[]{:S(2)}, u32[]{:S(2)}) collective-permute-start(bf16[512,512]{1,0:T(8,128)(2,1)S(1)} %collective-permute-done.19.refs_2_), channel_id=1, source_target_pairs={{2,0},{3,1},{4,6},{5,7},{10,8},{11,9},{12,14},{13,15},{18,16},{19,... | collective-permute-start | bytes 1572872 | tf_op jit(solution)/shard_map/ppermute | solution.py:606
  180.1 24.8 %collective-permute-start.29 = (bf16[1152,256]{1,0:T(8,128)(2,1)S(1)}, bf16[1152,256]{1,0:T(8,128)(2,1)S(1)}, u32[]{:S(2)}, u32[]{:S(2)}) collective-permute-start(bf16[1152,256]{1,0:T(8,128)(2,1)S(1)} %copy-done.39), channel_id=1, source_target_pairs={{2,4},{3,5},{4,2},{5,3},{10,12},{11,13},{12,10},{13,11},{18,20},{1... | collective-permute-start | bytes 1769480 | tf_op jit(solution)/shard_map/ppermute | solution.py:602
  181.0 25.2 %collective-permute-start.27 = (bf16[1152,256]{1,0:T(8,128)(2,1)S(1)}, bf16[1152,256]{1,0:T(8,128)(2,1)S(1)}, u32[]{:S(2)}, u32[]{:S(2)}) collective-permute-start(bf16[1152,256]{1,0:T(8,128)(2,1)S(1)} %get-tuple-element.354), channel_id=1, source_target_pairs={{2,4},{3,5},{4,2},{5,3},{10,12},{11,13},{12,10},{13,11},{18,20},{1... | collective-permute-start | bytes 1769480 | tf_op jit(solution)/shard_map/ppermute | solution.py:602
  196.2 18.1 %collective-permute-start.28 = (bf16[1152,256]{1,0:T(8,128)(2,1)S(1)}, bf16[1152,256]{1,0:T(8,128)(2,1)S(1)}, u32[]{:S(2)}, u32[]{:S(2)}) collective-permute-start(bf16[1152,256]{1,0:T(8,128)(2,1)S(1)} %get-tuple-element.355), channel_id=1, source_target_pairs={{2,0},{3,1},{4,6},{5,7},{10,8},{11,9},{12,14},{13,15},{18,16},{19,... | collective-permute-start | bytes 1769480 | tf_op jit(solution)/shard_map/ppermute | solution.py:606
  197.5 25.7 %collective-permute-start.26 = (bf16[1152,256]{1,0:T(8,128)(2,1)S(1)}, bf16[1152,256]{1,0:T(8,128)(2,1)S(1)}, u32[]{:S(2)}, u32[]{:S(2)}) collective-permute-start(bf16[1152,256]{1,0:T(8,128)(2,1)S(1)} %copy-done.22), channel_id=1, source_target_pairs={{0,2},{1,3},{6,4},{7,5},{8,10},{9,11},{14,12},{15,13},{16,18},{17,... | collective-permute-start | bytes 1769480 | tf_op jit(solution)/shard_map/ppermute | solution.py:598
  202.8 23.1 %collective-permute-start.31 = (bf16[1152,256]{1,0:T(8,128)(2,1)S(1)}, bf16[1152,256]{1,0:T(8,128)(2,1)}, u32[]{:S(2)}, u32[]{:S(2)}) collective-permute-start(bf16[1152,256]{1,0:T(8,128)(2,1)S(1)} %get-tuple-element.366.refs_0_), channel_id=1, source_target_pairs={{0,2},{1,3},{6,4},{7,5},{8,10},{9,11},{14,12},{15,13},{16,18},{17,... | collective-permute-start | bytes 1769480 | tf_op jit(solution)/shard_map/ppermute | solution.py:598
  204.9 18.3 %collective-permute-start.25 = (bf16[512,512]{1,0:T(8,128)(2,1)S(1)}, bf16[512,512]{1,0:T(8,128)(2,1)S(1)}, u32[]{:S(2)}, u32[]{:S(2)}) collective-permute-start(bf16[512,512]{1,0:T(8,128)(2,1)S(1)} %collective-permute-done.22.refs_2_), channel_id=1, source_target_pairs={{2,0},{3,1},{4,6},{5,7},{10,8},{11,9},{12,14},{13,15},{18,16},{19,... | collective-permute-start | bytes 1572872 | tf_op jit(solution)/shard_map/ppermute | solution.py:606
  225.6 2.7 %copy-start.15 = (f32[1152,256]{1,0:T(8,128)S(1)}, f32[1152,256]{1,0:T(8,128)}, u32[]{:S(2)}) copy-start(f32[1152,256]{1,0:T(8,128)} %copy-done.14) | copy-start | bytes 3538948
  225.6 2.7 %copy-start.24 = (bf16[1152,256]{1,0:T(8,128)(2,1)S(1)}, bf16[1152,256]{1,0:T(8,128)(2,1)}, u32[]{:S(2)}) copy-start(bf16[1152,256]{1,0:T(8,128)(2,1)} %copy-done.23) | copy-start | bytes 1769476
  225.9 12.4 %collective-permute-start.34 = (bf16[4,272,1664]{2,1,0:T(8,128)(2,1)}, bf16[4,272,1664]{2,1,0:T(8,128)(2,1)S(1)}, u32[]{:S(2)}, u32[]{:S(2)}) collective-permute-start(bf16[4,272,1664]{2,1,0:T(8,128)(2,1)} %all-to-all-done.1.refs_1_), channel_id=1, source_target_pairs={{0,1},{1,0},{2,3},{3,2},{4,5},{5,4},{6,7},{7,6},{8,9},{9,8},{10,11... | collective-permute-start | bytes 10862600 | tf_op jit(solution)/shard_map/ppermute | solution.py:586
  226.0 7.3 %collective-permute-start.32 = (bf16[1024,512]{1,0:T(8,128)(2,1)S(1)}, bf16[1024,512]{1,0:T(8,128)(2,1)S(1)}, u32[]{:S(2)}, u32[]{:S(2)}) collective-permute-start(bf16[1024,512]{1,0:T(8,128)(2,1)S(1)} %get-tuple-element.377), channel_id=1, source_target_pairs={{0,1},{1,0},{2,3},{3,2},{4,5},{5,4},{6,7},{7,6},{8,9},{9,8},{10,11... | collective-permute-start | bytes 3145736 | tf_op jit(solution)/shard_map/ppermute | solution.py:586
  226.6 8.6 %collective-permute-start.33 = (bf16[1024,512]{1,0:T(8,128)(2,1)S(1)}, bf16[1024,512]{1,0:T(8,128)(2,1)S(1)}, u32[]{:S(2)}, u32[]{:S(2)}) collective-permute-start(bf16[1024,512]{1,0:T(8,128)(2,1)S(1)} %get-tuple-element.378), channel_id=1, source_target_pairs={{0,1},{1,0},{2,3},{3,2},{4,5},{5,4},{6,7},{7,6},{8,9},{9,8},{10,11... | collective-permute-start | bytes 3145736 | tf_op jit(solution)/shard_map/ppermute | solution.py:586
  (17 other events, 22.0 us)

commit v6 on v5

--- a/solution.py
+++ b/solution.py
@@ -102,7 +102,7 @@
 SLOTS = ((3, 2, 1, 0), (3, 2, 0, 1), (0, 1, 3, 2), (0, 1, 2, 3))
 LANES = 128
 EXTRA = 16
-VMEM_LIMIT = 14 * 1024 * 1024
+VMEM_LIMIT = 22 * 1024 * 1024
 SMEM = pl.BlockSpec(memory_space=pltpu.SMEM)
 VMEM = pl.BlockSpec(memory_space=pltpu.VMEM)
 HBM = pl.BlockSpec(memory_space=pltpu.HBM)
@@ -143,7 +143,7 @@
 line = Line()
 
 
-def call(kernel, out_shape, in_specs, out_specs, name, scratch=()):
+def call(kernel, out_shape, in_specs, out_specs, name, scratch=(), aliases={}):
     single = not isinstance(out_shape, list)
     outs = [out_shape] if single else out_shape
     places = [out_specs] if single else out_specs
@@ -161,6 +161,7 @@
         in_specs=[*in_specs, *[HBM] * len(before)],
         out_specs=[*places, VMEM],
         scratch_shapes=scratch,
+        input_output_aliases=aliases,
         compiler_params=pltpu.CompilerParams(vmem_limit_bytes=VMEM_LIMIT),
         cost_estimate=LITTLE,
         name=name,
@@ -194,67 +195,102 @@
     )(where, marks, group, image)
 
 
-def load_kernel(where, weight, out, sems):
-    cols = out.shape[0] // 4
-    copies = []
-    for k in range(4):
-        block = 2 * (where[0] ^ k) + where[1]
-        copies.append(
-            pltpu.make_async_copy(
-                weight.at[pl.ds(pl.multiple_of(block * cols, cols), cols), :],
-                out.at[pl.ds(k * cols, cols), :],
-                sems.at[k],
-            )
-        )
-    for copy in copies:
-        copy.start()
-    for copy in copies:
-        copy.wait()
-
-
-def load(where, weight):
-    rows, units = weight.shape
-    weight = pltpu.with_memory_space_constraint(weight, pltpu.HBM)
-    return call(
-        load_kernel,
-        pltpu.VMEM((rows // 2, units), weight.dtype),
-        [SMEM, HBM],
-        VMEM,
-        "load_weight",
-        [pltpu.SemaphoreType.DMA((4,))],
-    )(where, weight)
+def in_hbm(x):
+    return pltpu.with_memory_space_constraint(x, pltpu.HBM)
 
 
 def dot(x, y):
     return jnp.dot(x, y, preferred_element_type=jnp.float32)
 
 
-def open_kernel(p0, p1, p2, mine, other, keep, send):
+def products(where, ks, mine, other, held, sems, emit):
+    cols = held.shape[2]
+
+    def copies(i):
+        block = 2 * (where[0] ^ ks[i]) + where[1]
+        rows = pl.ds(pl.multiple_of(block * cols, cols), cols)
+        return [
+            pltpu.make_async_copy(weight.at[rows, :], held.at[i, side], sems.at[i, side])
+            for side, weight in enumerate((mine, other))
+        ]
+
+    for i in range(len(ks)):
+        for copy in copies(i):
+            copy.start()
+    for i in range(len(ks)):
+        for copy in copies(i):
+            copy.wait()
+        emit(i, held[i, 0], held[i, 1])
+
+
+def open_kernel(where, p0, p1, p2, mine, other, keep, send, last, slot, held, sems):
+    pieces = (p0, p1, p2)
     cols = p0.shape[1]
-    for weight, out in ((mine, keep), (other, send)):
-        total = None
-        for k, piece in enumerate((p0, p1, p2)):
-            term = dot(piece[...], weight[k * cols : (k + 1) * cols, :])
-            total = term if total is None else total + term
-        out[...] = total
-
-
-def forward_open(p0, p1, p2, mine, other):
-    out = array((p0.shape[0], mine.shape[1]), jnp.float32)
-    return call(open_kernel, [out] * 2, [VMEM] * 5, [VMEM] * 2, "forward_open")(
-        p0, p1, p2, mine, other
-    )
-
-
-def close_kernel(p3, mine, other, keep, send, out, sent):
-    cols = p3.shape[1]
-    sent[...] = send[...] + dot(p3[...], other[3 * cols :, :])
-    out[...] = keep[...] + dot(p3[...], mine[3 * cols :, :])
-
-
-def forward_close(*operands):
-    out = array(operands[-1].shape, jnp.float32)
-    return call(close_kernel, [out] * 2, [VMEM] * 5, [VMEM] * 2, "forward_close")(*operands)
+    ahead = []
+    for at, (k, out) in enumerate(((3, last), (where[3], slot))):
+        block = 2 * (where[0] ^ k) + where[1]
+        rows = pl.ds(pl.multiple_of(block * cols, cols), cols)
+        for side, weight in enumerate((mine, other)):
+            ahead.append(
+                pltpu.make_async_copy(weight.at[rows, :], out.at[side], sems.at[3 + at, side])
+            )
+
+    def emit(i, own_block, other_block):
+        if i == 0:
+            for copy in ahead:
+                copy.start()
+            keep[...] = dot(p0[...], own_block)
+            send[...] = dot(p0[...], other_block)
+        else:
+            keep[...] += dot(pieces[i][...], own_block)
+            send[...] += dot(pieces[i][...], other_block)
+
+    products(where, (0, 1, 2), mine, other, held, sems, emit)
+    for copy in ahead:
+        copy.wait()
+
+
+def forward_open(where, p0, p1, p2, mine, other):
+    rows, cols = p0.shape
+    units = mine.shape[1]
+    blocks = pltpu.VMEM((2, cols, units), jnp.bfloat16)
+    return call(
+        open_kernel,
+        [array((rows, units), jnp.float32)] * 2 + [blocks] * 2,
+        [SMEM] + [VMEM] * 3 + [HBM] * 2,
+        [VMEM] * 4,
+        "forward_open",
+        [pltpu.VMEM((3, 2, cols, units), jnp.bfloat16), pltpu.SemaphoreType.DMA((5, 2))],
+    )(where, p0, p1, p2, in_hbm(mine), in_hbm(other))
+
+
+def close_kernel(p3, weights, keep, send, out, sent):
+    sent[...] = send[...] + dot(p3[...], weights[1])
+    out[...] = keep[...] + dot(p3[...], weights[0])
+
+
+def forward_close(p3, weights, keep, send):
+    return call(
+        close_kernel,
+        [array(keep.shape, jnp.float32)] * 2,
+        [VMEM] * 4,
+        [VMEM] * 2,
+        "forward_close",
+    )(p3, weights, keep, send)
+
+
+def slot_kernel(weights, dz_t, dzo_t, out):
+    out[...] = low(dot(weights[0], dz_t[...]) + dot(weights[1], dzo_t[...]))
+
+
+def first_slot(weights, dz_t, dzo_t):
+    return call(
+        slot_kernel,
+        array((weights.shape[1], dz_t.shape[1]), jnp.bfloat16),
+        [VMEM] * 3,
+        VMEM,
+        "first_slot",
+    )(weights, dz_t, dzo_t)
 
 
 def tower_math(pre, bias, unit_a, unit_b, upper_a, upper_b, dz, dz_t, sums):
@@ -322,24 +358,32 @@
     )(*operands)
 
 
-def part_kernel(slots, where, mine, other, dz_t, dzo_t, *outs):
-    cols = mine.shape[0] // 4
-    for slot, at, block in slots:
-        rows = pl.ds(pl.multiple_of(where[3 + slot] * cols, cols), cols)
-        total = dot(mine[rows, :], dz_t[...]) + dot(other[rows, :], dzo_t[...])
+def part_kernel(slots, where, mine, other, dz_t, dzo_t, *refs):
+    *outs, held, sems = refs
+    cols = held.shape[2]
+
+    def emit(i, own_block, other_block):
+        _, at, block = slots[i]
+        total = dot(own_block, dz_t[...]) + dot(other_block, dzo_t[...])
         outs[at][block * cols : (block + 1) * cols, :] = total.astype(outs[at].dtype)
 
+    products(where, [where[3 + slot] for slot, _, _ in slots], mine, other, held, sems, emit)
+
 
 def parts(slots, outs, where, mine, other, dz_t, dzo_t):
-    cols = mine.shape[0] // 4
-    rows = dz_t.shape[1]
+    units, rows = dz_t.shape
+    cols = mine.shape[0] // 8
     return call(
         functools.partial(part_kernel, slots),
         [array((blocks * cols, rows), dtype) for blocks, dtype in outs],
-        [SMEM] + [VMEM] * 4,
+        [SMEM, HBM, HBM, VMEM, VMEM],
         [VMEM] * len(outs),
         "parts",
-    )(where, mine, other, dz_t, dzo_t)
+        [
+            pltpu.VMEM((len(slots), 2, cols, units), jnp.bfloat16),
+            pltpu.SemaphoreType.DMA((len(slots), 2)),
+        ],
+    )(where, in_hbm(mine), in_hbm(other), dz_t, dzo_t)
 
 
 def choose_kernel(where, at_end, in_middle, out, sem):
@@ -404,40 +448,57 @@
     )(where, *sources)
 
 
-def add_kernel(one, two, out):
+def add_kernel(at, one, two, out):
     rows = out.shape[0]
-    out[...] = low(wide(one[...]) + wide(two[0:rows, :]))
-
-
-def add(one, two):
-    return call(add_kernel, array(one.shape, jnp.bfloat16), [VMEM, VMEM], VMEM, "add")(one, two)
-
-
-def finish_kernel(third_at, where, marks, group, kept, third, cross, last, out):
+    out[...] = low(wide(one[at : at + rows, :]) + wide(two[0:rows, :]))
+
+
+def add(one, two, block=0, rows=None):
+    rows = rows or min(one.shape[0], two.shape[0])
+    return call(
+        functools.partial(add_kernel, block * rows),
+        array((rows, one.shape[1]), jnp.bfloat16),
+        [VMEM, VMEM],
+        VMEM,
+        "add",
+    )(one, two)
+
+
+def finish_kernel(where, marks, group, kept, third, cross, last, out, held, own, sems):
     second = group[...] == 1
     cols = out.shape[0]
-    cross_at = cross.shape[0] - cols
+    copies = [pltpu.make_async_copy(kept, own, sems.at[3])]
+    for n, source in enumerate((third, cross, last)):
+        copies.append(pltpu.make_async_copy(source, held.at[n], sems.at[n]))
+    for copy in copies:
+        copy.start()
+    for copy in copies:
+        copy.wait()
     for chunk in range(cols // LANES):
         zero, one = marks_of(marks, where, cols, chunk)
         keep = wide(jnp.where(second, one, zero))
-        at = chunk * LANES
-        total = kept[at : at + LANES, :] + wide(last[at : at + LANES, :])
-        total += wide(third[third_at + at : third_at + at + LANES, :])
-        total += wide(cross[cross_at + at : cross_at + at + LANES, :])
-        out[at : at + LANES, :] = low(total * keep)
-
-
-def finish(third_at, where, marks, group, kept, third, cross, last):
-    return call(
-        functools.partial(finish_kernel, third_at * kept.shape[0]),
+        rows = slice(chunk * LANES, (chunk + 1) * LANES)
+        total = own[rows, :] + wide(held[0, rows, :])
+        total += wide(held[1, rows, :]) + wide(held[2, rows, :])
+        out[rows, :] = low(total * keep)
+
+
+def finish(where, marks, group, kept, third, cross, last):
+    return call(
+        finish_kernel,
         array(kept.shape, jnp.bfloat16),
-        [SMEM, SMEM] + [VMEM] * 5,
+        [SMEM, SMEM, VMEM] + [HBM] * 4,
         VMEM,
         "finish",
-    )(where, marks, group, kept, third, cross, last)
-
-
-def pack_kernel(where, p0, p1, p2, p3, dz, sums, out, sems):
+        [
+            pltpu.VMEM((3, *kept.shape), jnp.bfloat16),
+            pltpu.VMEM(kept.shape, jnp.float32),
+            pltpu.SemaphoreType.DMA((4,)),
+        ],
+    )(where, marks, group, *[in_hbm(x) for x in (kept, third, cross, last)])
+
+
+def pack_kernel(where, p0, p1, p2, p3, dz, sums, given, out, sems):
     rows, units = dz.shape
     cols = p0.shape[1]
     for q in range(4):
@@ -457,9 +518,13 @@
             for q in range(4):
                 out[q, row : row + 1, cols : cols + units] = piece
             rest = rest - wide(piece)
+    gives = [pltpu.make_async_copy(out.at[q], given.at[q], sems.at[4 + q]) for q in range(4)]
     for q in range(4):
         block = out.at[q, pl.ds(0, rows), pl.ds(0, cols)]
         pltpu.make_async_copy(p0, block, sems.at[q]).wait()
+        gives[q].start()
+    for give in gives:
+        give.wait()
 
 
 def pack(where, pieces, dz, sums):
@@ -467,78 +532,86 @@
     cols = pieces[0].shape[1]
     return call(
         pack_kernel,
-        array((4, rows + EXTRA, cols + units), jnp.bfloat16),
+        pltpu.HBM((4, rows + EXTRA, cols + units), jnp.bfloat16),
         [SMEM] + [ANY] * 4 + [VMEM] * 2,
-        VMEM,
+        HBM,
         "pack",
-        [pltpu.SemaphoreType.DMA((4,))],
+        [
+            pltpu.VMEM((4, rows + EXTRA, cols + units), jnp.bfloat16),
+            pltpu.SemaphoreType.DMA((8,)),
+        ],
     )(where, *pieces, dz, sums)
 
 
-def weight_kernel(where, near, far, out, images, dzs, tiles, sems):
+def weight_kernel(sides, where, *refs):
+    n = len(sides)
+    images_of, dz_of = refs[:n], refs[n]
+    before, (out, images, dzs, tiles, sems) = refs[n + 1 : -5], refs[-5:]
     rows, units = dzs.shape[1:]
     cols = images.shape[3]
     tile = tiles.shape[1]
     steps = cols // tile
 
     def fetch(q):
-        source = near.at[q, pl.ds(0, rows), pl.ds(cols, units)]
+        source = dz_of.at[q, pl.ds(0, rows), pl.ds(cols, units)]
         return pltpu.make_async_copy(source, dzs.at[q], sems.at[q])
 
-    def block(source, p, q):
-        image = source.at[q, pl.ds(0, rows), pl.ds(0, cols)]
-        return pltpu.make_async_copy(image, images.at[p, q], sems.at[4 + 4 * p + q])
-
-    def give(p, t):
-        slot = p * steps + t
+    def block(i, q):
+        image = images_of[i].at[q, pl.ds(0, rows), pl.ds(0, cols)]
+        return pltpu.make_async_copy(image, images.at[i, q], sems.at[4 + 4 * i + q])
+
+    def give(i, t):
+        at = pl.multiple_of((where[1] ^ sides[i]) * cols + t * tile, tile)
+        slot = i * steps + t
         return pltpu.make_async_copy(
-            tiles.at[slot], out.at[pl.ds(slot * tile, tile), :], sems.at[12 + slot]
+            tiles.at[slot], out.at[pl.ds(at, tile), :], sems.at[12 + slot]
         )
 
     for q in range(4):
         fetch(q).start()
-    for p in range(2):
+    for i in range(n):
         for q in range(4):
-            pl.when(where[1] == p)(block(near, p, q).start)
-            pl.when(where[1] != p)(block(far, p, q).start)
+            block(i, q).start()
     for q in range(4):
         fetch(q).wait()
-    for p in range(2):
+    for i in range(n):
         for q in range(4):
-            block(near, p, q).wait()
+            block(i, q).wait()
         for t in range(steps):
             total = None
             for q in range(4):
                 term = lax.dot_general(
-                    images[p, q, :, t * tile : (t + 1) * tile],
+                    images[i, q, :, t * tile : (t + 1) * tile],
                     dzs[q],
                     (((0,), (0,)), ((), ())),
                     preferred_element_type=jnp.float32,
                 )
                 total = term if total is None else total + term
-            tiles[p * steps + t] = total
-            give(p, t).start()
-    for p in range(2):
+            tiles[i * steps + t] = total
+            give(i, t).start()
+    for i in range(n):
         for t in range(steps):
-            give(p, t).wait()
-
-
-def weight_grad(rows, cols, where, near, far):
-    units = near.shape[2] - cols
+            give(i, t).wait()
+
+
+def weight_grad(sides, rows, cols, where, images, dz, *before):
+    units = dz.shape[2] - cols
     tile = cols // 3
-    return call(
-        weight_kernel,
-        array((2 * cols, units), jnp.float32),
-        [SMEM, ANY, ANY],
+    n = len(sides)
+    return call(
+        functools.partial(weight_kernel, sides),
+        pltpu.HBM((2 * cols, units), jnp.float32),
+        [SMEM] + [ANY] * (n + 1) + [HBM] * len(before),
         HBM,
         "weight_grad",
         [
-            pltpu.VMEM((2, 4, rows, cols), jnp.bfloat16),
+            pltpu.VMEM((n, 4, rows, cols), jnp.bfloat16),
             pltpu.VMEM((4, rows, units), jnp.bfloat16),
-            pltpu.VMEM((6, tile, units), jnp.float32),
+            pltpu.VMEM((3 * n, tile, units), jnp.float32),
             pltpu.SemaphoreType.DMA((18,)),
         ],
-    )(where, near, far)
+        {n + 2: 0} if before else {},
+    )(where, *images, dz, *before)
 
 
 def sums_kernel(rows, cols, got_a, got_b, bias, stitch, terms, sems):
@@ -644,18 +717,14 @@
     a2 = send(across, a0)
     a1 = send(along, a0)
     b0 = mask_image(where, position_mask, group, image_b)
-    mine_a = load(where, weight_a)
-    mine_b = load(where, weight_b)
     a1, a2 = wait(a1, a2)
     a3 = send(along, a2)
     b_mid = send(between, b0)
     b1 = send(along, b0)
     whole_a, whole_b = wait(whole_a, whole_b)
-    other_a = load(where, whole_a)
-    other_b = load(where, whole_b)
-    keep_a, give_a = forward_open(a0, a1, a2, mine_a, other_a)
+    keep_a, give_a, last_a, slot_a = forward_open(where, a0, a1, a2, weight_a, whole_a)
     a3 = wait(a3)
-    own_a, sent_a = forward_close(a3, mine_a, other_a, keep_a, give_a)
+    own_a, sent_a = forward_close(a3, last_a, keep_a, give_a)
     got_sum = wait(send(swap, sent_a))
     dz_a, dzt_a, sums_a, hidden_a = tower(
         first_kernel,
@@ -669,31 +738,33 @@
         cotan_b,
     )
     dzo_a = send(swap, dzt_a)
+    packed_a = pack(where, (a0, a1, a2, a3), dz_a, sums_a)
     b1, b_mid = wait(b1, b_mid)
-    got_a = send(exchange, pack(where, (a0, a1, a2, a3), dz_a, sums_a))
+    got_a = send(exchange, packed_a)
     b_end = send(outward, b_mid)
     b_mid2 = send(between, b1)
     dzo_a = wait(dzo_a)
-    first_a, second_a, third_a, kept_a = parts(
-        ((0, 0, 0), (1, 1, 0), (2, 2, 0), (3, 3, 0)),
-        [(1, bf16), (1, bf16), (1, bf16), (1, f32)],
+    first_a = first_slot(slot_a, dzt_a, dzo_a)
+    in1_a = send(inward, first_a)
+    second_a, third_a, kept_a = parts(
+        ((1, 0, 0), (2, 1, 0), (3, 2, 0)),
+        [(1, bf16), (1, bf16), (1, f32)],
         where,
-        mine_a,
-        other_a,
+        weight_a,
+        whole_a,
         dzt_a,
         dzo_a,
     )
-    in1_a = send(inward, first_a)
     in2_a = send(inward, second_a)
     b_end, b_mid2 = wait(b_end, b_mid2)
     b_end2 = send(outward, b_mid2)
     b2 = choose(where, b_end, b_mid2)
-    keep_b, give_b = forward_open(b0, b1, b2, mine_b, other_b)
+    keep_b, give_b, last_b, slot_b = forward_open(where, b0, b1, b2, weight_b, whole_b)
     in1_a = wait(in1_a)
     cross1_a = send(between, add(first_a, in1_a))
     b_end2 = wait(b_end2)
     b3 = choose(where, b_end2, b_mid)
-    own_b, sent_b = forward_close(b3, mine_b, other_b, keep_b, give_b)
+    own_b, sent_b = forward_close(b3, last_b, keep_b, give_b)
     got_sum = send(swap, sent_b)
     in2_a = wait(in2_a)
     sum2_a = add(second_a, in2_a)
@@ -711,56 +782,59 @@
         cotan_b,
     )
     dzo_b = send(swap, dzt_b)
+    packed_b = pack(where, (b0, b1, b2, b3), dz_b, sums_b)
     cross1_a = wait(cross1_a)
     sum3_a = add(third_a, cross1_a)
     got_a = wait(got_a)
     far_a = send(swap, got_a)
-    got_b = send(exchange, pack(where, (b0, b1, b2, b3), dz_b, sums_b))
+    got_b = send(exchange, packed_b)
+    cross2_a = send(between, sum2_a)
     dzo_b, far_a = wait(dzo_b, far_a)
-    (first_b,) = parts(((0, 0, 0),), [(1, bf16)], where, mine_b, other_b, dzt_b, dzo_b)
+    first_b = first_slot(slot_b, dzt_b, dzo_b)
     in1_b = send(inward, first_b)
     s1 = send(along, local)
     s_mid = send(between, local)
-    cross2_a = send(between, sum2_a)
-    out_a = send(outward, sum3_a)
     second_b, third_b, kept_b = parts(
         ((1, 0, 0), (2, 1, 0), (3, 2, 0)),
         [(1, bf16), (1, bf16), (1, f32)],
         where,
-        mine_b,
-        other_b,
+        weight_b,
+        whole_b,
         dzt_b,
         dzo_b,
     )
-    in2_b = send(inward, second_b)
-    grad_weight_a = weight_grad(rows, cols, where, got_a, far_a)
+    grad_weight_a = weight_grad((0, 1), rows, cols, where, (got_a, far_a), got_a)
+    cross2_a = wait(cross2_a)
     in1_b = wait(in1_b)
     cross1_b = send(between, add(first_b, in1_b))
+    in2_b = send(inward, second_b)
+    out_a = send(outward, sum3_a)
     s1, s_mid = wait(s1, s_mid)
     s_end = send(outward, s_mid)
     s_mid2 = send(between, s1)
+    cross1_b = wait(cross1_b)
+    out_b = send(outward, add(third_b, cross1_b))
     in2_b = wait(in2_b)
     cross2_b = send(between, add(second_b, in2_b))
-    cross1_b = wait(cross1_b)
-    out_b = send(outward, add(third_b, cross1_b))
+    out_a = wait(out_a)
+    in3_b = send(inward, third_b)
     s_end, s_mid2 = wait(s_end, s_mid2)
     s_end2 = send(outward, s_mid2)
     in3_a = send(inward, third_a)
     s2 = choose(where, s_end, s_mid2)
-    in3_b = send(inward, third_b)
-    cross2_a, out_a = wait(cross2_a, out_a)
-    cross2_b, out_b = wait(cross2_b, out_b)
+    got_b = wait(got_b)
+    grad_bias, grad_stitch = total_sums(rows, cols, got_a, got_b)
+    half_b = weight_grad((0,), rows, cols, where, (got_b,), got_b)
+    in3_b, out_b, cross2_b = wait(in3_b, out_b, cross2_b)
+    grad_image_b = finish(where, position_mask, group, kept_b, in3_b, cross2_b, out_b)
     s_end2, in3_a = wait(s_end2, in3_a)
     s3 = choose(where, s_end2, s_mid)
-    grad_image_a = finish(0, where, position_mask, group, kept_a, in3_a, cross2_a, out_a)
-    got_b, in3_b = wait(got_b, in3_b)
     far_b = send(swap, got_b)
     far_high = send(swap, join(s2, s3))
     far_low = send(swap, join(local, s1))
-    grad_bias, grad_stitch = total_sums(rows, cols, got_a, got_b)
-    grad_image_b = finish(0, where, position_mask, group, kept_b, in3_b, cross2_b, out_b)
+    grad_image_a = finish(where, position_mask, group, kept_a, in3_a, cross2_a, out_a)
     stitched_a, stitched_b = lay_out(where, local, s1, s2, s3, far_low, far_high)
-    grad_weight_b = weight_grad(rows, cols, where, got_b, far_b)
+    grad_weight_b = weight_grad((1,), rows, cols, where, (far_b,), got_b, half_b)
     return (
         stitched_a,
         stitched_b,

time: 247 us -> 222 us (0.90)
  waiting for transfers between devices: 96.3 us -> 74 us
  local copies, waits for them, and re-layouts: 29.1 us -> 13.5 us
  Pallas kernels: 57.7 us -> 68.1 us
  starting transfers between devices: 59.9 us -> 63.1 us
    unnamed x88 -> x74, local copies, waits for them, and re-layouts: 29.1 us -> 13.4 us
    ppermute x6, waiting for transfers between devices: 33.2 us -> 20 us  [outward(): return lax.ppermute(x, 'mp', ENDS_OUT)]
    pallas_call x35 -> x33, Pallas kernels: 57.7 us -> 68.1 us  [go(): *results, line.token = run(*operands, *before)]
    ppermute x4, waiting for transfers between devices: 41 us -> 32.7 us  [along(): return lax.ppermute(x, 'mp', NEAR_Z)]
  transfers between devices with their start and end apart: 37 -> 37, of which waited for: 18 -> 17; matrix products, arithmetic and copies ran while one was open for 0% -> 0% of each run, Pallas kernels for 20% -> 28%
where the time goes in v6:
time: 222 us; the launch traced here: 221 us
  waiting for transfers between devices  74 us (33%)
  Pallas kernels  68.1 us (31%)
  starting transfers between devices  63.1 us (28%)
  local copies, waits for them, and re-layouts  13.5 us (6%)
    pallas_call x33, Pallas kernels, go(): *results, line.token = run(*operands, *before)  68.1 us
    ppermute x4, waiting for transfers between devices, along(): return lax.ppermute(x, 'mp', NEAR_Z)  32.7 us
    ppermute x6, starting transfers between devices, inward(): return lax.ppermute(x, 'mp', ENDS_IN)  27.3 us
    ppermute x6, waiting for transfers between devices, outward(): return lax.ppermute(x, 'mp', ENDS_OUT)  20 us
    unnamed x74, local copies, waits for them, and re-layouts  13.4 us
    ppermute x10, waiting for transfers between devices, swap(): return lax.ppermute(x, 'mp', SWAP_CORE)  11 us
    all_to_all x2, starting transfers between devices, exchange(): return lax.all_to_all(x, 'dp', 0, 0)  9.59 us
    ppermute x6, starting transfers between devices, outward(): return lax.ppermute(x, 'mp', ENDS_OUT)  7.72 us
  transfers between devices with their start and end apart: 37, of which 17 were waited for; matrix products, arithmetic and copies ran while one was open for 0% of the time, Pallas kernels for 28%

profile of v6, /device:TPU:0, one launch (start us, length us, event | category | flops | bytes accessed | tf_op | source)
XLA Modules:
  0.0 220.9 jit_solution(4820351166382098846)
XLA Ops:
  2.0 1.1 copy-done.14
  4.4 1.1 mask_image.2
  5.5 3.1 %collective-permute-start = (bf16[256,1152]{1,0:T(8,128)(2,1)S(1)}, bf16[256,1152]{1,0:T(8,128)(2,1)S(1)}, u32[]{:S(2)}, u32[]{:S(2)}) collective-permute-start(bf16[256,1152]{1,0:T(8,128)(2,1)S(1)} %get-tuple-element.205.refs_1_), channel_id=1, source_target_pairs={{0,2},{1,3},{2,0},{3,1},{4,6},{5,7},{6,4},{7,5},{8,10},{9,11},{10,... | collective-permute-start | bytes 1769480 | tf_op jit(solution)/shard_map/ppermute | solution.py:663
  8.6 2.6 %collective-permute-start.1 = (bf16[256,1152]{1,0:T(8,128)(2,1)S(1)}, bf16[256,1152]{1,0:T(8,128)(2,1)S(1)}, u32[]{:S(2)}, u32[]{:S(2)}) collective-permute-start(bf16[256,1152]{1,0:T(8,128)(2,1)S(1)} %get-tuple-element.205.refs_1_), channel_id=1, source_target_pairs={{0,4},{1,5},{2,6},{3,7},{4,0},{5,1},{6,2},{7,3},{8,12},{9,13},{10,... | collective-permute-start | bytes 1769480 | tf_op jit(solution)/shard_map/ppermute | solution.py:667
  11.2 1.1 copy-done.15
  13.6 1.1 mask_image.3
  14.7 20.0 %collective-permute-done.refs_2_ = bf16[256,1152]{1,0:T(8,128)(2,1)S(1)} collective-permute-done((bf16[256,1152]{1,0:T(8,128)(2,1)S(1)}, bf16[256,1152]{1,0:T(8,128)(2,1)S(1)}, u32[]{:S(2)}, u32[]{:S(2)}) %collective-permute-start) | collective-permute-done | bytes 589856 | tf_op jit(solution)/shard_map/ppermute | solution.py:663
  34.7 2.5 %collective-permute-done.1.refs_3_ = bf16[256,1152]{1,0:T(8,128)(2,1)S(1)} collective-permute-done((bf16[256,1152]{1,0:T(8,128)(2,1)S(1)}, bf16[256,1152]{1,0:T(8,128)(2,1)S(1)}, u32[]{:S(2)}, u32[]{:S(2)}) %collective-permute-start.1) | collective-permute-done | bytes 589856 | tf_op jit(solution)/shard_map/ppermute | solution.py:667
  37.7 1.6 collective-permute-start.2
  40.0 5.3 %forward_open.2 = (f32[256,512]{1,0:T(8,128)S(1)}, f32[256,512]{1,0:T(8,128)S(1)}, bf16[2,1152,512]{2,1,0:T(8,128)(2,1)S(1)}, bf16[2,1152,512]{2,1,0:T(8,128)(2,1)S(1)}, f32[8,128]{1,0:T(8,128)S(1)}) custom-call(s32[9]{0:T(128)S(1)} %concatenate.3.refs_0_, bf16[256,1152]{1,0:T(8,128)(2,1)S(1)} %get-tuple-element.205.refs_1_, ...), custom_call_target="tpu_custom_call" | custom-call | flops 1 | bytes 1 | tf_op jit(solution)/shard_map/forward_open/pallas_call | solution.py:171
  45.3 8.2 %collective-permute-done.4.refs_0_.refs_4_ = bf16[256,1152]{1,0:T(8,128)(2,1)S(1)} collective-permute-done((bf16[256,1152]{1,0:T(8,128)(2,1)S(1)}, bf16[256,1152]{1,0:T(8,128)(2,1)S(1)}, u32[]{:S(2)}, u32[]{:S(2)}) %collective-permute-start.4) | collective-permute-done | bytes 589856 | tf_op jit(solution)/shard_map/ppermute | solution.py:663
  53.5 0.8 forward_close.2
  54.4 1.9 collective-permute-done.7.refs_1_
  56.8 2.9 %pack.2 = (bf16[4,272,1664]{2,1,0:T(8,128)(2,1)}, f32[8,128]{1,0:T(8,128)S(1)}) custom-call(s32[9]{0:T(128)S(1)} %concatenate.3.refs_0_, bf16[256,1152]{1,0:T(8,128)(2,1)S(1)} %get-tuple-element.205.refs_1_, bf16[256,1152]{1,0:T(8,128)(2,1)S(1)} %collective-permute-done.refs_2_, bf16[256,1152]{1,0:T(8,128)(2,1)S(1)} %collective-permute-done.1.refs_3_, ...), custom_call_target="tpu_custom_call" | custom-call | flops 1 | bytes 1 | tf_op jit(solution)/shard_map/pack/pallas_call | solution.py:171
  60.3 2.7 %collective-permute-done.2.refs_2_ = bf16[256,1152]{1,0:T(8,128)(2,1)S(1)} collective-permute-done((bf16[256,1152]{1,0:T(8,128)(2,1)S(1)}, bf16[256,1152]{1,0:T(8,128)(2,1)S(1)}, u32[]{:S(2)}, u32[]{:S(2)}) %collective-permute-start.2) | collective-permute-done | bytes 589856 | tf_op jit(solution)/shard_map/ppermute | solution.py:663
  63.8 4.7 %all-to-all-start = ((bf16[4,272,1664]{2,1,0:T(8,128)(2,1)}), bf16[4,272,1664]{2,1,0:T(8,128)(2,1)}, u32[]{:S(2)}, u32[]{:S(2)}) async-start(bf16[4,272,1664]{2,1,0:T(8,128)(2,1)} %get-tuple-element.297), calls=%async_computation | async-start | bytes 7241728 | tf_op jit(solution)/shard_map/all_to_all | solution.py:683
  69.3 1.3 collective-permute-start.8
  70.6 1.7 collective-permute-done.10.refs_2_.refs_4_
  72.4 0.9 copy-done.8
  74.8 6.1 %collective-permute-start.12 = (bf16[1152,256]{1,0:T(8,128)(2,1)S(1)}, bf16[1152,256]{1,0:T(8,128)(2,1)S(1)}, u32[]{:S(2)}, u32[]{:S(2)}) collective-permute-start(bf16[1152,256]{1,0:T(8,128)(2,1)S(1)} %get-tuple-element.263), channel_id=1, source_target_pairs={{0,2},{1,3},{6,4},{7,5},{8,10},{9,11},{14,12},{15,13},{16,18},{17,... | collective-permute-start | bytes 1769480 | tf_op jit(solution)/shard_map/ppermute | solution.py:671
  80.9 0.9 copy-done.9
  81.9 5.8 %parts.2 = (bf16[1152,256]{1,0:T(8,128)(2,1)S(1)}, bf16[1152,256]{1,0:T(8,128)(2,1)S(1)}, f32[1152,256]{1,0:T(8,128)S(1)}, f32[8,128]{1,0:T(8,128)S(1)}) custom-call(s32[9]{0:T(128)S(1)} %concatenate.3.refs_0_, bf16[9216,512]{1,0:T(8,128)(2,1)} %refs_1_.8, bf16[9216,512]{1,0:T(8,128)(2,1)} %collective-permute-done.5.refs_5_.refs_2_, ...), custom_call_target="tpu_custom_call" | custom-call | flops 1 | bytes 1 | tf_op jit(solution)/shard_map/parts/pallas_call | solution.py:171
  87.7 1.0 copy-done.2
  88.7 1.3 collective-permute-start.11
  90.0 4.6 %collective-permute-start.14 = (bf16[1152,256]{1,0:T(8,128)(2,1)S(1)}, bf16[1152,256]{1,0:T(8,128)(2,1)S(1)}, u32[]{:S(2)}, u32[]{:S(2)}) collective-permute-start(bf16[1152,256]{1,0:T(8,128)(2,1)S(1)} %get-tuple-element.284.refs_0_), channel_id=1, source_target_pairs={{0,2},{1,3},{6,4},{7,5},{8,10},{9,11},{14,12},{15,13},{16,18},{17,... | collective-permute-start | bytes 1769480 | tf_op jit(solution)/shard_map/ppermute | solution.py:671
  95.3 5.3 %forward_open.3 = (f32[256,512]{1,0:T(8,128)S(1)}, f32[256,512]{1,0:T(8,128)S(1)}, bf16[2,1152,512]{2,1,0:T(8,128)(2,1)S(1)}, bf16[2,1152,512]{2,1,0:T(8,128)(2,1)S(1)}, f32[8,128]{1,0:T(8,128)S(1)}) custom-call(s32[9]{0:T(128)S(1)} %concatenate.3.refs_0_, bf16[256,1152]{1,0:T(8,128)(2,1)S(1)} %get-tuple-element.208.refs_1_, ...), custom_call_target="tpu_custom_call" | custom-call | flops 1 | bytes 1 | tf_op jit(solution)/shard_map/forward_open/pallas_call | solution.py:171
  100.8 0.8 collective-permute-start.16
  101.6 4.1 %collective-permute-done.11.refs_1_ = bf16[256,1152]{1,0:T(8,128)(2,1)S(1)} collective-permute-done((bf16[256,1152]{1,0:T(8,128)(2,1)S(1)}, bf16[256,1152]{1,0:T(8,128)(2,1)S(1)}, u32[]{:S(2)}, u32[]{:S(2)}) %collective-permute-start.11) | collective-permute-done | bytes 589856 | tf_op jit(solution)/shard_map/ppermute | solution.py:679
  106.3 0.8 forward_close.3
  107.4 1.7 collective-permute-done.13.refs_1_
  110.5 3.0 %pack.3 = (bf16[4,272,1664]{2,1,0:T(8,128)(2,1)}, f32[8,128]{1,0:T(8,128)S(1)}) custom-call(s32[9]{0:T(128)S(1)} %concatenate.3.refs_0_, bf16[256,1152]{1,0:T(8,128)(2,1)S(1)} %get-tuple-element.208.refs_1_, bf16[256,1152]{1,0:T(8,128)(2,1)S(1)} %collective-permute-done.2.refs_2_, bf16[256,1152]{1,0:T(8,128)(2,1)S(1)} %get-tuple-element.266.refs_3_, ...), custom_call_target="tpu_custom_call" | custom-call | flops 1 | bytes 1 | tf_op jit(solution)/shard_map/pack/pallas_call | solution.py:171
  114.6 4.8 %all-to-all-start.1 = ((bf16[4,272,1664]{2,1,0:T(8,128)(2,1)}), bf16[4,272,1664]{2,1,0:T(8,128)(2,1)}, u32[]{:S(2)}, u32[]{:S(2)}) async-start(bf16[4,272,1664]{2,1,0:T(8,128)(2,1)} %get-tuple-element.366), calls=%async_computation.1 | async-start | bytes 7241728 | tf_op jit(solution)/shard_map/all_to_all | solution.py:683
  122.0 7.1 %collective-permute-start.20 = (bf16[1152,256]{1,0:T(8,128)(2,1)S(1)}, bf16[1152,256]{1,0:T(8,128)(2,1)S(1)}, u32[]{:S(2)}, u32[]{:S(2)}) collective-permute-start(bf16[1152,256]{1,0:T(8,128)(2,1)S(1)} %get-tuple-element.323), channel_id=1, source_target_pairs={{0,2},{1,3},{6,4},{7,5},{8,10},{9,11},{14,12},{15,13},{16,18},{17,... | collective-permute-start | bytes 1769480 | tf_op jit(solution)/shard_map/ppermute | solution.py:671
  129.9 1.5 collective-permute-start.18
  131.4 0.9 copy-done.6
  132.3 5.7 %parts.3 = (bf16[1152,256]{1,0:T(8,128)(2,1)S(1)}, bf16[1152,256]{1,0:T(8,128)(2,1)S(1)}, f32[1152,256]{1,0:T(8,128)S(1)}, f32[8,128]{1,0:T(8,128)S(1)}) custom-call(s32[9]{0:T(128)S(1)} %concatenate.3.refs_0_, bf16[9216,512]{1,0:T(8,128)(2,1)} %refs_1_.9, bf16[9216,512]{1,0:T(8,128)(2,1)} %collective-permute-done.6.refs_5_.refs_2_, ...), custom_call_target="tpu_custom_call" | custom-call | flops 1 | bytes 1 | tf_op jit(solution)/shard_map/parts/pallas_call | solution.py:171
  138.1 1.0 copy-done.3
  139.1 6.3 %weight_grad.3 = (f32[2304,512]{1,0:T(8,128)}, f32[8,128]{1,0:T(8,128)S(1)}) custom-call(s32[9]{0:T(128)S(1)} %concatenate.3.refs_0_, bf16[4,272,1664]{2,1,0:T(8,128)(2,1)} %all-to-all-done.refs_1_.refs_3_.refs_0_, bf16[4,272,1664]{2,1,0:T(8,128)(2,1)} %collective-permute-done.17.refs_2_, bf16[4,272,1664]{2,1,0:T(8,128)(2,1)} %all-to-all-done.refs_1_.refs_3_.refs_0_, ...), custom_call_target="tpu_custom_call" | custom-call | flops 1 | bytes 1 | tf_op jit(solution)/shard_map/weight_grad/pallas_call | solution.py:171
  146.3 4.6 %collective-permute-start.25 = (bf16[1152,256]{1,0:T(8,128)(2,1)S(1)}, bf16[1152,256]{1,0:T(8,128)(2,1)S(1)}, u32[]{:S(2)}, u32[]{:S(2)}) collective-permute-start(bf16[1152,256]{1,0:T(8,128)(2,1)S(1)} %get-tuple-element.343.refs_0_), channel_id=1, source_target_pairs={{0,2},{1,3},{6,4},{7,5},{8,10},{9,11},{14,12},{15,13},{16,18},{17,... | collective-permute-start | bytes 1769480 | tf_op jit(solution)/shard_map/ppermute | solution.py:671
  150.9 1.3 collective-permute-start.24
  152.3 1.8 collective-permute-done.18.refs_1_.refs_2_
  154.1 1.5 collective-permute-start.23
  155.5 1.3 collective-permute-start.22
  156.8 1.0 add.25
  157.8 7.7 %collective-permute-done.25.refs_1_ = bf16[1152,256]{1,0:T(8,128)(2,1)S(1)} collective-permute-done((bf16[1152,256]{1,0:T(8,128)(2,1)S(1)}, bf16[1152,256]{1,0:T(8,128)(2,1)S(1)}, u32[]{:S(2)}, u32[]{:S(2)}) %collective-permute-start.25) | collective-permute-done | bytes 589856 | tf_op jit(solution)/shard_map/ppermute | solution.py:671
  165.5 0.9 add.26
  166.4 2.7 %collective-permute-done.24.refs_6_ = bf16[1152,256]{1,0:T(8,128)(2,1)S(1)} collective-permute-done((bf16[1152,256]{1,0:T(8,128)(2,1)S(1)}, bf16[1152,256]{1,0:T(8,128)(2,1)S(1)}, u32[]{:S(2)}, u32[]{:S(2)}) %collective-permute-start.24) | collective-permute-done | bytes 589856 | tf_op jit(solution)/shard_map/ppermute | solution.py:679
  169.1 2.5 %collective-permute-start.29 = (bf16[1152,256]{1,0:T(8,128)(2,1)S(1)}, bf16[1152,256]{1,0:T(8,128)(2,1)}, u32[]{:S(2)}, u32[]{:S(2)}) collective-permute-start(bf16[1152,256]{1,0:T(8,128)(2,1)S(1)} %get-tuple-element.363.refs_0_), channel_id=1, source_target_pairs={{0,2},{1,3},{6,4},{7,5},{8,10},{9,11},{14,12},{15,13},{16,18},{17,... | collective-permute-start | bytes 1769480 | tf_op jit(solution)/shard_map/ppermute | solution.py:671
  171.7 1.5 collective-permute-start.31
  173.1 1.3 collective-permute-start.30
  174.4 4.9 %collective-permute-done.22.refs_1_ = bf16[512,512]{1,0:T(8,128)(2,1)S(1)} collective-permute-done((bf16[512,512]{1,0:T(8,128)(2,1)S(1)}, bf16[512,512]{1,0:T(8,128)(2,1)S(1)}, u32[]{:S(2)}, u32[]{:S(2)}) %collective-permute-start.22) | collective-permute-done | bytes 524320 | tf_op jit(solution)/shard_map/ppermute | solution.py:679
  179.3 2.3 %collective-permute-start.28 = (bf16[1152,256]{1,0:T(8,128)(2,1)S(1)}, bf16[1152,256]{1,0:T(8,128)(2,1)}, u32[]{:S(2)}, u32[]{:S(2)}) collective-permute-start(bf16[1152,256]{1,0:T(8,128)(2,1)S(1)} %copy-done.17), channel_id=1, source_target_pairs={{0,2},{1,3},{6,4},{7,5},{8,10},{9,11},{14,12},{15,13},{16,18},{17,... | collective-permute-start | bytes 1769480 | tf_op jit(solution)/shard_map/ppermute | solution.py:671
  181.6 1.3 collective-permute-start.27
  183.5 1.6 total_sums.1
  185.1 4.9 %weight_grad.4 = (f32[2304,512]{1,0:T(8,128)}, f32[8,128]{1,0:T(8,128)S(1)}) custom-call(s32[9]{0:T(128)S(1)} %concatenate.3.refs_0_, bf16[4,272,1664]{2,1,0:T(8,128)(2,1)} %all-to-all-done.1.refs_1_.refs_2_, bf16[4,272,1664]{2,1,0:T(8,128)(2,1)} %all-to-all-done.1.refs_1_.refs_2_, f32[8,128]{1,0:T(8,128)S(1)} %get-tuple-element.370.refs_3_), custom_call_target="tpu_custom_call" | custom-call | flops 1 | bytes 1 | tf_op jit(solution)/shard_map/weight_grad/pallas_call | solution.py:171
  190.1 2.0 collective-permute-done.30.refs_6_
  192.1 3.5 %finish.2 = (bf16[1152,256]{1,0:T(8,128)(2,1)}, f32[8,128]{1,0:T(8,128)S(1)}) custom-call(s32[9]{0:T(128)S(1)} %concatenate.3.refs_0_, s32[2,36]{1,0:T(2,128)S(1)} %copy-done.26, s32[1,256]{1,0:T(1,128)S(1)} %bitcast.10, f32[1152,256]{1,0:T(8,128)} %copy-done.3, bf16[1152,256]{1,0:T(8,128)(2,1)} %collective-permute-done.29.refs_4_, ...), custom_call_target="tpu_custom_call" | custom-call | flops 1 | bytes 1 | tf_op jit(solution)/shard_map/finish/pallas_call | solution.py:171
  195.5 6.4 %collective-permute-done.27.refs_1_ = bf16[512,512]{1,0:T(8,128)(2,1)} collective-permute-done((bf16[512,512]{1,0:T(8,128)(2,1)}, bf16[512,512]{1,0:T(8,128)(2,1)}, u32[]{:S(2)}, u32[]{:S(2)}) %collective-permute-start.27) | collective-permute-done | bytes 524320 | tf_op jit(solution)/shard_map/ppermute | solution.py:679
  201.9 1.6 choose.7
  204.4 3.5 %finish.3 = (bf16[1152,256]{1,0:T(8,128)(2,1)}, f32[8,128]{1,0:T(8,128)S(1)}) custom-call(s32[9]{0:T(128)S(1)} %concatenate.3.refs_0_, s32[2,36]{1,0:T(2,128)S(1)} %copy-done.26, s32[1,256]{1,0:T(1,128)S(1)} %bitcast.11, f32[1152,256]{1,0:T(8,128)} %copy-done.2, bf16[1152,256]{1,0:T(8,128)(2,1)} %collective-permute-done.28.refs_4_, ...), custom_call_target="tpu_custom_call" | custom-call | flops 1 | bytes 1 | tf_op jit(solution)/shard_map/finish/pallas_call | solution.py:171
  207.9 3.2 %collective-permute-done.32.refs_5_ = bf16[1024,512]{1,0:T(8,128)(2,1)S(1)} collective-permute-done((bf16[1024,512]{1,0:T(8,128)(2,1)S(1)}, bf16[1024,512]{1,0:T(8,128)(2,1)S(1)}, u32[]{:S(2)}, u32[]{:S(2)}) %collective-permute-start.32) | collective-permute-done | bytes 1048608 | tf_op jit(solution)/shard_map/ppermute | solution.py:659
  211.1 1.9 collective-permute-done.33.refs_6_
  212.9 3.1 %lay_out.1 = (bf16[256,4096]{1,0:T(8,128)(2,1)}, bf16[256,4096]{1,0:T(8,128)(2,1)}, f32[8,128]{1,0:T(8,128)S(1)}) custom-call(s32[9]{0:T(128)S(1)} %concatenate.3.refs_0_, bf16[512,512]{1,0:T(8,128)(2,1)S(1)} %copy-done.1, bf16[512,512]{1,0:T(8,128)(2,1)S(1)} %collective-permute-done.18.refs_1_.refs_2_, ...), custom_call_target="tpu_custom_call" | custom-call | flops 1 | bytes 1 | tf_op jit(solution)/shard_map/lay_out/pallas_call | solution.py:171
  216.0 4.8 %weight_grad.5 = (f32[2304,512]{1,0:T(8,128)}, f32[8,128]{1,0:T(8,128)}) custom-call(s32[9]{0:T(128)S(1)} %concatenate.3.refs_0_, bf16[4,272,1664]{2,1,0:T(8,128)(2,1)S(1)} %collective-permute-done.34.refs_1_, bf16[4,272,1664]{2,1,0:T(8,128)(2,1)} %all-to-all-done.1.refs_1_.refs_2_, ...), custom_call_target="tpu_custom_call", output_to_operand_aliasing={{0}: (3, {})} | custom-call | flops 1 | bytes 1 | tf_op jit(solution)/shard_map/weight_grad/pallas_call | solution.py:171
  (119 shorter events, 19.1 us)
Async XLA Ops:
  0.6 39.3 %collective-permute-start.5 = (bf16[9216,512]{1,0:T(8,128)(2,1)}, bf16[9216,512]{1,0:T(8,128)(2,1)}, u32[]{:S(2)}, u32[]{:S(2)}) collective-permute-start(bf16[9216,512]{1,0:T(8,128)(2,1)} %refs_1_.8), channel_id=1, source_target_pairs={{0,1},{1,0},{2,3},{3,2},{4,5},{5,4},{6,7},{7,6},{8,9},{9,8},{10,11... | collective-permute-start | bytes 28311560 | tf_op jit(solution)/shard_map/ppermute | solution.py:659
  1.1 38.8 %collective-permute-start.6 = (bf16[9216,512]{1,0:T(8,128)(2,1)}, bf16[9216,512]{1,0:T(8,128)(2,1)}, u32[]{:S(2)}, u32[]{:S(2)}) collective-permute-start(bf16[9216,512]{1,0:T(8,128)(2,1)} %refs_1_.9), channel_id=1, source_target_pairs={{0,1},{1,0},{2,3},{3,2},{4,5},{5,4},{6,7},{7,6},{8,9},{9,8},{10,11... | collective-permute-start | bytes 28311560 | tf_op jit(solution)/shard_map/ppermute | solution.py:659
  2.0 1.1 copy-start.14
  5.5 29.2 %collective-permute-start = (bf16[256,1152]{1,0:T(8,128)(2,1)S(1)}, bf16[256,1152]{1,0:T(8,128)(2,1)S(1)}, u32[]{:S(2)}, u32[]{:S(2)}) collective-permute-start(bf16[256,1152]{1,0:T(8,128)(2,1)S(1)} %get-tuple-element.205.refs_1_), channel_id=1, source_target_pairs={{0,2},{1,3},{2,0},{3,1},{4,6},{5,7},{6,4},{7,5},{8,10},{9,11},{10,... | collective-permute-start | bytes 1769480 | tf_op jit(solution)/shard_map/ppermute | solution.py:663
  8.6 28.6 %collective-permute-start.1 = (bf16[256,1152]{1,0:T(8,128)(2,1)S(1)}, bf16[256,1152]{1,0:T(8,128)(2,1)S(1)}, u32[]{:S(2)}, u32[]{:S(2)}) collective-permute-start(bf16[256,1152]{1,0:T(8,128)(2,1)S(1)} %get-tuple-element.205.refs_1_), channel_id=1, source_target_pairs={{0,4},{1,5},{2,6},{3,7},{4,0},{5,1},{6,2},{7,3},{8,12},{9,13},{10,... | collective-permute-start | bytes 1769480 | tf_op jit(solution)/shard_map/ppermute | solution.py:667
  11.2 1.1 copy-start.15
  37.2 16.3 %collective-permute-start.4 = (bf16[256,1152]{1,0:T(8,128)(2,1)S(1)}, bf16[256,1152]{1,0:T(8,128)(2,1)S(1)}, u32[]{:S(2)}, u32[]{:S(2)}) collective-permute-start(bf16[256,1152]{1,0:T(8,128)(2,1)S(1)} %collective-permute-done.1.refs_3_), channel_id=1, source_target_pairs={{0,2},{1,3},{2,0},{3,1},{4,6},{5,7},{6,4},{7,5},{8,10},{9,11},{10,... | collective-permute-start | bytes 1769480 | tf_op jit(solution)/shard_map/ppermute | solution.py:663
  37.7 25.3 %collective-permute-start.2 = (bf16[256,1152]{1,0:T(8,128)(2,1)S(1)}, bf16[256,1152]{1,0:T(8,128)(2,1)S(1)}, u32[]{:S(2)}, u32[]{:S(2)}) collective-permute-start(bf16[256,1152]{1,0:T(8,128)(2,1)S(1)} %get-tuple-element.208.refs_1_), channel_id=1, source_target_pairs={{0,2},{1,3},{2,0},{3,1},{4,6},{5,7},{6,4},{7,5},{8,10},{9,11},{10,... | collective-permute-start | bytes 1769480 | tf_op jit(solution)/shard_map/ppermute | solution.py:663
  39.2 23.7 %collective-permute-start.3 = (bf16[256,1152]{1,0:T(8,128)(2,1)S(1)}, bf16[256,1152]{1,0:T(8,128)(2,1)S(1)}, u32[]{:S(2)}, u32[]{:S(2)}) collective-permute-start(bf16[256,1152]{1,0:T(8,128)(2,1)S(1)} %get-tuple-element.208.refs_1_), channel_id=1, source_target_pairs={{2,4},{3,5},{4,2},{5,3},{10,12},{11,13},{12,10},{13,11},{18,20},{1... | collective-permute-start | bytes 1769480 | tf_op jit(solution)/shard_map/ppermute | solution.py:675
  45.2 11.1 %copy-start.10 = (bf16[256,512]{1,0:T(8,128)(2,1)S(1)}, bf16[256,512]{1,0:T(8,128)(2,1)}, u32[]{:S(2)}) copy-start(bf16[256,512]{1,0:T(8,128)(2,1)} %refs_5_.3) | copy-start | bytes 786436
  45.2 11.1 %copy-start.12 = (bf16[256,512]{1,0:T(8,128)(2,1)S(1)}, bf16[256,512]{1,0:T(8,128)(2,1)}, u32[]{:S(2)}) copy-start(bf16[256,512]{1,0:T(8,128)(2,1)} %refs_6_.1) | copy-start | bytes 786436
  45.2 11.1 %copy-start.22 = (f32[4,512]{1,0:T(4,128)S(1)}, f32[4,512]{1,0:T(4,128)}, u32[]{:S(2)}) copy-start(f32[4,512]{1,0:T(4,128)} %refs_4_.7) | copy-start | bytes 24580
  45.2 11.1 %copy-start.23 = (f32[2,512]{1,0:T(2,128)S(1)}, f32[2,512]{1,0:T(2,128)}, u32[]{:S(2)}) copy-start(f32[2,512]{1,0:T(2,128)} %refs_3_.7) | copy-start | bytes 12292
  54.3 2.0 collective-permute-start.7
  56.8 6.2 %copy-start.7 = (bf16[512,256]{1,0:T(8,128)(2,1)}, bf16[512,256]{1,0:T(8,128)(2,1)S(1)}, u32[]{:S(2)}) copy-start(bf16[512,256]{1,0:T(8,128)(2,1)S(1)} %get-tuple-element.250.refs_1_.refs_3_) | copy-start | bytes 786436
  56.8 6.2 %copy-start.20 = (f32[256,512]{1,0:T(8,128)}, f32[256,512]{1,0:T(8,128)S(1)}, u32[]{:S(2)}) copy-start(f32[256,512]{1,0:T(8,128)S(1)} %get-tuple-element.290.refs_2_) | copy-start | bytes 1572868
  63.8 50.7 %all-to-all-start = ((bf16[4,272,1664]{2,1,0:T(8,128)(2,1)}), bf16[4,272,1664]{2,1,0:T(8,128)(2,1)}, u32[]{:S(2)}, u32[]{:S(2)}) async-start(bf16[4,272,1664]{2,1,0:T(8,128)(2,1)} %get-tuple-element.297), calls=%async_computation | async-start | bytes 7241728 | tf_op jit(solution)/shard_map/all_to_all | solution.py:683
  68.6 20.1 %collective-permute-start.9 = (bf16[256,1152]{1,0:T(8,128)(2,1)S(1)}, bf16[256,1152]{1,0:T(8,128)(2,1)S(1)}, u32[]{:S(2)}, u32[]{:S(2)}) collective-permute-start(bf16[256,1152]{1,0:T(8,128)(2,1)S(1)} %collective-permute-done.2.refs_2_), channel_id=1, source_target_pairs={{2,4},{3,5},{4,2},{5,3},{10,12},{11,13},{12,10},{13,11},{18,20},{1... | collective-permute-start | bytes 1769480 | tf_op jit(solution)/shard_map/ppermute | solution.py:675
  69.3 19.4 %collective-permute-start.8 = (bf16[256,1152]{1,0:T(8,128)(2,1)}, bf16[256,1152]{1,0:T(8,128)(2,1)S(1)}, u32[]{:S(2)}, u32[]{:S(2)}) collective-permute-start(bf16[256,1152]{1,0:T(8,128)(2,1)} %copy-done.18), channel_id=1, source_target_pairs={{2,0},{3,1},{4,6},{5,7},{10,8},{11,9},{12,14},{13,15},{18,16},{19,... | collective-permute-start | bytes 1769480 | tf_op jit(solution)/shard_map/ppermute | solution.py:679
  70.6 1.8 collective-permute-start.10
  72.4 1.0 copy-start.8
  74.8 25.8 %collective-permute-start.12 = (bf16[1152,256]{1,0:T(8,128)(2,1)S(1)}, bf16[1152,256]{1,0:T(8,128)(2,1)S(1)}, u32[]{:S(2)}, u32[]{:S(2)}) collective-permute-start(bf16[1152,256]{1,0:T(8,128)(2,1)S(1)} %get-tuple-element.263), channel_id=1, source_target_pairs={{0,2},{1,3},{6,4},{7,5},{8,10},{9,11},{14,12},{15,13},{16,18},{17,... | collective-permute-start | bytes 1769480 | tf_op jit(solution)/shard_map/ppermute | solution.py:671
  80.9 1.0 copy-start.9
  87.6 1.0 copy-start.2
  88.7 24.9 %copy-start.16 = (bf16[1152,256]{1,0:T(8,128)(2,1)}, bf16[1152,256]{1,0:T(8,128)(2,1)S(1)}, u32[]{:S(2)}) copy-start(bf16[1152,256]{1,0:T(8,128)(2,1)S(1)} %get-tuple-element.361.refs_0_) | copy-start | bytes 1769476
  88.7 17.0 %collective-permute-start.11 = (bf16[256,1152]{1,0:T(8,128)(2,1)S(1)}, bf16[256,1152]{1,0:T(8,128)(2,1)S(1)}, u32[]{:S(2)}, u32[]{:S(2)}) collective-permute-start(bf16[256,1152]{1,0:T(8,128)(2,1)S(1)} %collective-permute-done.9.refs_2_), channel_id=1, source_target_pairs={{2,0},{3,1},{4,6},{5,7},{10,8},{11,9},{12,14},{13,15},{18,16},{19,... | collective-permute-start | bytes 1769480 | tf_op jit(solution)/shard_map/ppermute | solution.py:679
  90.0 17.3 %collective-permute-start.14 = (bf16[1152,256]{1,0:T(8,128)(2,1)S(1)}, bf16[1152,256]{1,0:T(8,128)(2,1)S(1)}, u32[]{:S(2)}, u32[]{:S(2)}) collective-permute-start(bf16[1152,256]{1,0:T(8,128)(2,1)S(1)} %get-tuple-element.284.refs_0_), channel_id=1, source_target_pairs={{0,2},{1,3},{6,4},{7,5},{8,10},{9,11},{14,12},{15,13},{16,18},{17,... | collective-permute-start | bytes 1769480 | tf_op jit(solution)/shard_map/ppermute | solution.py:671
  95.3 10.4 %copy-start.19 = (bf16[256,1152]{1,0:T(8,128)(2,1)S(1)}, bf16[256,1152]{1,0:T(8,128)(2,1)}, u32[]{:S(2)}) copy-start(bf16[256,1152]{1,0:T(8,128)(2,1)} %copy-done.18) | copy-start | bytes 1769476
  100.6 8.6 %copy-start.11 = (bf16[256,512]{1,0:T(8,128)(2,1)S(1)}, bf16[256,512]{1,0:T(8,128)(2,1)}, u32[]{:S(2)}) copy-start(bf16[256,512]{1,0:T(8,128)(2,1)} %refs_5_.3) | copy-start | bytes 786436
  100.6 8.6 %copy-start.13 = (bf16[256,512]{1,0:T(8,128)(2,1)S(1)}, bf16[256,512]{1,0:T(8,128)(2,1)}, u32[]{:S(2)}) copy-start(bf16[256,512]{1,0:T(8,128)(2,1)} %refs_6_.1) | copy-start | bytes 786436
  100.6 8.6 %copy-start.21 = (f32[256,512]{1,0:T(8,128)S(1)}, f32[256,512]{1,0:T(8,128)}, u32[]{:S(2)}) copy-start(f32[256,512]{1,0:T(8,128)} %copy-done.20) | copy-start | bytes 1572868
  100.8 12.8 %collective-permute-start.16 = (bf16[1152,256]{1,0:T(8,128)(2,1)S(1)}, bf16[1152,256]{1,0:T(8,128)(2,1)S(1)}, u32[]{:S(2)}, u32[]{:S(2)}) collective-permute-start(bf16[1152,256]{1,0:T(8,128)(2,1)S(1)} %get-tuple-element.299), channel_id=1, source_target_pairs={{2,4},{3,5},{4,2},{5,3},{10,12},{11,13},{12,10},{13,11},{18,20},{1... | collective-permute-start | bytes 1769480 | tf_op jit(solution)/shard_map/ppermute | solution.py:675
  107.2 2.0 collective-permute-start.13
  107.4 6.1 %copy-start.34 = (bf16[1152,256]{1,0:T(8,128)(2,1)}, bf16[1152,256]{1,0:T(8,128)(2,1)S(1)}, u32[]{:S(2)}) copy-start(bf16[1152,256]{1,0:T(8,128)(2,1)S(1)} %get-tuple-element.324) | copy-start | bytes 1769476
  110.5 3.0 %copy-start = (bf16[512,512]{1,0:T(8,128)(2,1)}, bf16[512,512]{1,0:T(8,128)(2,1)S(1)}, u32[]{:S(2)}) copy-start(bf16[512,512]{1,0:T(8,128)(2,1)S(1)} %get-tuple-element.318.refs_0_.refs_1_) | copy-start | bytes 1572868
  114.5 6.7 %collective-permute-start.17 = (bf16[4,272,1664]{2,1,0:T(8,128)(2,1)}, bf16[4,272,1664]{2,1,0:T(8,128)(2,1)}, u32[]{:S(2)}, u32[]{:S(2)}) collective-permute-start(bf16[4,272,1664]{2,1,0:T(8,128)(2,1)} %all-to-all-done.refs_1_.refs_3_.refs_0_), channel_id=1, source_target_pairs={{0,1},{1,0},{2,3},{3,2},{4,5},{5,4},{6,7},{7,6},{8,9},{9,8},{10,11... | collective-permute-start | bytes 10862600 | tf_op jit(solution)/shard_map/ppermute | solution.py:659
  114.6 4.9 %copy-start.5 = (bf16[512,256]{1,0:T(8,128)(2,1)S(1)}, bf16[512,256]{1,0:T(8,128)(2,1)}, u32[]{:S(2)}) copy-start(bf16[512,256]{1,0:T(8,128)(2,1)} %copy-done.4) | copy-start | bytes 786436
  114.6 14.5 %copy-start.1 = (bf16[512,512]{1,0:T(8,128)(2,1)S(1)}, bf16[512,512]{1,0:T(8,128)(2,1)}, u32[]{:S(2)}) copy-start(bf16[512,512]{1,0:T(8,128)(2,1)} %copy-done) | copy-start | bytes 1572868
  114.6 68.8 %all-to-all-start.1 = ((bf16[4,272,1664]{2,1,0:T(8,128)(2,1)}), bf16[4,272,1664]{2,1,0:T(8,128)(2,1)}, u32[]{:S(2)}, u32[]{:S(2)}) async-start(bf16[4,272,1664]{2,1,0:T(8,128)(2,1)} %get-tuple-element.366), calls=%async_computation.1 | async-start | bytes 7241728 | tf_op jit(solution)/shard_map/all_to_all | solution.py:683
  119.5 1.7 collective-permute-start.15
  120.0 25.5 %collective-permute-start.21 = (bf16[1152,256]{1,0:T(8,128)(2,1)}, bf16[1152,256]{1,0:T(8,128)(2,1)S(1)}, u32[]{:S(2)}, u32[]{:S(2)}) collective-permute-start(bf16[1152,256]{1,0:T(8,128)(2,1)} %copy-done.34), channel_id=1, source_target_pairs={{2,4},{3,5},{4,2},{5,3},{10,12},{11,13},{12,10},{13,11},{18,20},{1... | collective-permute-start | bytes 1769480 | tf_op jit(solution)/shard_map/ppermute | solution.py:675
  122.0 23.4 %collective-permute-start.20 = (bf16[1152,256]{1,0:T(8,128)(2,1)S(1)}, bf16[1152,256]{1,0:T(8,128)(2,1)S(1)}, u32[]{:S(2)}, u32[]{:S(2)}) collective-permute-start(bf16[1152,256]{1,0:T(8,128)(2,1)S(1)} %get-tuple-element.323), channel_id=1, source_target_pairs={{0,2},{1,3},{6,4},{7,5},{8,10},{9,11},{14,12},{15,13},{16,18},{17,... | collective-permute-start | bytes 1769480 | tf_op jit(solution)/shard_map/ppermute | solution.py:671
  129.2 23.1 %collective-permute-start.19 = (bf16[512,512]{1,0:T(8,128)(2,1)S(1)}, bf16[512,512]{1,0:T(8,128)(2,1)S(1)}, u32[]{:S(2)}, u32[]{:S(2)}) collective-permute-start(bf16[512,512]{1,0:T(8,128)(2,1)S(1)} %copy-done.1), channel_id=1, source_target_pairs={{2,4},{3,5},{4,2},{5,3},{10,12},{11,13},{12,10},{13,11},{18,20},{1... | collective-permute-start | bytes 1572872 | tf_op jit(solution)/shard_map/ppermute | solution.py:675
  129.9 24.2 %collective-permute-start.18 = (bf16[512,512]{1,0:T(8,128)(2,1)S(1)}, bf16[512,512]{1,0:T(8,128)(2,1)S(1)}, u32[]{:S(2)}, u32[]{:S(2)}) collective-permute-start(bf16[512,512]{1,0:T(8,128)(2,1)S(1)} %copy-done.1), channel_id=1, source_target_pairs={{0,2},{1,3},{2,0},{3,1},{4,6},{5,7},{6,4},{7,5},{8,10},{9,11},{10,... | collective-permute-start | bytes 1572872 | tf_op jit(solution)/shard_map/ppermute | solution.py:663
  138.1 1.0 copy-start.3
  139.1 11.8 %copy-start.33 = (bf16[1152,256]{1,0:T(8,128)(2,1)S(1)}, bf16[1152,256]{1,0:T(8,128)(2,1)}, u32[]{:S(2)}) copy-start(bf16[1152,256]{1,0:T(8,128)(2,1)} %copy-done.32) | copy-start | bytes 1769476
  139.1 40.2 %copy-start.17 = (bf16[1152,256]{1,0:T(8,128)(2,1)S(1)}, bf16[1152,256]{1,0:T(8,128)(2,1)}, u32[]{:S(2)}) copy-start(bf16[1152,256]{1,0:T(8,128)(2,1)} %copy-done.16) | copy-start | bytes 1769476
  145.4 36.1 %copy-start.35 = (bf16[1152,256]{1,0:T(8,128)(2,1)}, bf16[1152,256]{1,0:T(8,128)(2,1)S(1)}, u32[]{:S(2)}) copy-start(bf16[1152,256]{1,0:T(8,128)(2,1)S(1)} %collective-permute-done.21.refs_5_) | copy-start | bytes 1769476
  145.6 11.2 %collective-permute-start.26 = (bf16[1152,256]{1,0:T(8,128)(2,1)S(1)}, bf16[1152,256]{1,0:T(8,128)(2,1)S(1)}, u32[]{:S(2)}, u32[]{:S(2)}) collective-permute-start(bf16[1152,256]{1,0:T(8,128)(2,1)S(1)} %get-tuple-element.344), channel_id=1, source_target_pairs={{2,4},{3,5},{4,2},{5,3},{10,12},{11,13},{12,10},{13,11},{18,20},{1... | collective-permute-start | bytes 1769480 | tf_op jit(solution)/shard_map/ppermute | solution.py:675
  146.3 19.2 %collective-permute-start.25 = (bf16[1152,256]{1,0:T(8,128)(2,1)S(1)}, bf16[1152,256]{1,0:T(8,128)(2,1)S(1)}, u32[]{:S(2)}, u32[]{:S(2)}) collective-permute-start(bf16[1152,256]{1,0:T(8,128)(2,1)S(1)} %get-tuple-element.343.refs_0_), channel_id=1, source_target_pairs={{0,2},{1,3},{6,4},{7,5},{8,10},{9,11},{14,12},{15,13},{16,18},{17,... | collective-permute-start | bytes 1769480 | tf_op jit(solution)/shard_map/ppermute | solution.py:671
  150.9 18.2 %collective-permute-start.24 = (bf16[1152,256]{1,0:T(8,128)(2,1)S(1)}, bf16[1152,256]{1,0:T(8,128)(2,1)S(1)}, u32[]{:S(2)}, u32[]{:S(2)}) collective-permute-start(bf16[1152,256]{1,0:T(8,128)(2,1)S(1)} %copy-done.33), channel_id=1, source_target_pairs={{2,0},{3,1},{4,6},{5,7},{10,8},{11,9},{12,14},{13,15},{18,16},{19,... | collective-permute-start | bytes 1769480 | tf_op jit(solution)/shard_map/ppermute | solution.py:679
  154.1 20.3 %collective-permute-start.23 = (bf16[512,512]{1,0:T(8,128)(2,1)S(1)}, bf16[512,512]{1,0:T(8,128)(2,1)}, u32[]{:S(2)}, u32[]{:S(2)}) collective-permute-start(bf16[512,512]{1,0:T(8,128)(2,1)S(1)} %collective-permute-done.18.refs_1_.refs_2_), channel_id=1, source_target_pairs={{2,4},{3,5},{4,2},{5,3},{10,12},{11,13},{12,10},{13,11},{18,20},{1... | collective-permute-start | bytes 1572872 | tf_op jit(solution)/shard_map/ppermute | solution.py:675
  155.5 23.8 %collective-permute-start.22 = (bf16[512,512]{1,0:T(8,128)(2,1)S(1)}, bf16[512,512]{1,0:T(8,128)(2,1)S(1)}, u32[]{:S(2)}, u32[]{:S(2)}) collective-permute-start(bf16[512,512]{1,0:T(8,128)(2,1)S(1)} %collective-permute-done.19.refs_2_), channel_id=1, source_target_pairs={{2,0},{3,1},{4,6},{5,7},{10,8},{11,9},{12,14},{13,15},{18,16},{19,... | collective-permute-start | bytes 1572872 | tf_op jit(solution)/shard_map/ppermute | solution.py:679
  169.1 13.8 %copy-start.36 = (bf16[1152,256]{1,0:T(8,128)(2,1)}, bf16[1152,256]{1,0:T(8,128)(2,1)S(1)}, u32[]{:S(2)}) copy-start(bf16[1152,256]{1,0:T(8,128)(2,1)S(1)} %collective-permute-done.24.refs_6_) | copy-start | bytes 1769476
  169.1 20.9 %collective-permute-start.29 = (bf16[1152,256]{1,0:T(8,128)(2,1)S(1)}, bf16[1152,256]{1,0:T(8,128)(2,1)}, u32[]{:S(2)}, u32[]{:S(2)}) collective-permute-start(bf16[1152,256]{1,0:T(8,128)(2,1)S(1)} %get-tuple-element.363.refs_0_), channel_id=1, source_target_pairs={{0,2},{1,3},{6,4},{7,5},{8,10},{9,11},{14,12},{15,13},{16,18},{17,... | collective-permute-start | bytes 1769480 | tf_op jit(solution)/shard_map/ppermute | solution.py:671
  171.7 18.4 %collective-permute-start.31 = (bf16[1152,256]{1,0:T(8,128)(2,1)}, bf16[1152,256]{1,0:T(8,128)(2,1)}, u32[]{:S(2)}, u32[]{:S(2)}) collective-permute-start(bf16[1152,256]{1,0:T(8,128)(2,1)} %get-tuple-element.365), channel_id=1, source_target_pairs={{2,4},{3,5},{4,2},{5,3},{10,12},{11,13},{12,10},{13,11},{18,20},{1... | collective-permute-start | bytes 1769480 | tf_op jit(solution)/shard_map/ppermute | solution.py:675
  173.1 18.9 %collective-permute-start.30 = (bf16[1152,256]{1,0:T(8,128)(2,1)}, bf16[1152,256]{1,0:T(8,128)(2,1)}, u32[]{:S(2)}, u32[]{:S(2)}) collective-permute-start(bf16[1152,256]{1,0:T(8,128)(2,1)} %get-tuple-element.364), channel_id=1, source_target_pairs={{2,0},{3,1},{4,6},{5,7},{10,8},{11,9},{12,14},{13,15},{18,16},{19,... | collective-permute-start | bytes 1769480 | tf_op jit(solution)/shard_map/ppermute | solution.py:679
  179.3 22.6 %collective-permute-start.28 = (bf16[1152,256]{1,0:T(8,128)(2,1)S(1)}, bf16[1152,256]{1,0:T(8,128)(2,1)}, u32[]{:S(2)}, u32[]{:S(2)}) collective-permute-start(bf16[1152,256]{1,0:T(8,128)(2,1)S(1)} %copy-done.17), channel_id=1, source_target_pairs={{0,2},{1,3},{6,4},{7,5},{8,10},{9,11},{14,12},{15,13},{16,18},{17,... | collective-permute-start | bytes 1769480 | tf_op jit(solution)/shard_map/ppermute | solution.py:671
  181.6 20.3 %collective-permute-start.27 = (bf16[512,512]{1,0:T(8,128)(2,1)}, bf16[512,512]{1,0:T(8,128)(2,1)}, u32[]{:S(2)}, u32[]{:S(2)}) collective-permute-start(bf16[512,512]{1,0:T(8,128)(2,1)} %collective-permute-done.23.refs_2_), channel_id=1, source_target_pairs={{2,0},{3,1},{4,6},{5,7},{10,8},{11,9},{12,14},{13,15},{18,16},{19,... | collective-permute-start | bytes 1572872 | tf_op jit(solution)/shard_map/ppermute | solution.py:679
  185.1 7.0 %copy-start.26 = (s32[2,36]{1,0:T(2,128)S(1)}, s32[2,36]{1,0:T(2,128)}, u32[]{:S(2)}) copy-start(s32[2,36]{1,0:T(2,128)} %refs_1_.11) | copy-start | bytes 868
  185.1 7.0 %copy-start.29 = (s32[256]{0:T(256)S(1)}, s32[256]{0:T(256)}, u32[]{:S(2)}) copy-start(s32[256]{0:T(256)} %param.13) | copy-start | bytes 3076
  203.5 12.5 %collective-permute-start.34 = (bf16[4,272,1664]{2,1,0:T(8,128)(2,1)}, bf16[4,272,1664]{2,1,0:T(8,128)(2,1)S(1)}, u32[]{:S(2)}, u32[]{:S(2)}) collective-permute-start(bf16[4,272,1664]{2,1,0:T(8,128)(2,1)} %all-to-all-done.1.refs_1_.refs_2_), channel_id=1, source_target_pairs={{0,1},{1,0},{2,3},{3,2},{4,5},{5,4},{6,7},{7,6},{8,9},{9,8},{10,11... | collective-permute-start | bytes 10862600 | tf_op jit(solution)/shard_map/ppermute | solution.py:659
  203.8 7.3 %collective-permute-start.32 = (bf16[1024,512]{1,0:T(8,128)(2,1)S(1)}, bf16[1024,512]{1,0:T(8,128)(2,1)S(1)}, u32[]{:S(2)}, u32[]{:S(2)}) collective-permute-start(bf16[1024,512]{1,0:T(8,128)(2,1)S(1)} %get-tuple-element.383), channel_id=1, source_target_pairs={{0,1},{1,0},{2,3},{3,2},{4,5},{5,4},{6,7},{7,6},{8,9},{9,8},{10,11... | collective-permute-start | bytes 3145736 | tf_op jit(solution)/shard_map/ppermute | solution.py:659
  204.3 8.6 %collective-permute-start.33 = (bf16[1024,512]{1,0:T(8,128)(2,1)S(1)}, bf16[1024,512]{1,0:T(8,128)(2,1)S(1)}, u32[]{:S(2)}, u32[]{:S(2)}) collective-permute-start(bf16[1024,512]{1,0:T(8,128)(2,1)S(1)} %get-tuple-element.384), channel_id=1, source_target_pairs={{0,1},{1,0},{2,3},{3,2},{4,5},{5,4},{6,7},{7,6},{8,9},{9,8},{10,11... | collective-permute-start | bytes 3145736 | tf_op jit(solution)/shard_map/ppermute | solution.py:659
  (10 other events, 7.3 us)

commit v7 on v6

--- a/solution.py
+++ b/solution.py
@@ -174,25 +174,33 @@
     return go
 
 
-def marks_of(marks, where, cols, chunk):
-    position = (where[8] * cols + chunk * LANES) // CH
+def marks_of(marks, place, cols, chunk):
+    position = (place * cols + chunk * LANES) // CH
     return marks[0, position], marks[1, position]
 
 
-def mask_kernel(where, marks, group, image, out):
+def mask_kernel(place, marks, group, image, out, held, sem):
     rows, cols = image.shape
+    copy = pltpu.make_async_copy(image, held, sem)
+    copy.start()
     second = jnp.broadcast_to(jnp.where(group[...] == 1, 1.0, 0.0), (8, rows)).T[:, 0:1] > 0.5
+    copy.wait()
     for chunk in range(cols // LANES):
-        zero, one = marks_of(marks, where, cols, chunk)
+        zero, one = marks_of(marks, place[0], cols, chunk)
         keep = wide(jnp.where(second, one, zero))
         lanes = slice(chunk * LANES, (chunk + 1) * LANES)
-        out[:, lanes] = low(wide(image[:, lanes]) * keep)
-
-
-def mask_image(where, marks, group, image):
-    return call(
-        mask_kernel, array(image.shape, jnp.bfloat16), [SMEM, SMEM, VMEM, VMEM], VMEM, "mask_image"
-    )(where, marks, group, image)
+        out[:, lanes] = low(wide(held[:, lanes]) * keep)
+
+
+def mask_image(place, marks, group, image):
+    return call(
+        mask_kernel,
+        array(image.shape, jnp.bfloat16),
+        [SMEM, SMEM, VMEM, HBM],
+        VMEM,
+        "mask_image",
+        [pltpu.VMEM(image.shape, jnp.bfloat16), pltpu.SemaphoreType.DMA],
+    )(place, marks, group, in_hbm(image))
 
 
 def in_hbm(x):
@@ -475,7 +483,7 @@
     for copy in copies:
         copy.wait()
     for chunk in range(cols // LANES):
-        zero, one = marks_of(marks, where, cols, chunk)
+        zero, one = marks_of(marks, where[8], cols, chunk)
         keep = wide(jnp.where(second, one, zero))
         rows = slice(chunk * LANES, (chunk + 1) * LANES)
         total = own[rows, :] + wide(held[0, rows, :])
@@ -546,7 +554,8 @@
 def weight_kernel(sides, where, *refs):
     n = len(sides)
     images_of, dz_of = refs[:n], refs[n]
-    before, (out, images, dzs, tiles, sems) = refs[n + 1 : -5], refs[-5:]
+    *outs, images, dzs, tiles, sems = refs[n + 1 + (sides == (1,)) :]
+    out = outs[0]
     rows, units = dzs.shape[1:]
     cols = images.shape[3]
     tile = tiles.shape[1]
@@ -577,6 +586,9 @@
     for i in range(n):
         for q in range(4):
             block(i, q).wait()
+        if len(outs) > 1:
+            for q in range(4):
+                pltpu.make_async_copy(images.at[i, q], outs[1].at[q], sems.at[4 + q]).start()
         for t in range(steps):
             total = None
             for q in range(4):
@@ -592,17 +604,23 @@
     for i in range(n):
         for t in range(steps):
             give(i, t).wait()
+    if len(outs) > 1:
+        for q in range(4):
+            pltpu.make_async_copy(images.at[0, q], outs[1].at[q], sems.at[4 + q]).wait()
 
 
 def weight_grad(sides, rows, cols, where, images, dz, *before):
     units = dz.shape[2] - cols
     tile = cols // 3
     n = len(sides)
+    outs = [pltpu.HBM((2 * cols, units), jnp.float32)]
+    if sides == (0,):
+        outs.append(pltpu.HBM((4, rows, cols), jnp.bfloat16))
     return call(
         functools.partial(weight_kernel, sides),
-        pltpu.HBM((2 * cols, units), jnp.float32),
+        outs if len(outs) > 1 else outs[0],
         [SMEM] + [ANY] * (n + 1) + [HBM] * len(before),
-        HBM,
+        [HBM] * len(outs) if len(outs) > 1 else HBM,
         "weight_grad",
         [
             pltpu.VMEM((n, 4, rows, cols), jnp.bfloat16),
@@ -713,10 +731,10 @@
 
     whole_a = swap(weight_a)
     whole_b = swap(weight_b)
-    a0 = mask_image(where, position_mask, group, image_a)
+    a0 = mask_image(place[None], position_mask, group, image_a)
     a2 = send(across, a0)
     a1 = send(along, a0)
-    b0 = mask_image(where, position_mask, group, image_b)
+    b0 = mask_image(place[None], position_mask, group, image_b)
     a1, a2 = wait(a1, a2)
     a3 = send(along, a2)
     b_mid = send(between, b0)
@@ -824,14 +842,16 @@
     s2 = choose(where, s_end, s_mid2)
     got_b = wait(got_b)
     grad_bias, grad_stitch = total_sums(rows, cols, got_a, got_b)
-    half_b = weight_grad((0,), rows, cols, where, (got_b,), got_b)
+    half_b, block_b = weight_grad((0,), rows, cols, where, (got_b,), got_b)
     in3_b, out_b, cross2_b = wait(in3_b, out_b, cross2_b)
     grad_image_b = finish(where, position_mask, group, kept_b, in3_b, cross2_b, out_b)
     s_end2, in3_a = wait(s_end2, in3_a)
     s3 = choose(where, s_end2, s_mid)
-    far_b = send(swap, got_b)
-    far_high = send(swap, join(s2, s3))
-    far_low = send(swap, join(local, s1))
+    high = join(s2, s3)
+    low_half = join(local, s1)
+    far_high = send(swap, high)
+    far_low = send(swap, low_half)
+    far_b = send(swap, block_b)
     grad_image_a = finish(where, position_mask, group, kept_a, in3_a, cross2_a, out_a)
     stitched_a, stitched_b = lay_out(where, local, s1, s2, s3, far_low, far_high)
     grad_weight_b = weight_grad((1,), rows, cols, where, (far_b,), got_b, half_b)

time: 222 us -> 219 us (0.986)
  waiting for transfers between devices: 74 us -> 71 us
  local copies, waits for them, and re-layouts: 13.5 us -> 10.6 us
    unnamed x74 -> x72, local copies, waits for them, and re-layouts: 13.4 us -> 10.5 us
  transfers between devices with their start and end apart: 37 -> 37, of which waited for: 17 -> 17; matrix products, arithmetic and copies ran while one was open for 0% -> 0% of each run, Pallas kernels for 28% -> 29%
where the time goes in v7:
time: 219 us; the launch traced here: 218 us
  waiting for transfers between devices  71 us (32%)
  Pallas kernels  70 us (32%)
  starting transfers between devices  63.9 us (29%)
  local copies, waits for them, and re-layouts  10.6 us (5%)
    pallas_call x33, Pallas kernels, go(): *results, line.token = run(*operands, *before)  70 us
    ppermute x4, waiting for transfers between devices, along(): return lax.ppermute(x, 'mp', NEAR_Z)  31.3 us
    ppermute x6, starting transfers between devices, inward(): return lax.ppermute(x, 'mp', ENDS_IN)  27.2 us
    ppermute x6, waiting for transfers between devices, outward(): return lax.ppermute(x, 'mp', ENDS_OUT)  20 us
    unnamed x72, local copies, waits for them, and re-layouts  10.5 us
    all_to_all x2, starting transfers between devices, exchange(): return lax.all_to_all(x, 'dp', 0, 0)  9.74 us
    ppermute x10, waiting for transfers between devices, swap(): return lax.ppermute(x, 'mp', SWAP_CORE)  9.41 us
    ppermute x8, starting transfers between devices, between(): return lax.ppermute(x, 'mp', MIDS)  8.02 us
  transfers between devices with their start and end apart: 37, of which 17 were waited for; matrix products, arithmetic and copies ran while one was open for 0% of the time, Pallas kernels for 29%

profile of v7, /device:TPU:0, one launch (start us, length us, event | category | flops | bytes accessed | tf_op | source)
XLA Modules:
  0.0 217.7 jit_solution(8439939212916697061)
XLA Ops:
  2.6 2.0 mask_image.2
  4.6 3.1 %collective-permute-start = (bf16[256,1152]{1,0:T(8,128)(2,1)S(1)}, bf16[256,1152]{1,0:T(8,128)(2,1)S(1)}, u32[]{:S(2)}, u32[]{:S(2)}) collective-permute-start(bf16[256,1152]{1,0:T(8,128)(2,1)S(1)} %get-tuple-element.210.refs_1_), channel_id=1, source_target_pairs={{0,2},{1,3},{2,0},{3,1},{4,6},{5,7},{6,4},{7,5},{8,10},{9,11},{10,... | collective-permute-start | bytes 1769480 | tf_op jit(solution)/shard_map/ppermute | solution.py:681
  7.7 2.6 %collective-permute-start.1 = (bf16[256,1152]{1,0:T(8,128)(2,1)S(1)}, bf16[256,1152]{1,0:T(8,128)(2,1)S(1)}, u32[]{:S(2)}, u32[]{:S(2)}) collective-permute-start(bf16[256,1152]{1,0:T(8,128)(2,1)S(1)} %get-tuple-element.210.refs_1_), channel_id=1, source_target_pairs={{0,4},{1,5},{2,6},{3,7},{4,0},{5,1},{6,2},{7,3},{8,12},{9,13},{10,... | collective-permute-start | bytes 1769480 | tf_op jit(solution)/shard_map/ppermute | solution.py:685
  11.6 2.0 mask_image.3
  13.6 20.1 %collective-permute-done.refs_2_ = bf16[256,1152]{1,0:T(8,128)(2,1)S(1)} collective-permute-done((bf16[256,1152]{1,0:T(8,128)(2,1)S(1)}, bf16[256,1152]{1,0:T(8,128)(2,1)S(1)}, u32[]{:S(2)}, u32[]{:S(2)}) %collective-permute-start) | collective-permute-done | bytes 589856 | tf_op jit(solution)/shard_map/ppermute | solution.py:681
  33.8 2.5 %collective-permute-done.1.refs_3_ = bf16[256,1152]{1,0:T(8,128)(2,1)S(1)} collective-permute-done((bf16[256,1152]{1,0:T(8,128)(2,1)S(1)}, bf16[256,1152]{1,0:T(8,128)(2,1)S(1)}, u32[]{:S(2)}, u32[]{:S(2)}) %collective-permute-start.1) | collective-permute-done | bytes 589856 | tf_op jit(solution)/shard_map/ppermute | solution.py:685
  36.7 1.6 collective-permute-start.2
  38.3 1.5 collective-permute-start.3
  40.6 5.3 %forward_open.2 = (f32[256,512]{1,0:T(8,128)S(1)}, f32[256,512]{1,0:T(8,128)S(1)}, bf16[2,1152,512]{2,1,0:T(8,128)(2,1)S(1)}, bf16[2,1152,512]{2,1,0:T(8,128)(2,1)S(1)}, f32[8,128]{1,0:T(8,128)S(1)}) custom-call(s32[9]{0:T(128)S(1)} %concatenate.3.refs_0_, bf16[256,1152]{1,0:T(8,128)(2,1)S(1)} %get-tuple-element.210.refs_1_, ...), custom_call_target="tpu_custom_call" | custom-call | flops 1 | bytes 1 | tf_op jit(solution)/shard_map/forward_open/pallas_call | solution.py:171
  45.9 6.7 %collective-permute-done.4.refs_0_.refs_4_ = bf16[256,1152]{1,0:T(8,128)(2,1)S(1)} collective-permute-done((bf16[256,1152]{1,0:T(8,128)(2,1)S(1)}, bf16[256,1152]{1,0:T(8,128)(2,1)S(1)}, u32[]{:S(2)}, u32[]{:S(2)}) %collective-permute-start.4) | collective-permute-done | bytes 589856 | tf_op jit(solution)/shard_map/ppermute | solution.py:681
  52.5 0.8 forward_close.2
  53.5 1.9 collective-permute-done.7.refs_1_
  55.9 2.9 %pack.2 = (bf16[4,272,1664]{2,1,0:T(8,128)(2,1)}, f32[8,128]{1,0:T(8,128)S(1)}) custom-call(s32[9]{0:T(128)S(1)} %concatenate.3.refs_0_, bf16[256,1152]{1,0:T(8,128)(2,1)S(1)} %get-tuple-element.210.refs_1_, bf16[256,1152]{1,0:T(8,128)(2,1)S(1)} %collective-permute-done.refs_2_, bf16[256,1152]{1,0:T(8,128)(2,1)S(1)} %collective-permute-done.1.refs_3_, ...), custom_call_target="tpu_custom_call" | custom-call | flops 1 | bytes 1 | tf_op jit(solution)/shard_map/pack/pallas_call | solution.py:171
  59.3 2.7 %collective-permute-done.2.refs_2_ = bf16[256,1152]{1,0:T(8,128)(2,1)S(1)} collective-permute-done((bf16[256,1152]{1,0:T(8,128)(2,1)S(1)}, bf16[256,1152]{1,0:T(8,128)(2,1)S(1)}, u32[]{:S(2)}, u32[]{:S(2)}) %collective-permute-start.2) | collective-permute-done | bytes 589856 | tf_op jit(solution)/shard_map/ppermute | solution.py:681
  62.1 4.9 %all-to-all-start = ((bf16[4,272,1664]{2,1,0:T(8,128)(2,1)}), bf16[4,272,1664]{2,1,0:T(8,128)(2,1)}, u32[]{:S(2)}, u32[]{:S(2)}) async-start(bf16[4,272,1664]{2,1,0:T(8,128)(2,1)} %get-tuple-element.302), calls=%async_computation | async-start | bytes 7241728 | tf_op jit(solution)/shard_map/all_to_all | solution.py:701
  67.7 1.3 collective-permute-start.8
  69.1 1.7 collective-permute-done.10.refs_2_.refs_4_
  70.8 0.9 copy-done.10
  73.2 6.1 %collective-permute-start.12 = (bf16[1152,256]{1,0:T(8,128)(2,1)S(1)}, bf16[1152,256]{1,0:T(8,128)(2,1)S(1)}, u32[]{:S(2)}, u32[]{:S(2)}) collective-permute-start(bf16[1152,256]{1,0:T(8,128)(2,1)S(1)} %get-tuple-element.268), channel_id=1, source_target_pairs={{0,2},{1,3},{6,4},{7,5},{8,10},{9,11},{14,12},{15,13},{16,18},{17,... | collective-permute-start | bytes 1769480 | tf_op jit(solution)/shard_map/ppermute | solution.py:689
  79.3 0.9 copy-done.11
  80.3 5.8 %parts.2 = (bf16[1152,256]{1,0:T(8,128)(2,1)S(1)}, bf16[1152,256]{1,0:T(8,128)(2,1)S(1)}, f32[1152,256]{1,0:T(8,128)S(1)}, f32[8,128]{1,0:T(8,128)S(1)}) custom-call(s32[9]{0:T(128)S(1)} %concatenate.3.refs_0_, bf16[9216,512]{1,0:T(8,128)(2,1)} %refs_1_.8, bf16[9216,512]{1,0:T(8,128)(2,1)} %collective-permute-done.5.refs_5_.refs_2_, ...), custom_call_target="tpu_custom_call" | custom-call | flops 1 | bytes 1 | tf_op jit(solution)/shard_map/parts/pallas_call | solution.py:171
  86.1 1.0 copy-done.4
  87.1 1.3 collective-permute-start.11
  88.4 4.6 %collective-permute-start.14 = (bf16[1152,256]{1,0:T(8,128)(2,1)S(1)}, bf16[1152,256]{1,0:T(8,128)(2,1)S(1)}, u32[]{:S(2)}, u32[]{:S(2)}) collective-permute-start(bf16[1152,256]{1,0:T(8,128)(2,1)S(1)} %get-tuple-element.289.refs_0_), channel_id=1, source_target_pairs={{0,2},{1,3},{6,4},{7,5},{8,10},{9,11},{14,12},{15,13},{16,18},{17,... | collective-permute-start | bytes 1769480 | tf_op jit(solution)/shard_map/ppermute | solution.py:689
  93.7 5.3 %forward_open.3 = (f32[256,512]{1,0:T(8,128)S(1)}, f32[256,512]{1,0:T(8,128)S(1)}, bf16[2,1152,512]{2,1,0:T(8,128)(2,1)S(1)}, bf16[2,1152,512]{2,1,0:T(8,128)(2,1)S(1)}, f32[8,128]{1,0:T(8,128)S(1)}) custom-call(s32[9]{0:T(128)S(1)} %concatenate.3.refs_0_, bf16[256,1152]{1,0:T(8,128)(2,1)S(1)} %get-tuple-element.213.refs_1_, ...), custom_call_target="tpu_custom_call" | custom-call | flops 1 | bytes 1 | tf_op jit(solution)/shard_map/forward_open/pallas_call | solution.py:171
  99.2 0.8 collective-permute-start.16
  100.0 4.1 %collective-permute-done.11.refs_1_ = bf16[256,1152]{1,0:T(8,128)(2,1)S(1)} collective-permute-done((bf16[256,1152]{1,0:T(8,128)(2,1)S(1)}, bf16[256,1152]{1,0:T(8,128)(2,1)S(1)}, u32[]{:S(2)}, u32[]{:S(2)}) %collective-permute-start.11) | collective-permute-done | bytes 589856 | tf_op jit(solution)/shard_map/ppermute | solution.py:697
  104.8 0.8 forward_close.3
  105.9 1.7 collective-permute-done.13.refs_1_
  108.9 3.0 %pack.3 = (bf16[4,272,1664]{2,1,0:T(8,128)(2,1)}, f32[8,128]{1,0:T(8,128)S(1)}) custom-call(s32[9]{0:T(128)S(1)} %concatenate.3.refs_0_, bf16[256,1152]{1,0:T(8,128)(2,1)S(1)} %get-tuple-element.213.refs_1_, bf16[256,1152]{1,0:T(8,128)(2,1)S(1)} %collective-permute-done.2.refs_2_, bf16[256,1152]{1,0:T(8,128)(2,1)S(1)} %get-tuple-element.271.refs_3_, ...), custom_call_target="tpu_custom_call" | custom-call | flops 1 | bytes 1 | tf_op jit(solution)/shard_map/pack/pallas_call | solution.py:171
  112.1 0.8 copy-done.30
  113.1 4.9 %all-to-all-start.1 = ((bf16[4,272,1664]{2,1,0:T(8,128)(2,1)}), bf16[4,272,1664]{2,1,0:T(8,128)(2,1)}, u32[]{:S(2)}, u32[]{:S(2)}) async-start(bf16[4,272,1664]{2,1,0:T(8,128)(2,1)} %get-tuple-element.371), calls=%async_computation.1 | async-start | bytes 7241728 | tf_op jit(solution)/shard_map/all_to_all | solution.py:701
  120.5 7.1 %collective-permute-start.20 = (bf16[1152,256]{1,0:T(8,128)(2,1)S(1)}, bf16[1152,256]{1,0:T(8,128)(2,1)S(1)}, u32[]{:S(2)}, u32[]{:S(2)}) collective-permute-start(bf16[1152,256]{1,0:T(8,128)(2,1)S(1)} %get-tuple-element.328), channel_id=1, source_target_pairs={{0,2},{1,3},{6,4},{7,5},{8,10},{9,11},{14,12},{15,13},{16,18},{17,... | collective-permute-start | bytes 1769480 | tf_op jit(solution)/shard_map/ppermute | solution.py:689
  128.3 1.5 collective-permute-start.18
  129.8 0.9 copy-done.8
  130.7 5.8 %parts.3 = (bf16[1152,256]{1,0:T(8,128)(2,1)S(1)}, bf16[1152,256]{1,0:T(8,128)(2,1)S(1)}, f32[1152,256]{1,0:T(8,128)S(1)}, f32[8,128]{1,0:T(8,128)S(1)}) custom-call(s32[9]{0:T(128)S(1)} %concatenate.3.refs_0_, bf16[9216,512]{1,0:T(8,128)(2,1)} %refs_1_.9, bf16[9216,512]{1,0:T(8,128)(2,1)} %collective-permute-done.6.refs_5_.refs_2_, ...), custom_call_target="tpu_custom_call" | custom-call | flops 1 | bytes 1 | tf_op jit(solution)/shard_map/parts/pallas_call | solution.py:171
  136.5 1.0 copy-done.5
  137.5 6.3 %weight_grad.3 = (f32[2304,512]{1,0:T(8,128)}, f32[8,128]{1,0:T(8,128)S(1)}) custom-call(s32[9]{0:T(128)S(1)} %concatenate.3.refs_0_, bf16[4,272,1664]{2,1,0:T(8,128)(2,1)} %all-to-all-done.refs_1_.refs_3_.refs_0_, bf16[4,272,1664]{2,1,0:T(8,128)(2,1)} %collective-permute-done.17.refs_2_, bf16[4,272,1664]{2,1,0:T(8,128)(2,1)} %all-to-all-done.refs_1_.refs_3_.refs_0_, ...), custom_call_target="tpu_custom_call" | custom-call | flops 1 | bytes 1 | tf_op jit(solution)/shard_map/weight_grad/pallas_call | solution.py:171
  144.7 4.6 %collective-permute-start.25 = (bf16[1152,256]{1,0:T(8,128)(2,1)S(1)}, bf16[1152,256]{1,0:T(8,128)(2,1)S(1)}, u32[]{:S(2)}, u32[]{:S(2)}) collective-permute-start(bf16[1152,256]{1,0:T(8,128)(2,1)S(1)} %get-tuple-element.348.refs_0_), channel_id=1, source_target_pairs={{0,2},{1,3},{6,4},{7,5},{8,10},{9,11},{14,12},{15,13},{16,18},{17,... | collective-permute-start | bytes 1769480 | tf_op jit(solution)/shard_map/ppermute | solution.py:689
  149.4 1.3 collective-permute-start.24
  150.7 1.8 collective-permute-done.18.refs_1_.refs_2_
  152.5 1.4 collective-permute-start.23
  153.9 1.3 collective-permute-start.22
  155.2 1.0 add.25
  156.2 7.7 %collective-permute-done.25.refs_1_ = bf16[1152,256]{1,0:T(8,128)(2,1)S(1)} collective-permute-done((bf16[1152,256]{1,0:T(8,128)(2,1)S(1)}, bf16[1152,256]{1,0:T(8,128)(2,1)S(1)}, u32[]{:S(2)}, u32[]{:S(2)}) %collective-permute-start.25) | collective-permute-done | bytes 589856 | tf_op jit(solution)/shard_map/ppermute | solution.py:689
  163.9 0.9 add.26
  164.8 2.7 %collective-permute-done.24.refs_6_ = bf16[1152,256]{1,0:T(8,128)(2,1)S(1)} collective-permute-done((bf16[1152,256]{1,0:T(8,128)(2,1)S(1)}, bf16[1152,256]{1,0:T(8,128)(2,1)S(1)}, u32[]{:S(2)}, u32[]{:S(2)}) %collective-permute-start.24) | collective-permute-done | bytes 589856 | tf_op jit(solution)/shard_map/ppermute | solution.py:697
  167.5 2.5 %collective-permute-start.29 = (bf16[1152,256]{1,0:T(8,128)(2,1)S(1)}, bf16[1152,256]{1,0:T(8,128)(2,1)}, u32[]{:S(2)}, u32[]{:S(2)}) collective-permute-start(bf16[1152,256]{1,0:T(8,128)(2,1)S(1)} %get-tuple-element.368.refs_0_), channel_id=1, source_target_pairs={{0,2},{1,3},{6,4},{7,5},{8,10},{9,11},{14,12},{15,13},{16,18},{17,... | collective-permute-start | bytes 1769480 | tf_op jit(solution)/shard_map/ppermute | solution.py:689
  170.0 1.5 collective-permute-start.31
  171.5 1.3 collective-permute-start.30
  172.8 4.9 %collective-permute-done.22.refs_1_ = bf16[512,512]{1,0:T(8,128)(2,1)S(1)} collective-permute-done((bf16[512,512]{1,0:T(8,128)(2,1)S(1)}, bf16[512,512]{1,0:T(8,128)(2,1)S(1)}, u32[]{:S(2)}, u32[]{:S(2)}) %collective-permute-start.22) | collective-permute-done | bytes 524320 | tf_op jit(solution)/shard_map/ppermute | solution.py:697
  177.7 2.3 %collective-permute-start.28 = (bf16[1152,256]{1,0:T(8,128)(2,1)S(1)}, bf16[1152,256]{1,0:T(8,128)(2,1)}, u32[]{:S(2)}, u32[]{:S(2)}) collective-permute-start(bf16[1152,256]{1,0:T(8,128)(2,1)S(1)} %copy-done.17), channel_id=1, source_target_pairs={{0,2},{1,3},{6,4},{7,5},{8,10},{9,11},{14,12},{15,13},{16,18},{17,... | collective-permute-start | bytes 1769480 | tf_op jit(solution)/shard_map/ppermute | solution.py:689
  180.0 1.3 collective-permute-start.27
  181.9 1.6 total_sums.1
  183.5 4.9 %weight_grad.4 = (f32[2304,512]{1,0:T(8,128)}, bf16[4,256,1152]{2,1,0:T(8,128)(2,1)}, f32[8,128]{1,0:T(8,128)S(1)}) custom-call(s32[9]{0:T(128)S(1)} %concatenate.3.refs_0_, bf16[4,272,1664]{2,1,0:T(8,128)(2,1)} %all-to-all-done.1.refs_1_.refs_2_, bf16[4,272,1664]{2,1,0:T(8,128)(2,1)} %all-to-all-done.1.refs_1_.refs_2_, f32[8,128]{1,0:T(8,128)S(1)} %get-tuple-element.375.refs_3_), custom_call_target="tpu_custom_call" | custom-call | flops 1 | bytes 1 | tf_op jit(solution)/shard_map/weight_grad/pallas_call | solution.py:171
  188.5 2.0 collective-permute-done.30.refs_6_
  190.5 3.5 %finish.2 = (bf16[1152,256]{1,0:T(8,128)(2,1)}, f32[8,128]{1,0:T(8,128)S(1)}) custom-call(s32[9]{0:T(128)S(1)} %concatenate.3.refs_0_, s32[2,36]{1,0:T(2,128)S(1)} %copy-done.24, s32[1,256]{1,0:T(1,128)S(1)} %bitcast.10, f32[1152,256]{1,0:T(8,128)} %copy-done.5, bf16[1152,256]{1,0:T(8,128)(2,1)} %collective-permute-done.29.refs_4_, ...), custom_call_target="tpu_custom_call" | custom-call | flops 1 | bytes 1 | tf_op jit(solution)/shard_map/finish/pallas_call | solution.py:171
  194.0 6.4 %collective-permute-done.27.refs_1_ = bf16[512,512]{1,0:T(8,128)(2,1)} collective-permute-done((bf16[512,512]{1,0:T(8,128)(2,1)}, bf16[512,512]{1,0:T(8,128)(2,1)}, u32[]{:S(2)}, u32[]{:S(2)}) %collective-permute-start.27) | collective-permute-done | bytes 524320 | tf_op jit(solution)/shard_map/ppermute | solution.py:697
  200.3 1.6 choose.7
  202.8 3.5 %finish.3 = (bf16[1152,256]{1,0:T(8,128)(2,1)}, f32[8,128]{1,0:T(8,128)S(1)}) custom-call(s32[9]{0:T(128)S(1)} %concatenate.3.refs_0_, s32[2,36]{1,0:T(2,128)S(1)} %copy-done.24, s32[1,256]{1,0:T(1,128)S(1)} %bitcast.11, f32[1152,256]{1,0:T(8,128)} %copy-done.4, bf16[1152,256]{1,0:T(8,128)(2,1)} %collective-permute-done.28.refs_4_, ...), custom_call_target="tpu_custom_call" | custom-call | flops 1 | bytes 1 | tf_op jit(solution)/shard_map/finish/pallas_call | solution.py:171
  206.2 2.0 collective-permute-done.32.refs_5_
  208.2 1.5 collective-permute-done.33.refs_6_
  209.7 3.1 %lay_out.1 = (bf16[256,4096]{1,0:T(8,128)(2,1)}, bf16[256,4096]{1,0:T(8,128)(2,1)}, f32[8,128]{1,0:T(8,128)S(1)}) custom-call(s32[9]{0:T(128)S(1)} %concatenate.3.refs_0_, bf16[512,512]{1,0:T(8,128)(2,1)S(1)} %copy-done.3, bf16[512,512]{1,0:T(8,128)(2,1)S(1)} %collective-permute-done.18.refs_1_.refs_2_, ...), custom_call_target="tpu_custom_call" | custom-call | flops 1 | bytes 1 | tf_op jit(solution)/shard_map/lay_out/pallas_call | solution.py:171
  212.8 4.8 %weight_grad.5 = (f32[2304,512]{1,0:T(8,128)}, f32[8,128]{1,0:T(8,128)}) custom-call(s32[9]{0:T(128)S(1)} %concatenate.3.refs_0_, bf16[4,256,1152]{2,1,0:T(8,128)(2,1)S(1)} %collective-permute-done.34.refs_1_, bf16[4,272,1664]{2,1,0:T(8,128)(2,1)} %all-to-all-done.1.refs_1_.refs_2_, ...), custom_call_target="tpu_custom_call", output_to_operand_aliasing={{0}: (3, {})} | custom-call | flops 1 | bytes 1 | tf_op jit(solution)/shard_map/weight_grad/pallas_call | solution.py:171
  (117 shorter events, 16.8 us)
Async XLA Ops:
  0.6 39.9 %collective-permute-start.5 = (bf16[9216,512]{1,0:T(8,128)(2,1)}, bf16[9216,512]{1,0:T(8,128)(2,1)}, u32[]{:S(2)}, u32[]{:S(2)}) collective-permute-start(bf16[9216,512]{1,0:T(8,128)(2,1)} %refs_1_.8), channel_id=1, source_target_pairs={{0,1},{1,0},{2,3},{3,2},{4,5},{5,4},{6,7},{7,6},{8,9},{9,8},{10,11... | collective-permute-start | bytes 28311560 | tf_op jit(solution)/shard_map/ppermute | solution.py:677
  1.2 39.4 %collective-permute-start.6 = (bf16[9216,512]{1,0:T(8,128)(2,1)}, bf16[9216,512]{1,0:T(8,128)(2,1)}, u32[]{:S(2)}, u32[]{:S(2)}) collective-permute-start(bf16[9216,512]{1,0:T(8,128)(2,1)} %refs_1_.9), channel_id=1, source_target_pairs={{0,1},{1,0},{2,3},{3,2},{4,5},{5,4},{6,7},{7,6},{8,9},{9,8},{10,11... | collective-permute-start | bytes 28311560 | tf_op jit(solution)/shard_map/ppermute | solution.py:677
  4.6 29.2 %collective-permute-start = (bf16[256,1152]{1,0:T(8,128)(2,1)S(1)}, bf16[256,1152]{1,0:T(8,128)(2,1)S(1)}, u32[]{:S(2)}, u32[]{:S(2)}) collective-permute-start(bf16[256,1152]{1,0:T(8,128)(2,1)S(1)} %get-tuple-element.210.refs_1_), channel_id=1, source_target_pairs={{0,2},{1,3},{2,0},{3,1},{4,6},{5,7},{6,4},{7,5},{8,10},{9,11},{10,... | collective-permute-start | bytes 1769480 | tf_op jit(solution)/shard_map/ppermute | solution.py:681
  7.7 28.6 %collective-permute-start.1 = (bf16[256,1152]{1,0:T(8,128)(2,1)S(1)}, bf16[256,1152]{1,0:T(8,128)(2,1)S(1)}, u32[]{:S(2)}, u32[]{:S(2)}) collective-permute-start(bf16[256,1152]{1,0:T(8,128)(2,1)S(1)} %get-tuple-element.210.refs_1_), channel_id=1, source_target_pairs={{0,4},{1,5},{2,6},{3,7},{4,0},{5,1},{6,2},{7,3},{8,12},{9,13},{10,... | collective-permute-start | bytes 1769480 | tf_op jit(solution)/shard_map/ppermute | solution.py:685
  36.3 16.3 %collective-permute-start.4 = (bf16[256,1152]{1,0:T(8,128)(2,1)S(1)}, bf16[256,1152]{1,0:T(8,128)(2,1)S(1)}, u32[]{:S(2)}, u32[]{:S(2)}) collective-permute-start(bf16[256,1152]{1,0:T(8,128)(2,1)S(1)} %collective-permute-done.1.refs_3_), channel_id=1, source_target_pairs={{0,2},{1,3},{2,0},{3,1},{4,6},{5,7},{6,4},{7,5},{8,10},{9,11},{10,... | collective-permute-start | bytes 1769480 | tf_op jit(solution)/shard_map/ppermute | solution.py:681
  36.7 25.3 %collective-permute-start.2 = (bf16[256,1152]{1,0:T(8,128)(2,1)S(1)}, bf16[256,1152]{1,0:T(8,128)(2,1)S(1)}, u32[]{:S(2)}, u32[]{:S(2)}) collective-permute-start(bf16[256,1152]{1,0:T(8,128)(2,1)S(1)} %get-tuple-element.213.refs_1_), channel_id=1, source_target_pairs={{0,2},{1,3},{2,0},{3,1},{4,6},{5,7},{6,4},{7,5},{8,10},{9,11},{10,... | collective-permute-start | bytes 1769480 | tf_op jit(solution)/shard_map/ppermute | solution.py:681
  38.3 23.7 %collective-permute-start.3 = (bf16[256,1152]{1,0:T(8,128)(2,1)S(1)}, bf16[256,1152]{1,0:T(8,128)(2,1)}, u32[]{:S(2)}, u32[]{:S(2)}) collective-permute-start(bf16[256,1152]{1,0:T(8,128)(2,1)S(1)} %get-tuple-element.213.refs_1_), channel_id=1, source_target_pairs={{2,4},{3,5},{4,2},{5,3},{10,12},{11,13},{12,10},{13,11},{18,20},{1... | collective-permute-start | bytes 1769480 | tf_op jit(solution)/shard_map/ppermute | solution.py:693
  45.8 12.9 %copy-start = (bf16[2,1152,512]{2,1,0:T(8,128)(2,1)}, bf16[2,1152,512]{2,1,0:T(8,128)(2,1)S(1)}, u32[]{:S(2)}) copy-start(bf16[2,1152,512]{2,1,0:T(8,128)(2,1)S(1)} %get-tuple-element.258.refs_0_) | copy-start | bytes 7077892
  45.8 9.5 %copy-start.12 = (bf16[256,512]{1,0:T(8,128)(2,1)S(1)}, bf16[256,512]{1,0:T(8,128)(2,1)}, u32[]{:S(2)}) copy-start(bf16[256,512]{1,0:T(8,128)(2,1)} %refs_5_.3) | copy-start | bytes 786436
  45.8 9.5 %copy-start.14 = (bf16[256,512]{1,0:T(8,128)(2,1)S(1)}, bf16[256,512]{1,0:T(8,128)(2,1)}, u32[]{:S(2)}) copy-start(bf16[256,512]{1,0:T(8,128)(2,1)} %refs_6_.1) | copy-start | bytes 786436
  45.9 9.5 %copy-start.20 = (f32[4,512]{1,0:T(4,128)S(1)}, f32[4,512]{1,0:T(4,128)}, u32[]{:S(2)}) copy-start(f32[4,512]{1,0:T(4,128)} %refs_4_.7) | copy-start | bytes 24580
  45.9 9.5 %copy-start.21 = (f32[2,512]{1,0:T(2,128)S(1)}, f32[2,512]{1,0:T(2,128)}, u32[]{:S(2)}) copy-start(f32[2,512]{1,0:T(2,128)} %refs_3_.7) | copy-start | bytes 12292
  53.4 2.0 collective-permute-start.7
  55.8 6.2 %copy-start.9 = (bf16[512,256]{1,0:T(8,128)(2,1)}, bf16[512,256]{1,0:T(8,128)(2,1)S(1)}, u32[]{:S(2)}) copy-start(bf16[512,256]{1,0:T(8,128)(2,1)S(1)} %get-tuple-element.255.refs_1_.refs_3_) | copy-start | bytes 786436
  55.9 6.2 %copy-start.18 = (f32[256,512]{1,0:T(8,128)}, f32[256,512]{1,0:T(8,128)S(1)}, u32[]{:S(2)}) copy-start(f32[256,512]{1,0:T(8,128)S(1)} %get-tuple-element.295.refs_2_) | copy-start | bytes 1572868
  62.1 8.7 %copy-start.1 = (bf16[2,1152,512]{2,1,0:T(8,128)(2,1)S(1)}, bf16[2,1152,512]{2,1,0:T(8,128)(2,1)}, u32[]{:S(2)}) copy-start(bf16[2,1152,512]{2,1,0:T(8,128)(2,1)} %copy-done) | copy-start | bytes 7077892
  62.1 50.9 %all-to-all-start = ((bf16[4,272,1664]{2,1,0:T(8,128)(2,1)}), bf16[4,272,1664]{2,1,0:T(8,128)(2,1)}, u32[]{:S(2)}, u32[]{:S(2)}) async-start(bf16[4,272,1664]{2,1,0:T(8,128)(2,1)} %get-tuple-element.302), calls=%async_computation | async-start | bytes 7241728 | tf_op jit(solution)/shard_map/all_to_all | solution.py:701
  67.0 20.1 %collective-permute-start.9 = (bf16[256,1152]{1,0:T(8,128)(2,1)S(1)}, bf16[256,1152]{1,0:T(8,128)(2,1)S(1)}, u32[]{:S(2)}, u32[]{:S(2)}) collective-permute-start(bf16[256,1152]{1,0:T(8,128)(2,1)S(1)} %collective-permute-done.2.refs_2_), channel_id=1, source_target_pairs={{2,4},{3,5},{4,2},{5,3},{10,12},{11,13},{12,10},{13,11},{18,20},{1... | collective-permute-start | bytes 1769480 | tf_op jit(solution)/shard_map/ppermute | solution.py:693
  67.7 19.4 %collective-permute-start.8 = (bf16[256,1152]{1,0:T(8,128)(2,1)}, bf16[256,1152]{1,0:T(8,128)(2,1)S(1)}, u32[]{:S(2)}, u32[]{:S(2)}) collective-permute-start(bf16[256,1152]{1,0:T(8,128)(2,1)} %collective-permute-done.3.refs_2_), channel_id=1, source_target_pairs={{2,0},{3,1},{4,6},{5,7},{10,8},{11,9},{12,14},{13,15},{18,16},{19,... | collective-permute-start | bytes 1769480 | tf_op jit(solution)/shard_map/ppermute | solution.py:697
  69.0 1.8 collective-permute-start.10
  70.8 1.0 copy-start.10
  73.2 25.8 %collective-permute-start.12 = (bf16[1152,256]{1,0:T(8,128)(2,1)S(1)}, bf16[1152,256]{1,0:T(8,128)(2,1)S(1)}, u32[]{:S(2)}, u32[]{:S(2)}) collective-permute-start(bf16[1152,256]{1,0:T(8,128)(2,1)S(1)} %get-tuple-element.268), channel_id=1, source_target_pairs={{0,2},{1,3},{6,4},{7,5},{8,10},{9,11},{14,12},{15,13},{16,18},{17,... | collective-permute-start | bytes 1769480 | tf_op jit(solution)/shard_map/ppermute | solution.py:689
  79.3 1.0 copy-start.11
  86.1 1.0 copy-start.4
  87.1 24.9 %copy-start.16 = (bf16[1152,256]{1,0:T(8,128)(2,1)}, bf16[1152,256]{1,0:T(8,128)(2,1)S(1)}, u32[]{:S(2)}) copy-start(bf16[1152,256]{1,0:T(8,128)(2,1)S(1)} %get-tuple-element.366.refs_0_) | copy-start | bytes 1769476
  87.1 17.0 %collective-permute-start.11 = (bf16[256,1152]{1,0:T(8,128)(2,1)S(1)}, bf16[256,1152]{1,0:T(8,128)(2,1)S(1)}, u32[]{:S(2)}, u32[]{:S(2)}) collective-permute-start(bf16[256,1152]{1,0:T(8,128)(2,1)S(1)} %collective-permute-done.9.refs_2_), channel_id=1, source_target_pairs={{2,0},{3,1},{4,6},{5,7},{10,8},{11,9},{12,14},{13,15},{18,16},{19,... | collective-permute-start | bytes 1769480 | tf_op jit(solution)/shard_map/ppermute | solution.py:697
  88.4 17.3 %collective-permute-start.14 = (bf16[1152,256]{1,0:T(8,128)(2,1)S(1)}, bf16[1152,256]{1,0:T(8,128)(2,1)S(1)}, u32[]{:S(2)}, u32[]{:S(2)}) collective-permute-start(bf16[1152,256]{1,0:T(8,128)(2,1)S(1)} %get-tuple-element.289.refs_0_), channel_id=1, source_target_pairs={{0,2},{1,3},{6,4},{7,5},{8,10},{9,11},{14,12},{15,13},{16,18},{17,... | collective-permute-start | bytes 1769480 | tf_op jit(solution)/shard_map/ppermute | solution.py:689
  99.0 8.6 %copy-start.13 = (bf16[256,512]{1,0:T(8,128)(2,1)S(1)}, bf16[256,512]{1,0:T(8,128)(2,1)}, u32[]{:S(2)}) copy-start(bf16[256,512]{1,0:T(8,128)(2,1)} %refs_5_.3) | copy-start | bytes 786436
  99.0 8.6 %copy-start.15 = (bf16[256,512]{1,0:T(8,128)(2,1)S(1)}, bf16[256,512]{1,0:T(8,128)(2,1)}, u32[]{:S(2)}) copy-start(bf16[256,512]{1,0:T(8,128)(2,1)} %refs_6_.1) | copy-start | bytes 786436
  99.0 8.6 %copy-start.19 = (f32[256,512]{1,0:T(8,128)S(1)}, f32[256,512]{1,0:T(8,128)}, u32[]{:S(2)}) copy-start(f32[256,512]{1,0:T(8,128)} %copy-done.18) | copy-start | bytes 1572868
  99.2 12.8 %collective-permute-start.16 = (bf16[1152,256]{1,0:T(8,128)(2,1)S(1)}, bf16[1152,256]{1,0:T(8,128)(2,1)S(1)}, u32[]{:S(2)}, u32[]{:S(2)}) collective-permute-start(bf16[1152,256]{1,0:T(8,128)(2,1)S(1)} %get-tuple-element.304), channel_id=1, source_target_pairs={{2,4},{3,5},{4,2},{5,3},{10,12},{11,13},{12,10},{13,11},{18,20},{1... | collective-permute-start | bytes 1769480 | tf_op jit(solution)/shard_map/ppermute | solution.py:693
  105.6 2.0 collective-permute-start.13
  105.8 6.1 %copy-start.32 = (bf16[1152,256]{1,0:T(8,128)(2,1)}, bf16[1152,256]{1,0:T(8,128)(2,1)S(1)}, u32[]{:S(2)}) copy-start(bf16[1152,256]{1,0:T(8,128)(2,1)S(1)} %get-tuple-element.329) | copy-start | bytes 1769476
  108.9 3.0 %copy-start.2 = (bf16[512,512]{1,0:T(8,128)(2,1)}, bf16[512,512]{1,0:T(8,128)(2,1)S(1)}, u32[]{:S(2)}) copy-start(bf16[512,512]{1,0:T(8,128)(2,1)S(1)} %get-tuple-element.323.refs_0_.refs_1_) | copy-start | bytes 1572868
  113.0 6.7 %collective-permute-start.17 = (bf16[4,272,1664]{2,1,0:T(8,128)(2,1)}, bf16[4,272,1664]{2,1,0:T(8,128)(2,1)}, u32[]{:S(2)}, u32[]{:S(2)}) collective-permute-start(bf16[4,272,1664]{2,1,0:T(8,128)(2,1)} %all-to-all-done.refs_1_.refs_3_.refs_0_), channel_id=1, source_target_pairs={{0,1},{1,0},{2,3},{3,2},{4,5},{5,4},{6,7},{7,6},{8,9},{9,8},{10,11... | collective-permute-start | bytes 10862600 | tf_op jit(solution)/shard_map/ppermute | solution.py:677
  113.1 4.9 %copy-start.7 = (bf16[512,256]{1,0:T(8,128)(2,1)S(1)}, bf16[512,256]{1,0:T(8,128)(2,1)}, u32[]{:S(2)}) copy-start(bf16[512,256]{1,0:T(8,128)(2,1)} %copy-done.6) | copy-start | bytes 786436
  113.1 14.5 %copy-start.3 = (bf16[512,512]{1,0:T(8,128)(2,1)S(1)}, bf16[512,512]{1,0:T(8,128)(2,1)}, u32[]{:S(2)}) copy-start(bf16[512,512]{1,0:T(8,128)(2,1)} %copy-done.2) | copy-start | bytes 1572868
  113.1 68.8 %all-to-all-start.1 = ((bf16[4,272,1664]{2,1,0:T(8,128)(2,1)}), bf16[4,272,1664]{2,1,0:T(8,128)(2,1)}, u32[]{:S(2)}, u32[]{:S(2)}) async-start(bf16[4,272,1664]{2,1,0:T(8,128)(2,1)} %get-tuple-element.371), calls=%async_computation.1 | async-start | bytes 7241728 | tf_op jit(solution)/shard_map/all_to_all | solution.py:701
  118.0 1.7 collective-permute-start.15
  118.4 25.5 %collective-permute-start.21 = (bf16[1152,256]{1,0:T(8,128)(2,1)}, bf16[1152,256]{1,0:T(8,128)(2,1)S(1)}, u32[]{:S(2)}, u32[]{:S(2)}) collective-permute-start(bf16[1152,256]{1,0:T(8,128)(2,1)} %copy-done.32), channel_id=1, source_target_pairs={{2,4},{3,5},{4,2},{5,3},{10,12},{11,13},{12,10},{13,11},{18,20},{1... | collective-permute-start | bytes 1769480 | tf_op jit(solution)/shard_map/ppermute | solution.py:693
  120.5 23.4 %collective-permute-start.20 = (bf16[1152,256]{1,0:T(8,128)(2,1)S(1)}, bf16[1152,256]{1,0:T(8,128)(2,1)S(1)}, u32[]{:S(2)}, u32[]{:S(2)}) collective-permute-start(bf16[1152,256]{1,0:T(8,128)(2,1)S(1)} %get-tuple-element.328), channel_id=1, source_target_pairs={{0,2},{1,3},{6,4},{7,5},{8,10},{9,11},{14,12},{15,13},{16,18},{17,... | collective-permute-start | bytes 1769480 | tf_op jit(solution)/shard_map/ppermute | solution.py:689
  127.6 23.1 %collective-permute-start.19 = (bf16[512,512]{1,0:T(8,128)(2,1)S(1)}, bf16[512,512]{1,0:T(8,128)(2,1)S(1)}, u32[]{:S(2)}, u32[]{:S(2)}) collective-permute-start(bf16[512,512]{1,0:T(8,128)(2,1)S(1)} %copy-done.3), channel_id=1, source_target_pairs={{2,4},{3,5},{4,2},{5,3},{10,12},{11,13},{12,10},{13,11},{18,20},{1... | collective-permute-start | bytes 1572872 | tf_op jit(solution)/shard_map/ppermute | solution.py:693
  128.3 24.2 %collective-permute-start.18 = (bf16[512,512]{1,0:T(8,128)(2,1)S(1)}, bf16[512,512]{1,0:T(8,128)(2,1)S(1)}, u32[]{:S(2)}, u32[]{:S(2)}) collective-permute-start(bf16[512,512]{1,0:T(8,128)(2,1)S(1)} %copy-done.3), channel_id=1, source_target_pairs={{0,2},{1,3},{2,0},{3,1},{4,6},{5,7},{6,4},{7,5},{8,10},{9,11},{10,... | collective-permute-start | bytes 1572872 | tf_op jit(solution)/shard_map/ppermute | solution.py:681
  136.5 1.0 copy-start.5
  137.5 11.8 %copy-start.31 = (bf16[1152,256]{1,0:T(8,128)(2,1)S(1)}, bf16[1152,256]{1,0:T(8,128)(2,1)}, u32[]{:S(2)}) copy-start(bf16[1152,256]{1,0:T(8,128)(2,1)} %copy-done.30) | copy-start | bytes 1769476
  137.5 40.2 %copy-start.17 = (bf16[1152,256]{1,0:T(8,128)(2,1)S(1)}, bf16[1152,256]{1,0:T(8,128)(2,1)}, u32[]{:S(2)}) copy-start(bf16[1152,256]{1,0:T(8,128)(2,1)} %copy-done.16) | copy-start | bytes 1769476
  143.9 36.1 %copy-start.33 = (bf16[1152,256]{1,0:T(8,128)(2,1)}, bf16[1152,256]{1,0:T(8,128)(2,1)S(1)}, u32[]{:S(2)}) copy-start(bf16[1152,256]{1,0:T(8,128)(2,1)S(1)} %collective-permute-done.21.refs_5_) | copy-start | bytes 1769476
  144.0 11.2 %collective-permute-start.26 = (bf16[1152,256]{1,0:T(8,128)(2,1)S(1)}, bf16[1152,256]{1,0:T(8,128)(2,1)S(1)}, u32[]{:S(2)}, u32[]{:S(2)}) collective-permute-start(bf16[1152,256]{1,0:T(8,128)(2,1)S(1)} %get-tuple-element.349), channel_id=1, source_target_pairs={{2,4},{3,5},{4,2},{5,3},{10,12},{11,13},{12,10},{13,11},{18,20},{1... | collective-permute-start | bytes 1769480 | tf_op jit(solution)/shard_map/ppermute | solution.py:693
  144.7 19.1 %collective-permute-start.25 = (bf16[1152,256]{1,0:T(8,128)(2,1)S(1)}, bf16[1152,256]{1,0:T(8,128)(2,1)S(1)}, u32[]{:S(2)}, u32[]{:S(2)}) collective-permute-start(bf16[1152,256]{1,0:T(8,128)(2,1)S(1)} %get-tuple-element.348.refs_0_), channel_id=1, source_target_pairs={{0,2},{1,3},{6,4},{7,5},{8,10},{9,11},{14,12},{15,13},{16,18},{17,... | collective-permute-start | bytes 1769480 | tf_op jit(solution)/shard_map/ppermute | solution.py:689
  149.4 18.2 %collective-permute-start.24 = (bf16[1152,256]{1,0:T(8,128)(2,1)S(1)}, bf16[1152,256]{1,0:T(8,128)(2,1)S(1)}, u32[]{:S(2)}, u32[]{:S(2)}) collective-permute-start(bf16[1152,256]{1,0:T(8,128)(2,1)S(1)} %copy-done.31), channel_id=1, source_target_pairs={{2,0},{3,1},{4,6},{5,7},{10,8},{11,9},{12,14},{13,15},{18,16},{19,... | collective-permute-start | bytes 1769480 | tf_op jit(solution)/shard_map/ppermute | solution.py:697
  152.5 20.3 %collective-permute-start.23 = (bf16[512,512]{1,0:T(8,128)(2,1)S(1)}, bf16[512,512]{1,0:T(8,128)(2,1)}, u32[]{:S(2)}, u32[]{:S(2)}) collective-permute-start(bf16[512,512]{1,0:T(8,128)(2,1)S(1)} %collective-permute-done.18.refs_1_.refs_2_), channel_id=1, source_target_pairs={{2,4},{3,5},{4,2},{5,3},{10,12},{11,13},{12,10},{13,11},{18,20},{1... | collective-permute-start | bytes 1572872 | tf_op jit(solution)/shard_map/ppermute | solution.py:693
  153.9 23.8 %collective-permute-start.22 = (bf16[512,512]{1,0:T(8,128)(2,1)S(1)}, bf16[512,512]{1,0:T(8,128)(2,1)S(1)}, u32[]{:S(2)}, u32[]{:S(2)}) collective-permute-start(bf16[512,512]{1,0:T(8,128)(2,1)S(1)} %collective-permute-done.19.refs_2_), channel_id=1, source_target_pairs={{2,0},{3,1},{4,6},{5,7},{10,8},{11,9},{12,14},{13,15},{18,16},{19,... | collective-permute-start | bytes 1572872 | tf_op jit(solution)/shard_map/ppermute | solution.py:697
  167.5 13.8 %copy-start.34 = (bf16[1152,256]{1,0:T(8,128)(2,1)}, bf16[1152,256]{1,0:T(8,128)(2,1)S(1)}, u32[]{:S(2)}) copy-start(bf16[1152,256]{1,0:T(8,128)(2,1)S(1)} %collective-permute-done.24.refs_6_) | copy-start | bytes 1769476
  167.5 21.0 %collective-permute-start.29 = (bf16[1152,256]{1,0:T(8,128)(2,1)S(1)}, bf16[1152,256]{1,0:T(8,128)(2,1)}, u32[]{:S(2)}, u32[]{:S(2)}) collective-permute-start(bf16[1152,256]{1,0:T(8,128)(2,1)S(1)} %get-tuple-element.368.refs_0_), channel_id=1, source_target_pairs={{0,2},{1,3},{6,4},{7,5},{8,10},{9,11},{14,12},{15,13},{16,18},{17,... | collective-permute-start | bytes 1769480 | tf_op jit(solution)/shard_map/ppermute | solution.py:689
  170.0 18.5 %collective-permute-start.31 = (bf16[1152,256]{1,0:T(8,128)(2,1)}, bf16[1152,256]{1,0:T(8,128)(2,1)}, u32[]{:S(2)}, u32[]{:S(2)}) collective-permute-start(bf16[1152,256]{1,0:T(8,128)(2,1)} %get-tuple-element.370), channel_id=1, source_target_pairs={{2,4},{3,5},{4,2},{5,3},{10,12},{11,13},{12,10},{13,11},{18,20},{1... | collective-permute-start | bytes 1769480 | tf_op jit(solution)/shard_map/ppermute | solution.py:693
  171.5 18.9 %collective-permute-start.30 = (bf16[1152,256]{1,0:T(8,128)(2,1)}, bf16[1152,256]{1,0:T(8,128)(2,1)}, u32[]{:S(2)}, u32[]{:S(2)}) collective-permute-start(bf16[1152,256]{1,0:T(8,128)(2,1)} %get-tuple-element.369), channel_id=1, source_target_pairs={{2,0},{3,1},{4,6},{5,7},{10,8},{11,9},{12,14},{13,15},{18,16},{19,... | collective-permute-start | bytes 1769480 | tf_op jit(solution)/shard_map/ppermute | solution.py:697
  177.7 22.6 %collective-permute-start.28 = (bf16[1152,256]{1,0:T(8,128)(2,1)S(1)}, bf16[1152,256]{1,0:T(8,128)(2,1)}, u32[]{:S(2)}, u32[]{:S(2)}) collective-permute-start(bf16[1152,256]{1,0:T(8,128)(2,1)S(1)} %copy-done.17), channel_id=1, source_target_pairs={{0,2},{1,3},{6,4},{7,5},{8,10},{9,11},{14,12},{15,13},{16,18},{17,... | collective-permute-start | bytes 1769480 | tf_op jit(solution)/shard_map/ppermute | solution.py:689
  180.0 20.3 %collective-permute-start.27 = (bf16[512,512]{1,0:T(8,128)(2,1)}, bf16[512,512]{1,0:T(8,128)(2,1)}, u32[]{:S(2)}, u32[]{:S(2)}) collective-permute-start(bf16[512,512]{1,0:T(8,128)(2,1)} %collective-permute-done.23.refs_2_), channel_id=1, source_target_pairs={{2,0},{3,1},{4,6},{5,7},{10,8},{11,9},{12,14},{13,15},{18,16},{19,... | collective-permute-start | bytes 1572872 | tf_op jit(solution)/shard_map/ppermute | solution.py:697
  183.5 7.0 %copy-start.24 = (s32[2,36]{1,0:T(2,128)S(1)}, s32[2,36]{1,0:T(2,128)}, u32[]{:S(2)}) copy-start(s32[2,36]{1,0:T(2,128)} %refs_1_.11) | copy-start | bytes 868
  183.5 7.0 %copy-start.27 = (s32[256]{0:T(256)S(1)}, s32[256]{0:T(256)}, u32[]{:S(2)}) copy-start(s32[256]{0:T(256)} %param.13) | copy-start | bytes 3076
  188.5 13.6 %copy-start.35 = (bf16[4,256,1152]{2,1,0:T(8,128)(2,1)S(1)}, bf16[4,256,1152]{2,1,0:T(8,128)(2,1)}, u32[]{:S(2)}) copy-start(bf16[4,256,1152]{2,1,0:T(8,128)(2,1)} %get-tuple-element.406) | copy-start | bytes 7077892
  202.1 10.7 %collective-permute-start.34 = (bf16[4,256,1152]{2,1,0:T(8,128)(2,1)S(1)}, bf16[4,256,1152]{2,1,0:T(8,128)(2,1)S(1)}, u32[]{:S(2)}, u32[]{:S(2)}) collective-permute-start(bf16[4,256,1152]{2,1,0:T(8,128)(2,1)S(1)} %copy-done.35), channel_id=1, source_target_pairs={{0,1},{1,0},{2,3},{3,2},{4,5},{5,4},{6,7},{7,6},{8,9},{9,8},{10,11... | collective-permute-start | bytes 7077896 | tf_op jit(solution)/shard_map/ppermute | solution.py:677
  202.2 6.0 %collective-permute-start.32 = (bf16[1024,512]{1,0:T(8,128)(2,1)S(1)}, bf16[1024,512]{1,0:T(8,128)(2,1)S(1)}, u32[]{:S(2)}, u32[]{:S(2)}) collective-permute-start(bf16[1024,512]{1,0:T(8,128)(2,1)S(1)} %get-tuple-element.391), channel_id=1, source_target_pairs={{0,1},{1,0},{2,3},{3,2},{4,5},{5,4},{6,7},{7,6},{8,9},{9,8},{10,11... | collective-permute-start | bytes 3145736 | tf_op jit(solution)/shard_map/ppermute | solution.py:677
  202.7 7.0 %collective-permute-start.33 = (bf16[1024,512]{1,0:T(8,128)(2,1)S(1)}, bf16[1024,512]{1,0:T(8,128)(2,1)S(1)}, u32[]{:S(2)}, u32[]{:S(2)}) collective-permute-start(bf16[1024,512]{1,0:T(8,128)(2,1)S(1)} %get-tuple-element.392), channel_id=1, source_target_pairs={{0,1},{1,0},{2,3},{3,2},{4,5},{5,4},{6,7},{7,6},{8,9},{9,8},{10,11... | collective-permute-start | bytes 3145736 | tf_op jit(solution)/shard_map/ppermute | solution.py:677
  (9 other events, 6.5 us)

commit v8 on v7

--- a/solution.py
+++ b/solution.py
@@ -196,11 +196,11 @@
     return call(
         mask_kernel,
         array(image.shape, jnp.bfloat16),
-        [SMEM, SMEM, VMEM, HBM],
+        [SMEM, SMEM, VMEM, ANY],
         VMEM,
         "mask_image",
         [pltpu.VMEM(image.shape, jnp.bfloat16), pltpu.SemaphoreType.DMA],
-    )(place, marks, group, in_hbm(image))
+    )(place, marks, group, image)
 
 
 def in_hbm(x):
@@ -411,49 +411,72 @@
     )(where, at_end, in_middle)
 
 
-def join_kernel(one, two, out):
+def join_kernel(where, one, at_end, in_middle, out, sems):
     rows = one.shape[0]
-    out[0:rows, :] = one[...]
-    out[rows : 2 * rows, :] = two[...]
-
-
-def join(one, two):
+    copies = [pltpu.make_async_copy(one, out.at[pl.ds(0, rows), :], sems.at[0])]
+    copies[0].start()
+    rest = out.at[pl.ds(rows, rows), :]
+    for flag, source in enumerate((at_end, in_middle)):
+        pl.when(where[2] == flag)(pltpu.make_async_copy(source, rest, sems.at[1]).start)
+    copies[0].wait()
+    pltpu.make_async_copy(at_end, rest, sems.at[1]).wait()
+
+
+def join(where, one, at_end, in_middle):
     rows, cols = one.shape
-    return call(join_kernel, array((2 * rows, cols), one.dtype), [VMEM, VMEM], VMEM, "join")(
-        one, two
-    )
-
-
-def lay_kernel(where, *refs):
-    own, far, (out_a, out_b, sems) = refs[0:4], refs[4:6], refs[6:]
+    return call(
+        join_kernel,
+        array((2 * rows, cols), one.dtype),
+        [SMEM] + [ANY] * 3,
+        VMEM,
+        "join",
+        [pltpu.SemaphoreType.DMA((2,))],
+    )(where, one, at_end, in_middle)
+
+
+def lay_kernel(where, low, high, far_low, far_high, out_a, out_b, stage, sems):
     rows = out_a.shape[0]
-    units = own[0].shape[1]
-    copies = []
-    for side in range(2):
+    units = low.shape[1]
+    pieces = []
+    for side, (first, second) in enumerate(((low, high), (far_low, far_high))):
         for k in range(4):
             block = 2 * (where[0] ^ k) + (where[1] ^ side)
             lanes = pl.ds(pl.multiple_of(block * units, units), units)
-            source, start = (own[k], 0) if side == 0 else (far[k // 2], 2 * rows * (k % 2))
-            for half, out in enumerate((out_a, out_b)):
-                at = pl.ds(start + half * rows, rows)
-                sem = sems.at[side * 8 + k * 2 + half]
-                copies.append(pltpu.make_async_copy(source.at[at, :], out.at[:, lanes], sem))
-    for copy in copies:
+            source = (first, second)[k // 2]
+            for half in range(2):
+                at = pl.ds((2 * (k % 2) + half) * rows, rows)
+                sem = sems.at[half, 4 * side + k]
+                pieces.append(
+                    pltpu.make_async_copy(source.at[at, :], stage.at[half, :, lanes], sem)
+                )
+    gives = [
+        pltpu.make_async_copy(stage.at[half], out, sems.at[half, 8])
+        for half, out in enumerate((out_a, out_b))
+    ]
+    for copy in pieces:
         copy.start()
-    for copy in copies:
-        copy.wait()
-
-
-def lay_out(where, *sources):
-    rows, units = sources[0].shape
+    for half in range(2):
+        for copy in pieces[half::2]:
+            copy.wait()
+        gives[half].start()
+    for give in gives:
+        give.wait()
+
+
+def lay_out(where, low, high, far_low, far_high):
+    rows, units = low.shape[0] // 4, low.shape[1]
+    stitched = pltpu.HBM((rows, 8 * units), jnp.bfloat16)
     return call(
         lay_kernel,
-        [array((rows // 2, 8 * units), jnp.bfloat16)] * 2,
-        [SMEM] + [ANY] * 6,
-        [VMEM] * 2,
+        [stitched, stitched],
+        [SMEM] + [ANY] * 4,
+        [HBM] * 2,
         "lay_out",
-        [pltpu.SemaphoreType.DMA((16,))],
-    )(where, *sources)
+        [
+            pltpu.VMEM((2, rows, 8 * units), jnp.bfloat16),
+            pltpu.SemaphoreType.DMA((2, 9)),
+        ],
+    )(where, low, high, far_low, far_high)
 
 
 def add_kernel(at, one, two, out):
@@ -731,17 +754,23 @@
 
     whole_a = swap(weight_a)
     whole_b = swap(weight_b)
-    a0 = mask_image(place[None], position_mask, group, image_a)
-    a2 = send(across, a0)
-    a1 = send(along, a0)
-    b0 = mask_image(place[None], position_mask, group, image_b)
-    a1, a2 = wait(a1, a2)
-    a3 = send(along, a2)
+    def masked(k, image):
+        spot = (2 * (z ^ k) + core)[None]
+        return mask_image(spot, position_mask, group, image)
+
+    raw2 = across(image_a)
+    raw1 = along(image_a)
+    b0 = masked(0, in_hbm(image_b))
+    a0 = masked(0, in_hbm(image_a))
+    raw1, raw2 = wait(raw1, raw2)
+    raw3 = send(along, raw2)
     b_mid = send(between, b0)
     b1 = send(along, b0)
+    a1 = masked(1, raw1)
+    a2 = masked(2, raw2)
     whole_a, whole_b = wait(whole_a, whole_b)
     keep_a, give_a, last_a, slot_a = forward_open(where, a0, a1, a2, weight_a, whole_a)
-    a3 = wait(a3)
+    a3 = masked(3, wait(raw3))
     own_a, sent_a = forward_close(a3, last_a, keep_a, give_a)
     got_sum = wait(send(swap, sent_a))
     dz_a, dzt_a, sums_a, hidden_a = tower(
@@ -810,6 +839,7 @@
     dzo_b, far_a = wait(dzo_b, far_a)
     first_b = first_slot(slot_b, dzt_b, dzo_b)
     in1_b = send(inward, first_b)
+    out_a = send(outward, sum3_a)
     s1 = send(along, local)
     s_mid = send(between, local)
     second_b, third_b, kept_b = parts(
@@ -822,20 +852,19 @@
         dzo_b,
     )
     grad_weight_a = weight_grad((0, 1), rows, cols, where, (got_a, far_a), got_a)
-    cross2_a = wait(cross2_a)
+    cross2_a, out_a = wait(cross2_a, out_a)
     in1_b = wait(in1_b)
     cross1_b = send(between, add(first_b, in1_b))
     in2_b = send(inward, second_b)
-    out_a = send(outward, sum3_a)
+    in3_b = send(inward, third_b)
     s1, s_mid = wait(s1, s_mid)
     s_end = send(outward, s_mid)
     s_mid2 = send(between, s1)
+    low_half = join(where, local, s1, s1)
     cross1_b = wait(cross1_b)
     out_b = send(outward, add(third_b, cross1_b))
     in2_b = wait(in2_b)
     cross2_b = send(between, add(second_b, in2_b))
-    out_a = wait(out_a)
-    in3_b = send(inward, third_b)
     s_end, s_mid2 = wait(s_end, s_mid2)
     s_end2 = send(outward, s_mid2)
     in3_a = send(inward, third_a)
@@ -846,15 +875,13 @@
     in3_b, out_b, cross2_b = wait(in3_b, out_b, cross2_b)
     grad_image_b = finish(where, position_mask, group, kept_b, in3_b, cross2_b, out_b)
     s_end2, in3_a = wait(s_end2, in3_a)
-    s3 = choose(where, s_end2, s_mid)
-    high = join(s2, s3)
-    low_half = join(local, s1)
+    high = join(where, s2, s_end2, s_mid)
     far_high = send(swap, high)
     far_low = send(swap, low_half)
     far_b = send(swap, block_b)
     grad_image_a = finish(where, position_mask, group, kept_a, in3_a, cross2_a, out_a)
-    stitched_a, stitched_b = lay_out(where, local, s1, s2, s3, far_low, far_high)
     grad_weight_b = weight_grad((1,), rows, cols, where, (far_b,), got_b, half_b)
+    stitched_a, stitched_b = lay_out(where, low_half, high, far_low, far_high)
     return (
         stitched_a,
         stitched_b,

time: 219 us -> 208 us (0.950)
  waiting for transfers between devices: 71 us -> 46.2 us
  starting transfers between devices: 63.9 us -> 72.8 us
  Pallas kernels: 70 us -> 73.9 us
    ppermute x6, waiting for transfers between devices: 20 us -> 9.61 us  [outward(): return lax.ppermute(x, 'mp', ENDS_OUT)]
    ppermute x6, starting transfers between devices: 27.2 us -> 37 us  [inward(): return lax.ppermute(x, 'mp', ENDS_IN)]
    ppermute x6, waiting for transfers between devices: 7.71 us -> 1.68 us  [inward(): return lax.ppermute(x, 'mp', ENDS_IN)]
    ppermute x4, waiting for transfers between devices: 31.3 us -> 25.9 us  [along(): return lax.ppermute(x, 'mp', NEAR_Z)]
    pallas_call x33 -> x35, Pallas kernels: 70 us -> 73.9 us  [go(): *results, line.token = run(*operands, *before)]
    ppermute x10, waiting for transfers between devices: 9.41 us -> 6.4 us  [swap(): return lax.ppermute(x, 'mp', SWAP_CORE)]
    unnamed x72 -> x80, local copies, waits for them, and re-layouts: 10.5 us -> 12 us
  transfers between devices with their start and end apart: 37 -> 37, of which waited for: 17 -> 14; matrix products, arithmetic and copies ran while one was open for 0% -> 0% of each run, Pallas kernels for 29% -> 34%
where the time goes in v8:
time: 208 us; the launch traced here: 207 us
  Pallas kernels  73.9 us (36%)
  starting transfers between devices  72.8 us (35%)
  waiting for transfers between devices  46.2 us (22%)
  local copies, waits for them, and re-layouts  12 us (6%)
    pallas_call x35, Pallas kernels, go(): *results, line.token = run(*operands, *before)  73.9 us
    ppermute x6, starting transfers between devices, inward(): return lax.ppermute(x, 'mp', ENDS_IN)  37 us
    ppermute x4, waiting for transfers between devices, along(): return lax.ppermute(x, 'mp', NEAR_Z)  25.9 us
    unnamed x80, local copies, waits for them, and re-layouts  12 us
    all_to_all x2, starting transfers between devices, exchange(): return lax.all_to_all(x, 'dp', 0, 0)  9.75 us
    ppermute x6, waiting for transfers between devices, outward(): return lax.ppermute(x, 'mp', ENDS_OUT)  9.61 us
    ppermute x6, starting transfers between devices, outward(): return lax.ppermute(x, 'mp', ENDS_OUT)  7.72 us
    ppermute x8, starting transfers between devices, between(): return lax.ppermute(x, 'mp', MIDS)  7.23 us
  transfers between devices with their start and end apart: 37, of which 14 were waited for; matrix products, arithmetic and copies ran while one was open for 0% of the time, Pallas kernels for 34%

profile of v8, /device:TPU:0, one launch (start us, length us, event | category | flops | bytes accessed | tf_op | source)
XLA Modules:
  0.0 207.3 jit_solution(8065937991938098643)
XLA Ops:
  1.2 3.0 %collective-permute-start = (bf16[256,1152]{1,0:T(8,128)(2,1)}, bf16[256,1152]{1,0:T(8,128)(2,1)S(1)}, u32[]{:S(2)}, u32[]{:S(2)}) collective-permute-start(bf16[256,1152]{1,0:T(8,128)(2,1)} %refs_3_.5), channel_id=1, source_target_pairs={{0,2},{1,3},{2,0},{3,1},{4,6},{5,7},{6,4},{7,5},{8,10},{9,11},{10,... | collective-permute-start | bytes 1769480 | tf_op jit(solution)/shard_map/ppermute | solution.py:704
  4.2 2.6 %collective-permute-start.1 = (bf16[256,1152]{1,0:T(8,128)(2,1)}, bf16[256,1152]{1,0:T(8,128)(2,1)S(1)}, u32[]{:S(2)}, u32[]{:S(2)}) collective-permute-start(bf16[256,1152]{1,0:T(8,128)(2,1)} %refs_3_.5), channel_id=1, source_target_pairs={{0,4},{1,5},{2,6},{3,7},{4,0},{5,1},{6,2},{7,3},{8,12},{9,13},{10,... | collective-permute-start | bytes 1769480 | tf_op jit(solution)/shard_map/ppermute | solution.py:708
  8.2 2.0 mask_image.5
  10.2 2.0 mask_image.6
  12.2 18.3 %collective-permute-done.refs_3_ = bf16[256,1152]{1,0:T(8,128)(2,1)S(1)} collective-permute-done((bf16[256,1152]{1,0:T(8,128)(2,1)}, bf16[256,1152]{1,0:T(8,128)(2,1)S(1)}, u32[]{:S(2)}, u32[]{:S(2)}) %collective-permute-start) | collective-permute-done | bytes 589856 | tf_op jit(solution)/shard_map/ppermute | solution.py:704
  30.5 2.6 %collective-permute-done.1.refs_3_ = bf16[256,1152]{1,0:T(8,128)(2,1)S(1)} collective-permute-done((bf16[256,1152]{1,0:T(8,128)(2,1)}, bf16[256,1152]{1,0:T(8,128)(2,1)S(1)}, u32[]{:S(2)}, u32[]{:S(2)}) %collective-permute-start.1) | collective-permute-done | bytes 589856 | tf_op jit(solution)/shard_map/ppermute | solution.py:708
  33.5 1.6 collective-permute-start.2
  37.9 1.2 mask_image.7
  39.1 1.2 mask_image.8
  40.4 5.3 %forward_open.2 = (f32[256,512]{1,0:T(8,128)S(1)}, f32[256,512]{1,0:T(8,128)S(1)}, bf16[2,1152,512]{2,1,0:T(8,128)(2,1)S(1)}, bf16[2,1152,512]{2,1,0:T(8,128)(2,1)S(1)}, f32[8,128]{1,0:T(8,128)S(1)}) custom-call(s32[9]{0:T(128)S(1)} %concatenate.3.refs_0_, bf16[256,1152]{1,0:T(8,128)(2,1)S(1)} %get-tuple-element.218.refs_1_, ...), custom_call_target="tpu_custom_call" | custom-call | flops 1 | bytes 1 | tf_op jit(solution)/shard_map/forward_open/pallas_call | solution.py:171
  45.7 3.7 %collective-permute-done.4.refs_3_ = bf16[256,1152]{1,0:T(8,128)(2,1)} collective-permute-done((bf16[256,1152]{1,0:T(8,128)(2,1)S(1)}, bf16[256,1152]{1,0:T(8,128)(2,1)}, u32[]{:S(2)}, u32[]{:S(2)}) %collective-permute-start.4) | collective-permute-done | bytes 589856 | tf_op jit(solution)/shard_map/ppermute | solution.py:704
  49.5 2.0 mask_image.9
  51.5 0.8 forward_close.2
  52.4 1.9 collective-permute-done.7.refs_1_
  54.8 2.9 %pack.2 = (bf16[4,272,1664]{2,1,0:T(8,128)(2,1)}, f32[8,128]{1,0:T(8,128)S(1)}) custom-call(s32[9]{0:T(128)S(1)} %concatenate.3.refs_0_, bf16[256,1152]{1,0:T(8,128)(2,1)S(1)} %get-tuple-element.218.refs_1_, bf16[256,1152]{1,0:T(8,128)(2,1)S(1)} %get-tuple-element.221.refs_2_, bf16[256,1152]{1,0:T(8,128)(2,1)S(1)} %get-tuple-element.223.refs_3_, ...), custom_call_target="tpu_custom_call" | custom-call | flops 1 | bytes 1 | tf_op jit(solution)/shard_map/pack/pallas_call | solution.py:171
  58.9 0.8 copy-done.15
  59.7 4.9 %all-to-all-start = ((bf16[4,272,1664]{2,1,0:T(8,128)(2,1)}), bf16[4,272,1664]{2,1,0:T(8,128)(2,1)}, u32[]{:S(2)}, u32[]{:S(2)}) async-start(bf16[4,272,1664]{2,1,0:T(8,128)(2,1)} %get-tuple-element.313), calls=%async_computation | async-start | bytes 7241728 | tf_op jit(solution)/shard_map/all_to_all | solution.py:724
  65.3 1.3 collective-permute-start.8
  66.6 1.7 collective-permute-done.10.refs_2_.refs_4_
  68.4 0.9 copy-done.7
  70.8 6.1 %collective-permute-start.12 = (bf16[1152,256]{1,0:T(8,128)(2,1)S(1)}, bf16[1152,256]{1,0:T(8,128)(2,1)S(1)}, u32[]{:S(2)}, u32[]{:S(2)}) collective-permute-start(bf16[1152,256]{1,0:T(8,128)(2,1)S(1)} %get-tuple-element.270), channel_id=1, source_target_pairs={{0,2},{1,3},{6,4},{7,5},{8,10},{9,11},{14,12},{15,13},{16,18},{17,... | collective-permute-start | bytes 1769480 | tf_op jit(solution)/shard_map/ppermute | solution.py:712
  76.9 0.9 copy-done.8
  77.9 5.7 %parts.2 = (bf16[1152,256]{1,0:T(8,128)(2,1)S(1)}, bf16[1152,256]{1,0:T(8,128)(2,1)S(1)}, f32[1152,256]{1,0:T(8,128)S(1)}, f32[8,128]{1,0:T(8,128)S(1)}) custom-call(s32[9]{0:T(128)S(1)} %concatenate.3.refs_0_, bf16[9216,512]{1,0:T(8,128)(2,1)} %refs_1_.14, bf16[9216,512]{1,0:T(8,128)(2,1)} %collective-permute-done.5.refs_5_.refs_2_, ...), custom_call_target="tpu_custom_call" | custom-call | flops 1 | bytes 1 | tf_op jit(solution)/shard_map/parts/pallas_call | solution.py:171
  83.7 1.0 copy-done.2
  84.7 1.3 collective-permute-start.11
  86.0 4.6 %collective-permute-start.14 = (bf16[1152,256]{1,0:T(8,128)(2,1)S(1)}, bf16[1152,256]{1,0:T(8,128)(2,1)S(1)}, u32[]{:S(2)}, u32[]{:S(2)}) collective-permute-start(bf16[1152,256]{1,0:T(8,128)(2,1)S(1)} %get-tuple-element.291.refs_0_), channel_id=1, source_target_pairs={{0,2},{1,3},{6,4},{7,5},{8,10},{9,11},{14,12},{15,13},{16,18},{17,... | collective-permute-start | bytes 1769480 | tf_op jit(solution)/shard_map/ppermute | solution.py:712
  91.3 5.3 %forward_open.3 = (f32[256,512]{1,0:T(8,128)S(1)}, f32[256,512]{1,0:T(8,128)S(1)}, bf16[2,1152,512]{2,1,0:T(8,128)(2,1)S(1)}, bf16[2,1152,512]{2,1,0:T(8,128)(2,1)S(1)}, f32[8,128]{1,0:T(8,128)S(1)}) custom-call(s32[9]{0:T(128)S(1)} %concatenate.3.refs_0_, bf16[256,1152]{1,0:T(8,128)(2,1)S(1)} %get-tuple-element.217.refs_1_, ...), custom_call_target="tpu_custom_call" | custom-call | flops 1 | bytes 1 | tf_op jit(solution)/shard_map/forward_open/pallas_call | solution.py:171
  96.8 0.8 collective-permute-start.15
  97.6 4.1 %collective-permute-done.11.refs_1_ = bf16[256,1152]{1,0:T(8,128)(2,1)S(1)} collective-permute-done((bf16[256,1152]{1,0:T(8,128)(2,1)S(1)}, bf16[256,1152]{1,0:T(8,128)(2,1)S(1)}, u32[]{:S(2)}, u32[]{:S(2)}) %collective-permute-start.11) | collective-permute-done | bytes 589856 | tf_op jit(solution)/shard_map/ppermute | solution.py:720
  101.7 0.9 choose.4
  102.5 0.8 forward_close.3
  103.6 1.7 collective-permute-done.13.refs_1_
  106.7 2.8 %pack.3 = (bf16[4,272,1664]{2,1,0:T(8,128)(2,1)}, f32[8,128]{1,0:T(8,128)S(1)}) custom-call(s32[9]{0:T(128)S(1)} %concatenate.3.refs_0_, bf16[256,1152]{1,0:T(8,128)(2,1)S(1)} %get-tuple-element.217.refs_1_, bf16[256,1152]{1,0:T(8,128)(2,1)S(1)} %collective-permute-done.2.refs_2_, bf16[256,1152]{1,0:T(8,128)(2,1)S(1)} %get-tuple-element.273.refs_3_, ...), custom_call_target="tpu_custom_call" | custom-call | flops 1 | bytes 1 | tf_op jit(solution)/shard_map/pack/pallas_call | solution.py:171
  109.7 0.8 copy-done.36
  110.7 4.9 %all-to-all-start.1 = ((bf16[4,272,1664]{2,1,0:T(8,128)(2,1)}), bf16[4,272,1664]{2,1,0:T(8,128)(2,1)}, u32[]{:S(2)}, u32[]{:S(2)}) async-start(bf16[4,272,1664]{2,1,0:T(8,128)(2,1)} %get-tuple-element.374), calls=%async_computation.1 | async-start | bytes 7241728 | tf_op jit(solution)/shard_map/all_to_all | solution.py:724
  117.3 0.8 first_slot.3
  118.0 1.3 collective-permute-start.22
  119.3 7.2 %collective-permute-start.20 = (bf16[1152,256]{1,0:T(8,128)(2,1)S(1)}, bf16[1152,256]{1,0:T(8,128)(2,1)S(1)}, u32[]{:S(2)}, u32[]{:S(2)}) collective-permute-start(bf16[1152,256]{1,0:T(8,128)(2,1)S(1)} %get-tuple-element.332), channel_id=1, source_target_pairs={{0,2},{1,3},{6,4},{7,5},{8,10},{9,11},{14,12},{15,13},{16,18},{17,... | collective-permute-start | bytes 1769480 | tf_op jit(solution)/shard_map/ppermute | solution.py:712
  127.2 1.5 collective-permute-start.18
  128.7 5.7 %parts.3 = (bf16[1152,256]{1,0:T(8,128)(2,1)S(1)}, bf16[1152,256]{1,0:T(8,128)(2,1)S(1)}, f32[1152,256]{1,0:T(8,128)S(1)}, f32[8,128]{1,0:T(8,128)S(1)}) custom-call(s32[9]{0:T(128)S(1)} %concatenate.3.refs_0_, bf16[9216,512]{1,0:T(8,128)(2,1)} %refs_1_.15, bf16[9216,512]{1,0:T(8,128)(2,1)} %collective-permute-done.6.refs_5_.refs_2_, ...), custom_call_target="tpu_custom_call" | custom-call | flops 1 | bytes 1 | tf_op jit(solution)/shard_map/parts/pallas_call | solution.py:171
  134.5 1.0 copy-done.3
  135.5 6.3 %weight_grad.3 = (f32[2304,512]{1,0:T(8,128)}, f32[8,128]{1,0:T(8,128)S(1)}) custom-call(s32[9]{0:T(128)S(1)} %concatenate.3.refs_0_, bf16[4,272,1664]{2,1,0:T(8,128)(2,1)} %all-to-all-done.refs_1_.refs_3_.refs_0_, bf16[4,272,1664]{2,1,0:T(8,128)(2,1)} %collective-permute-done.17.refs_2_, bf16[4,272,1664]{2,1,0:T(8,128)(2,1)} %all-to-all-done.refs_1_.refs_3_.refs_0_, ...), custom_call_target="tpu_custom_call" | custom-call | flops 1 | bytes 1 | tf_op jit(solution)/shard_map/weight_grad/pallas_call | solution.py:171
  141.9 0.8 copy-done.38
  143.6 4.6 %collective-permute-start.25 = (bf16[1152,256]{1,0:T(8,128)(2,1)S(1)}, bf16[1152,256]{1,0:T(8,128)(2,1)S(1)}, u32[]{:S(2)}, u32[]{:S(2)}) collective-permute-start(bf16[1152,256]{1,0:T(8,128)(2,1)S(1)} %get-tuple-element.353.refs_0_), channel_id=1, source_target_pairs={{0,2},{1,3},{6,4},{7,5},{8,10},{9,11},{14,12},{15,13},{16,18},{17,... | collective-permute-start | bytes 1769480 | tf_op jit(solution)/shard_map/ppermute | solution.py:712
  148.2 3.2 %collective-permute-done.18.refs_2_.refs_3_ = bf16[512,512]{1,0:T(8,128)(2,1)S(1)} collective-permute-done((bf16[512,512]{1,0:T(8,128)(2,1)S(1)}, bf16[512,512]{1,0:T(8,128)(2,1)S(1)}, u32[]{:S(2)}, u32[]{:S(2)}) %collective-permute-start.18) | collective-permute-done | bytes 524320 | tf_op jit(solution)/shard_map/ppermute | solution.py:704
  151.4 1.5 collective-permute-start.24
  152.9 1.3 collective-permute-start.23
  154.9 6.6 %collective-permute-start.29 = (bf16[1152,256]{1,0:T(8,128)(2,1)S(1)}, bf16[1152,256]{1,0:T(8,128)(2,1)}, u32[]{:S(2)}, u32[]{:S(2)}) collective-permute-start(bf16[1152,256]{1,0:T(8,128)(2,1)S(1)} %get-tuple-element.371.refs_0_), channel_id=1, source_target_pairs={{0,2},{1,3},{6,4},{7,5},{8,10},{9,11},{14,12},{15,13},{16,18},{17,... | collective-permute-start | bytes 1769480 | tf_op jit(solution)/shard_map/ppermute | solution.py:712
  161.5 1.0 add.42
  162.4 1.7 collective-permute-done.25.refs_1_
  164.1 0.9 add.43
  165.0 1.5 collective-permute-start.31
  166.5 1.3 collective-permute-start.30
  167.8 7.8 %collective-permute-start.28 = (bf16[1152,256]{1,0:T(8,128)(2,1)S(1)}, bf16[1152,256]{1,0:T(8,128)(2,1)}, u32[]{:S(2)}, u32[]{:S(2)}) collective-permute-start(bf16[1152,256]{1,0:T(8,128)(2,1)S(1)} %copy-done.14), channel_id=1, source_target_pairs={{0,2},{1,3},{6,4},{7,5},{8,10},{9,11},{14,12},{15,13},{16,18},{17,... | collective-permute-start | bytes 1769480 | tf_op jit(solution)/shard_map/ppermute | solution.py:712
  175.7 1.3 collective-permute-start.27
  177.6 0.8 copy-done.20
  178.4 1.6 total_sums.1
  180.0 4.9 %weight_grad.4 = (f32[2304,512]{1,0:T(8,128)}, bf16[4,256,1152]{2,1,0:T(8,128)(2,1)}, f32[8,128]{1,0:T(8,128)S(1)}) custom-call(s32[9]{0:T(128)S(1)} %concatenate.3.refs_0_, bf16[4,272,1664]{2,1,0:T(8,128)(2,1)} %all-to-all-done.1.refs_1_.refs_2_, bf16[4,272,1664]{2,1,0:T(8,128)(2,1)} %all-to-all-done.1.refs_1_.refs_2_, f32[8,128]{1,0:T(8,128)S(1)} %get-tuple-element.378.refs_3_), custom_call_target="tpu_custom_call" | custom-call | flops 1 | bytes 1 | tf_op jit(solution)/shard_map/weight_grad/pallas_call | solution.py:171
  184.9 1.2 collective-permute-done.30.refs_6_
  186.1 3.5 %finish.2 = (bf16[1152,256]{1,0:T(8,128)(2,1)}, f32[8,128]{1,0:T(8,128)S(1)}) custom-call(s32[9]{0:T(128)S(1)} %concatenate.3.refs_0_, s32[2,36]{1,0:T(2,128)S(1)} %copy-done.26, s32[1,256]{1,0:T(1,128)S(1)} %bitcast.17, f32[1152,256]{1,0:T(8,128)} %copy-done.3, bf16[1152,256]{1,0:T(8,128)(2,1)} %collective-permute-done.29.refs_4_, ...), custom_call_target="tpu_custom_call" | custom-call | flops 1 | bytes 1 | tf_op jit(solution)/shard_map/finish/pallas_call | solution.py:171
  189.6 4.3 %collective-permute-done.27.refs_2_ = bf16[512,512]{1,0:T(8,128)(2,1)S(1)} collective-permute-done((bf16[512,512]{1,0:T(8,128)(2,1)}, bf16[512,512]{1,0:T(8,128)(2,1)S(1)}, u32[]{:S(2)}, u32[]{:S(2)}) %collective-permute-start.27) | collective-permute-done | bytes 524320 | tf_op jit(solution)/shard_map/ppermute | solution.py:720
  195.3 3.5 %finish.3 = (bf16[1152,256]{1,0:T(8,128)(2,1)}, f32[8,128]{1,0:T(8,128)S(1)}) custom-call(s32[9]{0:T(128)S(1)} %concatenate.3.refs_0_, s32[2,36]{1,0:T(2,128)S(1)} %copy-done.26, s32[1,256]{1,0:T(1,128)S(1)} %bitcast.18, f32[1152,256]{1,0:T(8,128)} %copy-done.2, bf16[1152,256]{1,0:T(8,128)(2,1)} %collective-permute-done.28.refs_4_, ...), custom_call_target="tpu_custom_call" | custom-call | flops 1 | bytes 1 | tf_op jit(solution)/shard_map/finish/pallas_call | solution.py:171
  199.2 4.2 %weight_grad.5 = (f32[2304,512]{1,0:T(8,128)}, f32[8,128]{1,0:T(8,128)S(1)}) custom-call(s32[9]{0:T(128)S(1)} %concatenate.3.refs_0_, bf16[4,256,1152]{2,1,0:T(8,128)(2,1)S(1)} %collective-permute-done.34.refs_1_, bf16[4,272,1664]{2,1,0:T(8,128)(2,1)} %all-to-all-done.1.refs_1_.refs_2_, ...), custom_call_target="tpu_custom_call", output_to_operand_aliasing={{0}: (3, {})} | custom-call | flops 1 | bytes 1 | tf_op jit(solution)/shard_map/weight_grad/pallas_call | solution.py:171
  203.4 3.7 %lay_out.1 = (bf16[256,4096]{1,0:T(8,128)(2,1)}, bf16[256,4096]{1,0:T(8,128)(2,1)}, f32[8,128]{1,0:T(8,128)}) custom-call(s32[9]{0:T(128)S(1)} %concatenate.3.refs_0_, bf16[1024,512]{1,0:T(8,128)(2,1)S(1)} %get-tuple-element.389.refs_1_, bf16[1024,512]{1,0:T(8,128)(2,1)S(1)} %get-tuple-element.387.refs_2_, ...), custom_call_target="tpu_custom_call" | custom-call | flops 1 | bytes 1 | tf_op jit(solution)/shard_map/lay_out/pallas_call | solution.py:171
  (127 shorter events, 18.2 us)
Async XLA Ops:
  0.6 39.7 %collective-permute-start.5 = (bf16[9216,512]{1,0:T(8,128)(2,1)}, bf16[9216,512]{1,0:T(8,128)(2,1)}, u32[]{:S(2)}, u32[]{:S(2)}) collective-permute-start(bf16[9216,512]{1,0:T(8,128)(2,1)} %refs_1_.14), channel_id=1, source_target_pairs={{0,1},{1,0},{2,3},{3,2},{4,5},{5,4},{6,7},{7,6},{8,9},{9,8},{10,11... | collective-permute-start | bytes 28311560 | tf_op jit(solution)/shard_map/ppermute | solution.py:700
  1.2 39.2 %collective-permute-start.6 = (bf16[9216,512]{1,0:T(8,128)(2,1)}, bf16[9216,512]{1,0:T(8,128)(2,1)}, u32[]{:S(2)}, u32[]{:S(2)}) collective-permute-start(bf16[9216,512]{1,0:T(8,128)(2,1)} %refs_1_.15), channel_id=1, source_target_pairs={{0,1},{1,0},{2,3},{3,2},{4,5},{5,4},{6,7},{7,6},{8,9},{9,8},{10,11... | collective-permute-start | bytes 28311560 | tf_op jit(solution)/shard_map/ppermute | solution.py:700
  1.2 29.3 %collective-permute-start = (bf16[256,1152]{1,0:T(8,128)(2,1)}, bf16[256,1152]{1,0:T(8,128)(2,1)S(1)}, u32[]{:S(2)}, u32[]{:S(2)}) collective-permute-start(bf16[256,1152]{1,0:T(8,128)(2,1)} %refs_3_.5), channel_id=1, source_target_pairs={{0,2},{1,3},{2,0},{3,1},{4,6},{5,7},{6,4},{7,5},{8,10},{9,11},{10,... | collective-permute-start | bytes 1769480 | tf_op jit(solution)/shard_map/ppermute | solution.py:704
  4.2 28.8 %collective-permute-start.1 = (bf16[256,1152]{1,0:T(8,128)(2,1)}, bf16[256,1152]{1,0:T(8,128)(2,1)S(1)}, u32[]{:S(2)}, u32[]{:S(2)}) collective-permute-start(bf16[256,1152]{1,0:T(8,128)(2,1)} %refs_3_.5), channel_id=1, source_target_pairs={{0,4},{1,5},{2,6},{3,7},{4,0},{5,1},{6,2},{7,3},{8,12},{9,13},{10,... | collective-permute-start | bytes 1769480 | tf_op jit(solution)/shard_map/ppermute | solution.py:708
  33.1 16.4 %collective-permute-start.4 = (bf16[256,1152]{1,0:T(8,128)(2,1)S(1)}, bf16[256,1152]{1,0:T(8,128)(2,1)}, u32[]{:S(2)}, u32[]{:S(2)}) collective-permute-start(bf16[256,1152]{1,0:T(8,128)(2,1)S(1)} %collective-permute-done.1.refs_3_), channel_id=1, source_target_pairs={{0,2},{1,3},{2,0},{3,1},{4,6},{5,7},{6,4},{7,5},{8,10},{9,11},{10,... | collective-permute-start | bytes 1769480 | tf_op jit(solution)/shard_map/ppermute | solution.py:704
  33.5 25.3 %collective-permute-start.2 = (bf16[256,1152]{1,0:T(8,128)(2,1)S(1)}, bf16[256,1152]{1,0:T(8,128)(2,1)S(1)}, u32[]{:S(2)}, u32[]{:S(2)}) collective-permute-start(bf16[256,1152]{1,0:T(8,128)(2,1)S(1)} %get-tuple-element.217.refs_1_), channel_id=1, source_target_pairs={{0,2},{1,3},{2,0},{3,1},{4,6},{5,7},{6,4},{7,5},{8,10},{9,11},{10,... | collective-permute-start | bytes 1769480 | tf_op jit(solution)/shard_map/ppermute | solution.py:704
  35.1 23.7 %collective-permute-start.3 = (bf16[256,1152]{1,0:T(8,128)(2,1)S(1)}, bf16[256,1152]{1,0:T(8,128)(2,1)S(1)}, u32[]{:S(2)}, u32[]{:S(2)}) collective-permute-start(bf16[256,1152]{1,0:T(8,128)(2,1)S(1)} %get-tuple-element.217.refs_1_), channel_id=1, source_target_pairs={{2,4},{3,5},{4,2},{5,3},{10,12},{11,13},{12,10},{13,11},{18,20},{1... | collective-permute-start | bytes 1769480 | tf_op jit(solution)/shard_map/ppermute | solution.py:716
  40.4 9.1 %copy-start.26 = (s32[2,36]{1,0:T(2,128)S(1)}, s32[2,36]{1,0:T(2,128)}, u32[]{:S(2)}) copy-start(s32[2,36]{1,0:T(2,128)} %refs_1_.17) | copy-start | bytes 868
  40.4 9.1 %copy-start.29 = (s32[256]{0:T(256)S(1)}, s32[256]{0:T(256)}, u32[]{:S(2)}) copy-start(s32[256]{0:T(256)} %param.13) | copy-start | bytes 3076
  45.6 12.0 %copy-start = (bf16[2,1152,512]{2,1,0:T(8,128)(2,1)}, bf16[2,1152,512]{2,1,0:T(8,128)(2,1)S(1)}, u32[]{:S(2)}) copy-start(bf16[2,1152,512]{2,1,0:T(8,128)(2,1)S(1)} %get-tuple-element.260.refs_0_) | copy-start | bytes 7077892
  45.7 8.6 %copy-start.9 = (bf16[256,512]{1,0:T(8,128)(2,1)S(1)}, bf16[256,512]{1,0:T(8,128)(2,1)}, u32[]{:S(2)}) copy-start(bf16[256,512]{1,0:T(8,128)(2,1)} %refs_5_.3) | copy-start | bytes 786436
  45.7 8.6 %copy-start.11 = (bf16[256,512]{1,0:T(8,128)(2,1)S(1)}, bf16[256,512]{1,0:T(8,128)(2,1)}, u32[]{:S(2)}) copy-start(bf16[256,512]{1,0:T(8,128)(2,1)} %refs_6_.1) | copy-start | bytes 786436
  45.7 8.6 %copy-start.30 = (f32[4,512]{1,0:T(4,128)S(1)}, f32[4,512]{1,0:T(4,128)}, u32[]{:S(2)}) copy-start(f32[4,512]{1,0:T(4,128)} %refs_4_.7) | copy-start | bytes 24580
  45.7 8.6 %copy-start.32 = (f32[2,512]{1,0:T(2,128)S(1)}, f32[2,512]{1,0:T(2,128)}, u32[]{:S(2)}) copy-start(f32[2,512]{1,0:T(2,128)} %refs_3_.7) | copy-start | bytes 12292
  52.3 2.0 collective-permute-start.7
  54.8 4.1 %copy-start.6 = (bf16[512,256]{1,0:T(8,128)(2,1)}, bf16[512,256]{1,0:T(8,128)(2,1)S(1)}, u32[]{:S(2)}) copy-start(bf16[512,256]{1,0:T(8,128)(2,1)S(1)} %get-tuple-element.257.refs_1_.refs_3_) | copy-start | bytes 786436
  54.8 4.1 %copy-start.22 = (f32[256,512]{1,0:T(8,128)}, f32[256,512]{1,0:T(8,128)S(1)}, u32[]{:S(2)}) copy-start(f32[256,512]{1,0:T(8,128)S(1)} %get-tuple-element.297.refs_2_) | copy-start | bytes 1572868
  59.7 8.7 %copy-start.1 = (bf16[2,1152,512]{2,1,0:T(8,128)(2,1)S(1)}, bf16[2,1152,512]{2,1,0:T(8,128)(2,1)}, u32[]{:S(2)}) copy-start(bf16[2,1152,512]{2,1,0:T(8,128)(2,1)} %copy-done) | copy-start | bytes 7077892
  59.7 50.9 %all-to-all-start = ((bf16[4,272,1664]{2,1,0:T(8,128)(2,1)}), bf16[4,272,1664]{2,1,0:T(8,128)(2,1)}, u32[]{:S(2)}, u32[]{:S(2)}) async-start(bf16[4,272,1664]{2,1,0:T(8,128)(2,1)} %get-tuple-element.313), calls=%async_computation | async-start | bytes 7241728 | tf_op jit(solution)/shard_map/all_to_all | solution.py:724
  64.6 20.1 %collective-permute-start.9 = (bf16[256,1152]{1,0:T(8,128)(2,1)S(1)}, bf16[256,1152]{1,0:T(8,128)(2,1)S(1)}, u32[]{:S(2)}, u32[]{:S(2)}) collective-permute-start(bf16[256,1152]{1,0:T(8,128)(2,1)S(1)} %collective-permute-done.2.refs_2_), channel_id=1, source_target_pairs={{2,4},{3,5},{4,2},{5,3},{10,12},{11,13},{12,10},{13,11},{18,20},{1... | collective-permute-start | bytes 1769480 | tf_op jit(solution)/shard_map/ppermute | solution.py:716
  65.3 19.4 %collective-permute-start.8 = (bf16[256,1152]{1,0:T(8,128)(2,1)}, bf16[256,1152]{1,0:T(8,128)(2,1)S(1)}, u32[]{:S(2)}, u32[]{:S(2)}) collective-permute-start(bf16[256,1152]{1,0:T(8,128)(2,1)} %copy-done.15), channel_id=1, source_target_pairs={{2,0},{3,1},{4,6},{5,7},{10,8},{11,9},{12,14},{13,15},{18,16},{19,... | collective-permute-start | bytes 1769480 | tf_op jit(solution)/shard_map/ppermute | solution.py:720
  66.6 1.8 collective-permute-start.10
  70.8 25.8 %collective-permute-start.12 = (bf16[1152,256]{1,0:T(8,128)(2,1)S(1)}, bf16[1152,256]{1,0:T(8,128)(2,1)S(1)}, u32[]{:S(2)}, u32[]{:S(2)}) collective-permute-start(bf16[1152,256]{1,0:T(8,128)(2,1)S(1)} %get-tuple-element.270), channel_id=1, source_target_pairs={{0,2},{1,3},{6,4},{7,5},{8,10},{9,11},{14,12},{15,13},{16,18},{17,... | collective-permute-start | bytes 1769480 | tf_op jit(solution)/shard_map/ppermute | solution.py:712
  83.6 1.0 copy-start.2
  84.7 24.9 %copy-start.13 = (bf16[1152,256]{1,0:T(8,128)(2,1)}, bf16[1152,256]{1,0:T(8,128)(2,1)S(1)}, u32[]{:S(2)}) copy-start(bf16[1152,256]{1,0:T(8,128)(2,1)S(1)} %get-tuple-element.369.refs_0_) | copy-start | bytes 1769476
  84.7 17.0 %collective-permute-start.11 = (bf16[256,1152]{1,0:T(8,128)(2,1)S(1)}, bf16[256,1152]{1,0:T(8,128)(2,1)S(1)}, u32[]{:S(2)}, u32[]{:S(2)}) collective-permute-start(bf16[256,1152]{1,0:T(8,128)(2,1)S(1)} %collective-permute-done.9.refs_2_), channel_id=1, source_target_pairs={{2,0},{3,1},{4,6},{5,7},{10,8},{11,9},{12,14},{13,15},{18,16},{19,... | collective-permute-start | bytes 1769480 | tf_op jit(solution)/shard_map/ppermute | solution.py:720
  86.0 17.5 %collective-permute-start.14 = (bf16[1152,256]{1,0:T(8,128)(2,1)S(1)}, bf16[1152,256]{1,0:T(8,128)(2,1)S(1)}, u32[]{:S(2)}, u32[]{:S(2)}) collective-permute-start(bf16[1152,256]{1,0:T(8,128)(2,1)S(1)} %get-tuple-element.291.refs_0_), channel_id=1, source_target_pairs={{0,2},{1,3},{6,4},{7,5},{8,10},{9,11},{14,12},{15,13},{16,18},{17,... | collective-permute-start | bytes 1769480 | tf_op jit(solution)/shard_map/ppermute | solution.py:712
  91.3 10.4 %copy-start.16 = (bf16[256,1152]{1,0:T(8,128)(2,1)S(1)}, bf16[256,1152]{1,0:T(8,128)(2,1)}, u32[]{:S(2)}) copy-start(bf16[256,1152]{1,0:T(8,128)(2,1)} %copy-done.15) | copy-start | bytes 1769476
  96.6 8.8 %copy-start.10 = (bf16[256,512]{1,0:T(8,128)(2,1)S(1)}, bf16[256,512]{1,0:T(8,128)(2,1)}, u32[]{:S(2)}) copy-start(bf16[256,512]{1,0:T(8,128)(2,1)} %refs_5_.3) | copy-start | bytes 786436
  96.6 8.8 %copy-start.12 = (bf16[256,512]{1,0:T(8,128)(2,1)S(1)}, bf16[256,512]{1,0:T(8,128)(2,1)}, u32[]{:S(2)}) copy-start(bf16[256,512]{1,0:T(8,128)(2,1)} %refs_6_.1) | copy-start | bytes 786436
  96.6 8.8 %copy-start.23 = (f32[256,512]{1,0:T(8,128)S(1)}, f32[256,512]{1,0:T(8,128)}, u32[]{:S(2)}) copy-start(f32[256,512]{1,0:T(8,128)} %copy-done.22) | copy-start | bytes 1572868
  96.6 8.8 %copy-start.31 = (f32[4,512]{1,0:T(4,128)S(1)}, f32[4,512]{1,0:T(4,128)}, u32[]{:S(2)}) copy-start(f32[4,512]{1,0:T(4,128)} %refs_4_.7) | copy-start | bytes 24580
  96.8 12.8 %collective-permute-start.15 = (bf16[1152,256]{1,0:T(8,128)(2,1)S(1)}, bf16[1152,256]{1,0:T(8,128)(2,1)S(1)}, u32[]{:S(2)}, u32[]{:S(2)}) collective-permute-start(bf16[1152,256]{1,0:T(8,128)(2,1)S(1)} %get-tuple-element.301), channel_id=1, source_target_pairs={{2,4},{3,5},{4,2},{5,3},{10,12},{11,13},{12,10},{13,11},{18,20},{1... | collective-permute-start | bytes 1769480 | tf_op jit(solution)/shard_map/ppermute | solution.py:716
  103.4 2.0 collective-permute-start.13
  103.6 5.9 %copy-start.35 = (bf16[1152,256]{1,0:T(8,128)(2,1)}, bf16[1152,256]{1,0:T(8,128)(2,1)S(1)}, u32[]{:S(2)}) copy-start(bf16[1152,256]{1,0:T(8,128)(2,1)S(1)} %get-tuple-element.333) | copy-start | bytes 1769476
  106.7 2.9 %copy-start.17 = (bf16[512,512]{1,0:T(8,128)(2,1)}, bf16[512,512]{1,0:T(8,128)(2,1)S(1)}, u32[]{:S(2)}) copy-start(bf16[512,512]{1,0:T(8,128)(2,1)S(1)} %get-tuple-element.327.refs_1_) | copy-start | bytes 1572868
  110.5 6.7 %collective-permute-start.17 = (bf16[4,272,1664]{2,1,0:T(8,128)(2,1)}, bf16[4,272,1664]{2,1,0:T(8,128)(2,1)}, u32[]{:S(2)}, u32[]{:S(2)}) collective-permute-start(bf16[4,272,1664]{2,1,0:T(8,128)(2,1)} %all-to-all-done.refs_1_.refs_3_.refs_0_), channel_id=1, source_target_pairs={{0,1},{1,0},{2,3},{3,2},{4,5},{5,4},{6,7},{7,6},{8,9},{9,8},{10,11... | collective-permute-start | bytes 10862600 | tf_op jit(solution)/shard_map/ppermute | solution.py:700
  110.7 4.9 %copy-start.5 = (bf16[512,256]{1,0:T(8,128)(2,1)S(1)}, bf16[512,256]{1,0:T(8,128)(2,1)}, u32[]{:S(2)}) copy-start(bf16[512,256]{1,0:T(8,128)(2,1)} %copy-done.4) | copy-start | bytes 786436
  110.7 15.9 %copy-start.18 = (bf16[512,512]{1,0:T(8,128)(2,1)S(1)}, bf16[512,512]{1,0:T(8,128)(2,1)}, u32[]{:S(2)}) copy-start(bf16[512,512]{1,0:T(8,128)(2,1)} %copy-done.17) | copy-start | bytes 1572868
  110.7 67.7 %all-to-all-start.1 = ((bf16[4,272,1664]{2,1,0:T(8,128)(2,1)}), bf16[4,272,1664]{2,1,0:T(8,128)(2,1)}, u32[]{:S(2)}, u32[]{:S(2)}) async-start(bf16[4,272,1664]{2,1,0:T(8,128)(2,1)} %get-tuple-element.374), calls=%async_computation.1 | async-start | bytes 7241728 | tf_op jit(solution)/shard_map/all_to_all | solution.py:724
  115.5 1.7 collective-permute-start.16
  116.0 25.9 %collective-permute-start.21 = (bf16[1152,256]{1,0:T(8,128)(2,1)}, bf16[1152,256]{1,0:T(8,128)(2,1)S(1)}, u32[]{:S(2)}, u32[]{:S(2)}) collective-permute-start(bf16[1152,256]{1,0:T(8,128)(2,1)} %copy-done.35), channel_id=1, source_target_pairs={{2,4},{3,5},{4,2},{5,3},{10,12},{11,13},{12,10},{13,11},{18,20},{1... | collective-permute-start | bytes 1769480 | tf_op jit(solution)/shard_map/ppermute | solution.py:716
  118.0 23.9 %collective-permute-start.22 = (bf16[1152,256]{1,0:T(8,128)(2,1)}, bf16[1152,256]{1,0:T(8,128)(2,1)S(1)}, u32[]{:S(2)}, u32[]{:S(2)}) collective-permute-start(bf16[1152,256]{1,0:T(8,128)(2,1)} %copy-done.36), channel_id=1, source_target_pairs={{2,0},{3,1},{4,6},{5,7},{10,8},{11,9},{12,14},{13,15},{18,16},{19,... | collective-permute-start | bytes 1769480 | tf_op jit(solution)/shard_map/ppermute | solution.py:720
  119.3 22.6 %collective-permute-start.20 = (bf16[1152,256]{1,0:T(8,128)(2,1)S(1)}, bf16[1152,256]{1,0:T(8,128)(2,1)S(1)}, u32[]{:S(2)}, u32[]{:S(2)}) collective-permute-start(bf16[1152,256]{1,0:T(8,128)(2,1)S(1)} %get-tuple-element.332), channel_id=1, source_target_pairs={{0,2},{1,3},{6,4},{7,5},{8,10},{9,11},{14,12},{15,13},{16,18},{17,... | collective-permute-start | bytes 1769480 | tf_op jit(solution)/shard_map/ppermute | solution.py:712
  126.5 21.7 %collective-permute-start.19 = (bf16[512,512]{1,0:T(8,128)(2,1)S(1)}, bf16[512,512]{1,0:T(8,128)(2,1)S(1)}, u32[]{:S(2)}, u32[]{:S(2)}) collective-permute-start(bf16[512,512]{1,0:T(8,128)(2,1)S(1)} %copy-done.18), channel_id=1, source_target_pairs={{2,4},{3,5},{4,2},{5,3},{10,12},{11,13},{12,10},{13,11},{18,20},{1... | collective-permute-start | bytes 1572872 | tf_op jit(solution)/shard_map/ppermute | solution.py:716
  127.2 24.2 %collective-permute-start.18 = (bf16[512,512]{1,0:T(8,128)(2,1)S(1)}, bf16[512,512]{1,0:T(8,128)(2,1)S(1)}, u32[]{:S(2)}, u32[]{:S(2)}) collective-permute-start(bf16[512,512]{1,0:T(8,128)(2,1)S(1)} %copy-done.18), channel_id=1, source_target_pairs={{0,2},{1,3},{2,0},{3,1},{4,6},{5,7},{6,4},{7,5},{8,10},{9,11},{10,... | collective-permute-start | bytes 1572872 | tf_op jit(solution)/shard_map/ppermute | solution.py:704
  134.5 1.0 copy-start.3
  135.5 18.7 %copy-start.19 = (bf16[512,512]{1,0:T(8,128)(2,1)S(1)}, bf16[512,512]{1,0:T(8,128)(2,1)}, u32[]{:S(2)}) copy-start(bf16[512,512]{1,0:T(8,128)(2,1)} %copy-done.17) | copy-start | bytes 1572868
  141.9 26.0 %copy-start.14 = (bf16[1152,256]{1,0:T(8,128)(2,1)S(1)}, bf16[1152,256]{1,0:T(8,128)(2,1)}, u32[]{:S(2)}) copy-start(bf16[1152,256]{1,0:T(8,128)(2,1)} %copy-done.13) | copy-start | bytes 1769476
  141.9 33.8 %copy-start.37 = (bf16[1152,256]{1,0:T(8,128)(2,1)}, bf16[1152,256]{1,0:T(8,128)(2,1)S(1)}, u32[]{:S(2)}) copy-start(bf16[1152,256]{1,0:T(8,128)(2,1)S(1)} %collective-permute-done.21.refs_5_) | copy-start | bytes 1769476
  142.9 18.6 %collective-permute-start.26 = (bf16[1152,256]{1,0:T(8,128)(2,1)S(1)}, bf16[1152,256]{1,0:T(8,128)(2,1)S(1)}, u32[]{:S(2)}, u32[]{:S(2)}) collective-permute-start(bf16[1152,256]{1,0:T(8,128)(2,1)S(1)} %get-tuple-element.354), channel_id=1, source_target_pairs={{2,4},{3,5},{4,2},{5,3},{10,12},{11,13},{12,10},{13,11},{18,20},{1... | collective-permute-start | bytes 1769480 | tf_op jit(solution)/shard_map/ppermute | solution.py:716
  143.6 20.5 %collective-permute-start.25 = (bf16[1152,256]{1,0:T(8,128)(2,1)S(1)}, bf16[1152,256]{1,0:T(8,128)(2,1)S(1)}, u32[]{:S(2)}, u32[]{:S(2)}) collective-permute-start(bf16[1152,256]{1,0:T(8,128)(2,1)S(1)} %get-tuple-element.353.refs_0_), channel_id=1, source_target_pairs={{0,2},{1,3},{6,4},{7,5},{8,10},{9,11},{14,12},{15,13},{16,18},{17,... | collective-permute-start | bytes 1769480 | tf_op jit(solution)/shard_map/ppermute | solution.py:712
  151.4 16.4 %collective-permute-start.24 = (bf16[512,512]{1,0:T(8,128)(2,1)S(1)}, bf16[512,512]{1,0:T(8,128)(2,1)}, u32[]{:S(2)}, u32[]{:S(2)}) collective-permute-start(bf16[512,512]{1,0:T(8,128)(2,1)S(1)} %collective-permute-done.18.refs_2_.refs_3_), channel_id=1, source_target_pairs={{2,4},{3,5},{4,2},{5,3},{10,12},{11,13},{12,10},{13,11},{18,20},{1... | collective-permute-start | bytes 1572872 | tf_op jit(solution)/shard_map/ppermute | solution.py:716
  152.9 14.9 %collective-permute-start.23 = (bf16[512,512]{1,0:T(8,128)(2,1)S(1)}, bf16[512,512]{1,0:T(8,128)(2,1)S(1)}, u32[]{:S(2)}, u32[]{:S(2)}) collective-permute-start(bf16[512,512]{1,0:T(8,128)(2,1)S(1)} %collective-permute-done.19.refs_3_), channel_id=1, source_target_pairs={{2,0},{3,1},{4,6},{5,7},{10,8},{11,9},{12,14},{13,15},{18,16},{19,... | collective-permute-start | bytes 1572872 | tf_op jit(solution)/shard_map/ppermute | solution.py:720
  154.9 30.1 %collective-permute-start.29 = (bf16[1152,256]{1,0:T(8,128)(2,1)S(1)}, bf16[1152,256]{1,0:T(8,128)(2,1)}, u32[]{:S(2)}, u32[]{:S(2)}) collective-permute-start(bf16[1152,256]{1,0:T(8,128)(2,1)S(1)} %get-tuple-element.371.refs_0_), channel_id=1, source_target_pairs={{0,2},{1,3},{6,4},{7,5},{8,10},{9,11},{14,12},{15,13},{16,18},{17,... | collective-permute-start | bytes 1769480 | tf_op jit(solution)/shard_map/ppermute | solution.py:712
  165.0 19.9 %collective-permute-start.31 = (bf16[1152,256]{1,0:T(8,128)(2,1)}, bf16[1152,256]{1,0:T(8,128)(2,1)}, u32[]{:S(2)}, u32[]{:S(2)}) collective-permute-start(bf16[1152,256]{1,0:T(8,128)(2,1)} %get-tuple-element.373), channel_id=1, source_target_pairs={{2,4},{3,5},{4,2},{5,3},{10,12},{11,13},{12,10},{13,11},{18,20},{1... | collective-permute-start | bytes 1769480 | tf_op jit(solution)/shard_map/ppermute | solution.py:716
  166.5 19.6 %collective-permute-start.30 = (bf16[1152,256]{1,0:T(8,128)(2,1)}, bf16[1152,256]{1,0:T(8,128)(2,1)}, u32[]{:S(2)}, u32[]{:S(2)}) collective-permute-start(bf16[1152,256]{1,0:T(8,128)(2,1)} %get-tuple-element.372), channel_id=1, source_target_pairs={{2,0},{3,1},{4,6},{5,7},{10,8},{11,9},{12,14},{13,15},{18,16},{19,... | collective-permute-start | bytes 1769480 | tf_op jit(solution)/shard_map/ppermute | solution.py:720
  167.8 26.1 %collective-permute-start.28 = (bf16[1152,256]{1,0:T(8,128)(2,1)S(1)}, bf16[1152,256]{1,0:T(8,128)(2,1)}, u32[]{:S(2)}, u32[]{:S(2)}) collective-permute-start(bf16[1152,256]{1,0:T(8,128)(2,1)S(1)} %copy-done.14), channel_id=1, source_target_pairs={{0,2},{1,3},{6,4},{7,5},{8,10},{9,11},{14,12},{15,13},{16,18},{17,... | collective-permute-start | bytes 1769480 | tf_op jit(solution)/shard_map/ppermute | solution.py:712
  175.7 18.3 %collective-permute-start.27 = (bf16[512,512]{1,0:T(8,128)(2,1)}, bf16[512,512]{1,0:T(8,128)(2,1)S(1)}, u32[]{:S(2)}, u32[]{:S(2)}) collective-permute-start(bf16[512,512]{1,0:T(8,128)(2,1)} %collective-permute-done.24.refs_2_), channel_id=1, source_target_pairs={{2,0},{3,1},{4,6},{5,7},{10,8},{11,9},{12,14},{13,15},{18,16},{19,... | collective-permute-start | bytes 1572872 | tf_op jit(solution)/shard_map/ppermute | solution.py:720
  180.0 14.0 %copy-start.21 = (bf16[512,512]{1,0:T(8,128)(2,1)S(1)}, bf16[512,512]{1,0:T(8,128)(2,1)}, u32[]{:S(2)}) copy-start(bf16[512,512]{1,0:T(8,128)(2,1)} %copy-done.20) | copy-start | bytes 1572868
  184.9 9.7 %copy-start.39 = (bf16[4,256,1152]{2,1,0:T(8,128)(2,1)S(1)}, bf16[4,256,1152]{2,1,0:T(8,128)(2,1)}, u32[]{:S(2)}) copy-start(bf16[4,256,1152]{2,1,0:T(8,128)(2,1)} %get-tuple-element.393) | copy-start | bytes 7077892
  194.6 4.6 %collective-permute-start.34 = (bf16[4,256,1152]{2,1,0:T(8,128)(2,1)S(1)}, bf16[4,256,1152]{2,1,0:T(8,128)(2,1)S(1)}, u32[]{:S(2)}, u32[]{:S(2)}) collective-permute-start(bf16[4,256,1152]{2,1,0:T(8,128)(2,1)S(1)} %copy-done.39), channel_id=1, source_target_pairs={{0,1},{1,0},{2,3},{3,2},{4,5},{5,4},{6,7},{7,6},{8,9},{9,8},{10,11... | collective-permute-start | bytes 7077896 | tf_op jit(solution)/shard_map/ppermute | solution.py:700
  194.7 8.7 %collective-permute-start.32 = (bf16[1024,512]{1,0:T(8,128)(2,1)S(1)}, bf16[1024,512]{1,0:T(8,128)(2,1)S(1)}, u32[]{:S(2)}, u32[]{:S(2)}) collective-permute-start(bf16[1024,512]{1,0:T(8,128)(2,1)S(1)} %get-tuple-element.389.refs_1_), channel_id=1, source_target_pairs={{0,1},{1,0},{2,3},{3,2},{4,5},{5,4},{6,7},{7,6},{8,9},{9,8},{10,11... | collective-permute-start | bytes 3145736 | tf_op jit(solution)/shard_map/ppermute | solution.py:700
  195.2 8.2 %collective-permute-start.33 = (bf16[1024,512]{1,0:T(8,128)(2,1)S(1)}, bf16[1024,512]{1,0:T(8,128)(2,1)S(1)}, u32[]{:S(2)}, u32[]{:S(2)}) collective-permute-start(bf16[1024,512]{1,0:T(8,128)(2,1)S(1)} %get-tuple-element.387.refs_2_), channel_id=1, source_target_pairs={{0,1},{1,0},{2,3},{3,2},{4,5},{5,4},{6,7},{7,6},{8,9},{9,8},{10,11... | collective-permute-start | bytes 3145736 | tf_op jit(solution)/shard_map/ppermute | solution.py:700
  (13 other events, 9.9 us)

commit v9 on v8

--- a/solution.py
+++ b/solution.py
@@ -122,6 +122,10 @@
     return jax.ShapeDtypeStruct(shape, dtype)
 
 
+def far_array(shape, dtype):
+    return pltpu.HBM(shape, dtype)
+
+
 class Line:
     def __init__(self):
         self.token = None
@@ -356,7 +360,7 @@
         kernel,
         [
             array((rows, units), jnp.bfloat16),
-            array((units, rows), jnp.bfloat16),
+            far_array((units, rows), jnp.bfloat16),
             array((4, units), jnp.float32),
             last,
         ],
@@ -383,7 +387,7 @@
     cols = mine.shape[0] // 8
     return call(
         functools.partial(part_kernel, slots),
-        [array((blocks * cols, rows), dtype) for blocks, dtype in outs],
+        [far_array((blocks * cols, rows), dtype) for blocks, dtype in outs],
         [SMEM, HBM, HBM, VMEM, VMEM],
         [VMEM] * len(outs),
         "parts",
@@ -488,43 +492,61 @@
     rows = rows or min(one.shape[0], two.shape[0])
     return call(
         functools.partial(add_kernel, block * rows),
-        array((rows, one.shape[1]), jnp.bfloat16),
+        far_array((rows, one.shape[1]), jnp.bfloat16),
         [VMEM, VMEM],
         VMEM,
         "add",
     )(one, two)
 
 
-def finish_kernel(where, marks, group, kept, third, cross, last, out, held, own, sems):
+def finish_kernel(where, marks, group, kept, third, cross, last, out, held, own, done, sems):
     second = group[...] == 1
-    cols = out.shape[0]
-    copies = [pltpu.make_async_copy(kept, own, sems.at[3])]
-    for n, source in enumerate((third, cross, last)):
-        copies.append(pltpu.make_async_copy(source, held.at[n], sems.at[n]))
-    for copy in copies:
-        copy.start()
-    for copy in copies:
-        copy.wait()
-    for chunk in range(cols // LANES):
-        zero, one = marks_of(marks, where[8], cols, chunk)
-        keep = wide(jnp.where(second, one, zero))
-        rows = slice(chunk * LANES, (chunk + 1) * LANES)
-        total = own[rows, :] + wide(held[0, rows, :])
-        total += wide(held[1, rows, :]) + wide(held[2, rows, :])
-        out[rows, :] = low(total * keep)
+    cols = own.shape[0]
+    tile = cols // 3
+
+    def fetch(t):
+        rows = pl.ds(t * tile, tile)
+        copies = [pltpu.make_async_copy(kept.at[rows, :], own.at[rows, :], sems.at[t, 3])]
+        for n, source in enumerate((third, cross, last)):
+            copies.append(
+                pltpu.make_async_copy(source.at[rows, :], held.at[n, rows, :], sems.at[t, n])
+            )
+        return copies
+
+    def give(t):
+        rows = pl.ds(t * tile, tile)
+        return pltpu.make_async_copy(done.at[rows, :], out.at[rows, :], sems.at[t, 4])
+
+    for t in range(3):
+        for copy in fetch(t):
+            copy.start()
+    for t in range(3):
+        for copy in fetch(t):
+            copy.wait()
+        for chunk in range(t * tile // LANES, (t + 1) * tile // LANES):
+            zero, one = marks_of(marks, where[8], cols, chunk)
+            keep = wide(jnp.where(second, one, zero))
+            rows = slice(chunk * LANES, (chunk + 1) * LANES)
+            total = own[rows, :] + wide(held[0, rows, :])
+            total += wide(held[1, rows, :]) + wide(held[2, rows, :])
+            done[rows, :] = low(total * keep)
+        give(t).start()
+    for t in range(3):
+        give(t).wait()
 
 
 def finish(where, marks, group, kept, third, cross, last):
     return call(
         finish_kernel,
-        array(kept.shape, jnp.bfloat16),
+        pltpu.HBM(kept.shape, jnp.bfloat16),
         [SMEM, SMEM, VMEM] + [HBM] * 4,
-        VMEM,
+        HBM,
         "finish",
         [
             pltpu.VMEM((3, *kept.shape), jnp.bfloat16),
             pltpu.VMEM(kept.shape, jnp.float32),
-            pltpu.SemaphoreType.DMA((4,)),
+            pltpu.VMEM(kept.shape, jnp.bfloat16),
+            pltpu.SemaphoreType.DMA((3, 5)),
         ],
     )(where, marks, group, *[in_hbm(x) for x in (kept, third, cross, last)])
 
@@ -776,7 +798,7 @@
     dz_a, dzt_a, sums_a, hidden_a = tower(
         first_kernel,
         "tower_a",
-        array((rows, units), f32),
+        far_array((rows, units), f32),
         own_a,
         got_sum,
         tower_bias,
@@ -803,8 +825,9 @@
         dzo_a,
     )
     in2_a = send(inward, second_a)
-    b_end, b_mid2 = wait(b_end, b_mid2)
+    b_mid2 = wait(b_mid2)
     b_end2 = send(outward, b_mid2)
+    b_end = wait(b_end)
     b2 = choose(where, b_end, b_mid2)
     keep_b, give_b, last_b, slot_b = forward_open(where, b0, b1, b2, weight_b, whole_b)
     in1_a = wait(in1_a)
@@ -819,7 +842,7 @@
     dz_b, dzt_b, sums_b, local = tower(
         second_kernel,
         "tower_b",
-        array((2 * rows, units), bf16),
+        far_array((2 * rows, units), bf16),
         own_b,
         got_sum,
         hidden_a,

time: 208 us -> 207 us (level)
  Pallas kernels: 73.9 us -> 80.4 us
  local copies, waits for them, and re-layouts: 12 us -> 6.75 us
  waiting for transfers between devices: 46.2 us -> 42.3 us
    pallas_call x35, Pallas kernels: 73.9 us -> 80.4 us  [go(): *results, line.token = run(*operands, *before)]
    unnamed x80 -> x68, local copies, waits for them, and re-layouts: 12 us -> 6.67 us
  transfers between devices with their start and end apart: 37 -> 37, of which waited for: 14 -> 13; matrix products, arithmetic and copies ran while one was open for 0% -> 0% of each run, Pallas kernels for 34% -> 37%
where the time goes in v9:
time: 207 us; the launch traced here: 206 us
  Pallas kernels  80.4 us (39%)
  starting transfers between devices  74.1 us (36%)
  waiting for transfers between devices  42.3 us (20%)
  local copies, waits for them, and re-layouts  6.75 us (3%)
    pallas_call x35, Pallas kernels, go(): *results, line.token = run(*operands, *before)  80.4 us
    ppermute x6, starting transfers between devices, inward(): return lax.ppermute(x, 'mp', ENDS_IN)  37.9 us
    ppermute x4, waiting for transfers between devices, along(): return lax.ppermute(x, 'mp', NEAR_Z)  24.8 us
    all_to_all x2, starting transfers between devices, exchange(): return lax.all_to_all(x, 'dp', 0, 0)  9.73 us
    ppermute x6, waiting for transfers between devices, outward(): return lax.ppermute(x, 'mp', ENDS_OUT)  9.04 us
    ppermute x6, starting transfers between devices, outward(): return lax.ppermute(x, 'mp', ENDS_OUT)  7.7 us
    ppermute x8, starting transfers between devices, between(): return lax.ppermute(x, 'mp', MIDS)  7.16 us
    ppermute x4, starting transfers between devices, along(): return lax.ppermute(x, 'mp', NEAR_Z)  6.84 us
  transfers between devices with their start and end apart: 37, of which 13 were waited for; matrix products, arithmetic and copies ran while one was open for 0% of the time, Pallas kernels for 37%

profile of v9, /device:TPU:0, one launch (start us, length us, event | category | flops | bytes accessed | tf_op | source)
XLA Modules:
  0.0 205.8 jit_solution(10662680372275851331)
XLA Ops:
  1.2 3.0 %collective-permute-start = (bf16[256,1152]{1,0:T(8,128)(2,1)}, bf16[256,1152]{1,0:T(8,128)(2,1)S(1)}, u32[]{:S(2)}, u32[]{:S(2)}) collective-permute-start(bf16[256,1152]{1,0:T(8,128)(2,1)} %refs_3_.5), channel_id=1, source_target_pairs={{0,2},{1,3},{2,0},{3,1},{4,6},{5,7},{6,4},{7,5},{8,10},{9,11},{10,... | collective-permute-start | bytes 1769480 | tf_op jit(solution)/shard_map/ppermute | solution.py:726
  4.2 2.6 %collective-permute-start.1 = (bf16[256,1152]{1,0:T(8,128)(2,1)}, bf16[256,1152]{1,0:T(8,128)(2,1)S(1)}, u32[]{:S(2)}, u32[]{:S(2)}) collective-permute-start(bf16[256,1152]{1,0:T(8,128)(2,1)} %refs_3_.5), channel_id=1, source_target_pairs={{0,4},{1,5},{2,6},{3,7},{4,0},{5,1},{6,2},{7,3},{8,12},{9,13},{10,... | collective-permute-start | bytes 1769480 | tf_op jit(solution)/shard_map/ppermute | solution.py:730
  8.2 2.0 mask_image.5
  10.2 2.0 mask_image.6
  12.2 18.3 %collective-permute-done.refs_3_ = bf16[256,1152]{1,0:T(8,128)(2,1)S(1)} collective-permute-done((bf16[256,1152]{1,0:T(8,128)(2,1)}, bf16[256,1152]{1,0:T(8,128)(2,1)S(1)}, u32[]{:S(2)}, u32[]{:S(2)}) %collective-permute-start) | collective-permute-done | bytes 589856 | tf_op jit(solution)/shard_map/ppermute | solution.py:726
  30.5 2.6 %collective-permute-done.1.refs_3_ = bf16[256,1152]{1,0:T(8,128)(2,1)S(1)} collective-permute-done((bf16[256,1152]{1,0:T(8,128)(2,1)}, bf16[256,1152]{1,0:T(8,128)(2,1)S(1)}, u32[]{:S(2)}, u32[]{:S(2)}) %collective-permute-start.1) | collective-permute-done | bytes 589856 | tf_op jit(solution)/shard_map/ppermute | solution.py:730
  33.5 1.6 collective-permute-start.2
  37.9 1.2 mask_image.7
  39.1 1.2 mask_image.8
  40.4 5.3 %forward_open.2 = (f32[256,512]{1,0:T(8,128)S(1)}, f32[256,512]{1,0:T(8,128)S(1)}, bf16[2,1152,512]{2,1,0:T(8,128)(2,1)S(1)}, bf16[2,1152,512]{2,1,0:T(8,128)(2,1)S(1)}, f32[8,128]{1,0:T(8,128)S(1)}) custom-call(s32[9]{0:T(128)S(1)} %concatenate.3.refs_0_, bf16[256,1152]{1,0:T(8,128)(2,1)S(1)} %get-tuple-element.218.refs_1_, ...), custom_call_target="tpu_custom_call" | custom-call | flops 1 | bytes 1 | tf_op jit(solution)/shard_map/forward_open/pallas_call | solution.py:175
  45.7 3.7 %collective-permute-done.4.refs_3_ = bf16[256,1152]{1,0:T(8,128)(2,1)} collective-permute-done((bf16[256,1152]{1,0:T(8,128)(2,1)S(1)}, bf16[256,1152]{1,0:T(8,128)(2,1)}, u32[]{:S(2)}, u32[]{:S(2)}) %collective-permute-start.4) | collective-permute-done | bytes 589856 | tf_op jit(solution)/shard_map/ppermute | solution.py:726
  49.5 2.0 mask_image.9
  51.5 0.8 forward_close.2
  52.4 1.9 collective-permute-done.7.refs_1_
  54.3 1.3 tower_a.1
  55.6 2.9 %pack.2 = (bf16[4,272,1664]{2,1,0:T(8,128)(2,1)}, f32[8,128]{1,0:T(8,128)S(1)}) custom-call(s32[9]{0:T(128)S(1)} %concatenate.3.refs_0_, bf16[256,1152]{1,0:T(8,128)(2,1)S(1)} %get-tuple-element.218.refs_1_, bf16[256,1152]{1,0:T(8,128)(2,1)S(1)} %get-tuple-element.221.refs_2_, bf16[256,1152]{1,0:T(8,128)(2,1)S(1)} %get-tuple-element.223.refs_3_, ...), custom_call_target="tpu_custom_call" | custom-call | flops 1 | bytes 1 | tf_op jit(solution)/shard_map/pack/pallas_call | solution.py:175
  59.1 0.8 copy-done.10
  59.9 4.9 %all-to-all-start = ((bf16[4,272,1664]{2,1,0:T(8,128)(2,1)}), bf16[4,272,1664]{2,1,0:T(8,128)(2,1)}, u32[]{:S(2)}, u32[]{:S(2)}) async-start(bf16[4,272,1664]{2,1,0:T(8,128)(2,1)} %get-tuple-element.313), calls=%async_computation | async-start | bytes 7241728 | tf_op jit(solution)/shard_map/all_to_all | solution.py:746
  65.7 1.3 collective-permute-start.12
  67.3 0.9 copy-done.3
  68.9 0.8 first_slot.2
  69.7 5.9 %collective-permute-start.11 = (bf16[1152,256]{1,0:T(8,128)(2,1)S(1)}, bf16[1152,256]{1,0:T(8,128)(2,1)S(1)}, u32[]{:S(2)}, u32[]{:S(2)}) collective-permute-start(bf16[1152,256]{1,0:T(8,128)(2,1)S(1)} %get-tuple-element.267), channel_id=1, source_target_pairs={{0,2},{1,3},{6,4},{7,5},{8,10},{9,11},{14,12},{15,13},{16,18},{17,... | collective-permute-start | bytes 1769480 | tf_op jit(solution)/shard_map/ppermute | solution.py:734
  75.6 6.8 %parts.2 = (bf16[1152,256]{1,0:T(8,128)(2,1)}, bf16[1152,256]{1,0:T(8,128)(2,1)}, f32[1152,256]{1,0:T(8,128)}, f32[8,128]{1,0:T(8,128)S(1)}) custom-call(s32[9]{0:T(128)S(1)} %concatenate.3.refs_0_, bf16[9216,512]{1,0:T(8,128)(2,1)} %refs_1_.14, bf16[9216,512]{1,0:T(8,128)(2,1)} %collective-permute-done.5.refs_5_.refs_2_, bf16[512,256]{1,0:T(8,128)(2,1)S(1)} %copy-done.3, ...), custom_call_target="tpu_custom_call" | custom-call | flops 1 | bytes 1 | tf_op jit(solution)/shard_map/parts/pallas_call | solution.py:175
  82.4 1.3 collective-permute-start.10
  83.7 4.6 %collective-permute-start.14 = (bf16[1152,256]{1,0:T(8,128)(2,1)}, bf16[1152,256]{1,0:T(8,128)(2,1)S(1)}, u32[]{:S(2)}, u32[]{:S(2)}) collective-permute-start(bf16[1152,256]{1,0:T(8,128)(2,1)} %get-tuple-element.291.refs_0_), channel_id=1, source_target_pairs={{0,2},{1,3},{6,4},{7,5},{8,10},{9,11},{14,12},{15,13},{16,18},{17,... | collective-permute-start | bytes 1769480 | tf_op jit(solution)/shard_map/ppermute | solution.py:734
  89.0 5.3 %forward_open.3 = (f32[256,512]{1,0:T(8,128)S(1)}, f32[256,512]{1,0:T(8,128)S(1)}, bf16[2,1152,512]{2,1,0:T(8,128)(2,1)S(1)}, bf16[2,1152,512]{2,1,0:T(8,128)(2,1)S(1)}, f32[8,128]{1,0:T(8,128)S(1)}) custom-call(s32[9]{0:T(128)S(1)} %concatenate.3.refs_0_, bf16[256,1152]{1,0:T(8,128)(2,1)S(1)} %get-tuple-element.217.refs_1_, ...), custom_call_target="tpu_custom_call" | custom-call | flops 1 | bytes 1 | tf_op jit(solution)/shard_map/forward_open/pallas_call | solution.py:175
  94.3 1.0 add.38
  96.0 3.4 %collective-permute-done.10.refs_1_ = bf16[256,1152]{1,0:T(8,128)(2,1)S(1)} collective-permute-done((bf16[256,1152]{1,0:T(8,128)(2,1)S(1)}, bf16[256,1152]{1,0:T(8,128)(2,1)S(1)}, u32[]{:S(2)}, u32[]{:S(2)}) %collective-permute-start.10) | collective-permute-done | bytes 589856 | tf_op jit(solution)/shard_map/ppermute | solution.py:742
  99.3 0.9 choose.4
  100.2 0.8 forward_close.3
  101.2 1.0 add.39
  102.1 0.9 collective-permute-done.13.refs_1_
  103.1 1.4 tower_b.1
  104.5 2.8 %pack.3 = (bf16[4,272,1664]{2,1,0:T(8,128)(2,1)}, f32[8,128]{1,0:T(8,128)S(1)}) custom-call(s32[9]{0:T(128)S(1)} %concatenate.3.refs_0_, bf16[256,1152]{1,0:T(8,128)(2,1)S(1)} %get-tuple-element.217.refs_1_, bf16[256,1152]{1,0:T(8,128)(2,1)S(1)} %collective-permute-done.2.refs_2_, bf16[256,1152]{1,0:T(8,128)(2,1)S(1)} %get-tuple-element.273.refs_3_, ...), custom_call_target="tpu_custom_call" | custom-call | flops 1 | bytes 1 | tf_op jit(solution)/shard_map/pack/pallas_call | solution.py:175
  107.4 1.0 add.40
  108.5 4.9 %all-to-all-start.1 = ((bf16[4,272,1664]{2,1,0:T(8,128)(2,1)}), bf16[4,272,1664]{2,1,0:T(8,128)(2,1)}, u32[]{:S(2)}, u32[]{:S(2)}) async-start(bf16[4,272,1664]{2,1,0:T(8,128)(2,1)} %get-tuple-element.374), calls=%async_computation.1 | async-start | bytes 7241728 | tf_op jit(solution)/shard_map/all_to_all | solution.py:746
  115.0 0.8 first_slot.3
  115.8 1.3 collective-permute-start.22
  117.1 7.6 %collective-permute-start.20 = (bf16[1152,256]{1,0:T(8,128)(2,1)S(1)}, bf16[1152,256]{1,0:T(8,128)(2,1)S(1)}, u32[]{:S(2)}, u32[]{:S(2)}) collective-permute-start(bf16[1152,256]{1,0:T(8,128)(2,1)S(1)} %get-tuple-element.332), channel_id=1, source_target_pairs={{0,2},{1,3},{6,4},{7,5},{8,10},{9,11},{14,12},{15,13},{16,18},{17,... | collective-permute-start | bytes 1769480 | tf_op jit(solution)/shard_map/ppermute | solution.py:734
  125.5 1.8 collective-permute-start.18
  127.3 6.8 %parts.3 = (bf16[1152,256]{1,0:T(8,128)(2,1)}, bf16[1152,256]{1,0:T(8,128)(2,1)}, f32[1152,256]{1,0:T(8,128)}, f32[8,128]{1,0:T(8,128)S(1)}) custom-call(s32[9]{0:T(128)S(1)} %concatenate.3.refs_0_, bf16[9216,512]{1,0:T(8,128)(2,1)} %refs_1_.15, bf16[9216,512]{1,0:T(8,128)(2,1)} %collective-permute-done.6.refs_5_.refs_2_, bf16[512,256]{1,0:T(8,128)(2,1)S(1)} %copy-done.2, ...), custom_call_target="tpu_custom_call" | custom-call | flops 1 | bytes 1 | tf_op jit(solution)/shard_map/parts/pallas_call | solution.py:175
  134.1 6.3 %weight_grad.3 = (f32[2304,512]{1,0:T(8,128)}, f32[8,128]{1,0:T(8,128)S(1)}) custom-call(s32[9]{0:T(128)S(1)} %concatenate.3.refs_0_, bf16[4,272,1664]{2,1,0:T(8,128)(2,1)} %all-to-all-done.refs_1_.refs_3_.refs_0_, bf16[4,272,1664]{2,1,0:T(8,128)(2,1)} %collective-permute-done.17.refs_2_, bf16[4,272,1664]{2,1,0:T(8,128)(2,1)} %all-to-all-done.refs_1_.refs_3_.refs_0_, ...), custom_call_target="tpu_custom_call" | custom-call | flops 1 | bytes 1 | tf_op jit(solution)/shard_map/weight_grad/pallas_call | solution.py:175
  140.5 1.0 add.41
  142.2 4.8 %collective-permute-start.25 = (bf16[1152,256]{1,0:T(8,128)(2,1)S(1)}, bf16[1152,256]{1,0:T(8,128)(2,1)S(1)}, u32[]{:S(2)}, u32[]{:S(2)}) collective-permute-start(bf16[1152,256]{1,0:T(8,128)(2,1)S(1)} %copy-done.14), channel_id=1, source_target_pairs={{0,2},{1,3},{6,4},{7,5},{8,10},{9,11},{14,12},{15,13},{16,18},{17,... | collective-permute-start | bytes 1769480 | tf_op jit(solution)/shard_map/ppermute | solution.py:734
  147.0 2.7 %collective-permute-done.18.refs_2_.refs_3_ = bf16[512,512]{1,0:T(8,128)(2,1)S(1)} collective-permute-done((bf16[512,512]{1,0:T(8,128)(2,1)S(1)}, bf16[512,512]{1,0:T(8,128)(2,1)S(1)}, u32[]{:S(2)}, u32[]{:S(2)}) %collective-permute-start.18) | collective-permute-done | bytes 524320 | tf_op jit(solution)/shard_map/ppermute | solution.py:726
  149.7 1.5 collective-permute-start.24
  151.2 1.3 collective-permute-start.23
  153.1 6.9 %collective-permute-start.29 = (bf16[1152,256]{1,0:T(8,128)(2,1)S(1)}, bf16[1152,256]{1,0:T(8,128)(2,1)}, u32[]{:S(2)}, u32[]{:S(2)}) collective-permute-start(bf16[1152,256]{1,0:T(8,128)(2,1)S(1)} %copy-done.12), channel_id=1, source_target_pairs={{0,2},{1,3},{6,4},{7,5},{8,10},{9,11},{14,12},{15,13},{16,18},{17,... | collective-permute-start | bytes 1769480 | tf_op jit(solution)/shard_map/ppermute | solution.py:734
  160.0 1.0 add.42
  161.0 1.4 collective-permute-done.25.refs_1_
  162.3 0.9 add.43
  163.3 1.5 collective-permute-start.31
  164.8 1.3 collective-permute-start.30
  166.2 8.2 %collective-permute-start.28 = (bf16[1152,256]{1,0:T(8,128)(2,1)S(1)}, bf16[1152,256]{1,0:T(8,128)(2,1)}, u32[]{:S(2)}, u32[]{:S(2)}) collective-permute-start(bf16[1152,256]{1,0:T(8,128)(2,1)S(1)} %copy-done.9), channel_id=1, source_target_pairs={{0,2},{1,3},{6,4},{7,5},{8,10},{9,11},{14,12},{15,13},{16,18},{17,... | collective-permute-start | bytes 1769480 | tf_op jit(solution)/shard_map/ppermute | solution.py:734
  174.3 1.3 collective-permute-start.27
  176.3 0.8 copy-done.17
  177.0 1.6 total_sums.1
  178.6 4.9 %weight_grad.4 = (f32[2304,512]{1,0:T(8,128)}, bf16[4,256,1152]{2,1,0:T(8,128)(2,1)}, f32[8,128]{1,0:T(8,128)S(1)}) custom-call(s32[9]{0:T(128)S(1)} %concatenate.3.refs_0_, bf16[4,272,1664]{2,1,0:T(8,128)(2,1)} %all-to-all-done.1.refs_1_.refs_2_, bf16[4,272,1664]{2,1,0:T(8,128)(2,1)} %all-to-all-done.1.refs_1_.refs_2_, f32[8,128]{1,0:T(8,128)S(1)} %get-tuple-element.378.refs_3_), custom_call_target="tpu_custom_call" | custom-call | flops 1 | bytes 1 | tf_op jit(solution)/shard_map/weight_grad/pallas_call | solution.py:175
  183.6 1.1 collective-permute-done.30.refs_6_
  184.7 3.2 %finish.2 = (bf16[1152,256]{1,0:T(8,128)(2,1)}, f32[8,128]{1,0:T(8,128)S(1)}) custom-call(s32[9]{0:T(128)S(1)} %concatenate.3.refs_0_, s32[2,36]{1,0:T(2,128)S(1)} %copy-done.22, s32[1,256]{1,0:T(1,128)S(1)} %bitcast.17, f32[1152,256]{1,0:T(8,128)} %get-tuple-element.370.refs_3_, bf16[1152,256]{1,0:T(8,128)(2,1)} %collective-permute-done.29.refs_4_, ...), custom_call_target="tpu_custom_call" | custom-call | flops 1 | bytes 1 | tf_op jit(solution)/shard_map/finish/pallas_call | solution.py:175
  188.0 4.6 %collective-permute-done.27.refs_2_ = bf16[512,512]{1,0:T(8,128)(2,1)S(1)} collective-permute-done((bf16[512,512]{1,0:T(8,128)(2,1)}, bf16[512,512]{1,0:T(8,128)(2,1)S(1)}, u32[]{:S(2)}, u32[]{:S(2)}) %collective-permute-start.27) | collective-permute-done | bytes 524320 | tf_op jit(solution)/shard_map/ppermute | solution.py:742
  193.8 3.2 %finish.3 = (bf16[1152,256]{1,0:T(8,128)(2,1)}, f32[8,128]{1,0:T(8,128)S(1)}) custom-call(s32[9]{0:T(128)S(1)} %concatenate.3.refs_0_, s32[2,36]{1,0:T(2,128)S(1)} %copy-done.22, s32[1,256]{1,0:T(1,128)S(1)} %bitcast.18, f32[1152,256]{1,0:T(8,128)} %get-tuple-element.395.refs_3_, bf16[1152,256]{1,0:T(8,128)(2,1)} %collective-permute-done.28.refs_4_, ...), custom_call_target="tpu_custom_call" | custom-call | flops 1 | bytes 1 | tf_op jit(solution)/shard_map/finish/pallas_call | solution.py:175
  197.8 4.2 %weight_grad.5 = (f32[2304,512]{1,0:T(8,128)}, f32[8,128]{1,0:T(8,128)S(1)}) custom-call(s32[9]{0:T(128)S(1)} %concatenate.3.refs_0_, bf16[4,256,1152]{2,1,0:T(8,128)(2,1)S(1)} %collective-permute-done.34.refs_1_, bf16[4,272,1664]{2,1,0:T(8,128)(2,1)} %all-to-all-done.1.refs_1_.refs_2_, ...), custom_call_target="tpu_custom_call", output_to_operand_aliasing={{0}: (3, {})} | custom-call | flops 1 | bytes 1 | tf_op jit(solution)/shard_map/weight_grad/pallas_call | solution.py:175
  202.0 3.7 %lay_out.1 = (bf16[256,4096]{1,0:T(8,128)(2,1)}, bf16[256,4096]{1,0:T(8,128)(2,1)}, f32[8,128]{1,0:T(8,128)}) custom-call(s32[9]{0:T(128)S(1)} %concatenate.3.refs_0_, bf16[1024,512]{1,0:T(8,128)(2,1)S(1)} %get-tuple-element.389.refs_1_, bf16[1024,512]{1,0:T(8,128)(2,1)S(1)} %get-tuple-element.387.refs_2_, ...), custom_call_target="tpu_custom_call" | custom-call | flops 1 | bytes 1 | tf_op jit(solution)/shard_map/lay_out/pallas_call | solution.py:175
  (115 shorter events, 15.9 us)
Async XLA Ops:
  0.6 39.7 %collective-permute-start.5 = (bf16[9216,512]{1,0:T(8,128)(2,1)}, bf16[9216,512]{1,0:T(8,128)(2,1)}, u32[]{:S(2)}, u32[]{:S(2)}) collective-permute-start(bf16[9216,512]{1,0:T(8,128)(2,1)} %refs_1_.14), channel_id=1, source_target_pairs={{0,1},{1,0},{2,3},{3,2},{4,5},{5,4},{6,7},{7,6},{8,9},{9,8},{10,11... | collective-permute-start | bytes 28311560 | tf_op jit(solution)/shard_map/ppermute | solution.py:722
  1.2 39.2 %collective-permute-start.6 = (bf16[9216,512]{1,0:T(8,128)(2,1)}, bf16[9216,512]{1,0:T(8,128)(2,1)}, u32[]{:S(2)}, u32[]{:S(2)}) collective-permute-start(bf16[9216,512]{1,0:T(8,128)(2,1)} %refs_1_.15), channel_id=1, source_target_pairs={{0,1},{1,0},{2,3},{3,2},{4,5},{5,4},{6,7},{7,6},{8,9},{9,8},{10,11... | collective-permute-start | bytes 28311560 | tf_op jit(solution)/shard_map/ppermute | solution.py:722
  1.2 29.3 %collective-permute-start = (bf16[256,1152]{1,0:T(8,128)(2,1)}, bf16[256,1152]{1,0:T(8,128)(2,1)S(1)}, u32[]{:S(2)}, u32[]{:S(2)}) collective-permute-start(bf16[256,1152]{1,0:T(8,128)(2,1)} %refs_3_.5), channel_id=1, source_target_pairs={{0,2},{1,3},{2,0},{3,1},{4,6},{5,7},{6,4},{7,5},{8,10},{9,11},{10,... | collective-permute-start | bytes 1769480 | tf_op jit(solution)/shard_map/ppermute | solution.py:726
  4.2 28.8 %collective-permute-start.1 = (bf16[256,1152]{1,0:T(8,128)(2,1)}, bf16[256,1152]{1,0:T(8,128)(2,1)S(1)}, u32[]{:S(2)}, u32[]{:S(2)}) collective-permute-start(bf16[256,1152]{1,0:T(8,128)(2,1)} %refs_3_.5), channel_id=1, source_target_pairs={{0,4},{1,5},{2,6},{3,7},{4,0},{5,1},{6,2},{7,3},{8,12},{9,13},{10,... | collective-permute-start | bytes 1769480 | tf_op jit(solution)/shard_map/ppermute | solution.py:730
  33.1 16.4 %collective-permute-start.4 = (bf16[256,1152]{1,0:T(8,128)(2,1)S(1)}, bf16[256,1152]{1,0:T(8,128)(2,1)}, u32[]{:S(2)}, u32[]{:S(2)}) collective-permute-start(bf16[256,1152]{1,0:T(8,128)(2,1)S(1)} %collective-permute-done.1.refs_3_), channel_id=1, source_target_pairs={{0,2},{1,3},{2,0},{3,1},{4,6},{5,7},{6,4},{7,5},{8,10},{9,11},{10,... | collective-permute-start | bytes 1769480 | tf_op jit(solution)/shard_map/ppermute | solution.py:726
  33.5 25.5 %collective-permute-start.2 = (bf16[256,1152]{1,0:T(8,128)(2,1)S(1)}, bf16[256,1152]{1,0:T(8,128)(2,1)S(1)}, u32[]{:S(2)}, u32[]{:S(2)}) collective-permute-start(bf16[256,1152]{1,0:T(8,128)(2,1)S(1)} %get-tuple-element.217.refs_1_), channel_id=1, source_target_pairs={{0,2},{1,3},{2,0},{3,1},{4,6},{5,7},{6,4},{7,5},{8,10},{9,11},{10,... | collective-permute-start | bytes 1769480 | tf_op jit(solution)/shard_map/ppermute | solution.py:726
  35.1 23.9 %collective-permute-start.3 = (bf16[256,1152]{1,0:T(8,128)(2,1)S(1)}, bf16[256,1152]{1,0:T(8,128)(2,1)S(1)}, u32[]{:S(2)}, u32[]{:S(2)}) collective-permute-start(bf16[256,1152]{1,0:T(8,128)(2,1)S(1)} %get-tuple-element.217.refs_1_), channel_id=1, source_target_pairs={{2,4},{3,5},{4,2},{5,3},{10,12},{11,13},{12,10},{13,11},{18,20},{1... | collective-permute-start | bytes 1769480 | tf_op jit(solution)/shard_map/ppermute | solution.py:738
  40.4 9.1 %copy-start.22 = (s32[2,36]{1,0:T(2,128)S(1)}, s32[2,36]{1,0:T(2,128)}, u32[]{:S(2)}) copy-start(s32[2,36]{1,0:T(2,128)} %refs_1_.17) | copy-start | bytes 868
  40.4 9.1 %copy-start.25 = (s32[256]{0:T(256)S(1)}, s32[256]{0:T(256)}, u32[]{:S(2)}) copy-start(s32[256]{0:T(256)} %param.13) | copy-start | bytes 3076
  45.6 12.8 %copy-start = (bf16[2,1152,512]{2,1,0:T(8,128)(2,1)}, bf16[2,1152,512]{2,1,0:T(8,128)(2,1)S(1)}, u32[]{:S(2)}) copy-start(bf16[2,1152,512]{2,1,0:T(8,128)(2,1)S(1)} %get-tuple-element.259.refs_0_) | copy-start | bytes 7077892
  45.7 8.6 %copy-start.4 = (bf16[256,512]{1,0:T(8,128)(2,1)S(1)}, bf16[256,512]{1,0:T(8,128)(2,1)}, u32[]{:S(2)}) copy-start(bf16[256,512]{1,0:T(8,128)(2,1)} %refs_5_.3) | copy-start | bytes 786436
  45.7 8.6 %copy-start.6 = (bf16[256,512]{1,0:T(8,128)(2,1)S(1)}, bf16[256,512]{1,0:T(8,128)(2,1)}, u32[]{:S(2)}) copy-start(bf16[256,512]{1,0:T(8,128)(2,1)} %refs_6_.1) | copy-start | bytes 786436
  45.7 8.6 %copy-start.26 = (f32[4,512]{1,0:T(4,128)S(1)}, f32[4,512]{1,0:T(4,128)}, u32[]{:S(2)}) copy-start(f32[4,512]{1,0:T(4,128)} %refs_4_.7) | copy-start | bytes 24580
  45.7 8.6 %copy-start.28 = (f32[2,512]{1,0:T(2,128)S(1)}, f32[2,512]{1,0:T(2,128)}, u32[]{:S(2)}) copy-start(f32[2,512]{1,0:T(2,128)} %refs_3_.7) | copy-start | bytes 12292
  52.3 2.0 collective-permute-start.7
  59.1 0.8 copy-start.10
  59.9 7.4 %copy-start.1 = (bf16[2,1152,512]{2,1,0:T(8,128)(2,1)S(1)}, bf16[2,1152,512]{2,1,0:T(8,128)(2,1)}, u32[]{:S(2)}) copy-start(bf16[2,1152,512]{2,1,0:T(8,128)(2,1)} %copy-done) | copy-start | bytes 7077892
  59.9 48.4 %all-to-all-start = ((bf16[4,272,1664]{2,1,0:T(8,128)(2,1)}), bf16[4,272,1664]{2,1,0:T(8,128)(2,1)}, u32[]{:S(2)}, u32[]{:S(2)}) async-start(bf16[4,272,1664]{2,1,0:T(8,128)(2,1)} %get-tuple-element.313), calls=%async_computation | async-start | bytes 7241728 | tf_op jit(solution)/shard_map/all_to_all | solution.py:746
  64.8 17.6 %collective-permute-start.8 = (bf16[256,1152]{1,0:T(8,128)(2,1)S(1)}, bf16[256,1152]{1,0:T(8,128)(2,1)S(1)}, u32[]{:S(2)}, u32[]{:S(2)}) collective-permute-start(bf16[256,1152]{1,0:T(8,128)(2,1)S(1)} %collective-permute-done.2.refs_2_), channel_id=1, source_target_pairs={{2,4},{3,5},{4,2},{5,3},{10,12},{11,13},{12,10},{13,11},{18,20},{1... | collective-permute-start | bytes 1769480 | tf_op jit(solution)/shard_map/ppermute | solution.py:738
  65.5 1.8 collective-permute-start.9
  65.7 22.6 %collective-permute-start.12 = (bf16[256,1152]{1,0:T(8,128)(2,1)}, bf16[256,1152]{1,0:T(8,128)(2,1)S(1)}, u32[]{:S(2)}, u32[]{:S(2)}) collective-permute-start(bf16[256,1152]{1,0:T(8,128)(2,1)} %copy-done.10), channel_id=1, source_target_pairs={{2,0},{3,1},{4,6},{5,7},{10,8},{11,9},{12,14},{13,15},{18,16},{19,... | collective-permute-start | bytes 1769480 | tf_op jit(solution)/shard_map/ppermute | solution.py:742
  67.3 1.0 copy-start.3
  69.7 24.6 %collective-permute-start.11 = (bf16[1152,256]{1,0:T(8,128)(2,1)S(1)}, bf16[1152,256]{1,0:T(8,128)(2,1)S(1)}, u32[]{:S(2)}, u32[]{:S(2)}) collective-permute-start(bf16[1152,256]{1,0:T(8,128)(2,1)S(1)} %get-tuple-element.267), channel_id=1, source_target_pairs={{0,2},{1,3},{6,4},{7,5},{8,10},{9,11},{14,12},{15,13},{16,18},{17,... | collective-permute-start | bytes 1769480 | tf_op jit(solution)/shard_map/ppermute | solution.py:734
  82.4 17.0 %collective-permute-start.10 = (bf16[256,1152]{1,0:T(8,128)(2,1)S(1)}, bf16[256,1152]{1,0:T(8,128)(2,1)S(1)}, u32[]{:S(2)}, u32[]{:S(2)}) collective-permute-start(bf16[256,1152]{1,0:T(8,128)(2,1)S(1)} %collective-permute-done.8.refs_2_), channel_id=1, source_target_pairs={{2,0},{3,1},{4,6},{5,7},{10,8},{11,9},{12,14},{13,15},{18,16},{19,... | collective-permute-start | bytes 1769480 | tf_op jit(solution)/shard_map/ppermute | solution.py:742
  83.7 17.5 %collective-permute-start.14 = (bf16[1152,256]{1,0:T(8,128)(2,1)}, bf16[1152,256]{1,0:T(8,128)(2,1)S(1)}, u32[]{:S(2)}, u32[]{:S(2)}) collective-permute-start(bf16[1152,256]{1,0:T(8,128)(2,1)} %get-tuple-element.291.refs_0_), channel_id=1, source_target_pairs={{0,2},{1,3},{6,4},{7,5},{8,10},{9,11},{14,12},{15,13},{16,18},{17,... | collective-permute-start | bytes 1769480 | tf_op jit(solution)/shard_map/ppermute | solution.py:734
  89.0 10.4 %copy-start.11 = (bf16[256,1152]{1,0:T(8,128)(2,1)S(1)}, bf16[256,1152]{1,0:T(8,128)(2,1)}, u32[]{:S(2)}) copy-start(bf16[256,1152]{1,0:T(8,128)(2,1)} %copy-done.10) | copy-start | bytes 1769476
  94.3 6.9 %copy-start.13 = (bf16[1152,256]{1,0:T(8,128)(2,1)S(1)}, bf16[1152,256]{1,0:T(8,128)(2,1)}, u32[]{:S(2)}) copy-start(bf16[1152,256]{1,0:T(8,128)(2,1)} %get-tuple-element.291.refs_0_) | copy-start | bytes 1769476
  94.3 8.8 %copy-start.5 = (bf16[256,512]{1,0:T(8,128)(2,1)S(1)}, bf16[256,512]{1,0:T(8,128)(2,1)}, u32[]{:S(2)}) copy-start(bf16[256,512]{1,0:T(8,128)(2,1)} %refs_5_.3) | copy-start | bytes 786436
  94.3 8.8 %copy-start.7 = (bf16[256,512]{1,0:T(8,128)(2,1)S(1)}, bf16[256,512]{1,0:T(8,128)(2,1)}, u32[]{:S(2)}) copy-start(bf16[256,512]{1,0:T(8,128)(2,1)} %refs_6_.1) | copy-start | bytes 786436
  94.3 8.8 %copy-start.19 = (f32[256,512]{1,0:T(8,128)S(1)}, f32[256,512]{1,0:T(8,128)}, u32[]{:S(2)}) copy-start(f32[256,512]{1,0:T(8,128)} %get-tuple-element.297.refs_2_) | copy-start | bytes 1572868
  94.3 8.8 %copy-start.27 = (f32[4,512]{1,0:T(4,128)S(1)}, f32[4,512]{1,0:T(4,128)}, u32[]{:S(2)}) copy-start(f32[4,512]{1,0:T(4,128)} %refs_4_.7) | copy-start | bytes 24580
  95.3 12.1 %collective-permute-start.15 = (bf16[1152,256]{1,0:T(8,128)(2,1)}, bf16[1152,256]{1,0:T(8,128)(2,1)S(1)}, u32[]{:S(2)}, u32[]{:S(2)}) collective-permute-start(bf16[1152,256]{1,0:T(8,128)(2,1)} %get-tuple-element.301), channel_id=1, source_target_pairs={{2,4},{3,5},{4,2},{5,3},{10,12},{11,13},{12,10},{13,11},{18,20},{1... | collective-permute-start | bytes 1769480 | tf_op jit(solution)/shard_map/ppermute | solution.py:738
  101.1 6.3 %copy-start.8 = (bf16[1152,256]{1,0:T(8,128)(2,1)S(1)}, bf16[1152,256]{1,0:T(8,128)(2,1)}, u32[]{:S(2)}) copy-start(bf16[1152,256]{1,0:T(8,128)(2,1)} %get-tuple-element.369.refs_0_) | copy-start | bytes 1769476
  101.1 2.0 collective-permute-start.13
  108.3 6.7 %collective-permute-start.17 = (bf16[4,272,1664]{2,1,0:T(8,128)(2,1)}, bf16[4,272,1664]{2,1,0:T(8,128)(2,1)}, u32[]{:S(2)}, u32[]{:S(2)}) collective-permute-start(bf16[4,272,1664]{2,1,0:T(8,128)(2,1)} %all-to-all-done.refs_1_.refs_3_.refs_0_), channel_id=1, source_target_pairs={{0,1},{1,0},{2,3},{3,2},{4,5},{5,4},{6,7},{7,6},{8,9},{9,8},{10,11... | collective-permute-start | bytes 10862600 | tf_op jit(solution)/shard_map/ppermute | solution.py:722
  108.5 4.9 %copy-start.2 = (bf16[512,256]{1,0:T(8,128)(2,1)S(1)}, bf16[512,256]{1,0:T(8,128)(2,1)}, u32[]{:S(2)}) copy-start(bf16[512,256]{1,0:T(8,128)(2,1)} %get-tuple-element.312.refs_1_.refs_3_) | copy-start | bytes 786436
  108.5 16.3 %copy-start.15 = (bf16[512,512]{1,0:T(8,128)(2,1)S(1)}, bf16[512,512]{1,0:T(8,128)(2,1)}, u32[]{:S(2)}) copy-start(bf16[512,512]{1,0:T(8,128)(2,1)} %get-tuple-element.327.refs_1_) | copy-start | bytes 1572868
  108.5 68.6 %all-to-all-start.1 = ((bf16[4,272,1664]{2,1,0:T(8,128)(2,1)}), bf16[4,272,1664]{2,1,0:T(8,128)(2,1)}, u32[]{:S(2)}, u32[]{:S(2)}) async-start(bf16[4,272,1664]{2,1,0:T(8,128)(2,1)} %get-tuple-element.374), calls=%async_computation.1 | async-start | bytes 7241728 | tf_op jit(solution)/shard_map/all_to_all | solution.py:746
  113.3 1.7 collective-permute-start.16
  113.8 26.7 %collective-permute-start.21 = (bf16[1152,256]{1,0:T(8,128)(2,1)}, bf16[1152,256]{1,0:T(8,128)(2,1)S(1)}, u32[]{:S(2)}, u32[]{:S(2)}) collective-permute-start(bf16[1152,256]{1,0:T(8,128)(2,1)} %get-tuple-element.333), channel_id=1, source_target_pairs={{2,4},{3,5},{4,2},{5,3},{10,12},{11,13},{12,10},{13,11},{18,20},{1... | collective-permute-start | bytes 1769480 | tf_op jit(solution)/shard_map/ppermute | solution.py:738
  115.8 24.7 %collective-permute-start.22 = (bf16[1152,256]{1,0:T(8,128)(2,1)}, bf16[1152,256]{1,0:T(8,128)(2,1)S(1)}, u32[]{:S(2)}, u32[]{:S(2)}) collective-permute-start(bf16[1152,256]{1,0:T(8,128)(2,1)} %get-tuple-element.334), channel_id=1, source_target_pairs={{2,0},{3,1},{4,6},{5,7},{10,8},{11,9},{12,14},{13,15},{18,16},{19,... | collective-permute-start | bytes 1769480 | tf_op jit(solution)/shard_map/ppermute | solution.py:742
  117.1 23.4 %collective-permute-start.20 = (bf16[1152,256]{1,0:T(8,128)(2,1)S(1)}, bf16[1152,256]{1,0:T(8,128)(2,1)S(1)}, u32[]{:S(2)}, u32[]{:S(2)}) collective-permute-start(bf16[1152,256]{1,0:T(8,128)(2,1)S(1)} %get-tuple-element.332), channel_id=1, source_target_pairs={{0,2},{1,3},{6,4},{7,5},{8,10},{9,11},{14,12},{15,13},{16,18},{17,... | collective-permute-start | bytes 1769480 | tf_op jit(solution)/shard_map/ppermute | solution.py:734
  124.8 22.2 %collective-permute-start.19 = (bf16[512,512]{1,0:T(8,128)(2,1)S(1)}, bf16[512,512]{1,0:T(8,128)(2,1)S(1)}, u32[]{:S(2)}, u32[]{:S(2)}) collective-permute-start(bf16[512,512]{1,0:T(8,128)(2,1)S(1)} %copy-done.15), channel_id=1, source_target_pairs={{2,4},{3,5},{4,2},{5,3},{10,12},{11,13},{12,10},{13,11},{18,20},{1... | collective-permute-start | bytes 1572872 | tf_op jit(solution)/shard_map/ppermute | solution.py:738
  125.5 24.2 %collective-permute-start.18 = (bf16[512,512]{1,0:T(8,128)(2,1)S(1)}, bf16[512,512]{1,0:T(8,128)(2,1)S(1)}, u32[]{:S(2)}, u32[]{:S(2)}) collective-permute-start(bf16[512,512]{1,0:T(8,128)(2,1)S(1)} %copy-done.15), channel_id=1, source_target_pairs={{0,2},{1,3},{2,0},{3,1},{4,6},{5,7},{6,4},{7,5},{8,10},{9,11},{10,... | collective-permute-start | bytes 1572872 | tf_op jit(solution)/shard_map/ppermute | solution.py:726
  134.1 8.1 %copy-start.14 = (bf16[1152,256]{1,0:T(8,128)(2,1)S(1)}, bf16[1152,256]{1,0:T(8,128)(2,1)}, u32[]{:S(2)}) copy-start(bf16[1152,256]{1,0:T(8,128)(2,1)} %get-tuple-element.353.refs_0_) | copy-start | bytes 1769476
  134.1 18.4 %copy-start.16 = (bf16[512,512]{1,0:T(8,128)(2,1)S(1)}, bf16[512,512]{1,0:T(8,128)(2,1)}, u32[]{:S(2)}) copy-start(bf16[512,512]{1,0:T(8,128)(2,1)} %get-tuple-element.327.refs_1_) | copy-start | bytes 1572868
  134.1 19.0 %copy-start.12 = (bf16[1152,256]{1,0:T(8,128)(2,1)S(1)}, bf16[1152,256]{1,0:T(8,128)(2,1)}, u32[]{:S(2)}) copy-start(bf16[1152,256]{1,0:T(8,128)(2,1)} %get-tuple-element.371.refs_0_) | copy-start | bytes 1769476
  140.4 25.7 %copy-start.9 = (bf16[1152,256]{1,0:T(8,128)(2,1)S(1)}, bf16[1152,256]{1,0:T(8,128)(2,1)}, u32[]{:S(2)}) copy-start(bf16[1152,256]{1,0:T(8,128)(2,1)} %get-tuple-element.369.refs_0_) | copy-start | bytes 1769476
  140.5 33.9 %copy-start.31 = (bf16[1152,256]{1,0:T(8,128)(2,1)}, bf16[1152,256]{1,0:T(8,128)(2,1)S(1)}, u32[]{:S(2)}) copy-start(bf16[1152,256]{1,0:T(8,128)(2,1)S(1)} %collective-permute-done.21.refs_5_) | copy-start | bytes 1769476
  140.5 25.7 %copy-start.32 = (bf16[1152,256]{1,0:T(8,128)(2,1)}, bf16[1152,256]{1,0:T(8,128)(2,1)S(1)}, u32[]{:S(2)}) copy-start(bf16[1152,256]{1,0:T(8,128)(2,1)S(1)} %collective-permute-done.22.refs_6_) | copy-start | bytes 1769476
  141.5 18.5 %collective-permute-start.26 = (bf16[1152,256]{1,0:T(8,128)(2,1)}, bf16[1152,256]{1,0:T(8,128)(2,1)S(1)}, u32[]{:S(2)}, u32[]{:S(2)}) collective-permute-start(bf16[1152,256]{1,0:T(8,128)(2,1)} %get-tuple-element.354), channel_id=1, source_target_pairs={{2,4},{3,5},{4,2},{5,3},{10,12},{11,13},{12,10},{13,11},{18,20},{1... | collective-permute-start | bytes 1769480 | tf_op jit(solution)/shard_map/ppermute | solution.py:738
  142.2 20.2 %collective-permute-start.25 = (bf16[1152,256]{1,0:T(8,128)(2,1)S(1)}, bf16[1152,256]{1,0:T(8,128)(2,1)S(1)}, u32[]{:S(2)}, u32[]{:S(2)}) collective-permute-start(bf16[1152,256]{1,0:T(8,128)(2,1)S(1)} %copy-done.14), channel_id=1, source_target_pairs={{0,2},{1,3},{6,4},{7,5},{8,10},{9,11},{14,12},{15,13},{16,18},{17,... | collective-permute-start | bytes 1769480 | tf_op jit(solution)/shard_map/ppermute | solution.py:734
  149.7 16.4 %collective-permute-start.24 = (bf16[512,512]{1,0:T(8,128)(2,1)S(1)}, bf16[512,512]{1,0:T(8,128)(2,1)}, u32[]{:S(2)}, u32[]{:S(2)}) collective-permute-start(bf16[512,512]{1,0:T(8,128)(2,1)S(1)} %collective-permute-done.18.refs_2_.refs_3_), channel_id=1, source_target_pairs={{2,4},{3,5},{4,2},{5,3},{10,12},{11,13},{12,10},{13,11},{18,20},{1... | collective-permute-start | bytes 1572872 | tf_op jit(solution)/shard_map/ppermute | solution.py:738
  151.2 15.0 %collective-permute-start.23 = (bf16[512,512]{1,0:T(8,128)(2,1)S(1)}, bf16[512,512]{1,0:T(8,128)(2,1)S(1)}, u32[]{:S(2)}, u32[]{:S(2)}) collective-permute-start(bf16[512,512]{1,0:T(8,128)(2,1)S(1)} %collective-permute-done.19.refs_3_), channel_id=1, source_target_pairs={{2,0},{3,1},{4,6},{5,7},{10,8},{11,9},{12,14},{13,15},{18,16},{19,... | collective-permute-start | bytes 1572872 | tf_op jit(solution)/shard_map/ppermute | solution.py:742
  153.1 30.4 %collective-permute-start.29 = (bf16[1152,256]{1,0:T(8,128)(2,1)S(1)}, bf16[1152,256]{1,0:T(8,128)(2,1)}, u32[]{:S(2)}, u32[]{:S(2)}) collective-permute-start(bf16[1152,256]{1,0:T(8,128)(2,1)S(1)} %copy-done.12), channel_id=1, source_target_pairs={{0,2},{1,3},{6,4},{7,5},{8,10},{9,11},{14,12},{15,13},{16,18},{17,... | collective-permute-start | bytes 1769480 | tf_op jit(solution)/shard_map/ppermute | solution.py:734
  163.3 20.3 %collective-permute-start.31 = (bf16[1152,256]{1,0:T(8,128)(2,1)}, bf16[1152,256]{1,0:T(8,128)(2,1)}, u32[]{:S(2)}, u32[]{:S(2)}) collective-permute-start(bf16[1152,256]{1,0:T(8,128)(2,1)} %get-tuple-element.373), channel_id=1, source_target_pairs={{2,4},{3,5},{4,2},{5,3},{10,12},{11,13},{12,10},{13,11},{18,20},{1... | collective-permute-start | bytes 1769480 | tf_op jit(solution)/shard_map/ppermute | solution.py:738
  164.8 19.9 %collective-permute-start.30 = (bf16[1152,256]{1,0:T(8,128)(2,1)}, bf16[1152,256]{1,0:T(8,128)(2,1)}, u32[]{:S(2)}, u32[]{:S(2)}) collective-permute-start(bf16[1152,256]{1,0:T(8,128)(2,1)} %get-tuple-element.372), channel_id=1, source_target_pairs={{2,0},{3,1},{4,6},{5,7},{10,8},{11,9},{12,14},{13,15},{18,16},{19,... | collective-permute-start | bytes 1769480 | tf_op jit(solution)/shard_map/ppermute | solution.py:742
  166.2 26.4 %collective-permute-start.28 = (bf16[1152,256]{1,0:T(8,128)(2,1)S(1)}, bf16[1152,256]{1,0:T(8,128)(2,1)}, u32[]{:S(2)}, u32[]{:S(2)}) collective-permute-start(bf16[1152,256]{1,0:T(8,128)(2,1)S(1)} %copy-done.9), channel_id=1, source_target_pairs={{0,2},{1,3},{6,4},{7,5},{8,10},{9,11},{14,12},{15,13},{16,18},{17,... | collective-permute-start | bytes 1769480 | tf_op jit(solution)/shard_map/ppermute | solution.py:734
  174.3 18.2 %collective-permute-start.27 = (bf16[512,512]{1,0:T(8,128)(2,1)}, bf16[512,512]{1,0:T(8,128)(2,1)S(1)}, u32[]{:S(2)}, u32[]{:S(2)}) collective-permute-start(bf16[512,512]{1,0:T(8,128)(2,1)} %collective-permute-done.24.refs_2_), channel_id=1, source_target_pairs={{2,0},{3,1},{4,6},{5,7},{10,8},{11,9},{12,14},{13,15},{18,16},{19,... | collective-permute-start | bytes 1572872 | tf_op jit(solution)/shard_map/ppermute | solution.py:742
  178.6 13.9 %copy-start.18 = (bf16[512,512]{1,0:T(8,128)(2,1)S(1)}, bf16[512,512]{1,0:T(8,128)(2,1)}, u32[]{:S(2)}) copy-start(bf16[512,512]{1,0:T(8,128)(2,1)} %copy-done.17) | copy-start | bytes 1572868
  183.6 9.6 %copy-start.33 = (bf16[4,256,1152]{2,1,0:T(8,128)(2,1)S(1)}, bf16[4,256,1152]{2,1,0:T(8,128)(2,1)}, u32[]{:S(2)}) copy-start(bf16[4,256,1152]{2,1,0:T(8,128)(2,1)} %get-tuple-element.393) | copy-start | bytes 7077892
  193.2 4.6 %collective-permute-start.34 = (bf16[4,256,1152]{2,1,0:T(8,128)(2,1)S(1)}, bf16[4,256,1152]{2,1,0:T(8,128)(2,1)S(1)}, u32[]{:S(2)}, u32[]{:S(2)}) collective-permute-start(bf16[4,256,1152]{2,1,0:T(8,128)(2,1)S(1)} %copy-done.33), channel_id=1, source_target_pairs={{0,1},{1,0},{2,3},{3,2},{4,5},{5,4},{6,7},{7,6},{8,9},{9,8},{10,11... | collective-permute-start | bytes 7077896 | tf_op jit(solution)/shard_map/ppermute | solution.py:722
  193.3 8.7 %collective-permute-start.32 = (bf16[1024,512]{1,0:T(8,128)(2,1)S(1)}, bf16[1024,512]{1,0:T(8,128)(2,1)S(1)}, u32[]{:S(2)}, u32[]{:S(2)}) collective-permute-start(bf16[1024,512]{1,0:T(8,128)(2,1)S(1)} %get-tuple-element.389.refs_1_), channel_id=1, source_target_pairs={{0,1},{1,0},{2,3},{3,2},{4,5},{5,4},{6,7},{7,6},{8,9},{9,8},{10,11... | collective-permute-start | bytes 3145736 | tf_op jit(solution)/shard_map/ppermute | solution.py:722
  193.8 8.2 %collective-permute-start.33 = (bf16[1024,512]{1,0:T(8,128)(2,1)S(1)}, bf16[1024,512]{1,0:T(8,128)(2,1)S(1)}, u32[]{:S(2)}, u32[]{:S(2)}) collective-permute-start(bf16[1024,512]{1,0:T(8,128)(2,1)S(1)} %get-tuple-element.387.refs_2_), channel_id=1, source_target_pairs={{0,1},{1,0},{2,3},{3,2},{4,5},{5,4},{6,7},{7,6},{8,9},{9,8},{10,11... | collective-permute-start | bytes 3145736 | tf_op jit(solution)/shard_map/ppermute | solution.py:722
  (7 other events, 4.8 us)

commit v10 on v9

--- a/solution.py
+++ b/solution.py
@@ -499,7 +499,9 @@
     )(one, two)
 
 
-def finish_kernel(where, marks, group, kept, third, cross, last, out, held, own, done, sems):
+def finish_kernel(
+    block, where, marks, group, kept, third, cross, last, out, held, own, done, sems
+):
     second = group[...] == 1
     cols = own.shape[0]
     tile = cols // 3
@@ -508,9 +510,9 @@
         rows = pl.ds(t * tile, tile)
         copies = [pltpu.make_async_copy(kept.at[rows, :], own.at[rows, :], sems.at[t, 3])]
         for n, source in enumerate((third, cross, last)):
-            copies.append(
-                pltpu.make_async_copy(source.at[rows, :], held.at[n, rows, :], sems.at[t, n])
-            )
+            start = block * cols + t * tile if n == 0 else t * tile
+            part = source.at[pl.ds(start, tile), :]
+            copies.append(pltpu.make_async_copy(part, held.at[n, rows, :], sems.at[t, n]))
         return copies
 
     def give(t):
@@ -535,9 +537,9 @@
         give(t).wait()
 
 
-def finish(where, marks, group, kept, third, cross, last):
-    return call(
-        finish_kernel,
+def finish(block, where, marks, group, kept, third, cross, last):
+    return call(
+        functools.partial(finish_kernel, block),
         pltpu.HBM(kept.shape, jnp.bfloat16),
         [SMEM, SMEM, VMEM] + [HBM] * 4,
         HBM,
@@ -874,12 +876,13 @@
         dzt_b,
         dzo_b,
     )
+    thirds = join(where, third_b, third_a, third_a)
     grad_weight_a = weight_grad((0, 1), rows, cols, where, (got_a, far_a), got_a)
     cross2_a, out_a = wait(cross2_a, out_a)
     in1_b = wait(in1_b)
     cross1_b = send(between, add(first_b, in1_b))
     in2_b = send(inward, second_b)
-    in3_b = send(inward, third_b)
+    in3 = send(inward, thirds)
     s1, s_mid = wait(s1, s_mid)
     s_end = send(outward, s_mid)
     s_mid2 = send(between, s1)
@@ -890,19 +893,18 @@
     cross2_b = send(between, add(second_b, in2_b))
     s_end, s_mid2 = wait(s_end, s_mid2)
     s_end2 = send(outward, s_mid2)
-    in3_a = send(inward, third_a)
     s2 = choose(where, s_end, s_mid2)
     got_b = wait(got_b)
     grad_bias, grad_stitch = total_sums(rows, cols, got_a, got_b)
     half_b, block_b = weight_grad((0,), rows, cols, where, (got_b,), got_b)
-    in3_b, out_b, cross2_b = wait(in3_b, out_b, cross2_b)
-    grad_image_b = finish(where, position_mask, group, kept_b, in3_b, cross2_b, out_b)
-    s_end2, in3_a = wait(s_end2, in3_a)
+    in3, out_b, cross2_b = wait(in3, out_b, cross2_b)
+    grad_image_b = finish(0, where, position_mask, group, kept_b, in3, cross2_b, out_b)
+    s_end2 = wait(s_end2)
     high = join(where, s2, s_end2, s_mid)
     far_high = send(swap, high)
     far_low = send(swap, low_half)
     far_b = send(swap, block_b)
-    grad_image_a = finish(where, position_mask, group, kept_a, in3_a, cross2_a, out_a)
+    grad_image_a = finish(1, where, position_mask, group, kept_a, in3, cross2_a, out_a)
     grad_weight_b = weight_grad((1,), rows, cols, where, (far_b,), got_b, half_b)
     stitched_a, stitched_b = lay_out(where, low_half, high, far_low, far_high)
     return (

time: 207 us -> 206 us (level)
  starting transfers between devices: 74.1 us -> 61 us
  waiting for transfers between devices: 42.3 us -> 51 us
  Pallas kernels: 80.4 us -> 82.6 us
    ppermute x6 -> x5, starting transfers between devices: 37.9 us -> 25.5 us  [inward(): return lax.ppermute(x, 'mp', ENDS_IN)]
    ppermute x6 -> x5, waiting for transfers between devices: 1.39 us -> 8.95 us  [inward(): return lax.ppermute(x, 'mp', ENDS_IN)]
    ppermute x6, waiting for transfers between devices: 9.04 us -> 14.7 us  [outward(): return lax.ppermute(x, 'mp', ENDS_OUT)]
    ppermute x4, waiting for transfers between devices: 24.8 us -> 21.4 us  [along(): return lax.ppermute(x, 'mp', NEAR_Z)]
    pallas_call x35 -> x36, Pallas kernels: 80.4 us -> 82.6 us  [go(): *results, line.token = run(*operands, *before)]
    unnamed x68 -> x56, local copies, waits for them, and re-layouts: 6.67 us -> 7.43 us
  transfers between devices with their start and end apart: 37 -> 36, of which waited for: 13 -> 14; matrix products, arithmetic and copies ran while one was open for 0% -> 0% of each run, Pallas kernels for 37% -> 38%
where the time goes in v10:
time: 206 us; the launch traced here: 204 us
  Pallas kernels  82.6 us (40%)
  starting transfers between devices  61 us (30%)
  waiting for transfers between devices  51 us (25%)
  local copies, waits for them, and re-layouts  7.51 us (4%)
    pallas_call x36, Pallas kernels, go(): *results, line.token = run(*operands, *before)  82.6 us
    ppermute x5, starting transfers between devices, inward(): return lax.ppermute(x, 'mp', ENDS_IN)  25.5 us
    ppermute x4, waiting for transfers between devices, along(): return lax.ppermute(x, 'mp', NEAR_Z)  21.4 us
    ppermute x6, waiting for transfers between devices, outward(): return lax.ppermute(x, 'mp', ENDS_OUT)  14.7 us
    all_to_all x2, starting transfers between devices, exchange(): return lax.all_to_all(x, 'dp', 0, 0)  9.88 us
    ppermute x5, waiting for transfers between devices, inward(): return lax.ppermute(x, 'mp', ENDS_IN)  8.95 us
    ppermute x6, starting transfers between devices, outward(): return lax.ppermute(x, 'mp', ENDS_OUT)  7.74 us
    unnamed x56, local copies, waits for them, and re-layouts  7.43 us
  transfers between devices with their start and end apart: 36, of which 14 were waited for; matrix products, arithmetic and copies ran while one was open for 0% of the time, Pallas kernels for 38%

profile of v10, /device:TPU:0, one launch (start us, length us, event | category | flops | bytes accessed | tf_op | source)
XLA Modules:
  0.0 204.3 jit_solution(6009898520471875117)
XLA Ops:
  1.2 3.0 %collective-permute-start = (bf16[256,1152]{1,0:T(8,128)(2,1)}, bf16[256,1152]{1,0:T(8,128)(2,1)S(1)}, u32[]{:S(2)}, u32[]{:S(2)}) collective-permute-start(bf16[256,1152]{1,0:T(8,128)(2,1)} %refs_3_.5), channel_id=1, source_target_pairs={{0,2},{1,3},{2,0},{3,1},{4,6},{5,7},{6,4},{7,5},{8,10},{9,11},{10,... | collective-permute-start | bytes 1769480 | tf_op jit(solution)/shard_map/ppermute | solution.py:728
  4.2 2.6 %collective-permute-start.1 = (bf16[256,1152]{1,0:T(8,128)(2,1)}, bf16[256,1152]{1,0:T(8,128)(2,1)S(1)}, u32[]{:S(2)}, u32[]{:S(2)}) collective-permute-start(bf16[256,1152]{1,0:T(8,128)(2,1)} %refs_3_.5), channel_id=1, source_target_pairs={{0,4},{1,5},{2,6},{3,7},{4,0},{5,1},{6,2},{7,3},{8,12},{9,13},{10,... | collective-permute-start | bytes 1769480 | tf_op jit(solution)/shard_map/ppermute | solution.py:732
  8.2 2.0 mask_image.5
  10.2 2.0 mask_image.6
  12.2 18.3 %collective-permute-done.refs_3_ = bf16[256,1152]{1,0:T(8,128)(2,1)S(1)} collective-permute-done((bf16[256,1152]{1,0:T(8,128)(2,1)}, bf16[256,1152]{1,0:T(8,128)(2,1)S(1)}, u32[]{:S(2)}, u32[]{:S(2)}) %collective-permute-start) | collective-permute-done | bytes 589856 | tf_op jit(solution)/shard_map/ppermute | solution.py:728
  30.5 0.8 copy-done.11
  31.3 1.7 collective-permute-done.1.refs_3_
  33.5 1.6 collective-permute-start.2
  36.6 1.1 copy-done.12
  39.0 1.2 mask_image.7
  40.2 1.2 mask_image.8
  41.4 5.3 %forward_open.2 = (f32[256,512]{1,0:T(8,128)S(1)}, f32[256,512]{1,0:T(8,128)S(1)}, bf16[2,1152,512]{2,1,0:T(8,128)(2,1)S(1)}, bf16[2,1152,512]{2,1,0:T(8,128)(2,1)S(1)}, f32[8,128]{1,0:T(8,128)S(1)}) custom-call(s32[9]{0:T(128)S(1)} %concatenate.3.refs_0_, bf16[256,1152]{1,0:T(8,128)(2,1)S(1)} %get-tuple-element.217.refs_1_, ...), custom_call_target="tpu_custom_call" | custom-call | flops 1 | bytes 1 | tf_op jit(solution)/shard_map/forward_open/pallas_call | solution.py:175
  46.7 2.7 %collective-permute-done.4.refs_3_ = bf16[256,1152]{1,0:T(8,128)(2,1)} collective-permute-done((bf16[256,1152]{1,0:T(8,128)(2,1)S(1)}, bf16[256,1152]{1,0:T(8,128)(2,1)}, u32[]{:S(2)}, u32[]{:S(2)}) %collective-permute-start.4) | collective-permute-done | bytes 589856 | tf_op jit(solution)/shard_map/ppermute | solution.py:728
  49.4 2.0 mask_image.9
  51.5 0.9 forward_close.2
  52.4 1.9 collective-permute-done.7.refs_1_
  54.3 1.3 tower_a.1
  55.6 2.9 %pack.2 = (bf16[4,272,1664]{2,1,0:T(8,128)(2,1)}, f32[8,128]{1,0:T(8,128)S(1)}) custom-call(s32[9]{0:T(128)S(1)} %concatenate.3.refs_0_, bf16[256,1152]{1,0:T(8,128)(2,1)S(1)} %get-tuple-element.217.refs_1_, bf16[256,1152]{1,0:T(8,128)(2,1)S(1)} %get-tuple-element.220.refs_2_, bf16[256,1152]{1,0:T(8,128)(2,1)S(1)} %get-tuple-element.222.refs_3_, ...), custom_call_target="tpu_custom_call" | custom-call | flops 1 | bytes 1 | tf_op jit(solution)/shard_map/pack/pallas_call | solution.py:175
  58.8 4.9 %all-to-all-start = ((bf16[4,272,1664]{2,1,0:T(8,128)(2,1)}), bf16[4,272,1664]{2,1,0:T(8,128)(2,1)}, u32[]{:S(2)}, u32[]{:S(2)}) async-start(bf16[4,272,1664]{2,1,0:T(8,128)(2,1)} %get-tuple-element.312), calls=%async_computation | async-start | bytes 7241728 | tf_op jit(solution)/shard_map/all_to_all | solution.py:748
  64.5 1.3 collective-permute-start.12
  66.1 1.7 copy-done.4
  68.5 6.1 %collective-permute-start.11 = (bf16[1152,256]{1,0:T(8,128)(2,1)S(1)}, bf16[1152,256]{1,0:T(8,128)(2,1)S(1)}, u32[]{:S(2)}, u32[]{:S(2)}) collective-permute-start(bf16[1152,256]{1,0:T(8,128)(2,1)S(1)} %get-tuple-element.266), channel_id=1, source_target_pairs={{0,2},{1,3},{6,4},{7,5},{8,10},{9,11},{14,12},{15,13},{16,18},{17,... | collective-permute-start | bytes 1769480 | tf_op jit(solution)/shard_map/ppermute | solution.py:736
  74.6 6.8 %parts.2 = (bf16[1152,256]{1,0:T(8,128)(2,1)}, bf16[1152,256]{1,0:T(8,128)(2,1)}, f32[1152,256]{1,0:T(8,128)}, f32[8,128]{1,0:T(8,128)S(1)}) custom-call(s32[9]{0:T(128)S(1)} %concatenate.3.refs_0_, bf16[9216,512]{1,0:T(8,128)(2,1)} %refs_1_.14, bf16[9216,512]{1,0:T(8,128)(2,1)} %collective-permute-done.5.refs_5_.refs_2_, bf16[512,256]{1,0:T(8,128)(2,1)S(1)} %copy-done.8, ...), custom_call_target="tpu_custom_call" | custom-call | flops 1 | bytes 1 | tf_op jit(solution)/shard_map/parts/pallas_call | solution.py:175
  81.4 1.3 collective-permute-start.10
  82.7 4.6 %collective-permute-start.14 = (bf16[1152,256]{1,0:T(8,128)(2,1)}, bf16[1152,256]{1,0:T(8,128)(2,1)S(1)}, u32[]{:S(2)}, u32[]{:S(2)}) collective-permute-start(bf16[1152,256]{1,0:T(8,128)(2,1)} %get-tuple-element.290.refs_0_), channel_id=1, source_target_pairs={{0,2},{1,3},{6,4},{7,5},{8,10},{9,11},{14,12},{15,13},{16,18},{17,... | collective-permute-start | bytes 1769480 | tf_op jit(solution)/shard_map/ppermute | solution.py:736
  88.0 5.3 %forward_open.3 = (f32[256,512]{1,0:T(8,128)S(1)}, f32[256,512]{1,0:T(8,128)S(1)}, bf16[2,1152,512]{2,1,0:T(8,128)(2,1)S(1)}, bf16[2,1152,512]{2,1,0:T(8,128)(2,1)S(1)}, f32[8,128]{1,0:T(8,128)S(1)}) custom-call(s32[9]{0:T(128)S(1)} %concatenate.3.refs_0_, bf16[256,1152]{1,0:T(8,128)(2,1)S(1)} %get-tuple-element.216.refs_1_, ...), custom_call_target="tpu_custom_call" | custom-call | flops 1 | bytes 1 | tf_op jit(solution)/shard_map/forward_open/pallas_call | solution.py:175
  93.3 1.0 add.38
  94.3 0.8 collective-permute-start.15
  95.1 3.5 %collective-permute-done.10.refs_1_ = bf16[256,1152]{1,0:T(8,128)(2,1)S(1)} collective-permute-done((bf16[256,1152]{1,0:T(8,128)(2,1)S(1)}, bf16[256,1152]{1,0:T(8,128)(2,1)S(1)}, u32[]{:S(2)}, u32[]{:S(2)}) %collective-permute-start.10) | collective-permute-done | bytes 589856 | tf_op jit(solution)/shard_map/ppermute | solution.py:744
  98.5 0.9 choose.4
  99.4 0.9 forward_close.3
  100.4 1.0 add.39
  101.4 0.9 collective-permute-done.13.refs_1_
  102.3 1.5 tower_b.1
  103.8 2.9 %pack.3 = (bf16[4,272,1664]{2,1,0:T(8,128)(2,1)}, f32[8,128]{1,0:T(8,128)S(1)}) custom-call(s32[9]{0:T(128)S(1)} %concatenate.3.refs_0_, bf16[256,1152]{1,0:T(8,128)(2,1)S(1)} %get-tuple-element.216.refs_1_, bf16[256,1152]{1,0:T(8,128)(2,1)S(1)} %collective-permute-done.2.refs_2_, bf16[256,1152]{1,0:T(8,128)(2,1)S(1)} %get-tuple-element.272.refs_3_, ...), custom_call_target="tpu_custom_call" | custom-call | flops 1 | bytes 1 | tf_op jit(solution)/shard_map/pack/pallas_call | solution.py:175
  106.7 1.0 add.40
  107.8 5.0 %all-to-all-start.1 = ((bf16[4,272,1664]{2,1,0:T(8,128)(2,1)}), bf16[4,272,1664]{2,1,0:T(8,128)(2,1)}, u32[]{:S(2)}, u32[]{:S(2)}) async-start(bf16[4,272,1664]{2,1,0:T(8,128)(2,1)} %get-tuple-element.373), calls=%async_computation.1 | async-start | bytes 7241728 | tf_op jit(solution)/shard_map/all_to_all | solution.py:748
  114.4 0.8 first_slot.3
  115.2 1.3 collective-permute-start.22
  116.5 7.8 %collective-permute-start.20 = (bf16[1152,256]{1,0:T(8,128)(2,1)S(1)}, bf16[1152,256]{1,0:T(8,128)(2,1)S(1)}, u32[]{:S(2)}, u32[]{:S(2)}) collective-permute-start(bf16[1152,256]{1,0:T(8,128)(2,1)S(1)} %get-tuple-element.333), channel_id=1, source_target_pairs={{0,2},{1,3},{6,4},{7,5},{8,10},{9,11},{14,12},{15,13},{16,18},{17,... | collective-permute-start | bytes 1769480 | tf_op jit(solution)/shard_map/ppermute | solution.py:736
  125.0 1.8 collective-permute-start.18
  126.7 6.8 %parts.3 = (bf16[1152,256]{1,0:T(8,128)(2,1)}, bf16[1152,256]{1,0:T(8,128)(2,1)}, f32[1152,256]{1,0:T(8,128)}, f32[8,128]{1,0:T(8,128)S(1)}) custom-call(s32[9]{0:T(128)S(1)} %concatenate.3.refs_0_, bf16[9216,512]{1,0:T(8,128)(2,1)} %refs_1_.15, bf16[9216,512]{1,0:T(8,128)(2,1)} %collective-permute-done.6.refs_5_.refs_2_, bf16[512,256]{1,0:T(8,128)(2,1)S(1)} %copy-done.7, ...), custom_call_target="tpu_custom_call" | custom-call | flops 1 | bytes 1 | tf_op jit(solution)/shard_map/parts/pallas_call | solution.py:175
  133.5 1.1 copy-done.5
  134.6 1.8 join.3
  136.5 6.3 %weight_grad.3 = (f32[2304,512]{1,0:T(8,128)}, f32[8,128]{1,0:T(8,128)S(1)}) custom-call(s32[9]{0:T(128)S(1)} %concatenate.3.refs_0_, bf16[4,272,1664]{2,1,0:T(8,128)(2,1)} %all-to-all-done.refs_1_.refs_3_.refs_0_, bf16[4,272,1664]{2,1,0:T(8,128)(2,1)} %collective-permute-done.17.refs_2_, bf16[4,272,1664]{2,1,0:T(8,128)(2,1)} %all-to-all-done.refs_1_.refs_3_.refs_0_, ...), custom_call_target="tpu_custom_call" | custom-call | flops 1 | bytes 1 | tf_op jit(solution)/shard_map/weight_grad/pallas_call | solution.py:175
  142.8 1.1 add.41
  144.7 4.6 %collective-permute-start.25 = (bf16[1152,256]{1,0:T(8,128)(2,1)S(1)}, bf16[1152,256]{1,0:T(8,128)(2,1)S(1)}, u32[]{:S(2)}, u32[]{:S(2)}) collective-permute-start(bf16[1152,256]{1,0:T(8,128)(2,1)S(1)} %copy-done.13), channel_id=1, source_target_pairs={{0,2},{1,3},{6,4},{7,5},{8,10},{9,11},{14,12},{15,13},{16,18},{17,... | collective-permute-start | bytes 1769480 | tf_op jit(solution)/shard_map/ppermute | solution.py:736
  149.3 2.4 %collective-permute-start.28 = (bf16[2304,256]{1,0:T(8,128)(2,1)}, bf16[2304,256]{1,0:T(8,128)(2,1)}, u32[]{:S(2)}, u32[]{:S(2)}) collective-permute-start(bf16[2304,256]{1,0:T(8,128)(2,1)} %get-tuple-element.370), channel_id=1, source_target_pairs={{0,2},{1,3},{6,4},{7,5},{8,10},{9,11},{14,12},{15,13},{16,18},{17,... | collective-permute-start | bytes 3538952 | tf_op jit(solution)/shard_map/ppermute | solution.py:736
  152.4 1.3 collective-permute-start.23
  154.4 1.0 add.42
  155.3 7.7 %collective-permute-done.25.refs_1_ = bf16[1152,256]{1,0:T(8,128)(2,1)S(1)} collective-permute-done((bf16[1152,256]{1,0:T(8,128)(2,1)S(1)}, bf16[1152,256]{1,0:T(8,128)(2,1)S(1)}, u32[]{:S(2)}, u32[]{:S(2)}) %collective-permute-start.25) | collective-permute-done | bytes 589856 | tf_op jit(solution)/shard_map/ppermute | solution.py:736
  163.0 0.9 add.43
  164.0 1.5 collective-permute-start.30
  165.5 1.3 collective-permute-start.29
  166.8 1.3 collective-permute-start.27
  168.7 1.6 total_sums.1
  170.3 4.9 %weight_grad.4 = (f32[2304,512]{1,0:T(8,128)}, bf16[4,256,1152]{2,1,0:T(8,128)(2,1)}, f32[8,128]{1,0:T(8,128)S(1)}) custom-call(s32[9]{0:T(128)S(1)} %concatenate.3.refs_0_, bf16[4,272,1664]{2,1,0:T(8,128)(2,1)} %all-to-all-done.1.refs_1_.refs_2_, bf16[4,272,1664]{2,1,0:T(8,128)(2,1)} %all-to-all-done.1.refs_1_.refs_2_, f32[8,128]{1,0:T(8,128)S(1)} %get-tuple-element.377.refs_3_), custom_call_target="tpu_custom_call" | custom-call | flops 1 | bytes 1 | tf_op jit(solution)/shard_map/weight_grad/pallas_call | solution.py:175
  175.3 9.8 %collective-permute-done.29.refs_6_ = bf16[1152,256]{1,0:T(8,128)(2,1)} collective-permute-done((bf16[1152,256]{1,0:T(8,128)(2,1)}, bf16[1152,256]{1,0:T(8,128)(2,1)}, u32[]{:S(2)}, u32[]{:S(2)}) %collective-permute-start.29) | collective-permute-done | bytes 589856 | tf_op jit(solution)/shard_map/ppermute | solution.py:744
  185.1 1.2 collective-permute-done.28.refs_4_
  186.3 3.2 %finish.2 = (bf16[1152,256]{1,0:T(8,128)(2,1)}, f32[8,128]{1,0:T(8,128)S(1)}) custom-call(s32[9]{0:T(128)S(1)} %concatenate.3.refs_0_, s32[2,36]{1,0:T(2,128)S(1)} %copy-done.19, s32[1,256]{1,0:T(1,128)S(1)} %bitcast.17, f32[1152,256]{1,0:T(8,128)} %get-tuple-element.369.refs_3_, bf16[2304,256]{1,0:T(8,128)(2,1)} %collective-permute-done.28.refs_4_, ...), custom_call_target="tpu_custom_call" | custom-call | flops 1 | bytes 1 | tf_op jit(solution)/shard_map/finish/pallas_call | solution.py:175
  189.5 1.5 collective-permute-done.27.refs_2_
  192.3 3.2 %finish.3 = (bf16[1152,256]{1,0:T(8,128)(2,1)}, f32[8,128]{1,0:T(8,128)S(1)}) custom-call(s32[9]{0:T(128)S(1)} %concatenate.3.refs_0_, s32[2,36]{1,0:T(2,128)S(1)} %copy-done.19, s32[1,256]{1,0:T(1,128)S(1)} %bitcast.18, f32[1152,256]{1,0:T(8,128)} %get-tuple-element.394.refs_3_, bf16[2304,256]{1,0:T(8,128)(2,1)} %collective-permute-done.28.refs_4_, ...), custom_call_target="tpu_custom_call" | custom-call | flops 1 | bytes 1 | tf_op jit(solution)/shard_map/finish/pallas_call | solution.py:175
  196.3 4.2 %weight_grad.5 = (f32[2304,512]{1,0:T(8,128)}, f32[8,128]{1,0:T(8,128)S(1)}) custom-call(s32[9]{0:T(128)S(1)} %concatenate.3.refs_0_, bf16[4,256,1152]{2,1,0:T(8,128)(2,1)S(1)} %collective-permute-done.33.refs_1_, bf16[4,272,1664]{2,1,0:T(8,128)(2,1)} %all-to-all-done.1.refs_1_.refs_2_, ...), custom_call_target="tpu_custom_call", output_to_operand_aliasing={{0}: (3, {})} | custom-call | flops 1 | bytes 1 | tf_op jit(solution)/shard_map/weight_grad/pallas_call | solution.py:175
  200.5 3.7 %lay_out.1 = (bf16[256,4096]{1,0:T(8,128)(2,1)}, bf16[256,4096]{1,0:T(8,128)(2,1)}, f32[8,128]{1,0:T(8,128)}) custom-call(s32[9]{0:T(128)S(1)} %concatenate.3.refs_0_, bf16[1024,512]{1,0:T(8,128)(2,1)S(1)} %get-tuple-element.388.refs_1_, bf16[1024,512]{1,0:T(8,128)(2,1)S(1)} %get-tuple-element.386.refs_2_, ...), custom_call_target="tpu_custom_call" | custom-call | flops 1 | bytes 1 | tf_op jit(solution)/shard_map/lay_out/pallas_call | solution.py:175
  (102 shorter events, 15.4 us)
Async XLA Ops:
  0.6 40.8 %collective-permute-start.5 = (bf16[9216,512]{1,0:T(8,128)(2,1)}, bf16[9216,512]{1,0:T(8,128)(2,1)}, u32[]{:S(2)}, u32[]{:S(2)}) collective-permute-start(bf16[9216,512]{1,0:T(8,128)(2,1)} %refs_1_.14), channel_id=1, source_target_pairs={{0,1},{1,0},{2,3},{3,2},{4,5},{5,4},{6,7},{7,6},{8,9},{9,8},{10,11... | collective-permute-start | bytes 28311560 | tf_op jit(solution)/shard_map/ppermute | solution.py:724
  1.2 40.3 %collective-permute-start.6 = (bf16[9216,512]{1,0:T(8,128)(2,1)}, bf16[9216,512]{1,0:T(8,128)(2,1)}, u32[]{:S(2)}, u32[]{:S(2)}) collective-permute-start(bf16[9216,512]{1,0:T(8,128)(2,1)} %refs_1_.15), channel_id=1, source_target_pairs={{0,1},{1,0},{2,3},{3,2},{4,5},{5,4},{6,7},{7,6},{8,9},{9,8},{10,11... | collective-permute-start | bytes 28311560 | tf_op jit(solution)/shard_map/ppermute | solution.py:724
  1.2 29.3 %collective-permute-start = (bf16[256,1152]{1,0:T(8,128)(2,1)}, bf16[256,1152]{1,0:T(8,128)(2,1)S(1)}, u32[]{:S(2)}, u32[]{:S(2)}) collective-permute-start(bf16[256,1152]{1,0:T(8,128)(2,1)} %refs_3_.5), channel_id=1, source_target_pairs={{0,2},{1,3},{2,0},{3,1},{4,6},{5,7},{6,4},{7,5},{8,10},{9,11},{10,... | collective-permute-start | bytes 1769480 | tf_op jit(solution)/shard_map/ppermute | solution.py:728
  4.2 28.8 %collective-permute-start.1 = (bf16[256,1152]{1,0:T(8,128)(2,1)}, bf16[256,1152]{1,0:T(8,128)(2,1)S(1)}, u32[]{:S(2)}, u32[]{:S(2)}) collective-permute-start(bf16[256,1152]{1,0:T(8,128)(2,1)} %refs_3_.5), channel_id=1, source_target_pairs={{0,4},{1,5},{2,6},{3,7},{4,0},{5,1},{6,2},{7,3},{8,12},{9,13},{10,... | collective-permute-start | bytes 1769480 | tf_op jit(solution)/shard_map/ppermute | solution.py:732
  6.8 0.7 copy-start.17
  7.5 0.7 copy-start.20
  30.5 0.8 copy-start.11
  33.1 16.4 %collective-permute-start.4 = (bf16[256,1152]{1,0:T(8,128)(2,1)S(1)}, bf16[256,1152]{1,0:T(8,128)(2,1)}, u32[]{:S(2)}, u32[]{:S(2)}) collective-permute-start(bf16[256,1152]{1,0:T(8,128)(2,1)S(1)} %collective-permute-done.1.refs_3_), channel_id=1, source_target_pairs={{0,2},{1,3},{2,0},{3,1},{4,6},{5,7},{6,4},{7,5},{8,10},{9,11},{10,... | collective-permute-start | bytes 1769480 | tf_op jit(solution)/shard_map/ppermute | solution.py:728
  33.5 25.3 %collective-permute-start.2 = (bf16[256,1152]{1,0:T(8,128)(2,1)S(1)}, bf16[256,1152]{1,0:T(8,128)(2,1)S(1)}, u32[]{:S(2)}, u32[]{:S(2)}) collective-permute-start(bf16[256,1152]{1,0:T(8,128)(2,1)S(1)} %get-tuple-element.216.refs_1_), channel_id=1, source_target_pairs={{0,2},{1,3},{2,0},{3,1},{4,6},{5,7},{6,4},{7,5},{8,10},{9,11},{10,... | collective-permute-start | bytes 1769480 | tf_op jit(solution)/shard_map/ppermute | solution.py:728
  35.1 23.7 %collective-permute-start.3 = (bf16[256,1152]{1,0:T(8,128)(2,1)S(1)}, bf16[256,1152]{1,0:T(8,128)(2,1)S(1)}, u32[]{:S(2)}, u32[]{:S(2)}) collective-permute-start(bf16[256,1152]{1,0:T(8,128)(2,1)S(1)} %get-tuple-element.216.refs_1_), channel_id=1, source_target_pairs={{2,4},{3,5},{4,2},{5,3},{10,12},{11,13},{12,10},{13,11},{18,20},{1... | collective-permute-start | bytes 1769480 | tf_op jit(solution)/shard_map/ppermute | solution.py:740
  36.6 1.1 copy-start.12
  37.6 0.7 copy-start.18
  38.3 0.7 copy-start.21
  46.7 11.8 %copy-start.3 = (bf16[2,1152,512]{2,1,0:T(8,128)(2,1)}, bf16[2,1152,512]{2,1,0:T(8,128)(2,1)S(1)}, u32[]{:S(2)}) copy-start(bf16[2,1152,512]{2,1,0:T(8,128)(2,1)S(1)} %get-tuple-element.258.refs_0_) | copy-start | bytes 7077892
  46.7 7.6 %copy-start.9 = (bf16[256,512]{1,0:T(8,128)(2,1)S(1)}, bf16[256,512]{1,0:T(8,128)(2,1)}, u32[]{:S(2)}) copy-start(bf16[256,512]{1,0:T(8,128)(2,1)} %refs_5_.3) | copy-start | bytes 786436
  46.7 7.6 %copy-start.10 = (bf16[256,512]{1,0:T(8,128)(2,1)S(1)}, bf16[256,512]{1,0:T(8,128)(2,1)}, u32[]{:S(2)}) copy-start(bf16[256,512]{1,0:T(8,128)(2,1)} %refs_6_.1) | copy-start | bytes 786436
  46.7 7.6 %copy-start.23 = (f32[4,512]{1,0:T(4,128)S(1)}, f32[4,512]{1,0:T(4,128)}, u32[]{:S(2)}) copy-start(f32[4,512]{1,0:T(4,128)} %refs_4_.7) | copy-start | bytes 24580
  46.7 7.6 %copy-start.24 = (f32[2,512]{1,0:T(2,128)S(1)}, f32[2,512]{1,0:T(2,128)}, u32[]{:S(2)}) copy-start(f32[2,512]{1,0:T(2,128)} %refs_3_.7) | copy-start | bytes 12292
  52.3 2.0 collective-permute-start.7
  58.8 5.6 %copy-start.8 = (bf16[512,256]{1,0:T(8,128)(2,1)S(1)}, bf16[512,256]{1,0:T(8,128)(2,1)}, u32[]{:S(2)}) copy-start(bf16[512,256]{1,0:T(8,128)(2,1)} %get-tuple-element.255.refs_1_.refs_3_) | copy-start | bytes 786436
  58.8 48.8 %all-to-all-start = ((bf16[4,272,1664]{2,1,0:T(8,128)(2,1)}), bf16[4,272,1664]{2,1,0:T(8,128)(2,1)}, u32[]{:S(2)}, u32[]{:S(2)}) async-start(bf16[4,272,1664]{2,1,0:T(8,128)(2,1)} %get-tuple-element.312), calls=%async_computation | async-start | bytes 7241728 | tf_op jit(solution)/shard_map/all_to_all | solution.py:748
  63.7 17.6 %collective-permute-start.8 = (bf16[256,1152]{1,0:T(8,128)(2,1)S(1)}, bf16[256,1152]{1,0:T(8,128)(2,1)S(1)}, u32[]{:S(2)}, u32[]{:S(2)}) collective-permute-start(bf16[256,1152]{1,0:T(8,128)(2,1)S(1)} %collective-permute-done.2.refs_2_), channel_id=1, source_target_pairs={{2,4},{3,5},{4,2},{5,3},{10,12},{11,13},{12,10},{13,11},{18,20},{1... | collective-permute-start | bytes 1769480 | tf_op jit(solution)/shard_map/ppermute | solution.py:740
  64.4 1.6 collective-permute-start.9
  64.5 22.8 %collective-permute-start.12 = (bf16[256,1152]{1,0:T(8,128)(2,1)S(1)}, bf16[256,1152]{1,0:T(8,128)(2,1)S(1)}, u32[]{:S(2)}, u32[]{:S(2)}) collective-permute-start(bf16[256,1152]{1,0:T(8,128)(2,1)S(1)} %collective-permute-done.3.refs_2_), channel_id=1, source_target_pairs={{2,0},{3,1},{4,6},{5,7},{10,8},{11,9},{12,14},{13,15},{18,16},{19,... | collective-permute-start | bytes 1769480 | tf_op jit(solution)/shard_map/ppermute | solution.py:744
  66.1 1.7 copy-start.4
  68.5 24.8 %collective-permute-start.11 = (bf16[1152,256]{1,0:T(8,128)(2,1)S(1)}, bf16[1152,256]{1,0:T(8,128)(2,1)S(1)}, u32[]{:S(2)}, u32[]{:S(2)}) collective-permute-start(bf16[1152,256]{1,0:T(8,128)(2,1)S(1)} %get-tuple-element.266), channel_id=1, source_target_pairs={{0,2},{1,3},{6,4},{7,5},{8,10},{9,11},{14,12},{15,13},{16,18},{17,... | collective-permute-start | bytes 1769480 | tf_op jit(solution)/shard_map/ppermute | solution.py:736
  81.4 17.2 %collective-permute-start.10 = (bf16[256,1152]{1,0:T(8,128)(2,1)S(1)}, bf16[256,1152]{1,0:T(8,128)(2,1)S(1)}, u32[]{:S(2)}, u32[]{:S(2)}) collective-permute-start(bf16[256,1152]{1,0:T(8,128)(2,1)S(1)} %collective-permute-done.8.refs_2_), channel_id=1, source_target_pairs={{2,0},{3,1},{4,6},{5,7},{10,8},{11,9},{12,14},{13,15},{18,16},{19,... | collective-permute-start | bytes 1769480 | tf_op jit(solution)/shard_map/ppermute | solution.py:744
  82.7 17.7 %collective-permute-start.14 = (bf16[1152,256]{1,0:T(8,128)(2,1)}, bf16[1152,256]{1,0:T(8,128)(2,1)S(1)}, u32[]{:S(2)}, u32[]{:S(2)}) collective-permute-start(bf16[1152,256]{1,0:T(8,128)(2,1)} %get-tuple-element.290.refs_0_), channel_id=1, source_target_pairs={{0,2},{1,3},{6,4},{7,5},{8,10},{9,11},{14,12},{15,13},{16,18},{17,... | collective-permute-start | bytes 1769480 | tf_op jit(solution)/shard_map/ppermute | solution.py:736
  93.3 8.1 %copy-start.1 = (bf16[2,1152,512]{2,1,0:T(8,128)(2,1)}, bf16[2,1152,512]{2,1,0:T(8,128)(2,1)S(1)}, u32[]{:S(2)}) copy-start(bf16[2,1152,512]{2,1,0:T(8,128)(2,1)S(1)} %get-tuple-element.310.refs_0_) | copy-start | bytes 7077892
  93.3 7.1 %copy-start.14 = (bf16[1152,256]{1,0:T(8,128)(2,1)S(1)}, bf16[1152,256]{1,0:T(8,128)(2,1)}, u32[]{:S(2)}) copy-start(bf16[1152,256]{1,0:T(8,128)(2,1)} %get-tuple-element.290.refs_0_) | copy-start | bytes 1769476
  93.3 9.0 %copy-start.16 = (f32[256,512]{1,0:T(8,128)S(1)}, f32[256,512]{1,0:T(8,128)}, u32[]{:S(2)}) copy-start(f32[256,512]{1,0:T(8,128)} %get-tuple-element.296.refs_2_) | copy-start | bytes 1572868
  94.3 12.4 %collective-permute-start.15 = (bf16[1152,256]{1,0:T(8,128)(2,1)}, bf16[1152,256]{1,0:T(8,128)(2,1)S(1)}, u32[]{:S(2)}, u32[]{:S(2)}) collective-permute-start(bf16[1152,256]{1,0:T(8,128)(2,1)} %get-tuple-element.300), channel_id=1, source_target_pairs={{2,4},{3,5},{4,2},{5,3},{10,12},{11,13},{12,10},{13,11},{18,20},{1... | collective-permute-start | bytes 1769480 | tf_op jit(solution)/shard_map/ppermute | solution.py:740
  100.3 6.4 %copy-start = (bf16[1152,256]{1,0:T(8,128)(2,1)S(1)}, bf16[1152,256]{1,0:T(8,128)(2,1)}, u32[]{:S(2)}) copy-start(bf16[1152,256]{1,0:T(8,128)(2,1)} %get-tuple-element.299.refs_0_.refs_2_.refs_3_) | copy-start | bytes 1769476
  100.3 2.0 collective-permute-start.13
  107.6 6.7 %collective-permute-start.17 = (bf16[4,272,1664]{2,1,0:T(8,128)(2,1)}, bf16[4,272,1664]{2,1,0:T(8,128)(2,1)}, u32[]{:S(2)}, u32[]{:S(2)}) collective-permute-start(bf16[4,272,1664]{2,1,0:T(8,128)(2,1)} %all-to-all-done.refs_1_.refs_3_.refs_0_), channel_id=1, source_target_pairs={{0,1},{1,0},{2,3},{3,2},{4,5},{5,4},{6,7},{7,6},{8,9},{9,8},{10,11... | collective-permute-start | bytes 10862600 | tf_op jit(solution)/shard_map/ppermute | solution.py:724
  107.8 5.0 %copy-start.7 = (bf16[512,256]{1,0:T(8,128)(2,1)S(1)}, bf16[512,256]{1,0:T(8,128)(2,1)}, u32[]{:S(2)}) copy-start(bf16[512,256]{1,0:T(8,128)(2,1)} %get-tuple-element.311.refs_1_.refs_3_) | copy-start | bytes 786436
  107.8 6.6 %copy-start.2 = (bf16[2,1152,512]{2,1,0:T(8,128)(2,1)S(1)}, bf16[2,1152,512]{2,1,0:T(8,128)(2,1)}, u32[]{:S(2)}) copy-start(bf16[2,1152,512]{2,1,0:T(8,128)(2,1)} %copy-done.1) | copy-start | bytes 7077892
  107.8 60.9 %all-to-all-start.1 = ((bf16[4,272,1664]{2,1,0:T(8,128)(2,1)}), bf16[4,272,1664]{2,1,0:T(8,128)(2,1)}, u32[]{:S(2)}, u32[]{:S(2)}) async-start(bf16[4,272,1664]{2,1,0:T(8,128)(2,1)} %get-tuple-element.373), calls=%async_computation.1 | async-start | bytes 7241728 | tf_op jit(solution)/shard_map/all_to_all | solution.py:748
  112.8 1.6 collective-permute-start.16
  113.2 29.6 %collective-permute-start.21 = (bf16[1152,256]{1,0:T(8,128)(2,1)}, bf16[1152,256]{1,0:T(8,128)(2,1)S(1)}, u32[]{:S(2)}, u32[]{:S(2)}) collective-permute-start(bf16[1152,256]{1,0:T(8,128)(2,1)} %get-tuple-element.334), channel_id=1, source_target_pairs={{2,4},{3,5},{4,2},{5,3},{10,12},{11,13},{12,10},{13,11},{18,20},{1... | collective-permute-start | bytes 1769480 | tf_op jit(solution)/shard_map/ppermute | solution.py:740
  115.2 27.6 %collective-permute-start.22 = (bf16[1152,256]{1,0:T(8,128)(2,1)}, bf16[1152,256]{1,0:T(8,128)(2,1)S(1)}, u32[]{:S(2)}, u32[]{:S(2)}) collective-permute-start(bf16[1152,256]{1,0:T(8,128)(2,1)} %get-tuple-element.335), channel_id=1, source_target_pairs={{2,0},{3,1},{4,6},{5,7},{10,8},{11,9},{12,14},{13,15},{18,16},{19,... | collective-permute-start | bytes 1769480 | tf_op jit(solution)/shard_map/ppermute | solution.py:744
  116.5 26.4 %collective-permute-start.20 = (bf16[1152,256]{1,0:T(8,128)(2,1)S(1)}, bf16[1152,256]{1,0:T(8,128)(2,1)S(1)}, u32[]{:S(2)}, u32[]{:S(2)}) collective-permute-start(bf16[1152,256]{1,0:T(8,128)(2,1)S(1)} %get-tuple-element.333), channel_id=1, source_target_pairs={{0,2},{1,3},{6,4},{7,5},{8,10},{9,11},{14,12},{15,13},{16,18},{17,... | collective-permute-start | bytes 1769480 | tf_op jit(solution)/shard_map/ppermute | solution.py:736
  124.3 27.4 %collective-permute-start.19 = (bf16[512,512]{1,0:T(8,128)(2,1)}, bf16[512,512]{1,0:T(8,128)(2,1)S(1)}, u32[]{:S(2)}, u32[]{:S(2)}) collective-permute-start(bf16[512,512]{1,0:T(8,128)(2,1)} %get-tuple-element.326.refs_1_), channel_id=1, source_target_pairs={{2,4},{3,5},{4,2},{5,3},{10,12},{11,13},{12,10},{13,11},{18,20},{1... | collective-permute-start | bytes 1572872 | tf_op jit(solution)/shard_map/ppermute | solution.py:740
  125.0 26.7 %collective-permute-start.18 = (bf16[512,512]{1,0:T(8,128)(2,1)}, bf16[512,512]{1,0:T(8,128)(2,1)S(1)}, u32[]{:S(2)}, u32[]{:S(2)}) collective-permute-start(bf16[512,512]{1,0:T(8,128)(2,1)} %get-tuple-element.326.refs_1_), channel_id=1, source_target_pairs={{0,2},{1,3},{2,0},{3,1},{4,6},{5,7},{6,4},{7,5},{8,10},{9,11},{10,... | collective-permute-start | bytes 1572872 | tf_op jit(solution)/shard_map/ppermute | solution.py:728
  133.5 1.1 copy-start.5
  136.4 8.3 %copy-start.13 = (bf16[1152,256]{1,0:T(8,128)(2,1)S(1)}, bf16[1152,256]{1,0:T(8,128)(2,1)}, u32[]{:S(2)}) copy-start(bf16[1152,256]{1,0:T(8,128)(2,1)} %get-tuple-element.354.refs_0_) | copy-start | bytes 1769476
  136.4 17.2 %copy-start.15 = (bf16[512,512]{1,0:T(8,128)(2,1)S(1)}, bf16[512,512]{1,0:T(8,128)(2,1)}, u32[]{:S(2)}) copy-start(bf16[512,512]{1,0:T(8,128)(2,1)} %get-tuple-element.326.refs_1_) | copy-start | bytes 1572868
  136.4 17.9 %copy-start.6 = (bf16[1152,256]{1,0:T(8,128)(2,1)S(1)}, bf16[1152,256]{1,0:T(8,128)(2,1)}, u32[]{:S(2)}) copy-start(bf16[1152,256]{1,0:T(8,128)(2,1)} %get-tuple-element.328.refs_1_.refs_0_) | copy-start | bytes 1769476
  142.8 24.0 %copy-start.25 = (bf16[1152,256]{1,0:T(8,128)(2,1)}, bf16[1152,256]{1,0:T(8,128)(2,1)S(1)}, u32[]{:S(2)}) copy-start(bf16[1152,256]{1,0:T(8,128)(2,1)S(1)} %collective-permute-done.21.refs_5_) | copy-start | bytes 1769476
  142.8 24.0 %copy-start.26 = (bf16[1152,256]{1,0:T(8,128)(2,1)}, bf16[1152,256]{1,0:T(8,128)(2,1)S(1)}, u32[]{:S(2)}) copy-start(bf16[1152,256]{1,0:T(8,128)(2,1)S(1)} %collective-permute-done.22.refs_6_) | copy-start | bytes 1769476
  144.0 10.4 %collective-permute-start.26 = (bf16[1152,256]{1,0:T(8,128)(2,1)}, bf16[1152,256]{1,0:T(8,128)(2,1)S(1)}, u32[]{:S(2)}, u32[]{:S(2)}) collective-permute-start(bf16[1152,256]{1,0:T(8,128)(2,1)} %get-tuple-element.355), channel_id=1, source_target_pairs={{2,4},{3,5},{4,2},{5,3},{10,12},{11,13},{12,10},{13,11},{18,20},{1... | collective-permute-start | bytes 1769480 | tf_op jit(solution)/shard_map/ppermute | solution.py:740
  144.7 18.3 %collective-permute-start.25 = (bf16[1152,256]{1,0:T(8,128)(2,1)S(1)}, bf16[1152,256]{1,0:T(8,128)(2,1)S(1)}, u32[]{:S(2)}, u32[]{:S(2)}) collective-permute-start(bf16[1152,256]{1,0:T(8,128)(2,1)S(1)} %copy-done.13), channel_id=1, source_target_pairs={{0,2},{1,3},{6,4},{7,5},{8,10},{9,11},{14,12},{15,13},{16,18},{17,... | collective-permute-start | bytes 1769480 | tf_op jit(solution)/shard_map/ppermute | solution.py:736
  149.3 37.0 %collective-permute-start.28 = (bf16[2304,256]{1,0:T(8,128)(2,1)}, bf16[2304,256]{1,0:T(8,128)(2,1)}, u32[]{:S(2)}, u32[]{:S(2)}) collective-permute-start(bf16[2304,256]{1,0:T(8,128)(2,1)} %get-tuple-element.370), channel_id=1, source_target_pairs={{0,2},{1,3},{6,4},{7,5},{8,10},{9,11},{14,12},{15,13},{16,18},{17,... | collective-permute-start | bytes 3538952 | tf_op jit(solution)/shard_map/ppermute | solution.py:736
  151.7 15.1 %collective-permute-start.24 = (bf16[512,512]{1,0:T(8,128)(2,1)S(1)}, bf16[512,512]{1,0:T(8,128)(2,1)S(1)}, u32[]{:S(2)}, u32[]{:S(2)}) collective-permute-start(bf16[512,512]{1,0:T(8,128)(2,1)S(1)} %collective-permute-done.18.refs_2_.refs_3_), channel_id=1, source_target_pairs={{2,4},{3,5},{4,2},{5,3},{10,12},{11,13},{12,10},{13,11},{18,20},{1... | collective-permute-start | bytes 1572872 | tf_op jit(solution)/shard_map/ppermute | solution.py:740
  152.4 14.4 %collective-permute-start.23 = (bf16[512,512]{1,0:T(8,128)(2,1)S(1)}, bf16[512,512]{1,0:T(8,128)(2,1)S(1)}, u32[]{:S(2)}, u32[]{:S(2)}) collective-permute-start(bf16[512,512]{1,0:T(8,128)(2,1)S(1)} %collective-permute-done.19.refs_3_), channel_id=1, source_target_pairs={{2,0},{3,1},{4,6},{5,7},{10,8},{11,9},{12,14},{13,15},{18,16},{19,... | collective-permute-start | bytes 1572872 | tf_op jit(solution)/shard_map/ppermute | solution.py:744
  164.0 11.3 %collective-permute-start.30 = (bf16[1152,256]{1,0:T(8,128)(2,1)}, bf16[1152,256]{1,0:T(8,128)(2,1)}, u32[]{:S(2)}, u32[]{:S(2)}) collective-permute-start(bf16[1152,256]{1,0:T(8,128)(2,1)} %get-tuple-element.372), channel_id=1, source_target_pairs={{2,4},{3,5},{4,2},{5,3},{10,12},{11,13},{12,10},{13,11},{18,20},{1... | collective-permute-start | bytes 1769480 | tf_op jit(solution)/shard_map/ppermute | solution.py:740
  165.5 19.6 %collective-permute-start.29 = (bf16[1152,256]{1,0:T(8,128)(2,1)}, bf16[1152,256]{1,0:T(8,128)(2,1)}, u32[]{:S(2)}, u32[]{:S(2)}) collective-permute-start(bf16[1152,256]{1,0:T(8,128)(2,1)} %get-tuple-element.371), channel_id=1, source_target_pairs={{2,0},{3,1},{4,6},{5,7},{10,8},{11,9},{12,14},{13,15},{18,16},{19,... | collective-permute-start | bytes 1769480 | tf_op jit(solution)/shard_map/ppermute | solution.py:744
  166.8 24.2 %collective-permute-start.27 = (bf16[512,512]{1,0:T(8,128)(2,1)S(1)}, bf16[512,512]{1,0:T(8,128)(2,1)S(1)}, u32[]{:S(2)}, u32[]{:S(2)}) collective-permute-start(bf16[512,512]{1,0:T(8,128)(2,1)S(1)} %collective-permute-done.24.refs_2_), channel_id=1, source_target_pairs={{2,0},{3,1},{4,6},{5,7},{10,8},{11,9},{12,14},{13,15},{18,16},{19,... | collective-permute-start | bytes 1572872 | tf_op jit(solution)/shard_map/ppermute | solution.py:744
  170.3 16.0 %copy-start.19 = (s32[2,36]{1,0:T(2,128)S(1)}, s32[2,36]{1,0:T(2,128)}, u32[]{:S(2)}) copy-start(s32[2,36]{1,0:T(2,128)} %refs_1_.17) | copy-start | bytes 868
  170.3 16.0 %copy-start.22 = (s32[256]{0:T(256)S(1)}, s32[256]{0:T(256)}, u32[]{:S(2)}) copy-start(s32[256]{0:T(256)} %param.13) | copy-start | bytes 3076
  175.3 16.4 %copy-start.27 = (bf16[4,256,1152]{2,1,0:T(8,128)(2,1)S(1)}, bf16[4,256,1152]{2,1,0:T(8,128)(2,1)}, u32[]{:S(2)}) copy-start(bf16[4,256,1152]{2,1,0:T(8,128)(2,1)} %get-tuple-element.392) | copy-start | bytes 7077892
  191.7 4.6 %collective-permute-start.33 = (bf16[4,256,1152]{2,1,0:T(8,128)(2,1)S(1)}, bf16[4,256,1152]{2,1,0:T(8,128)(2,1)S(1)}, u32[]{:S(2)}, u32[]{:S(2)}) collective-permute-start(bf16[4,256,1152]{2,1,0:T(8,128)(2,1)S(1)} %copy-done.27), channel_id=1, source_target_pairs={{0,1},{1,0},{2,3},{3,2},{4,5},{5,4},{6,7},{7,6},{8,9},{9,8},{10,11... | collective-permute-start | bytes 7077896 | tf_op jit(solution)/shard_map/ppermute | solution.py:724
  191.8 8.7 %collective-permute-start.31 = (bf16[1024,512]{1,0:T(8,128)(2,1)S(1)}, bf16[1024,512]{1,0:T(8,128)(2,1)S(1)}, u32[]{:S(2)}, u32[]{:S(2)}) collective-permute-start(bf16[1024,512]{1,0:T(8,128)(2,1)S(1)} %get-tuple-element.388.refs_1_), channel_id=1, source_target_pairs={{0,1},{1,0},{2,3},{3,2},{4,5},{5,4},{6,7},{7,6},{8,9},{9,8},{10,11... | collective-permute-start | bytes 3145736 | tf_op jit(solution)/shard_map/ppermute | solution.py:724
  192.3 8.2 %collective-permute-start.32 = (bf16[1024,512]{1,0:T(8,128)(2,1)S(1)}, bf16[1024,512]{1,0:T(8,128)(2,1)S(1)}, u32[]{:S(2)}, u32[]{:S(2)}) collective-permute-start(bf16[1024,512]{1,0:T(8,128)(2,1)S(1)} %get-tuple-element.386.refs_2_), channel_id=1, source_target_pairs={{0,1},{1,0},{2,3},{3,2},{4,5},{5,4},{6,7},{7,6},{8,9},{9,8},{10,11... | collective-permute-start | bytes 3145736 | tf_op jit(solution)/shard_map/ppermute | solution.py:724

commit v11 on v10

--- a/solution.py
+++ b/solution.py
@@ -876,11 +876,11 @@
         dzt_b,
         dzo_b,
     )
-    thirds = join(where, third_b, third_a, third_a)
     grad_weight_a = weight_grad((0, 1), rows, cols, where, (got_a, far_a), got_a)
     cross2_a, out_a = wait(cross2_a, out_a)
     in1_b = wait(in1_b)
     cross1_b = send(between, add(first_b, in1_b))
+    thirds = join(where, third_b, third_a, third_a)
     in2_b = send(inward, second_b)
     in3 = send(inward, thirds)
     s1, s_mid = wait(s1, s_mid)

time: 206 us -> 206 us (level)
  waiting for transfers between devices: 51 us -> 53.1 us
    unnamed x56 -> x54, local copies, waits for them, and re-layouts: 7.43 us -> 6.37 us
where the time goes in v11:
time: 206 us; the launch traced here: 205 us
  Pallas kernels  82.6 us (40%)
  starting transfers between devices  60.9 us (30%)
  waiting for transfers between devices  53.1 us (26%)
  local copies, waits for them, and re-layouts  6.45 us (3%)
    pallas_call x36, Pallas kernels, go(): *results, line.token = run(*operands, *before)  82.6 us
    ppermute x5, starting transfers between devices, inward(): return lax.ppermute(x, 'mp', ENDS_IN)  25.4 us
    ppermute x4, waiting for transfers between devices, along(): return lax.ppermute(x, 'mp', NEAR_Z)  21.4 us
    ppermute x6, waiting for transfers between devices, outward(): return lax.ppermute(x, 'mp', ENDS_OUT)  16 us
    all_to_all x2, starting transfers between devices, exchange(): return lax.all_to_all(x, 'dp', 0, 0)  9.88 us
    ppermute x5, waiting for transfers between devices, inward(): return lax.ppermute(x, 'mp', ENDS_IN)  9.71 us
    ppermute x6, starting transfers between devices, outward(): return lax.ppermute(x, 'mp', ENDS_OUT)  7.74 us
    ppermute x4, starting transfers between devices, along(): return lax.ppermute(x, 'mp', NEAR_Z)  6.81 us
  transfers between devices with their start and end apart: 36, of which 14 were waited for; matrix products, arithmetic and copies ran while one was open for 0% of the time, Pallas kernels for 38%

profile of v11, /device:TPU:0, one launch (start us, length us, event | category | flops | bytes accessed | tf_op | source)
XLA Modules:
  0.0 205.3 jit_solution(11139933621003225283)
XLA Ops:
  1.2 3.0 %collective-permute-start = (bf16[256,1152]{1,0:T(8,128)(2,1)}, bf16[256,1152]{1,0:T(8,128)(2,1)S(1)}, u32[]{:S(2)}, u32[]{:S(2)}) collective-permute-start(bf16[256,1152]{1,0:T(8,128)(2,1)} %refs_3_.5), channel_id=1, source_target_pairs={{0,2},{1,3},{2,0},{3,1},{4,6},{5,7},{6,4},{7,5},{8,10},{9,11},{10,... | collective-permute-start | bytes 1769480 | tf_op jit(solution)/shard_map/ppermute | solution.py:728
  4.2 2.6 %collective-permute-start.1 = (bf16[256,1152]{1,0:T(8,128)(2,1)}, bf16[256,1152]{1,0:T(8,128)(2,1)S(1)}, u32[]{:S(2)}, u32[]{:S(2)}) collective-permute-start(bf16[256,1152]{1,0:T(8,128)(2,1)} %refs_3_.5), channel_id=1, source_target_pairs={{0,4},{1,5},{2,6},{3,7},{4,0},{5,1},{6,2},{7,3},{8,12},{9,13},{10,... | collective-permute-start | bytes 1769480 | tf_op jit(solution)/shard_map/ppermute | solution.py:732
  8.2 2.0 mask_image.5
  10.2 2.0 mask_image.6
  12.2 18.3 %collective-permute-done.refs_3_ = bf16[256,1152]{1,0:T(8,128)(2,1)S(1)} collective-permute-done((bf16[256,1152]{1,0:T(8,128)(2,1)}, bf16[256,1152]{1,0:T(8,128)(2,1)S(1)}, u32[]{:S(2)}, u32[]{:S(2)}) %collective-permute-start) | collective-permute-done | bytes 589856 | tf_op jit(solution)/shard_map/ppermute | solution.py:728
  30.5 0.8 copy-done.10
  31.3 1.7 collective-permute-done.1.refs_3_
  33.5 1.6 collective-permute-start.2
  36.6 1.1 copy-done.11
  39.0 1.2 mask_image.7
  40.2 1.2 mask_image.8
  41.4 5.3 %forward_open.2 = (f32[256,512]{1,0:T(8,128)S(1)}, f32[256,512]{1,0:T(8,128)S(1)}, bf16[2,1152,512]{2,1,0:T(8,128)(2,1)S(1)}, bf16[2,1152,512]{2,1,0:T(8,128)(2,1)S(1)}, f32[8,128]{1,0:T(8,128)S(1)}) custom-call(s32[9]{0:T(128)S(1)} %concatenate.3.refs_0_, bf16[256,1152]{1,0:T(8,128)(2,1)S(1)} %get-tuple-element.217.refs_1_, ...), custom_call_target="tpu_custom_call" | custom-call | flops 1 | bytes 1 | tf_op jit(solution)/shard_map/forward_open/pallas_call | solution.py:175
  46.7 2.7 %collective-permute-done.4.refs_3_ = bf16[256,1152]{1,0:T(8,128)(2,1)} collective-permute-done((bf16[256,1152]{1,0:T(8,128)(2,1)S(1)}, bf16[256,1152]{1,0:T(8,128)(2,1)}, u32[]{:S(2)}, u32[]{:S(2)}) %collective-permute-start.4) | collective-permute-done | bytes 589856 | tf_op jit(solution)/shard_map/ppermute | solution.py:728
  49.4 2.0 mask_image.9
  51.5 0.9 forward_close.2
  52.4 1.9 collective-permute-done.7.refs_1_
  54.3 1.3 tower_a.1
  55.6 2.9 %pack.2 = (bf16[4,272,1664]{2,1,0:T(8,128)(2,1)}, f32[8,128]{1,0:T(8,128)S(1)}) custom-call(s32[9]{0:T(128)S(1)} %concatenate.3.refs_0_, bf16[256,1152]{1,0:T(8,128)(2,1)S(1)} %get-tuple-element.217.refs_1_, bf16[256,1152]{1,0:T(8,128)(2,1)S(1)} %get-tuple-element.220.refs_2_, bf16[256,1152]{1,0:T(8,128)(2,1)S(1)} %get-tuple-element.222.refs_3_, ...), custom_call_target="tpu_custom_call" | custom-call | flops 1 | bytes 1 | tf_op jit(solution)/shard_map/pack/pallas_call | solution.py:175
  58.8 4.9 %all-to-all-start = ((bf16[4,272,1664]{2,1,0:T(8,128)(2,1)}), bf16[4,272,1664]{2,1,0:T(8,128)(2,1)}, u32[]{:S(2)}, u32[]{:S(2)}) async-start(bf16[4,272,1664]{2,1,0:T(8,128)(2,1)} %get-tuple-element.312), calls=%async_computation | async-start | bytes 7241728 | tf_op jit(solution)/shard_map/all_to_all | solution.py:748
  64.5 1.3 collective-permute-start.12
  66.1 1.7 copy-done.4
  67.7 0.8 first_slot.2
  68.5 6.1 %collective-permute-start.11 = (bf16[1152,256]{1,0:T(8,128)(2,1)S(1)}, bf16[1152,256]{1,0:T(8,128)(2,1)S(1)}, u32[]{:S(2)}, u32[]{:S(2)}) collective-permute-start(bf16[1152,256]{1,0:T(8,128)(2,1)S(1)} %get-tuple-element.266), channel_id=1, source_target_pairs={{0,2},{1,3},{6,4},{7,5},{8,10},{9,11},{14,12},{15,13},{16,18},{17,... | collective-permute-start | bytes 1769480 | tf_op jit(solution)/shard_map/ppermute | solution.py:736
  74.6 6.8 %parts.2 = (bf16[1152,256]{1,0:T(8,128)(2,1)}, bf16[1152,256]{1,0:T(8,128)(2,1)}, f32[1152,256]{1,0:T(8,128)}, f32[8,128]{1,0:T(8,128)S(1)}) custom-call(s32[9]{0:T(128)S(1)} %concatenate.3.refs_0_, bf16[9216,512]{1,0:T(8,128)(2,1)} %refs_1_.14, bf16[9216,512]{1,0:T(8,128)(2,1)} %collective-permute-done.5.refs_5_.refs_2_, bf16[512,256]{1,0:T(8,128)(2,1)S(1)} %copy-done.7, ...), custom_call_target="tpu_custom_call" | custom-call | flops 1 | bytes 1 | tf_op jit(solution)/shard_map/parts/pallas_call | solution.py:175
  81.4 1.3 collective-permute-start.10
  82.7 4.6 %collective-permute-start.14 = (bf16[1152,256]{1,0:T(8,128)(2,1)}, bf16[1152,256]{1,0:T(8,128)(2,1)S(1)}, u32[]{:S(2)}, u32[]{:S(2)}) collective-permute-start(bf16[1152,256]{1,0:T(8,128)(2,1)} %get-tuple-element.290.refs_0_), channel_id=1, source_target_pairs={{0,2},{1,3},{6,4},{7,5},{8,10},{9,11},{14,12},{15,13},{16,18},{17,... | collective-permute-start | bytes 1769480 | tf_op jit(solution)/shard_map/ppermute | solution.py:736
  88.0 5.3 %forward_open.3 = (f32[256,512]{1,0:T(8,128)S(1)}, f32[256,512]{1,0:T(8,128)S(1)}, bf16[2,1152,512]{2,1,0:T(8,128)(2,1)S(1)}, bf16[2,1152,512]{2,1,0:T(8,128)(2,1)S(1)}, f32[8,128]{1,0:T(8,128)S(1)}) custom-call(s32[9]{0:T(128)S(1)} %concatenate.3.refs_0_, bf16[256,1152]{1,0:T(8,128)(2,1)S(1)} %get-tuple-element.216.refs_1_, ...), custom_call_target="tpu_custom_call" | custom-call | flops 1 | bytes 1 | tf_op jit(solution)/shard_map/forward_open/pallas_call | solution.py:175
  93.3 1.0 add.38
  94.3 0.8 collective-permute-start.15
  95.1 3.4 %collective-permute-done.10.refs_1_ = bf16[256,1152]{1,0:T(8,128)(2,1)S(1)} collective-permute-done((bf16[256,1152]{1,0:T(8,128)(2,1)S(1)}, bf16[256,1152]{1,0:T(8,128)(2,1)S(1)}, u32[]{:S(2)}, u32[]{:S(2)}) %collective-permute-start.10) | collective-permute-done | bytes 589856 | tf_op jit(solution)/shard_map/ppermute | solution.py:744
  98.5 0.9 choose.4
  99.4 0.9 forward_close.3
  100.4 1.0 add.39
  101.4 0.9 collective-permute-done.13.refs_1_
  102.3 1.5 tower_b.1
  103.7 2.9 %pack.3 = (bf16[4,272,1664]{2,1,0:T(8,128)(2,1)}, f32[8,128]{1,0:T(8,128)S(1)}) custom-call(s32[9]{0:T(128)S(1)} %concatenate.3.refs_0_, bf16[256,1152]{1,0:T(8,128)(2,1)S(1)} %get-tuple-element.216.refs_1_, bf16[256,1152]{1,0:T(8,128)(2,1)S(1)} %collective-permute-done.2.refs_2_, bf16[256,1152]{1,0:T(8,128)(2,1)S(1)} %get-tuple-element.272.refs_3_, ...), custom_call_target="tpu_custom_call" | custom-call | flops 1 | bytes 1 | tf_op jit(solution)/shard_map/pack/pallas_call | solution.py:175
  106.6 1.0 add.40
  107.8 5.0 %all-to-all-start.1 = ((bf16[4,272,1664]{2,1,0:T(8,128)(2,1)}), bf16[4,272,1664]{2,1,0:T(8,128)(2,1)}, u32[]{:S(2)}, u32[]{:S(2)}) async-start(bf16[4,272,1664]{2,1,0:T(8,128)(2,1)} %get-tuple-element.373), calls=%async_computation.1 | async-start | bytes 7241728 | tf_op jit(solution)/shard_map/all_to_all | solution.py:748
  114.4 0.8 first_slot.3
  115.2 1.3 collective-permute-start.22
  116.5 7.8 %collective-permute-start.20 = (bf16[1152,256]{1,0:T(8,128)(2,1)S(1)}, bf16[1152,256]{1,0:T(8,128)(2,1)S(1)}, u32[]{:S(2)}, u32[]{:S(2)}) collective-permute-start(bf16[1152,256]{1,0:T(8,128)(2,1)S(1)} %get-tuple-element.330), channel_id=1, source_target_pairs={{0,2},{1,3},{6,4},{7,5},{8,10},{9,11},{14,12},{15,13},{16,18},{17,... | collective-permute-start | bytes 1769480 | tf_op jit(solution)/shard_map/ppermute | solution.py:736
  125.0 1.8 collective-permute-start.18
  126.8 6.8 %parts.3 = (bf16[1152,256]{1,0:T(8,128)(2,1)}, bf16[1152,256]{1,0:T(8,128)(2,1)}, f32[1152,256]{1,0:T(8,128)}, f32[8,128]{1,0:T(8,128)S(1)}) custom-call(s32[9]{0:T(128)S(1)} %concatenate.3.refs_0_, bf16[9216,512]{1,0:T(8,128)(2,1)} %refs_1_.15, bf16[9216,512]{1,0:T(8,128)(2,1)} %collective-permute-done.6.refs_5_.refs_2_, bf16[512,256]{1,0:T(8,128)(2,1)S(1)} %copy-done.6, ...), custom_call_target="tpu_custom_call" | custom-call | flops 1 | bytes 1 | tf_op jit(solution)/shard_map/parts/pallas_call | solution.py:175
  133.6 6.3 %weight_grad.3 = (f32[2304,512]{1,0:T(8,128)}, f32[8,128]{1,0:T(8,128)S(1)}) custom-call(s32[9]{0:T(128)S(1)} %concatenate.3.refs_0_, bf16[4,272,1664]{2,1,0:T(8,128)(2,1)} %all-to-all-done.refs_1_.refs_3_.refs_0_, bf16[4,272,1664]{2,1,0:T(8,128)(2,1)} %collective-permute-done.17.refs_2_, bf16[4,272,1664]{2,1,0:T(8,128)(2,1)} %all-to-all-done.refs_1_.refs_3_.refs_0_, ...), custom_call_target="tpu_custom_call" | custom-call | flops 1 | bytes 1 | tf_op jit(solution)/shard_map/weight_grad/pallas_call | solution.py:175
  140.0 1.2 add.41
  141.8 1.8 join.3
  143.7 4.6 %collective-permute-start.25 = (bf16[1152,256]{1,0:T(8,128)(2,1)S(1)}, bf16[1152,256]{1,0:T(8,128)(2,1)S(1)}, u32[]{:S(2)}, u32[]{:S(2)}) collective-permute-start(bf16[1152,256]{1,0:T(8,128)(2,1)S(1)} %copy-done.12), channel_id=1, source_target_pairs={{0,2},{1,3},{6,4},{7,5},{8,10},{9,11},{14,12},{15,13},{16,18},{17,... | collective-permute-start | bytes 1769480 | tf_op jit(solution)/shard_map/ppermute | solution.py:736
  148.3 2.3 %collective-permute-start.28 = (bf16[2304,256]{1,0:T(8,128)(2,1)}, bf16[2304,256]{1,0:T(8,128)(2,1)}, u32[]{:S(2)}, u32[]{:S(2)}) collective-permute-start(bf16[2304,256]{1,0:T(8,128)(2,1)} %get-tuple-element.370), channel_id=1, source_target_pairs={{0,2},{1,3},{6,4},{7,5},{8,10},{9,11},{14,12},{15,13},{16,18},{17,... | collective-permute-start | bytes 3538952 | tf_op jit(solution)/shard_map/ppermute | solution.py:736
  151.3 1.3 collective-permute-start.23
  153.3 1.0 add.42
  154.2 7.8 %collective-permute-done.25.refs_1_ = bf16[1152,256]{1,0:T(8,128)(2,1)S(1)} collective-permute-done((bf16[1152,256]{1,0:T(8,128)(2,1)S(1)}, bf16[1152,256]{1,0:T(8,128)(2,1)S(1)}, u32[]{:S(2)}, u32[]{:S(2)}) %collective-permute-start.25) | collective-permute-done | bytes 589856 | tf_op jit(solution)/shard_map/ppermute | solution.py:736
  162.0 0.9 add.43
  163.0 1.5 collective-permute-start.30
  164.4 1.3 collective-permute-start.29
  165.8 1.3 collective-permute-start.27
  167.7 1.6 total_sums.1
  169.3 4.9 %weight_grad.4 = (f32[2304,512]{1,0:T(8,128)}, bf16[4,256,1152]{2,1,0:T(8,128)(2,1)}, f32[8,128]{1,0:T(8,128)S(1)}) custom-call(s32[9]{0:T(128)S(1)} %concatenate.3.refs_0_, bf16[4,272,1664]{2,1,0:T(8,128)(2,1)} %all-to-all-done.1.refs_1_.refs_2_, bf16[4,272,1664]{2,1,0:T(8,128)(2,1)} %all-to-all-done.1.refs_1_.refs_2_, f32[8,128]{1,0:T(8,128)S(1)} %get-tuple-element.377.refs_3_), custom_call_target="tpu_custom_call" | custom-call | flops 1 | bytes 1 | tf_op jit(solution)/shard_map/weight_grad/pallas_call | solution.py:175
  174.3 9.8 %collective-permute-done.29.refs_6_ = bf16[1152,256]{1,0:T(8,128)(2,1)} collective-permute-done((bf16[1152,256]{1,0:T(8,128)(2,1)}, bf16[1152,256]{1,0:T(8,128)(2,1)}, u32[]{:S(2)}, u32[]{:S(2)}) %collective-permute-start.29) | collective-permute-done | bytes 589856 | tf_op jit(solution)/shard_map/ppermute | solution.py:744
  184.1 1.9 collective-permute-done.28.refs_4_
  186.0 3.2 %finish.2 = (bf16[1152,256]{1,0:T(8,128)(2,1)}, f32[8,128]{1,0:T(8,128)S(1)}) custom-call(s32[9]{0:T(128)S(1)} %concatenate.3.refs_0_, s32[2,36]{1,0:T(2,128)S(1)} %copy-done.18, s32[1,256]{1,0:T(1,128)S(1)} %bitcast.17, f32[1152,256]{1,0:T(8,128)} %get-tuple-element.369.refs_3_, bf16[2304,256]{1,0:T(8,128)(2,1)} %collective-permute-done.28.refs_4_, ...), custom_call_target="tpu_custom_call" | custom-call | flops 1 | bytes 1 | tf_op jit(solution)/shard_map/finish/pallas_call | solution.py:175
  189.2 2.7 %collective-permute-done.27.refs_2_ = bf16[512,512]{1,0:T(8,128)(2,1)S(1)} collective-permute-done((bf16[512,512]{1,0:T(8,128)(2,1)S(1)}, bf16[512,512]{1,0:T(8,128)(2,1)S(1)}, u32[]{:S(2)}, u32[]{:S(2)}) %collective-permute-start.27) | collective-permute-done | bytes 524320 | tf_op jit(solution)/shard_map/ppermute | solution.py:744
  193.3 3.2 %finish.3 = (bf16[1152,256]{1,0:T(8,128)(2,1)}, f32[8,128]{1,0:T(8,128)S(1)}) custom-call(s32[9]{0:T(128)S(1)} %concatenate.3.refs_0_, s32[2,36]{1,0:T(2,128)S(1)} %copy-done.18, s32[1,256]{1,0:T(1,128)S(1)} %bitcast.18, f32[1152,256]{1,0:T(8,128)} %get-tuple-element.394.refs_3_, bf16[2304,256]{1,0:T(8,128)(2,1)} %collective-permute-done.28.refs_4_, ...), custom_call_target="tpu_custom_call" | custom-call | flops 1 | bytes 1 | tf_op jit(solution)/shard_map/finish/pallas_call | solution.py:175
  197.2 4.2 %weight_grad.5 = (f32[2304,512]{1,0:T(8,128)}, f32[8,128]{1,0:T(8,128)S(1)}) custom-call(s32[9]{0:T(128)S(1)} %concatenate.3.refs_0_, bf16[4,256,1152]{2,1,0:T(8,128)(2,1)S(1)} %collective-permute-done.33.refs_1_, bf16[4,272,1664]{2,1,0:T(8,128)(2,1)} %all-to-all-done.1.refs_1_.refs_2_, ...), custom_call_target="tpu_custom_call", output_to_operand_aliasing={{0}: (3, {})} | custom-call | flops 1 | bytes 1 | tf_op jit(solution)/shard_map/weight_grad/pallas_call | solution.py:175
  201.5 3.7 %lay_out.1 = (bf16[256,4096]{1,0:T(8,128)(2,1)}, bf16[256,4096]{1,0:T(8,128)(2,1)}, f32[8,128]{1,0:T(8,128)}) custom-call(s32[9]{0:T(128)S(1)} %concatenate.3.refs_0_, bf16[1024,512]{1,0:T(8,128)(2,1)S(1)} %get-tuple-element.388.refs_1_, bf16[1024,512]{1,0:T(8,128)(2,1)S(1)} %get-tuple-element.386.refs_2_, ...), custom_call_target="tpu_custom_call" | custom-call | flops 1 | bytes 1 | tf_op jit(solution)/shard_map/lay_out/pallas_call | solution.py:175
  (100 shorter events, 14.6 us)
Async XLA Ops:
  0.6 40.8 %collective-permute-start.5 = (bf16[9216,512]{1,0:T(8,128)(2,1)}, bf16[9216,512]{1,0:T(8,128)(2,1)}, u32[]{:S(2)}, u32[]{:S(2)}) collective-permute-start(bf16[9216,512]{1,0:T(8,128)(2,1)} %refs_1_.14), channel_id=1, source_target_pairs={{0,1},{1,0},{2,3},{3,2},{4,5},{5,4},{6,7},{7,6},{8,9},{9,8},{10,11... | collective-permute-start | bytes 28311560 | tf_op jit(solution)/shard_map/ppermute | solution.py:724
  1.2 40.3 %collective-permute-start.6 = (bf16[9216,512]{1,0:T(8,128)(2,1)}, bf16[9216,512]{1,0:T(8,128)(2,1)}, u32[]{:S(2)}, u32[]{:S(2)}) collective-permute-start(bf16[9216,512]{1,0:T(8,128)(2,1)} %refs_1_.15), channel_id=1, source_target_pairs={{0,1},{1,0},{2,3},{3,2},{4,5},{5,4},{6,7},{7,6},{8,9},{9,8},{10,11... | collective-permute-start | bytes 28311560 | tf_op jit(solution)/shard_map/ppermute | solution.py:724
  1.2 29.3 %collective-permute-start = (bf16[256,1152]{1,0:T(8,128)(2,1)}, bf16[256,1152]{1,0:T(8,128)(2,1)S(1)}, u32[]{:S(2)}, u32[]{:S(2)}) collective-permute-start(bf16[256,1152]{1,0:T(8,128)(2,1)} %refs_3_.5), channel_id=1, source_target_pairs={{0,2},{1,3},{2,0},{3,1},{4,6},{5,7},{6,4},{7,5},{8,10},{9,11},{10,... | collective-permute-start | bytes 1769480 | tf_op jit(solution)/shard_map/ppermute | solution.py:728
  4.2 28.8 %collective-permute-start.1 = (bf16[256,1152]{1,0:T(8,128)(2,1)}, bf16[256,1152]{1,0:T(8,128)(2,1)S(1)}, u32[]{:S(2)}, u32[]{:S(2)}) collective-permute-start(bf16[256,1152]{1,0:T(8,128)(2,1)} %refs_3_.5), channel_id=1, source_target_pairs={{0,4},{1,5},{2,6},{3,7},{4,0},{5,1},{6,2},{7,3},{8,12},{9,13},{10,... | collective-permute-start | bytes 1769480 | tf_op jit(solution)/shard_map/ppermute | solution.py:732
  6.8 0.7 copy-start.16
  7.5 0.7 copy-start.19
  30.5 0.8 copy-start.10
  33.1 16.4 %collective-permute-start.4 = (bf16[256,1152]{1,0:T(8,128)(2,1)S(1)}, bf16[256,1152]{1,0:T(8,128)(2,1)}, u32[]{:S(2)}, u32[]{:S(2)}) collective-permute-start(bf16[256,1152]{1,0:T(8,128)(2,1)S(1)} %collective-permute-done.1.refs_3_), channel_id=1, source_target_pairs={{0,2},{1,3},{2,0},{3,1},{4,6},{5,7},{6,4},{7,5},{8,10},{9,11},{10,... | collective-permute-start | bytes 1769480 | tf_op jit(solution)/shard_map/ppermute | solution.py:728
  33.5 25.3 %collective-permute-start.2 = (bf16[256,1152]{1,0:T(8,128)(2,1)S(1)}, bf16[256,1152]{1,0:T(8,128)(2,1)S(1)}, u32[]{:S(2)}, u32[]{:S(2)}) collective-permute-start(bf16[256,1152]{1,0:T(8,128)(2,1)S(1)} %get-tuple-element.216.refs_1_), channel_id=1, source_target_pairs={{0,2},{1,3},{2,0},{3,1},{4,6},{5,7},{6,4},{7,5},{8,10},{9,11},{10,... | collective-permute-start | bytes 1769480 | tf_op jit(solution)/shard_map/ppermute | solution.py:728
  35.1 23.7 %collective-permute-start.3 = (bf16[256,1152]{1,0:T(8,128)(2,1)S(1)}, bf16[256,1152]{1,0:T(8,128)(2,1)S(1)}, u32[]{:S(2)}, u32[]{:S(2)}) collective-permute-start(bf16[256,1152]{1,0:T(8,128)(2,1)S(1)} %get-tuple-element.216.refs_1_), channel_id=1, source_target_pairs={{2,4},{3,5},{4,2},{5,3},{10,12},{11,13},{12,10},{13,11},{18,20},{1... | collective-permute-start | bytes 1769480 | tf_op jit(solution)/shard_map/ppermute | solution.py:740
  36.6 1.1 copy-start.11
  37.6 0.7 copy-start.17
  38.3 0.7 copy-start.20
  46.7 11.8 %copy-start.3 = (bf16[2,1152,512]{2,1,0:T(8,128)(2,1)}, bf16[2,1152,512]{2,1,0:T(8,128)(2,1)S(1)}, u32[]{:S(2)}) copy-start(bf16[2,1152,512]{2,1,0:T(8,128)(2,1)S(1)} %get-tuple-element.258.refs_0_) | copy-start | bytes 7077892
  46.7 7.6 %copy-start.8 = (bf16[256,512]{1,0:T(8,128)(2,1)S(1)}, bf16[256,512]{1,0:T(8,128)(2,1)}, u32[]{:S(2)}) copy-start(bf16[256,512]{1,0:T(8,128)(2,1)} %refs_5_.3) | copy-start | bytes 786436
  46.7 7.6 %copy-start.9 = (bf16[256,512]{1,0:T(8,128)(2,1)S(1)}, bf16[256,512]{1,0:T(8,128)(2,1)}, u32[]{:S(2)}) copy-start(bf16[256,512]{1,0:T(8,128)(2,1)} %refs_6_.1) | copy-start | bytes 786436
  46.7 7.6 %copy-start.22 = (f32[4,512]{1,0:T(4,128)S(1)}, f32[4,512]{1,0:T(4,128)}, u32[]{:S(2)}) copy-start(f32[4,512]{1,0:T(4,128)} %refs_4_.7) | copy-start | bytes 24580
  46.7 7.6 %copy-start.23 = (f32[2,512]{1,0:T(2,128)S(1)}, f32[2,512]{1,0:T(2,128)}, u32[]{:S(2)}) copy-start(f32[2,512]{1,0:T(2,128)} %refs_3_.7) | copy-start | bytes 12292
  52.3 2.0 collective-permute-start.7
  58.8 5.6 %copy-start.7 = (bf16[512,256]{1,0:T(8,128)(2,1)S(1)}, bf16[512,256]{1,0:T(8,128)(2,1)}, u32[]{:S(2)}) copy-start(bf16[512,256]{1,0:T(8,128)(2,1)} %get-tuple-element.255.refs_1_.refs_3_) | copy-start | bytes 786436
  58.8 48.8 %all-to-all-start = ((bf16[4,272,1664]{2,1,0:T(8,128)(2,1)}), bf16[4,272,1664]{2,1,0:T(8,128)(2,1)}, u32[]{:S(2)}, u32[]{:S(2)}) async-start(bf16[4,272,1664]{2,1,0:T(8,128)(2,1)} %get-tuple-element.312), calls=%async_computation | async-start | bytes 7241728 | tf_op jit(solution)/shard_map/all_to_all | solution.py:748
  63.7 17.6 %collective-permute-start.8 = (bf16[256,1152]{1,0:T(8,128)(2,1)S(1)}, bf16[256,1152]{1,0:T(8,128)(2,1)S(1)}, u32[]{:S(2)}, u32[]{:S(2)}) collective-permute-start(bf16[256,1152]{1,0:T(8,128)(2,1)S(1)} %collective-permute-done.2.refs_2_), channel_id=1, source_target_pairs={{2,4},{3,5},{4,2},{5,3},{10,12},{11,13},{12,10},{13,11},{18,20},{1... | collective-permute-start | bytes 1769480 | tf_op jit(solution)/shard_map/ppermute | solution.py:740
  64.5 1.6 collective-permute-start.9
  64.5 22.8 %collective-permute-start.12 = (bf16[256,1152]{1,0:T(8,128)(2,1)S(1)}, bf16[256,1152]{1,0:T(8,128)(2,1)S(1)}, u32[]{:S(2)}, u32[]{:S(2)}) collective-permute-start(bf16[256,1152]{1,0:T(8,128)(2,1)S(1)} %collective-permute-done.3.refs_2_), channel_id=1, source_target_pairs={{2,0},{3,1},{4,6},{5,7},{10,8},{11,9},{12,14},{13,15},{18,16},{19,... | collective-permute-start | bytes 1769480 | tf_op jit(solution)/shard_map/ppermute | solution.py:744
  66.1 1.7 copy-start.4
  68.5 24.8 %collective-permute-start.11 = (bf16[1152,256]{1,0:T(8,128)(2,1)S(1)}, bf16[1152,256]{1,0:T(8,128)(2,1)S(1)}, u32[]{:S(2)}, u32[]{:S(2)}) collective-permute-start(bf16[1152,256]{1,0:T(8,128)(2,1)S(1)} %get-tuple-element.266), channel_id=1, source_target_pairs={{0,2},{1,3},{6,4},{7,5},{8,10},{9,11},{14,12},{15,13},{16,18},{17,... | collective-permute-start | bytes 1769480 | tf_op jit(solution)/shard_map/ppermute | solution.py:736
  81.4 17.2 %collective-permute-start.10 = (bf16[256,1152]{1,0:T(8,128)(2,1)S(1)}, bf16[256,1152]{1,0:T(8,128)(2,1)S(1)}, u32[]{:S(2)}, u32[]{:S(2)}) collective-permute-start(bf16[256,1152]{1,0:T(8,128)(2,1)S(1)} %collective-permute-done.8.refs_2_), channel_id=1, source_target_pairs={{2,0},{3,1},{4,6},{5,7},{10,8},{11,9},{12,14},{13,15},{18,16},{19,... | collective-permute-start | bytes 1769480 | tf_op jit(solution)/shard_map/ppermute | solution.py:744
  82.7 17.7 %collective-permute-start.14 = (bf16[1152,256]{1,0:T(8,128)(2,1)}, bf16[1152,256]{1,0:T(8,128)(2,1)S(1)}, u32[]{:S(2)}, u32[]{:S(2)}) collective-permute-start(bf16[1152,256]{1,0:T(8,128)(2,1)} %get-tuple-element.290.refs_0_), channel_id=1, source_target_pairs={{0,2},{1,3},{6,4},{7,5},{8,10},{9,11},{14,12},{15,13},{16,18},{17,... | collective-permute-start | bytes 1769480 | tf_op jit(solution)/shard_map/ppermute | solution.py:736
  93.3 8.1 %copy-start.1 = (bf16[2,1152,512]{2,1,0:T(8,128)(2,1)}, bf16[2,1152,512]{2,1,0:T(8,128)(2,1)S(1)}, u32[]{:S(2)}) copy-start(bf16[2,1152,512]{2,1,0:T(8,128)(2,1)S(1)} %get-tuple-element.310.refs_0_) | copy-start | bytes 7077892
  93.3 7.1 %copy-start.13 = (bf16[1152,256]{1,0:T(8,128)(2,1)S(1)}, bf16[1152,256]{1,0:T(8,128)(2,1)}, u32[]{:S(2)}) copy-start(bf16[1152,256]{1,0:T(8,128)(2,1)} %get-tuple-element.290.refs_0_) | copy-start | bytes 1769476
  93.3 9.0 %copy-start.15 = (f32[256,512]{1,0:T(8,128)S(1)}, f32[256,512]{1,0:T(8,128)}, u32[]{:S(2)}) copy-start(f32[256,512]{1,0:T(8,128)} %get-tuple-element.296.refs_2_) | copy-start | bytes 1572868
  94.3 12.4 %collective-permute-start.15 = (bf16[1152,256]{1,0:T(8,128)(2,1)}, bf16[1152,256]{1,0:T(8,128)(2,1)S(1)}, u32[]{:S(2)}, u32[]{:S(2)}) collective-permute-start(bf16[1152,256]{1,0:T(8,128)(2,1)} %get-tuple-element.300), channel_id=1, source_target_pairs={{2,4},{3,5},{4,2},{5,3},{10,12},{11,13},{12,10},{13,11},{18,20},{1... | collective-permute-start | bytes 1769480 | tf_op jit(solution)/shard_map/ppermute | solution.py:740
  100.3 6.3 %copy-start = (bf16[1152,256]{1,0:T(8,128)(2,1)S(1)}, bf16[1152,256]{1,0:T(8,128)(2,1)}, u32[]{:S(2)}) copy-start(bf16[1152,256]{1,0:T(8,128)(2,1)} %get-tuple-element.299.refs_0_.refs_2_.refs_3_) | copy-start | bytes 1769476
  100.3 2.0 collective-permute-start.13
  107.6 6.8 %collective-permute-start.17 = (bf16[4,272,1664]{2,1,0:T(8,128)(2,1)}, bf16[4,272,1664]{2,1,0:T(8,128)(2,1)}, u32[]{:S(2)}, u32[]{:S(2)}) collective-permute-start(bf16[4,272,1664]{2,1,0:T(8,128)(2,1)} %all-to-all-done.refs_1_.refs_3_.refs_0_), channel_id=1, source_target_pairs={{0,1},{1,0},{2,3},{3,2},{4,5},{5,4},{6,7},{7,6},{8,9},{9,8},{10,11... | collective-permute-start | bytes 10862600 | tf_op jit(solution)/shard_map/ppermute | solution.py:724
  107.8 5.0 %copy-start.6 = (bf16[512,256]{1,0:T(8,128)(2,1)S(1)}, bf16[512,256]{1,0:T(8,128)(2,1)}, u32[]{:S(2)}) copy-start(bf16[512,256]{1,0:T(8,128)(2,1)} %get-tuple-element.311.refs_1_.refs_3_) | copy-start | bytes 786436
  107.8 6.6 %copy-start.2 = (bf16[2,1152,512]{2,1,0:T(8,128)(2,1)S(1)}, bf16[2,1152,512]{2,1,0:T(8,128)(2,1)}, u32[]{:S(2)}) copy-start(bf16[2,1152,512]{2,1,0:T(8,128)(2,1)} %copy-done.1) | copy-start | bytes 7077892
  107.8 59.9 %all-to-all-start.1 = ((bf16[4,272,1664]{2,1,0:T(8,128)(2,1)}), bf16[4,272,1664]{2,1,0:T(8,128)(2,1)}, u32[]{:S(2)}, u32[]{:S(2)}) async-start(bf16[4,272,1664]{2,1,0:T(8,128)(2,1)} %get-tuple-element.373), calls=%async_computation.1 | async-start | bytes 7241728 | tf_op jit(solution)/shard_map/all_to_all | solution.py:748
  112.8 1.6 collective-permute-start.16
  113.2 26.7 %collective-permute-start.21 = (bf16[1152,256]{1,0:T(8,128)(2,1)}, bf16[1152,256]{1,0:T(8,128)(2,1)S(1)}, u32[]{:S(2)}, u32[]{:S(2)}) collective-permute-start(bf16[1152,256]{1,0:T(8,128)(2,1)} %get-tuple-element.331), channel_id=1, source_target_pairs={{2,4},{3,5},{4,2},{5,3},{10,12},{11,13},{12,10},{13,11},{18,20},{1... | collective-permute-start | bytes 1769480 | tf_op jit(solution)/shard_map/ppermute | solution.py:740
  115.2 24.8 %collective-permute-start.22 = (bf16[1152,256]{1,0:T(8,128)(2,1)}, bf16[1152,256]{1,0:T(8,128)(2,1)S(1)}, u32[]{:S(2)}, u32[]{:S(2)}) collective-permute-start(bf16[1152,256]{1,0:T(8,128)(2,1)} %get-tuple-element.332), channel_id=1, source_target_pairs={{2,0},{3,1},{4,6},{5,7},{10,8},{11,9},{12,14},{13,15},{18,16},{19,... | collective-permute-start | bytes 1769480 | tf_op jit(solution)/shard_map/ppermute | solution.py:744
  116.5 23.5 %collective-permute-start.20 = (bf16[1152,256]{1,0:T(8,128)(2,1)S(1)}, bf16[1152,256]{1,0:T(8,128)(2,1)S(1)}, u32[]{:S(2)}, u32[]{:S(2)}) collective-permute-start(bf16[1152,256]{1,0:T(8,128)(2,1)S(1)} %get-tuple-element.330), channel_id=1, source_target_pairs={{0,2},{1,3},{6,4},{7,5},{8,10},{9,11},{14,12},{15,13},{16,18},{17,... | collective-permute-start | bytes 1769480 | tf_op jit(solution)/shard_map/ppermute | solution.py:736
  124.3 26.3 %collective-permute-start.19 = (bf16[512,512]{1,0:T(8,128)(2,1)}, bf16[512,512]{1,0:T(8,128)(2,1)S(1)}, u32[]{:S(2)}, u32[]{:S(2)}) collective-permute-start(bf16[512,512]{1,0:T(8,128)(2,1)} %get-tuple-element.326.refs_1_), channel_id=1, source_target_pairs={{2,4},{3,5},{4,2},{5,3},{10,12},{11,13},{12,10},{13,11},{18,20},{1... | collective-permute-start | bytes 1572872 | tf_op jit(solution)/shard_map/ppermute | solution.py:740
  125.0 25.6 %collective-permute-start.18 = (bf16[512,512]{1,0:T(8,128)(2,1)}, bf16[512,512]{1,0:T(8,128)(2,1)S(1)}, u32[]{:S(2)}, u32[]{:S(2)}) collective-permute-start(bf16[512,512]{1,0:T(8,128)(2,1)} %get-tuple-element.326.refs_1_), channel_id=1, source_target_pairs={{0,2},{1,3},{2,0},{3,1},{4,6},{5,7},{6,4},{7,5},{8,10},{9,11},{10,... | collective-permute-start | bytes 1572872 | tf_op jit(solution)/shard_map/ppermute | solution.py:728
  133.5 8.3 %copy-start.5 = (bf16[1152,256]{1,0:T(8,128)(2,1)S(1)}, bf16[1152,256]{1,0:T(8,128)(2,1)}, u32[]{:S(2)}) copy-start(bf16[1152,256]{1,0:T(8,128)(2,1)} %get-tuple-element.328.refs_1_.refs_0_) | copy-start | bytes 1769476
  133.5 10.1 %copy-start.12 = (bf16[1152,256]{1,0:T(8,128)(2,1)S(1)}, bf16[1152,256]{1,0:T(8,128)(2,1)}, u32[]{:S(2)}) copy-start(bf16[1152,256]{1,0:T(8,128)(2,1)} %get-tuple-element.354.refs_0_) | copy-start | bytes 1769476
  133.6 19.0 %copy-start.14 = (bf16[512,512]{1,0:T(8,128)(2,1)S(1)}, bf16[512,512]{1,0:T(8,128)(2,1)}, u32[]{:S(2)}) copy-start(bf16[512,512]{1,0:T(8,128)(2,1)} %get-tuple-element.326.refs_1_) | copy-start | bytes 1572868
  139.9 25.9 %copy-start.24 = (bf16[1152,256]{1,0:T(8,128)(2,1)}, bf16[1152,256]{1,0:T(8,128)(2,1)S(1)}, u32[]{:S(2)}) copy-start(bf16[1152,256]{1,0:T(8,128)(2,1)S(1)} %collective-permute-done.21.refs_5_) | copy-start | bytes 1769476
  139.9 25.8 %copy-start.25 = (bf16[1152,256]{1,0:T(8,128)(2,1)}, bf16[1152,256]{1,0:T(8,128)(2,1)S(1)}, u32[]{:S(2)}) copy-start(bf16[1152,256]{1,0:T(8,128)(2,1)S(1)} %collective-permute-done.22.refs_6_) | copy-start | bytes 1769476
  141.1 12.1 %collective-permute-start.26 = (bf16[1152,256]{1,0:T(8,128)(2,1)}, bf16[1152,256]{1,0:T(8,128)(2,1)S(1)}, u32[]{:S(2)}, u32[]{:S(2)}) collective-permute-start(bf16[1152,256]{1,0:T(8,128)(2,1)} %get-tuple-element.355), channel_id=1, source_target_pairs={{2,4},{3,5},{4,2},{5,3},{10,12},{11,13},{12,10},{13,11},{18,20},{1... | collective-permute-start | bytes 1769480 | tf_op jit(solution)/shard_map/ppermute | solution.py:740
  143.7 18.4 %collective-permute-start.25 = (bf16[1152,256]{1,0:T(8,128)(2,1)S(1)}, bf16[1152,256]{1,0:T(8,128)(2,1)S(1)}, u32[]{:S(2)}, u32[]{:S(2)}) collective-permute-start(bf16[1152,256]{1,0:T(8,128)(2,1)S(1)} %copy-done.12), channel_id=1, source_target_pairs={{0,2},{1,3},{6,4},{7,5},{8,10},{9,11},{14,12},{15,13},{16,18},{17,... | collective-permute-start | bytes 1769480 | tf_op jit(solution)/shard_map/ppermute | solution.py:736
  148.3 37.7 %collective-permute-start.28 = (bf16[2304,256]{1,0:T(8,128)(2,1)}, bf16[2304,256]{1,0:T(8,128)(2,1)}, u32[]{:S(2)}, u32[]{:S(2)}) collective-permute-start(bf16[2304,256]{1,0:T(8,128)(2,1)} %get-tuple-element.370), channel_id=1, source_target_pairs={{0,2},{1,3},{6,4},{7,5},{8,10},{9,11},{14,12},{15,13},{16,18},{17,... | collective-permute-start | bytes 3538952 | tf_op jit(solution)/shard_map/ppermute | solution.py:736
  150.6 15.1 %collective-permute-start.24 = (bf16[512,512]{1,0:T(8,128)(2,1)S(1)}, bf16[512,512]{1,0:T(8,128)(2,1)S(1)}, u32[]{:S(2)}, u32[]{:S(2)}) collective-permute-start(bf16[512,512]{1,0:T(8,128)(2,1)S(1)} %collective-permute-done.18.refs_2_.refs_3_), channel_id=1, source_target_pairs={{2,4},{3,5},{4,2},{5,3},{10,12},{11,13},{12,10},{13,11},{18,20},{1... | collective-permute-start | bytes 1572872 | tf_op jit(solution)/shard_map/ppermute | solution.py:740
  151.3 14.5 %collective-permute-start.23 = (bf16[512,512]{1,0:T(8,128)(2,1)S(1)}, bf16[512,512]{1,0:T(8,128)(2,1)S(1)}, u32[]{:S(2)}, u32[]{:S(2)}) collective-permute-start(bf16[512,512]{1,0:T(8,128)(2,1)S(1)} %collective-permute-done.19.refs_3_), channel_id=1, source_target_pairs={{2,0},{3,1},{4,6},{5,7},{10,8},{11,9},{12,14},{13,15},{18,16},{19,... | collective-permute-start | bytes 1572872 | tf_op jit(solution)/shard_map/ppermute | solution.py:744
  163.0 11.3 %collective-permute-start.30 = (bf16[1152,256]{1,0:T(8,128)(2,1)}, bf16[1152,256]{1,0:T(8,128)(2,1)}, u32[]{:S(2)}, u32[]{:S(2)}) collective-permute-start(bf16[1152,256]{1,0:T(8,128)(2,1)} %get-tuple-element.372), channel_id=1, source_target_pairs={{2,4},{3,5},{4,2},{5,3},{10,12},{11,13},{12,10},{13,11},{18,20},{1... | collective-permute-start | bytes 1769480 | tf_op jit(solution)/shard_map/ppermute | solution.py:740
  164.4 19.6 %collective-permute-start.29 = (bf16[1152,256]{1,0:T(8,128)(2,1)}, bf16[1152,256]{1,0:T(8,128)(2,1)}, u32[]{:S(2)}, u32[]{:S(2)}) collective-permute-start(bf16[1152,256]{1,0:T(8,128)(2,1)} %get-tuple-element.371), channel_id=1, source_target_pairs={{2,0},{3,1},{4,6},{5,7},{10,8},{11,9},{12,14},{13,15},{18,16},{19,... | collective-permute-start | bytes 1769480 | tf_op jit(solution)/shard_map/ppermute | solution.py:744
  165.8 26.2 %collective-permute-start.27 = (bf16[512,512]{1,0:T(8,128)(2,1)S(1)}, bf16[512,512]{1,0:T(8,128)(2,1)S(1)}, u32[]{:S(2)}, u32[]{:S(2)}) collective-permute-start(bf16[512,512]{1,0:T(8,128)(2,1)S(1)} %collective-permute-done.24.refs_2_), channel_id=1, source_target_pairs={{2,0},{3,1},{4,6},{5,7},{10,8},{11,9},{12,14},{13,15},{18,16},{19,... | collective-permute-start | bytes 1572872 | tf_op jit(solution)/shard_map/ppermute | solution.py:744
  169.3 16.7 %copy-start.18 = (s32[2,36]{1,0:T(2,128)S(1)}, s32[2,36]{1,0:T(2,128)}, u32[]{:S(2)}) copy-start(s32[2,36]{1,0:T(2,128)} %refs_1_.17) | copy-start | bytes 868
  169.3 16.7 %copy-start.21 = (s32[256]{0:T(256)S(1)}, s32[256]{0:T(256)}, u32[]{:S(2)}) copy-start(s32[256]{0:T(256)} %param.13) | copy-start | bytes 3076
  174.3 18.4 %copy-start.26 = (bf16[4,256,1152]{2,1,0:T(8,128)(2,1)S(1)}, bf16[4,256,1152]{2,1,0:T(8,128)(2,1)}, u32[]{:S(2)}) copy-start(bf16[4,256,1152]{2,1,0:T(8,128)(2,1)} %get-tuple-element.392) | copy-start | bytes 7077892
  192.6 4.6 %collective-permute-start.33 = (bf16[4,256,1152]{2,1,0:T(8,128)(2,1)S(1)}, bf16[4,256,1152]{2,1,0:T(8,128)(2,1)S(1)}, u32[]{:S(2)}, u32[]{:S(2)}) collective-permute-start(bf16[4,256,1152]{2,1,0:T(8,128)(2,1)S(1)} %copy-done.26), channel_id=1, source_target_pairs={{0,1},{1,0},{2,3},{3,2},{4,5},{5,4},{6,7},{7,6},{8,9},{9,8},{10,11... | collective-permute-start | bytes 7077896 | tf_op jit(solution)/shard_map/ppermute | solution.py:724
  192.7 8.7 %collective-permute-start.31 = (bf16[1024,512]{1,0:T(8,128)(2,1)S(1)}, bf16[1024,512]{1,0:T(8,128)(2,1)S(1)}, u32[]{:S(2)}, u32[]{:S(2)}) collective-permute-start(bf16[1024,512]{1,0:T(8,128)(2,1)S(1)} %get-tuple-element.388.refs_1_), channel_id=1, source_target_pairs={{0,1},{1,0},{2,3},{3,2},{4,5},{5,4},{6,7},{7,6},{8,9},{9,8},{10,11... | collective-permute-start | bytes 3145736 | tf_op jit(solution)/shard_map/ppermute | solution.py:724
  193.2 8.2 %collective-permute-start.32 = (bf16[1024,512]{1,0:T(8,128)(2,1)S(1)}, bf16[1024,512]{1,0:T(8,128)(2,1)S(1)}, u32[]{:S(2)}, u32[]{:S(2)}) collective-permute-start(bf16[1024,512]{1,0:T(8,128)(2,1)S(1)} %get-tuple-element.386.refs_2_), channel_id=1, source_target_pairs={{0,1},{1,0},{2,3},{3,2},{4,5},{5,4},{6,7},{7,6},{8,9},{9,8},{10,11... | collective-permute-start | bytes 3145736 | tf_op jit(solution)/shard_map/ppermute | solution.py:724
